TPU v7x, 128 devices: a whole 4x4x4 slice. The times are simulated.
128 devices in a mesh: dp: 16 (over y, z), ctx: 8 (over x, core).
Axes of the slice: x: 4, y: 4, z: 4, core: 2. Of those that a mesh axis runs over, the one named last changes fastest.
Arguments:
- input_entries: bfloat16 [16, 2048, 8192], P('dp', 'ctx'), may hold values from -6 to 6
- segment_entry_counts: int32 [16, 8, 8], P('dp'), may hold values from 1 to 64, as said below
- segment_destination_part: int32 [16, 8, 8], P('dp'), may hold values from 0 to 7, as said below
- norm_gain: float32 [8192], replicated, may hold values from 0.25 to 1.75
- kv_weight: bfloat16 [8192, 2048], P('dp'), may hold values from -0.0625 to 0.0625
- kv_bias: float32 [2048], replicated, may hold values from -3 to 3
Outputs:
- evened_residual_entries: bfloat16 [16, 2048, 8192], P('dp', 'ctx')
- lookup_stored_tensors: bfloat16 [16, 2048, 2, 8, 128], P('dp', None, None, 'ctx')
Inputs may be any that keep to these rules, and one draw needn't show every extreme that they name: `segment_entry_counts`: in each sequence the runs of one shard cover its 256 rows; every shard receives exactly 256 rows; at most 64 rows go from one shard to one shard, and every sequence has a run of exactly 64. The numbers of rows between shards form a Latin arrangement: every shard sends the same list of 8 numbers, one to each shard, and receives each number of that list once. `segment_destination_part`: the 8 runs of one shard go to 8 different shards.
All inputs are finite; a program needn't handle non-finite values.
Results may differ from a plain program's by a relative error of at most 0.0046.
Values may be sent and summed in bfloat16 or wider, within the bound.
A program may use at most 192 MiB of HBM per device.

v0:
```python
import jax
import jax.numpy as jnp
from jax import lax
from jax.sharding import PartitionSpec as P

KVH = 8
HD = 128


def plan_tables(lengths, targets, peer_count):
    labels = jnp.arange(peer_count, dtype=jnp.int32)
    starts = jnp.cumsum(lengths, axis=1) - lengths
    matches = (targets[:, :, None] == labels[None, None, :]).astype(jnp.int32)
    counts = jnp.sum(lengths[:, :, None] * matches, axis=1)
    anchors = jnp.sum(starts[:, :, None] * matches, axis=1)
    run_ends = jnp.cumsum(counts, axis=0)
    offsets = run_ends - counts
    return (counts, anchors, offsets, run_ends)


def source_of(positions, ends_column, offsets_column, anchors_column, peer_count):
    labels = jnp.arange(peer_count, dtype=jnp.int32)
    source = jnp.sum((ends_column[None, :] <= positions[:, None]).astype(jnp.int32), axis=1)
    chosen = (source[:, None] == labels[None, :]).astype(jnp.int32)
    within = positions - jnp.sum(chosen * offsets_column[None, :], axis=1)
    anchor = jnp.sum(chosen * anchors_column[None, :], axis=1)
    return (source, within, anchor)


def rms_normed(rows, norm_gain):
    as_float = rows.astype(jnp.float32)
    inverse_rms = lax.rsqrt(jnp.mean(as_float * as_float, axis=-1, keepdims=True) + 1e-06)
    return (as_float * inverse_rms * norm_gain[None, :]).astype(jnp.bfloat16)


def pack_document_runs(rows, counts, anchors, myself, peer_count):
    row_count = rows.shape[0]
    capacity = 2 * row_count // peer_count
    slot_index = jnp.arange(capacity, dtype=jnp.int32)
    my_counts = counts[myself]
    my_anchors = anchors[myself]
    wanted = jnp.minimum(my_anchors[:, None] + slot_index[None, :], row_count - 1)
    is_live = slot_index[None, :] < my_counts[:, None]
    picked = jnp.take(rows, wanted.reshape(-1), axis=0).reshape(peer_count, capacity, -1)
    return jnp.where(is_live[:, :, None], picked, jnp.zeros_like(picked))


def unpack_runs(arriving_rows, positions, run_ends, offsets, anchors, myself, peer_count):
    capacity = arriving_rows.shape[1]
    source, within, anchor = source_of(
        positions, run_ends[:, myself], offsets[:, myself], anchors[:, myself], peer_count
    )
    flat_rows = arriving_rows.reshape(peer_count * capacity, -1)
    return jnp.take(flat_rows, source * capacity + within, axis=0)


def on_device(
    input_entries, segment_entry_counts, segment_destination_part, norm_gain, kv_weight, kv_bias
):
    peer_count = lax.axis_size("ctx")
    myself = lax.axis_index("ctx")
    row_count = input_entries.shape[1]
    counts, anchors, offsets, run_ends = plan_tables(
        segment_entry_counts[0], segment_destination_part[0], peer_count
    )
    positions = jnp.arange(row_count, dtype=jnp.int32)
    outgoing = pack_document_runs(input_entries[0], counts, anchors, myself, peer_count)
    arriving_rows = lax.all_to_all(outgoing, "ctx", split_axis=0, concat_axis=0, tiled=True)
    moved_rows = unpack_runs(
        arriving_rows, positions, run_ends, offsets, anchors, myself, peer_count
    )
    normed = rms_normed(moved_rows, norm_gain)
    summed_squares = jnp.dot(
        normed,
        lax.all_gather(kv_weight, "dp", axis=0, tiled=True),
        preferred_element_type=jnp.float32,
    )
    mapped_outputs = (
        (summed_squares + kv_bias[None, :]).astype(jnp.bfloat16).reshape(1, row_count, 2, KVH, HD)
    )
    by_heads = lax.all_to_all(mapped_outputs, "ctx", split_axis=3, concat_axis=1, tiled=True)
    return (moved_rows[None], by_heads)


def solution(mesh):
    in_specs = (
        P("dp", "ctx", None),
        P("dp", None, None),
        P("dp", None, None),
        P(),
        P("dp", None),
        P(),
    )
    out_specs = (P("dp", "ctx", None), P("dp", None, None, "ctx", None))
    return jax.shard_map(
        on_device, mesh=mesh, in_specs=in_specs, out_specs=out_specs, check_vma=False
    )
```

profile of v0, /device:TPU:1, one launch (start us, length us, event | category | flops | bytes accessed | tf_op | source)
XLA Modules:
  0.0 256.8 jit_solution(8461394061242989045)
XLA Ops:
  7.2 0.0 all-gather.2.cloned.1.call-start
  7.2 0.7 all-gather.2.cloned.1.call-update
  7.9 0.8 reduce_window_sum.23
  8.7 0.7 bitcast_subtract_fusion
  9.4 0.8 select_reduce_fusion.1
  10.3 0.1 add_minimum_fusion
  10.3 0.1 min.22
  10.4 18.2 %gather_fusion = bf16[512,8192]{1,0:T(8,128)(2,1)} fusion(bf16[256,8192]{1,0:T(8,128)(2,1)} %bitcast.28, s32[1024]{0:T(1024)S(1)} %pad_clamp_fusion.1), kind=kCustom, calls=%fused_computation | custom fusion | bytes 16779264 | tf_op jit(solution)/shard_map/jit(_take)/gather | solution.py:44
  28.6 0.1 compare_and_fusion
  28.7 0.1 iota_compare_fusion.3
  28.8 7.6 %select_select_fusion = bf16[8,64,8192]{2,1,0:T(8,128)(2,1)} fusion(bf16[8,64,8192]{2,1,0:T(8,128)(2,1)} %bitcast.29, pred[8,64]{1,0:T(8,128)(4,1)S(1)} %compare_and_fusion, pred[8,64]{1,0:T(8,128)(4,1)S(1)} %iota_compare_fusion.3), kind=kLoop, calls=%fused_computation.7 | loop fusion | flops 8388608 | bytes 16778240 | tf_op jit(solution)/shard_map/jit(_where)/select_n | solution.py:45
  36.4 6.3 %all-to-all-start = ((bf16[8,64,8192]{2,1,0:T(8,128)(2,1)}), bf16[8,64,8192]{2,1,0:T(8,128)(2,1)}, u32[]{:S(2)}, u32[]{:S(2)}) async-start(bf16[8,64,8192]{2,1,0:T(8,128)(2,1)} %select_select_fusion), calls=%async_computation | async-start | bytes 16777216 | tf_op jit(solution)/shard_map/all_to_all | solution.py:68
  42.7 0.2 dynamic-slice_reduce_fusion
  42.9 0.1 convert_reduce_fusion
  43.0 0.1 select_reduce_fusion.2
  43.1 93.4 %all-to-all-done = bf16[8,64,8192]{2,1,0:T(8,128)(2,1)} async-done(((bf16[8,64,8192]{2,1,0:T(8,128)(2,1)}), bf16[8,64,8192]{2,1,0:T(8,128)(2,1)}, u32[]{:S(2)}, u32[]{:S(2)}) %all-to-all-start) | async-done | bytes 8388640 | tf_op jit(solution)/shard_map/all_to_all | solution.py:68
  136.5 13.6 %gather_fusion.1 = bf16[256,8192]{1,0:T(8,128)(2,1)} fusion(bf16[512,8192]{1,0:T(8,128)(2,1)} %bitcast.7, s32[1024]{0:T(1024)S(1)} %pad_clamp_fusion), kind=kCustom, calls=%fused_computation.1 | custom fusion | bytes 8389632 | tf_op jit(solution)/shard_map/jit(_take)/gather | solution.py:54
  150.1 0.0 copy-start
  150.1 0.0 copy-start.1
  150.1 3.4 %fusion = f32[256]{0:T(256)S(1)} fusion(bf16[256,8192]{1,0:T(8,128)(2,1)} %gather_fusion.1, pred[256]{0:T(512)(128)(4,1)S(1)} %compare_and_fusion.1), kind=kLoop, calls=%fused_computation.4 | loop fusion | flops 8388352 | bytes 4195584 | tf_op jit(solution)/shard_map/reduce_sum | solution.py:32
  153.6 57.0 %all-gather.2.cloned.1.call-done = bf16[8192,2048]{1,0:T(8,128)(2,1)} async-done(((bf16[512,2048]{1,0:T(8,128)(2,1)}), bf16[8192,2048]{1,0:T(8,128)(2,1)}) %all-gather.2.cloned.1.call-update) | async-done | bytes 33554448 | tf_op jit(solution)/shard_map/all_gather | solution.py:75
  210.6 0.0 copy-done
  210.6 0.0 copy-done.1
  210.6 16.3 %fusion.13 = bf16[32,8,16,128]{3,1,2,0:T(8,128)(2,1)S(1)} fusion(bf16[8192,2048]{1,0:T(8,128)(2,1)} %all-gather.2.cloned.1.call-done, f32[8192]{0:T(1024)S(1)} %copy-done, f32[256]{0:T(256)S(1)} %add_rsqrt_fusion, bf16[256,8192]{1,0:T(8,128)(2,1)} %gather_fusion.1, pred[256]{0:T(512)(128)(4,1)S(1)} %compare_and_fusion.1, f32[2048]{0:T(1024)S(1)} %copy-done.1), kind=kOutput, calls=%fused_computation.15 | convolution fusion | flops 8601468928 | bytes 38839552 | tf_op jit(solution)/shard_map/dot_general | solution.py:73
  226.9 0.2 copy.14
  227.2 1.8 copy.12
  228.9 4.9 %all-to-all-start.1 = ((bf16[1,256,2,8,128]{4,2,1,0,3:T(2,128)(2,1)}), bf16[1,256,2,8,128]{4,2,1,0,3:T(2,128)(2,1)S(1)}, u32[]{:S(2)}, u32[]{:S(2)}) async-start(bf16[1,256,2,8,128]{4,2,1,0,3:T(2,128)(2,1)} %copy.12), calls=%async_computation.1 | async-start | bytes 2097152 | tf_op jit(solution)/shard_map/all_to_all | solution.py:81
  233.9 4.7 %bitcast_select_fusion = bf16[1,256,8192]{2,1,0:T(8,128)(2,1)} fusion(bf16[256,8192]{1,0:T(8,128)(2,1)} %gather_fusion.1, pred[256]{0:T(512)(128)(4,1)S(1)} %compare_and_fusion.1), kind=kLoop, calls=%fused_computation.9 | loop fusion | flops 2097152 | bytes 8388864 | tf_op jit(solution)/shard_map/jit(_take)/select_n | solution.py:54
  238.5 10.4 %all-to-all-done.1 = bf16[1,256,2,8,128]{4,2,1,0,3:T(2,128)(2,1)S(1)} async-done(((bf16[1,256,2,8,128]{4,2,1,0,3:T(2,128)(2,1)}), bf16[1,256,2,8,128]{4,2,1,0,3:T(2,128)(2,1)S(1)}, u32[]{:S(2)}, u32[]{:S(2)}) %all-to-all-start.1) | async-done | bytes 1048608 | tf_op jit(solution)/shard_map/all_to_all | solution.py:81
  249.0 1.0 copy.16
  (10 shorter events, 0.1 us)
Async XLA Ops:
  7.2 203.4 %all-gather.2.cloned.1.call-start = ((), (), s32[]{:S(2)}) async-start(), calls=%async_computation.2 | async-start | bytes 35651584 | tf_op jit(solution)/shard_map/all_gather | solution.py:75
  36.4 100.2 %all-to-all-start = ((bf16[8,64,8192]{2,1,0:T(8,128)(2,1)}), bf16[8,64,8192]{2,1,0:T(8,128)(2,1)}, u32[]{:S(2)}, u32[]{:S(2)}) async-start(bf16[8,64,8192]{2,1,0:T(8,128)(2,1)} %select_select_fusion), calls=%async_computation | async-start | bytes 16777216 | tf_op jit(solution)/shard_map/all_to_all | solution.py:68
  150.1 60.5 %copy-start = (f32[8192]{0:T(1024)S(1)}, f32[8192]{0:T(1024)}, u32[]{:S(2)}) copy-start(f32[8192]{0:T(1024)} %param.9) | copy-start | bytes 98308
  150.1 60.5 %copy-start.1 = (f32[2048]{0:T(1024)S(1)}, f32[2048]{0:T(1024)}, u32[]{:S(2)}) copy-start(f32[2048]{0:T(1024)} %param.11) | copy-start | bytes 24580
  228.9 20.0 %all-to-all-start.1 = ((bf16[1,256,2,8,128]{4,2,1,0,3:T(2,128)(2,1)}), bf16[1,256,2,8,128]{4,2,1,0,3:T(2,128)(2,1)S(1)}, u32[]{:S(2)}, u32[]{:S(2)}) async-start(bf16[1,256,2,8,128]{4,2,1,0,3:T(2,128)(2,1)} %copy.12), calls=%async_computation.1 | async-start | bytes 2097152 | tf_op jit(solution)/shard_map/all_to_all | solution.py:81
Sparse Core Ops, SparseCore 0:
  10.1 200.4 all-gather.1
where the time goes:
time: 257 us
  waiting for transfers between devices  162 us (63%)
  local copies, waits for them, and re-layouts  35.1 us (14%)
  other arithmetic  18.5 us (7%)
  matrix products  16.3 us (6%)
  between operations  14.1 us (5%)
  starting transfers between devices  11.3 us (4%)
    all_to_all x1, waiting for transfers between devices, on_device(): lax.all_to_all(outgoing, 'ctx', split_axis=0, concat_axis=0, tiled=True)  93.4 us
    all_gather x1, waiting for transfers between devices, on_device(): lax.all_gather(kv_weight, 'dp', axis=0, tiled=True)  57 us
    gather x1, local copies, waits for them, and re-layouts, pack_document_runs(): jnp.take(rows, wanted.reshape(-1), axis=0).reshape(peer_count, capacity, -1)  18.2 us
    dot_general x1, matrix products, on_device(): jnp.dot(normed, lax.all_gather(kv_weight, 'dp', axis=0, tiled=True), pref...  16.3 us
    gather x1, local copies, waits for them, and re-layouts, unpack_runs(): return jnp.take(flat_rows, source * capacity + within, axis=0)  13.6 us
    all_to_all x1, waiting for transfers between devices, on_device(): lax.all_to_all(mapped_outputs, 'ctx', split_axis=3, concat_axis=1, tiled=...  10.4 us
    select_n x1, other arithmetic, pack_document_runs(): return jnp.where(is_live[:, :, None], picked, jnp.zeros_like(picked))  7.59 us
    all_to_all x1, starting transfers between devices, on_device(): lax.all_to_all(outgoing, 'ctx', split_axis=0, concat_axis=0, tiled=True)  6.29 us
  transfers between devices with their start and end apart: 3, of which 3 were waited for; matrix products, arithmetic and copies ran while one was open for 20% of the time, Pallas kernels for 0%

commit v1 on v0

--- a/solution.py
+++ b/solution.py
@@ -1,7 +1,8 @@
 import jax
 import jax.numpy as jnp
+import numpy as np
 from jax import lax
-from jax.sharding import PartitionSpec as P
+from jax.sharding import Mesh, PartitionSpec as P
 
 KVH = 8
 HD = 128
@@ -54,44 +55,60 @@
     return jnp.take(flat_rows, source * capacity + within, axis=0)
 
 
+CTX = ("cx", "cc")
+
+
 def on_device(
     input_entries, segment_entry_counts, segment_destination_part, norm_gain, kv_weight, kv_bias
 ):
-    peer_count = lax.axis_size("ctx")
-    myself = lax.axis_index("ctx")
+    chips = lax.axis_size("cx")
+    cores = lax.axis_size("cc")
+    peer_count = chips * cores
+    core = lax.axis_index("cc")
+    myself = lax.axis_index("cx") * cores + core
     row_count = input_entries.shape[1]
+    width = kv_weight.shape[0]
+    heads_per_core = KVH // cores
+    local_weight = kv_weight.reshape(width, 2, heads_per_core, cores, HD)
+    local_weight = lax.dynamic_index_in_dim(local_weight, core, axis=3, keepdims=False)
+    local_weight = local_weight.reshape(width, 2 * heads_per_core * HD)
+    local_bias = lax.dynamic_index_in_dim(
+        kv_bias.reshape(2, heads_per_core, cores, HD), core, axis=2, keepdims=False
+    ).reshape(-1)
+    gathered_weight = lax.all_gather(local_weight, "dp", axis=0, tiled=True)
+
     counts, anchors, offsets, run_ends = plan_tables(
         segment_entry_counts[0], segment_destination_part[0], peer_count
     )
     positions = jnp.arange(row_count, dtype=jnp.int32)
     outgoing = pack_document_runs(input_entries[0], counts, anchors, myself, peer_count)
-    arriving_rows = lax.all_to_all(outgoing, "ctx", split_axis=0, concat_axis=0, tiled=True)
+    arriving_rows = lax.all_to_all(outgoing, CTX, split_axis=0, concat_axis=0, tiled=True)
     moved_rows = unpack_runs(
         arriving_rows, positions, run_ends, offsets, anchors, myself, peer_count
     )
     normed = rms_normed(moved_rows, norm_gain)
-    summed_squares = jnp.dot(
-        normed,
-        lax.all_gather(kv_weight, "dp", axis=0, tiled=True),
-        preferred_element_type=jnp.float32,
-    )
-    mapped_outputs = (
-        (summed_squares + kv_bias[None, :]).astype(jnp.bfloat16).reshape(1, row_count, 2, KVH, HD)
-    )
-    by_heads = lax.all_to_all(mapped_outputs, "ctx", split_axis=3, concat_axis=1, tiled=True)
+    chip_rows = lax.all_gather(normed, "cc", axis=0, tiled=True)
+    products = jnp.dot(chip_rows, gathered_weight, preferred_element_type=jnp.float32)
+    mapped = (products + local_bias[None, :]).astype(jnp.bfloat16)
+    mapped = mapped.reshape(1, cores * row_count, 2, heads_per_core, HD)
+    by_heads = lax.all_to_all(mapped, "cx", split_axis=3, concat_axis=1, tiled=True)
     return (moved_rows[None], by_heads)
 
 
 def solution(mesh):
+    dp_size, ctx_size = mesh.devices.shape
+    cores = 2
+    devices = np.asarray(mesh.devices).reshape(dp_size, ctx_size // cores, cores)
+    split_mesh = Mesh(devices, ("dp", "cx", "cc"))
     in_specs = (
-        P("dp", "ctx", None),
+        P("dp", CTX, None),
         P("dp", None, None),
         P("dp", None, None),
         P(),
         P("dp", None),
         P(),
     )
-    out_specs = (P("dp", "ctx", None), P("dp", None, None, "ctx", None))
+    out_specs = (P("dp", CTX, None), P("dp", None, None, CTX, None))
     return jax.shard_map(
-        on_device, mesh=mesh, in_specs=in_specs, out_specs=out_specs, check_vma=False
+        on_device, mesh=split_mesh, in_specs=in_specs, out_specs=out_specs, check_vma=False
     )

time: 257 us -> 349 us (1.36)
  waiting for transfers between devices: 162 us -> 246 us
  local copies, waits for them, and re-layouts: 35.1 us -> 39.5 us
  other arithmetic: 18.5 us -> 22.6 us
    all_gather x1 -> x2, waiting for transfers between devices: 57 us -> 144 us  [the longest x1 124 us: on_device(): gathered_weight = lax.all_gather(local_weight, 'dp', axis=0, tiled=True)]
    convert_element_type x0 -> x1, other arithmetic: none -> 3.88 us  [rms_normed(): return (as_float * inverse_rms * norm_gain[None, :]).astype(jnp.bfloat16)]
  transfers between devices with their start and end apart: 3 -> 4, of which waited for: 3 -> 4; matrix products, arithmetic and copies ran while one was open for 20% -> 3% of each run, Pallas kernels for 0% -> 0%
where the time goes in v1:
time: 349 us; the launch traced here: 347 us
  waiting for transfers between devices  246 us (70%)
  local copies, waits for them, and re-layouts  39.5 us (11%)
  other arithmetic  22.6 us (6%)
  matrix products  14.8 us (4%)
  between operations  14.1 us (4%)
  starting transfers between devices  10.6 us (3%)
    all_gather x1, waiting for transfers between devices, on_device(): gathered_weight = lax.all_gather(local_weight, 'dp', axis=0, tiled=True)  124 us
    all_to_all x1, waiting for transfers between devices, on_device(): lax.all_to_all(outgoing, CTX, split_axis=0, concat_axis=0, tiled=True)  93.4 us
    all_gather x1, waiting for transfers between devices, on_device(): chip_rows = lax.all_gather(normed, 'cc', axis=0, tiled=True)  19.6 us
    gather x1, local copies, waits for them, and re-layouts, pack_document_runs(): jnp.take(rows, wanted.reshape(-1), axis=0).reshape(peer_count, capacity, -1)  18.2 us
    dot_general x1, matrix products, on_device(): jnp.dot(chip_rows, gathered_weight, preferred_element_type=jnp.float32)  14.8 us
    gather x1, local copies, waits for them, and re-layouts, unpack_runs(): return jnp.take(flat_rows, source * capacity + within, axis=0)  13.5 us
    all_to_all x1, waiting for transfers between devices, on_device(): lax.all_to_all(mapped, 'cx', split_axis=3, concat_axis=1, tiled=True)  8.64 us
    select_n x1, other arithmetic, pack_document_runs(): return jnp.where(is_live[:, :, None], picked, jnp.zeros_like(picked))  7.62 us
  transfers between devices with their start and end apart: 4, of which 4 were waited for; matrix products, arithmetic and copies ran while one was open for 3% of the time, Pallas kernels for 0%

profile of v1, /device:TPU:1, one launch (start us, length us, event | category | flops | bytes accessed | tf_op | source)
XLA Modules:
  0.0 347.3 jit_solution(18176526704638708991)
XLA Ops:
  7.2 0.0 copy-start
  7.2 0.8 reduce_window_sum.23
  8.0 0.7 bitcast_subtract_fusion
  8.7 0.8 select_reduce_fusion.1
  9.5 0.1 add_minimum_fusion
  9.6 0.1 compare_and_fusion
  9.7 0.1 min.22
  9.8 0.1 iota_compare_fusion.3
  9.9 18.2 %gather_fusion = bf16[512,8192]{1,0:T(8,128)(2,1)} fusion(bf16[256,8192]{1,0:T(8,128)(2,1)} %bitcast.30, s32[1024]{0:T(1024)S(1)} %pad_clamp_fusion.1), kind=kCustom, calls=%fused_computation | custom fusion | bytes 16779264 | tf_op jit(solution)/shard_map/jit(_take)/gather | solution.py:45
  28.1 7.6 %select_select_fusion = bf16[8,64,8192]{2,1,0:T(8,128)(2,1)} fusion(bf16[8,64,8192]{2,1,0:T(8,128)(2,1)} %bitcast.31, pred[8,64]{1,0:T(8,128)(4,1)S(1)} %compare_and_fusion, pred[8,64]{1,0:T(8,128)(4,1)S(1)} %iota_compare_fusion.3), kind=kLoop, calls=%fused_computation.7 | loop fusion | flops 8388608 | bytes 16778240 | tf_op jit(solution)/shard_map/jit(_where)/select_n | solution.py:46
  35.7 6.3 %all-to-all-start = ((bf16[8,64,8192]{2,1,0:T(8,128)(2,1)}), bf16[8,64,8192]{2,1,0:T(8,128)(2,1)}, u32[]{:S(2)}, u32[]{:S(2)}) async-start(bf16[8,64,8192]{2,1,0:T(8,128)(2,1)} %select_select_fusion), calls=%async_computation | async-start | bytes 16777216 | tf_op jit(solution)/shard_map/all_to_all | solution.py:85
  42.0 0.0 all-gather.3.cloned.1.call-start
  42.1 0.2 dynamic-slice_reduce_fusion
  42.3 0.1 convert_reduce_fusion
  42.4 0.1 select_reduce_fusion.2
  42.5 93.4 %all-to-all-done = bf16[8,64,8192]{2,1,0:T(8,128)(2,1)} async-done(((bf16[8,64,8192]{2,1,0:T(8,128)(2,1)}), bf16[8,64,8192]{2,1,0:T(8,128)(2,1)}, u32[]{:S(2)}, u32[]{:S(2)}) %all-to-all-start) | async-done | bytes 8388640 | tf_op jit(solution)/shard_map/all_to_all | solution.py:85
  135.9 0.0 copy-start.2
  135.9 13.5 %gather_fusion.1 = bf16[256,8192]{1,0:T(8,128)(2,1)} fusion(bf16[512,8192]{1,0:T(8,128)(2,1)} %bitcast.7, s32[1024]{0:T(1024)S(1)} %pad_clamp_fusion), kind=kCustom, calls=%fused_computation.1 | custom fusion | bytes 8389632 | tf_op jit(solution)/shard_map/jit(_take)/gather | solution.py:55
  149.4 0.0 copy-start.1
  149.4 3.6 %fusion = f32[256]{0:T(256)S(1)} fusion(bf16[256,8192]{1,0:T(8,128)(2,1)} %gather_fusion.1, pred[256]{0:T(512)(128)(4,1)S(1)} %compare_and_fusion.1), kind=kLoop, calls=%fused_computation.4 | loop fusion | flops 8388352 | bytes 4195584 | tf_op jit(solution)/shard_map/reduce_sum | solution.py:33
  153.0 0.0 copy-done.2
  153.0 0.0 copy-done.1
  153.0 3.9 %fusion.2 = bf16[256,8192]{1,0:T(8,128)(2,1)} fusion(f32[8192]{0:T(1024)S(1)} %copy-done.2, f32[256]{0:T(256)S(1)} %add_rsqrt_fusion, bf16[256,8192]{1,0:T(8,128)(2,1)S(1)} %copy-done.1, pred[256]{0:T(512)(128)(4,1)S(1)} %compare_and_fusion.1), kind=kLoop, calls=%fused_computation.6 | loop fusion | flops 10485760 | bytes 8422656 | tf_op jit(solution)/shard_map/convert_element_type | solution.py:34
  156.9 0.0 all-gather.3.cloned.1.call-update
  156.9 0.3 all-gather.5.cloned.1.call-start
  157.2 2.9 copy.15
  160.0 1.1 constant_dynamic-slice_fusion.3
  161.1 0.0 all-gather.5.cloned.1.call-update
  161.1 0.0 copy-done
  161.2 19.6 %all-gather.3.cloned.1.call-done = bf16[512,8192]{1,0:T(8,128)(2,1)} async-done(((bf16[256,8192]{1,0:T(8,128)(2,1)}), bf16[512,8192]{1,0:T(8,128)(2,1)}) %all-gather.3.cloned.1.call-update) | async-done | bytes 8388624 | tf_op jit(solution)/shard_map/all_gather | solution.py:90
  180.8 124.0 %all-gather.5.cloned.1.call-done = bf16[8192,1024]{0,1:T(8,128)(2,1)} async-done(((bf16[512,1024]{0,1:T(8,128)(2,1)}), bf16[8192,1024]{0,1:T(8,128)(2,1)}) %all-gather.5.cloned.1.call-update) | async-done | bytes 16777232 | tf_op jit(solution)/shard_map/all_gather | solution.py:78
  304.8 14.8 %add_convert_fusion = bf16[512,1024]{1,0:T(8,128)(2,1)S(1)} fusion(bf16[512,8192]{1,0:T(8,128)(2,1)} %all-gather.3.cloned.1.call-done, bf16[8192,1024]{0,1:T(8,128)(2,1)} %all-gather.5.cloned.1.call-done, f32[1024]{0:T(1024)S(1)} %bitcast.42), kind=kOutput, calls=%fused_computation.10 | convolution fusion | flops 8590983168 | bytes 26218496 | tf_op jit(solution)/shard_map/dot_general | solution.py:91
  319.6 0.8 reshape.188
  320.4 1.8 copy.16
  322.2 4.0 %all-to-all-start.1 = ((bf16[1,512,2,4,128]{4,2,1,0,3:T(2,128)(2,1)}), bf16[1,512,2,4,128]{4,2,1,0,3:T(2,128)(2,1)S(1)}, u32[]{:S(2)}, u32[]{:S(2)}) async-start(bf16[1,512,2,4,128]{4,2,1,0,3:T(2,128)(2,1)} %copy.16), calls=%async_computation.1 | async-start | bytes 2097152 | tf_op jit(solution)/shard_map/all_to_all | solution.py:94
  326.1 4.7 %bitcast_select_fusion = bf16[1,256,8192]{2,1,0:T(8,128)(2,1)} fusion(bf16[256,8192]{1,0:T(8,128)(2,1)} %gather_fusion.1, pred[256]{0:T(512)(128)(4,1)S(1)} %compare_and_fusion.1), kind=kLoop, calls=%fused_computation.8 | loop fusion | flops 2097152 | bytes 8388864 | tf_op jit(solution)/shard_map/jit(_take)/select_n | solution.py:55
  330.8 8.6 %all-to-all-done.1 = bf16[1,512,2,4,128]{4,2,1,0,3:T(2,128)(2,1)S(1)} async-done(((bf16[1,512,2,4,128]{4,2,1,0,3:T(2,128)(2,1)}), bf16[1,512,2,4,128]{4,2,1,0,3:T(2,128)(2,1)S(1)}, u32[]{:S(2)}, u32[]{:S(2)}) %all-to-all-start.1) | async-done | bytes 1048608 | tf_op jit(solution)/shard_map/all_to_all | solution.py:94
  339.5 1.0 copy.19
  (11 shorter events, 0.1 us)
Async XLA Ops:
  7.2 154.0 %copy-start = (f32[2048]{0:T(1024)S(1)}, f32[2048]{0:T(1024)}, u32[]{:S(2)}) copy-start(f32[2048]{0:T(1024)} %param.11) | copy-start | bytes 24580
  35.7 100.2 %all-to-all-start = ((bf16[8,64,8192]{2,1,0:T(8,128)(2,1)}), bf16[8,64,8192]{2,1,0:T(8,128)(2,1)}, u32[]{:S(2)}, u32[]{:S(2)}) async-start(bf16[8,64,8192]{2,1,0:T(8,128)(2,1)} %select_select_fusion), calls=%async_computation | async-start | bytes 16777216 | tf_op jit(solution)/shard_map/all_to_all | solution.py:85
  42.0 138.8 %all-gather.3.cloned.1.call-start = ((), (), s32[]{:S(2)}) async-start(), calls=%async_computation.2 | async-start | bytes 12582912 | tf_op jit(solution)/shard_map/all_gather | solution.py:90
  135.9 17.1 %copy-start.2 = (f32[8192]{0:T(1024)S(1)}, f32[8192]{0:T(1024)}, u32[]{:S(2)}) copy-start(f32[8192]{0:T(1024)} %param.9) | copy-start | bytes 98308
  149.4 3.6 %copy-start.1 = (bf16[256,8192]{1,0:T(8,128)(2,1)S(1)}, bf16[256,8192]{1,0:T(8,128)(2,1)}, u32[]{:S(2)}) copy-start(bf16[256,8192]{1,0:T(8,128)(2,1)} %gather_fusion.1) | copy-start | bytes 12582916
  156.9 147.9 %all-gather.5.cloned.1.call-start = ((), (), s32[]{:S(2)}) async-start(), calls=%async_computation.3 | async-start | bytes 17825792 | tf_op jit(solution)/shard_map/all_gather | solution.py:78
  322.2 17.3 %all-to-all-start.1 = ((bf16[1,512,2,4,128]{4,2,1,0,3:T(2,128)(2,1)}), bf16[1,512,2,4,128]{4,2,1,0,3:T(2,128)(2,1)S(1)}, u32[]{:S(2)}, u32[]{:S(2)}) async-start(bf16[1,512,2,4,128]{4,2,1,0,3:T(2,128)(2,1)} %copy.16), calls=%async_computation.1 | async-start | bytes 2097152 | tf_op jit(solution)/shard_map/all_to_all | solution.py:94
Sparse Core Ops, SparseCore 0:
  157.0 23.7 all-gather.2
  183.5 121.2 all-gather.4

commit v2 on v1

--- a/solution.py
+++ b/solution.py
@@ -75,6 +75,9 @@
     local_bias = lax.dynamic_index_in_dim(
         kv_bias.reshape(2, heads_per_core, cores, HD), core, axis=2, keepdims=False
     ).reshape(-1)
+    local_weight, local_bias, input_entries = lax.optimization_barrier(
+        (local_weight, local_bias, input_entries)
+    )
     gathered_weight = lax.all_gather(local_weight, "dp", axis=0, tiled=True)
 
     counts, anchors, offsets, run_ends = plan_tables(
@@ -87,9 +90,17 @@
         arriving_rows, positions, run_ends, offsets, anchors, myself, peer_count
     )
     normed = rms_normed(moved_rows, norm_gain)
-    chip_rows = lax.all_gather(normed, "cc", axis=0, tiled=True)
-    products = jnp.dot(chip_rows, gathered_weight, preferred_element_type=jnp.float32)
-    mapped = (products + local_bias[None, :]).astype(jnp.bfloat16)
+    sibling_rows = lax.ppermute(normed, "cc", perm=[(0, 1), (1, 0)])
+
+    def project(rows):
+        products = jnp.dot(rows, gathered_weight, preferred_element_type=jnp.float32)
+        return (products + local_bias[None, :]).astype(jnp.bfloat16)
+
+    own = project(normed)
+    other = project(sibling_rows)
+    first = jnp.where(core == 0, own, other)
+    second = jnp.where(core == 0, other, own)
+    mapped = jnp.concatenate([first, second], axis=0)
     mapped = mapped.reshape(1, cores * row_count, 2, heads_per_core, HD)
     by_heads = lax.all_to_all(mapped, "cx", split_axis=3, concat_axis=1, tiled=True)
     return (moved_rows[None], by_heads)

time: 349 us -> 213 us (0.61)
  waiting for transfers between devices: 246 us -> 104 us
  matrix products: 14.8 us -> 23.1 us
    all_gather x1, waiting for transfers between devices: 124 us -> 0.01 us  [on_device(): gathered_weight = lax.all_gather(local_weight, 'dp', axis=0, tiled=True)]
    all_gather x1 -> x0, waiting for transfers between devices: 19.6 us -> none  [on_device(): chip_rows = lax.all_gather(normed, 'cc', axis=0, tiled=True)]
    dot_general x1 -> x2, matrix products: 14.8 us -> 23.1 us  [project(): jnp.dot(rows, gathered_weight, preferred_element_type=jnp.float32)]
  transfers between devices with their start and end apart: 4 -> 4, of which waited for: 4 -> 2; matrix products, arithmetic and copies ran while one was open for 3% -> 30% of each run, Pallas kernels for 0% -> 0%
where the time goes in v2:
time: 213 us; the launch traced here: 212 us
  waiting for transfers between devices  104 us (49%)
  local copies, waits for them, and re-layouts  39.5 us (19%)
  matrix products  23.1 us (11%)
  other arithmetic  20.6 us (10%)
  between operations  14.2 us (7%)
  starting transfers between devices  10.8 us (5%)
    all_to_all x1, waiting for transfers between devices, on_device(): lax.all_to_all(outgoing, CTX, split_axis=0, concat_axis=0, tiled=True)  93.4 us
    dot_general x2, matrix products, project(): jnp.dot(rows, gathered_weight, preferred_element_type=jnp.float32)  23.1 us
    gather x1, local copies, waits for them, and re-layouts, pack_document_runs(): jnp.take(rows, wanted.reshape(-1), axis=0).reshape(peer_count, capacity, -1)  18.2 us
    gather x1, local copies, waits for them, and re-layouts, unpack_runs(): return jnp.take(flat_rows, source * capacity + within, axis=0)  13.5 us
    all_to_all x1, waiting for transfers between devices, on_device(): lax.all_to_all(mapped, 'cx', split_axis=3, concat_axis=1, tiled=True)  10.6 us
    select_n x1, other arithmetic, pack_document_runs(): return jnp.where(is_live[:, :, None], picked, jnp.zeros_like(picked))  7.62 us
    all_to_all x1, starting transfers between devices, on_device(): lax.all_to_all(outgoing, CTX, split_axis=0, concat_axis=0, tiled=True)  6.34 us
    select_n x2, other arithmetic, unpack_runs(): return jnp.take(flat_rows, source * capacity + within, axis=0)  4.68 us
  transfers between devices with their start and end apart: 4, of which 2 were waited for; matrix products, arithmetic and copies ran while one was open for 30% of the time, Pallas kernels for 0%

profile of v2, /device:TPU:1, one launch (start us, length us, event | category | flops | bytes accessed | tf_op | source)
XLA Modules:
  0.0 212.1 jit_solution(627782510518240446)
XLA Ops:
  7.2 0.0 copy-start
  7.2 0.0 copy-start.3
  7.2 0.0 copy-start.5
  7.2 0.0 all-gather.2.cloned.1.call-start
  7.3 2.9 %copy.15 = bf16[512,2048]{0,1:T(8,128)(2,1)S(1)} copy(bf16[512,2048]{1,0:T(8,128)(2,1)} %param.10) | data formatting | bytes 4194304 | tf_op args[4]
  10.1 1.1 constant_dynamic-slice_fusion.1
  11.2 0.0 copy-done
  11.2 0.0 all-gather.2.cloned.1.call-update
  11.3 0.0 copy-done.3
  11.3 0.2 reduce_window_sum.23
  11.4 0.0 copy-done.5
  11.4 0.1 select_reduce_fusion.1
  11.6 0.1 add_minimum_fusion
  11.6 0.1 min.22
  11.7 18.2 %gather_fusion = bf16[512,8192]{1,0:T(8,128)(2,1)} fusion(bf16[256,8192]{1,0:T(8,128)(2,1)} %bitcast.32, s32[1024]{0:T(1024)S(1)} %pad_clamp_fusion.1), kind=kCustom, calls=%fused_computation | custom fusion | bytes 16779264 | tf_op jit(solution)/shard_map/jit(_take)/gather | solution.py:45
  29.9 0.1 compare_and_fusion
  30.0 0.1 iota_compare_fusion.3
  30.1 7.6 %select_select_fusion = bf16[8,64,8192]{2,1,0:T(8,128)(2,1)} fusion(bf16[8,64,8192]{2,1,0:T(8,128)(2,1)} %bitcast.33, pred[8,64]{1,0:T(8,128)(4,1)S(1)} %compare_and_fusion, pred[8,64]{1,0:T(8,128)(4,1)S(1)} %iota_compare_fusion.3), kind=kLoop, calls=%fused_computation.7 | loop fusion | flops 8388608 | bytes 16778240 | tf_op jit(solution)/shard_map/jit(_where)/select_n | solution.py:46
  37.7 6.3 %all-to-all-start = ((bf16[8,64,8192]{2,1,0:T(8,128)(2,1)}), bf16[8,64,8192]{2,1,0:T(8,128)(2,1)}, u32[]{:S(2)}, u32[]{:S(2)}) async-start(bf16[8,64,8192]{2,1,0:T(8,128)(2,1)} %select_select_fusion), calls=%async_computation | async-start | bytes 16777216 | tf_op jit(solution)/shard_map/all_to_all | solution.py:88
  44.1 0.2 dynamic-slice_reduce_fusion
  44.3 0.1 convert_reduce_fusion
  44.4 0.1 select_reduce_fusion.2
  44.5 93.4 %all-to-all-done = bf16[8,64,8192]{2,1,0:T(8,128)(2,1)} async-done(((bf16[8,64,8192]{2,1,0:T(8,128)(2,1)}), bf16[8,64,8192]{2,1,0:T(8,128)(2,1)}, u32[]{:S(2)}, u32[]{:S(2)}) %all-to-all-start) | async-done | bytes 8388640 | tf_op jit(solution)/shard_map/all_to_all | solution.py:88
  137.9 0.0 copy-start.4
  137.9 13.5 %gather_fusion.1 = bf16[256,8192]{1,0:T(8,128)(2,1)} fusion(bf16[512,8192]{1,0:T(8,128)(2,1)} %bitcast.11, s32[1024]{0:T(1024)S(1)} %pad_clamp_fusion), kind=kCustom, calls=%fused_computation.1 | custom fusion | bytes 8389632 | tf_op jit(solution)/shard_map/jit(_take)/gather | solution.py:55
  151.4 0.0 copy-start.2
  151.4 3.6 %fusion = f32[256]{0:T(256)S(1)} fusion(bf16[256,8192]{1,0:T(8,128)(2,1)} %gather_fusion.1, pred[256]{0:T(512)(128)(4,1)S(1)} %compare_and_fusion.1), kind=kLoop, calls=%fused_computation.4 | loop fusion | flops 8388352 | bytes 4195584 | tf_op jit(solution)/shard_map/reduce_sum | solution.py:33
  155.0 0.0 copy-done.4
  155.0 0.0 copy-done.2
  155.0 3.9 %fusion.2 = bf16[256,8192]{1,0:T(8,128)(2,1)} fusion(f32[8192]{0:T(1024)S(1)} %copy-done.4, f32[256]{0:T(256)S(1)} %add_rsqrt_fusion, bf16[256,8192]{1,0:T(8,128)(2,1)S(1)} %copy-done.2, pred[256]{0:T(512)(128)(4,1)S(1)} %compare_and_fusion.1), kind=kLoop, calls=%fused_computation.6 | loop fusion | flops 10485760 | bytes 8422656 | tf_op jit(solution)/shard_map/convert_element_type | solution.py:34
  158.9 0.9 collective-permute-start
  159.7 0.0 all-gather.2.cloned.1.call-done
  159.7 11.6 %fusion.3 = bf16[256,1024]{1,0:T(8,128)(2,1)S(1)} fusion(bf16[256,8192]{1,0:T(8,128)(2,1)} %fusion.2, bf16[8192,1024]{0,1:T(8,128)(2,1)} %all-gather.2.cloned.1.call-done, f32[1024]{0:T(1024)S(1)} %bitcast.44), kind=kOutput, calls=%fused_computation.12 | convolution fusion | flops 4295491584 | bytes 21499904 | tf_op jit(solution)/shard_map/dot_general | solution.py:96
  171.3 0.0 collective-permute-done
  171.3 11.6 %broadcast_select_fusion.2 = (bf16[256,1024]{1,0:T(8,128)(2,1)S(1)}, bf16[256,1024]{1,0:T(8,128)(2,1)S(1)}) fusion(bf16[256,1024]{1,0:T(8,128)(2,1)S(1)} %fusion.3, pred[]{:T(512)S(6)} %eq.39, f32[1024]{0:T(1024)S(1)} %bitcast.45, bf16[256,8192]{1,0:T(8,128)(2,1)} %collective-permute-done, bf16[8192,1024]{0,1:T(8,128)(2,1)} %all-gather.2.cloned.1.call-done), kind=kOutput, calls=%fused_computation.16 | convolution fusion | flops 4296015872 | bytes 22548480 | tf_op jit(solution)/shard_map/dot_general | solution.py:96
  182.9 0.1 pad_maximum_fusion
  183.0 0.8 reshape.192
  183.8 1.8 copy.16
  185.5 3.5 %all-to-all-start.1 = ((bf16[1,512,2,4,128]{4,2,1,0,3:T(2,128)(2,1)}), bf16[1,512,2,4,128]{4,2,1,0,3:T(2,128)(2,1)S(1)}, u32[]{:S(2)}, u32[]{:S(2)}) async-start(bf16[1,512,2,4,128]{4,2,1,0,3:T(2,128)(2,1)} %copy.16), calls=%async_computation.1 | async-start | bytes 2097152 | tf_op jit(solution)/shard_map/all_to_all | solution.py:105
  189.1 0.0 copy-start.1
  189.1 4.7 %bitcast_select_fusion = bf16[1,256,8192]{2,1,0:T(8,128)(2,1)} fusion(bf16[256,8192]{1,0:T(8,128)(2,1)} %gather_fusion.1, pred[256]{0:T(512)(128)(4,1)S(1)} %compare_and_fusion.1), kind=kLoop, calls=%fused_computation.8 | loop fusion | flops 2097152 | bytes 8388864 | tf_op jit(solution)/shard_map/jit(_take)/select_n | solution.py:55
  193.7 10.6 %all-to-all-done.1 = bf16[1,512,2,4,128]{4,2,1,0,3:T(2,128)(2,1)S(1)} async-done(((bf16[1,512,2,4,128]{4,2,1,0,3:T(2,128)(2,1)}), bf16[1,512,2,4,128]{4,2,1,0,3:T(2,128)(2,1)S(1)}, u32[]{:S(2)}, u32[]{:S(2)}) %all-to-all-start.1) | async-done | bytes 1048608 | tf_op jit(solution)/shard_map/all_to_all | solution.py:105
  204.3 1.0 copy.19
  205.3 0.0 copy-done.1
  (12 shorter events, 0.1 us)
Async XLA Ops:
  7.2 4.1 %copy-start = (f32[2048]{0:T(1024)S(1)}, f32[2048]{0:T(1024)}, u32[]{:S(2)}) copy-start(f32[2048]{0:T(1024)} %param.11) | copy-start | bytes 24580
  7.2 4.1 %copy-start.3 = (s32[1,8,8]{2,1,0:T(8,128)S(1)}, s32[1,8,8]{2,1,0:T(8,128)}, u32[]{:S(2)}) copy-start(s32[1,8,8]{2,1,0:T(8,128)} %param.7) | copy-start | bytes 772
  7.2 4.2 %copy-start.5 = (s32[1,8,8]{2,1,0:T(8,128)S(1)}, s32[1,8,8]{2,1,0:T(8,128)}, u32[]{:S(2)}) copy-start(s32[1,8,8]{2,1,0:T(8,128)} %param.8) | copy-start | bytes 772
  7.2 152.5 %all-gather.2.cloned.1.call-start = ((), (), s32[]{:S(2)}) async-start(), calls=%async_computation.2 | async-start | bytes 17825792 | tf_op jit(solution)/shard_map/all_gather | solution.py:81
  37.7 100.2 %all-to-all-start = ((bf16[8,64,8192]{2,1,0:T(8,128)(2,1)}), bf16[8,64,8192]{2,1,0:T(8,128)(2,1)}, u32[]{:S(2)}, u32[]{:S(2)}) async-start(bf16[8,64,8192]{2,1,0:T(8,128)(2,1)} %select_select_fusion), calls=%async_computation | async-start | bytes 16777216 | tf_op jit(solution)/shard_map/all_to_all | solution.py:88
  137.9 17.1 %copy-start.4 = (f32[8192]{0:T(1024)S(1)}, f32[8192]{0:T(1024)}, u32[]{:S(2)}) copy-start(f32[8192]{0:T(1024)} %param.9) | copy-start | bytes 98308
  151.4 3.6 %copy-start.2 = (bf16[256,8192]{1,0:T(8,128)(2,1)S(1)}, bf16[256,8192]{1,0:T(8,128)(2,1)}, u32[]{:S(2)}) copy-start(bf16[256,8192]{1,0:T(8,128)(2,1)} %gather_fusion.1) | copy-start | bytes 12582916
  158.9 12.4 %collective-permute-start = (bf16[256,8192]{1,0:T(8,128)(2,1)}, bf16[256,8192]{1,0:T(8,128)(2,1)}, u32[]{:S(2)}, u32[]{:S(2)}) collective-permute-start(bf16[256,8192]{1,0:T(8,128)(2,1)} %fusion.2), channel_id=1, source_target_pairs={{0,1},{1,0},{2,3},{3,2},{4,5},{5,4},{6,7},{7,6},{8,9},{9,8},{10,11... | collective-permute-start | bytes 12582920 | tf_op jit(solution)/shard_map/ppermute | solution.py:93
  185.5 18.8 %all-to-all-start.1 = ((bf16[1,512,2,4,128]{4,2,1,0,3:T(2,128)(2,1)}), bf16[1,512,2,4,128]{4,2,1,0,3:T(2,128)(2,1)S(1)}, u32[]{:S(2)}, u32[]{:S(2)}) async-start(bf16[1,512,2,4,128]{4,2,1,0,3:T(2,128)(2,1)} %copy.16), calls=%async_computation.1 | async-start | bytes 2097152 | tf_op jit(solution)/shard_map/all_to_all | solution.py:105
  189.1 16.2 %copy-start.1 = (f32[2048]{0:T(1024)S(1)}, f32[2048]{0:T(1024)}, u32[]{:S(2)}) copy-start(f32[2048]{0:T(1024)} %param.11) | copy-start | bytes 24580
Sparse Core Ops, SparseCore 0:
  11.4 123.5 all-gather.1

commit v3 on v1

--- a/solution.py
+++ b/solution.py
@@ -38,12 +38,9 @@
     row_count = rows.shape[0]
     capacity = 2 * row_count // peer_count
     slot_index = jnp.arange(capacity, dtype=jnp.int32)
-    my_counts = counts[myself]
     my_anchors = anchors[myself]
     wanted = jnp.minimum(my_anchors[:, None] + slot_index[None, :], row_count - 1)
-    is_live = slot_index[None, :] < my_counts[:, None]
-    picked = jnp.take(rows, wanted.reshape(-1), axis=0).reshape(peer_count, capacity, -1)
-    return jnp.where(is_live[:, :, None], picked, jnp.zeros_like(picked))
+    return jnp.take(rows, wanted.reshape(-1), axis=0, mode="clip").reshape(peer_count, capacity, -1)
 
 
 def unpack_runs(arriving_rows, positions, run_ends, offsets, anchors, myself, peer_count):
@@ -52,7 +49,19 @@
         positions, run_ends[:, myself], offsets[:, myself], anchors[:, myself], peer_count
     )
     flat_rows = arriving_rows.reshape(peer_count * capacity, -1)
-    return jnp.take(flat_rows, source * capacity + within, axis=0)
+    return jnp.take(flat_rows, source * capacity + within, axis=0, mode="clip")
+
+
+def gather_map(run_ends, offsets, anchors, row_count, peer_count):
+    positions = jnp.arange(row_count, dtype=jnp.int32)
+
+    def for_shard(shard):
+        source, within, anchor = source_of(
+            positions, run_ends[:, shard], offsets[:, shard], anchors[:, shard], peer_count
+        )
+        return source * row_count + anchor + within
+
+    return jax.vmap(for_shard)(jnp.arange(peer_count, dtype=jnp.int32)).reshape(-1)
 
 
 CTX = ("cx", "cc")
@@ -71,28 +80,45 @@
     heads_per_core = KVH // cores
     local_weight = kv_weight.reshape(width, 2, heads_per_core, cores, HD)
     local_weight = lax.dynamic_index_in_dim(local_weight, core, axis=3, keepdims=False)
-    local_weight = local_weight.reshape(width, 2 * heads_per_core * HD)
+    local_weight = jnp.transpose(local_weight, (2, 0, 1, 3)).reshape(
+        heads_per_core, width, 2 * HD
+    )
     local_bias = lax.dynamic_index_in_dim(
         kv_bias.reshape(2, heads_per_core, cores, HD), core, axis=2, keepdims=False
-    ).reshape(-1)
-    gathered_weight = lax.all_gather(local_weight, "dp", axis=0, tiled=True)
+    )
+    local_bias = jnp.transpose(local_bias, (1, 0, 2)).reshape(heads_per_core, 2 * HD)
+    local_weight, local_bias, input_entries = lax.optimization_barrier(
+        (local_weight, local_bias, input_entries)
+    )
+    rows = input_entries[0]
+
+    normed = rms_normed(rows, norm_gain)
+    sibling_rows = lax.ppermute(normed, "cc", perm=[(0, 1), (1, 0)])
+    blocks = []
+    for head in range(heads_per_core):
+        head_weight = lax.all_gather(local_weight[head], "dp", axis=0, tiled=True)
+        own = jnp.dot(normed, head_weight, preferred_element_type=jnp.float32)
+        other = jnp.dot(sibling_rows, head_weight, preferred_element_type=jnp.float32)
+        own = (own + local_bias[head][None, :]).astype(jnp.bfloat16)
+        other = (other + local_bias[head][None, :]).astype(jnp.bfloat16)
+        first = jnp.where(core == 0, own, other)
+        second = jnp.where(core == 0, other, own)
+        blocks.append(jnp.concatenate([first, second], axis=0))
+    mapped = jnp.stack(blocks, axis=1).reshape(1, cores * row_count, heads_per_core, 2, HD)
+    by_heads = lax.all_to_all(mapped, "cx", split_axis=2, concat_axis=1, tiled=True)
 
     counts, anchors, offsets, run_ends = plan_tables(
         segment_entry_counts[0], segment_destination_part[0], peer_count
     )
     positions = jnp.arange(row_count, dtype=jnp.int32)
-    outgoing = pack_document_runs(input_entries[0], counts, anchors, myself, peer_count)
+    outgoing = pack_document_runs(rows, counts, anchors, myself, peer_count)
     arriving_rows = lax.all_to_all(outgoing, CTX, split_axis=0, concat_axis=0, tiled=True)
     moved_rows = unpack_runs(
         arriving_rows, positions, run_ends, offsets, anchors, myself, peer_count
     )
-    normed = rms_normed(moved_rows, norm_gain)
-    chip_rows = lax.all_gather(normed, "cc", axis=0, tiled=True)
-    products = jnp.dot(chip_rows, gathered_weight, preferred_element_type=jnp.float32)
-    mapped = (products + local_bias[None, :]).astype(jnp.bfloat16)
-    mapped = mapped.reshape(1, cores * row_count, 2, heads_per_core, HD)
-    by_heads = lax.all_to_all(mapped, "cx", split_axis=3, concat_axis=1, tiled=True)
-    return (moved_rows[None], by_heads)
+    order = gather_map(run_ends, offsets, anchors, row_count, peer_count)
+    evened = jnp.take(by_heads.reshape(peer_count * row_count, 2, HD), order, axis=0, mode="clip")
+    return (moved_rows[None], evened.reshape(1, peer_count * row_count, 2, 1, HD))
 
 
 def solution(mesh):

time: 349 us -> 300 us (0.86)
  waiting for transfers between devices: 246 us -> 178 us
  matrix products: 14.8 us -> 33.5 us
  local copies, waits for them, and re-layouts: 39.5 us -> 52 us
  other arithmetic: 22.6 us -> 10.3 us
    all_to_all x1, waiting for transfers between devices: 93.4 us -> 0.01 us  [on_device(): lax.all_to_all(outgoing, CTX, split_axis=0, concat_axis=0, tiled=True)]
    all_gather x2 -> x4, waiting for transfers between devices: 144 us -> 176 us  [on_device(): head_weight = lax.all_gather(local_weight[head], 'dp', axis=0, tiled=True)]
    dot_general x1 -> x8, matrix products: 14.8 us -> 33.5 us  [the longest x4 19.5 us: on_device(): own = jnp.dot(normed, head_weight, preferred_element_type=jnp.float32)]
    gather x2 -> x6, local copies, waits for them, and re-layouts: 31.7 us -> 47.3 us  [the longest x1 18.2 us: pack_document_runs(): jnp.take(rows, wanted.reshape(-1), axis=0, mode='clip')]
    select_n x4 -> x0, other arithmetic: 12.3 us -> none  [the longest x1 7.62 us: pack_document_runs(): return jnp.where(is_live[:, :, None], picked, jnp.zeros_like(picked))]
    all_to_all x1, waiting for transfers between devices: 8.64 us -> 0.01 us  [on_device(): lax.all_to_all(mapped, 'cx', split_axis=2, concat_axis=1, tiled=True)]
  transfers between devices with their start and end apart: 4 -> 7, of which waited for: 4 -> 4; matrix products, arithmetic and copies ran while one was open for 3% -> 26% of each run, Pallas kernels for 0% -> 0%
where the time goes in v3:
time: 300 us; the launch traced here: 298 us
  waiting for transfers between devices  178 us (59%)
  local copies, waits for them, and re-layouts  52 us (17%)
  matrix products  33.5 us (11%)
  between operations  14.1 us (5%)
  starting transfers between devices  10.7 us (4%)
  other arithmetic  10.3 us (3%)
    all_gather x4, waiting for transfers between devices, on_device(): head_weight = lax.all_gather(local_weight[head], 'dp', axis=0, tiled=True)  176 us
    dot_general x4, matrix products, on_device(): own = jnp.dot(normed, head_weight, preferred_element_type=jnp.float32)  19.5 us
    gather x1, local copies, waits for them, and re-layouts, pack_document_runs(): jnp.take(rows, wanted.reshape(-1), axis=0, mode='clip')  18.2 us
    dot_general x4, matrix products, on_device(): jnp.dot(sibling_rows, head_weight, preferred_element_type=jnp.float32)  14 us
    gather x1, local copies, waits for them, and re-layouts, on_device(): jnp.take(by_heads.reshape(peer_count * row_count, 2, HD), order, axis=0,...  13.9 us
    gather x1, local copies, waits for them, and re-layouts, unpack_runs(): return jnp.take(flat_rows, source * capacity + within, axis=0, mode='clip')  13.5 us
  transfers between devices with their start and end apart: 7, of which 4 were waited for; matrix products, arithmetic and copies ran while one was open for 26% of the time, Pallas kernels for 0%

profile of v3, /device:TPU:1, one launch (start us, length us, event | category | flops | bytes accessed | tf_op | source)
XLA Modules:
  0.0 298.1 jit_solution(14663585255499715846)
XLA Ops:
  7.2 0.0 copy-start
  7.2 0.0 all-gather.9.cloned.1.call-start
  7.2 2.9 copy.19
  10.1 0.1 dynamic-slice_bitcast_fusion
  10.2 0.1 copy.21
  10.3 0.0 copy-done
  10.3 0.0 copy-start.3
  10.3 1.0 fusion.70
  11.3 0.0 all-gather.9.cloned.1.call-update
  11.3 0.0 all-gather.11.cloned.1.call-start
  11.4 0.7 all-gather.11.cloned.1.call-update
  12.1 0.0 all-gather.13.cloned.1.call-start
  12.1 0.7 all-gather.13.cloned.1.call-update
  12.8 0.0 all-gather.15.cloned.1.call-start
  12.8 0.5 all-gather.15.cloned.1.call-update
  13.4 0.0 copy-start.1
  13.4 3.3 %fusion = f32[256]{0:T(256)S(1)} fusion(bf16[1,256,8192]{2,1,0:T(8,128)(2,1)} %param.6), kind=kLoop, calls=%fused_computation.8 | loop fusion | flops 6291200 | bytes 4195328 | tf_op jit(solution)/shard_map/reduce_sum | solution.py:33
  16.7 0.0 copy-done.3
  16.7 0.2 copy-done.1
  16.8 3.2 %fusion.2 = bf16[256,8192]{1,0:T(8,128)(2,1)} fusion(f32[8192]{0:T(1024)S(1)} %copy-done.3, f32[256]{0:T(256)S(1)} %add_rsqrt_fusion, bf16[1,256,8192]{2,1,0:T(8,128)(2,1)S(1)} %copy-done.1), kind=kLoop, calls=%fused_computation.10 | loop fusion | flops 8388608 | bytes 8422400 | tf_op jit(solution)/shard_map/convert_element_type | solution.py:34
  20.0 1.4 collective-permute-start
  21.4 0.0 copy-done.2
  21.4 0.2 reduce_window_sum.25
  21.6 0.0 copy-done.4
  21.6 0.1 select_reduce_fusion.2
  21.7 0.1 add_minimum_fusion
  21.8 0.1 reshape.180
  21.9 18.2 %gather_fusion = bf16[512,8192]{1,0:T(8,128)(2,1)} fusion(bf16[256,8192]{1,0:T(8,128)(2,1)} %bitcast.116, s32[1024]{0:T(1024)S(1)} %pad_clamp_fusion.1), kind=kCustom, calls=%fused_computation | custom fusion | bytes 16779264 | tf_op jit(solution)/shard_map/jit(_take)/gather | solution.py:43
  40.1 5.1 %all-to-all-start = ((bf16[8,64,8192]{2,1,0:T(8,128)(2,1)}), bf16[8,64,8192]{2,1,0:T(8,128)(2,1)}, u32[]{:S(2)}, u32[]{:S(2)}) async-start(bf16[8,64,8192]{2,1,0:T(8,128)(2,1)} %bitcast.117), calls=%async_computation | async-start | bytes 16777216 | tf_op jit(solution)/shard_map/all_to_all | solution.py:115
  45.2 0.1 copy.28
  45.3 0.1 copy.22
  45.4 0.2 reduce_window_sum.26
  45.6 0.6 gather_fusion.2
  46.1 0.6 gather_fusion.4
  46.7 0.6 gather_fusion.3
  47.3 0.1 convert_reduce_fusion.1
  47.3 0.1 convert_reduce_fusion
  47.4 0.1 select_reduce_fusion.1
  47.6 24.0 %all-gather.9.cloned.1.call-done = bf16[1,8192,256]{1,2,0:T(8,128)(2,1)} async-done(((bf16[1,512,256]{1,2,0:T(8,128)(2,1)}), bf16[1,8192,256]{1,2,0:T(8,128)(2,1)}) %all-gather.9.cloned.1.call-update) | async-done | bytes 4194320 | tf_op jit(solution)/shard_map/all_gather | solution.py:99
  71.5 4.9 %fusion.64 = bf16[256,256]{1,0:T(8,128)(2,1)S(1)} fusion(bf16[256,8192]{1,0:T(8,128)(2,1)} %fusion.2, bf16[1,8192,256]{1,2,0:T(8,128)(2,1)} %all-gather.9.cloned.1.call-done, f32[256]{0:T(256)S(1)} %bitcast.141), kind=kOutput, calls=%fused_computation.42 | convolution fusion | flops 1073872896 | bytes 8520704 | tf_op jit(solution)/shard_map/dot_general | solution.py:100
  76.4 0.0 collective-permute-done
  76.4 0.0 copy-done.8
  76.4 3.5 %broadcast_select_fusion.7 = (bf16[256,256]{1,0:T(8,128)(2,1)S(1)}, bf16[256,256]{1,0:T(8,128)(2,1)S(1)}) fusion(bf16[256,256]{1,0:T(8,128)(2,1)S(1)} %fusion.64, pred[]{:T(512)S(6)} %eq.58, f32[256]{0:T(256)S(1)} %bitcast.142, bf16[256,8192]{1,0:T(8,128)(2,1)} %collective-permute-done, bf16[1,8192,256]{1,2,0:T(8,128)(2,1)S(1)} %copy-done.8), kind=kOutput, calls=%fused_computation.56 | convolution fusion | flops 1074003968 | bytes 8782849 | tf_op jit(solution)/shard_map/dot_general | solution.py:101
  80.0 0.1 stack.15
  80.0 50.6 %all-gather.11.cloned.1.call-done = bf16[1,8192,256]{1,2,0:T(8,128)(2,1)} async-done(((bf16[1,512,256]{1,2,0:T(8,128)(2,1)}), bf16[1,8192,256]{1,2,0:T(8,128)(2,1)}) %all-gather.11.cloned.1.call-update) | async-done | bytes 4194320 | tf_op jit(solution)/shard_map/all_gather | solution.py:99
  130.6 4.9 %fusion.58 = bf16[256,256]{1,0:T(8,128)(2,1)S(1)} fusion(bf16[256,8192]{1,0:T(8,128)(2,1)} %fusion.2, bf16[1,8192,256]{1,2,0:T(8,128)(2,1)} %all-gather.11.cloned.1.call-done, f32[256]{0:T(256)S(1)} %bitcast.139), kind=kOutput, calls=%fused_computation.40 | convolution fusion | flops 1073872896 | bytes 8520704 | tf_op jit(solution)/shard_map/dot_general | solution.py:100
  135.5 3.5 %broadcast_select_fusion.5 = (bf16[256,256]{1,0:T(8,128)(2,1)S(1)}, bf16[256,256]{1,0:T(8,128)(2,1)S(1)}) fusion(bf16[256,256]{1,0:T(8,128)(2,1)S(1)} %fusion.58, pred[]{:T(512)S(6)} %eq.58, f32[256]{0:T(256)S(1)} %bitcast.140, bf16[256,8192]{1,0:T(8,128)(2,1)} %collective-permute-done, bf16[1,8192,256]{1,2,0:T(8,128)(2,1)S(1)} %copy-done.7), kind=kOutput, calls=%fused_computation.54 | convolution fusion | flops 1074003968 | bytes 8782849 | tf_op jit(solution)/shard_map/dot_general | solution.py:101
  139.1 0.1 stack.16
  139.1 50.6 %all-gather.13.cloned.1.call-done = bf16[1,8192,256]{1,2,0:T(8,128)(2,1)} async-done(((bf16[1,512,256]{1,2,0:T(8,128)(2,1)}), bf16[1,8192,256]{1,2,0:T(8,128)(2,1)}) %all-gather.13.cloned.1.call-update) | async-done | bytes 4194320 | tf_op jit(solution)/shard_map/all_gather | solution.py:99
  189.8 4.9 %fusion.52 = bf16[256,256]{1,0:T(8,128)(2,1)S(1)} fusion(bf16[256,8192]{1,0:T(8,128)(2,1)} %fusion.2, bf16[1,8192,256]{1,2,0:T(8,128)(2,1)} %all-gather.13.cloned.1.call-done, f32[256]{0:T(256)S(1)} %bitcast.137), kind=kOutput, calls=%fused_computation.38 | convolution fusion | flops 1073872896 | bytes 8520704 | tf_op jit(solution)/shard_map/dot_general | solution.py:100
  194.6 0.0 copy-done.6
  194.7 3.5 %broadcast_select_fusion.3 = (bf16[256,256]{1,0:T(8,128)(2,1)S(1)}, bf16[256,256]{1,0:T(8,128)(2,1)S(1)}) fusion(bf16[256,256]{1,0:T(8,128)(2,1)S(1)} %fusion.52, pred[]{:T(512)S(6)} %eq.58, f32[256]{0:T(256)S(1)} %bitcast.138, bf16[256,8192]{1,0:T(8,128)(2,1)} %collective-permute-done, bf16[1,8192,256]{1,2,0:T(8,128)(2,1)S(1)} %copy-done.6), kind=kOutput, calls=%fused_computation.52 | convolution fusion | flops 1074003968 | bytes 8782849 | tf_op jit(solution)/shard_map/dot_general | solution.py:101
  198.2 0.1 stack.17
  198.3 50.5 %all-gather.15.cloned.1.call-done = bf16[1,8192,256]{1,2,0:T(8,128)(2,1)} async-done(((bf16[1,512,256]{1,2,0:T(8,128)(2,1)}), bf16[1,8192,256]{1,2,0:T(8,128)(2,1)}) %all-gather.15.cloned.1.call-update) | async-done | bytes 4194320 | tf_op jit(solution)/shard_map/all_gather | solution.py:99
  248.7 4.9 %fusion.46 = bf16[256,256]{1,0:T(8,128)(2,1)S(1)} fusion(bf16[256,8192]{1,0:T(8,128)(2,1)} %fusion.2, bf16[1,8192,256]{1,2,0:T(8,128)(2,1)} %all-gather.15.cloned.1.call-done, f32[256]{0:T(256)S(1)} %bitcast.135), kind=kOutput, calls=%fused_computation.36 | convolution fusion | flops 1073872896 | bytes 8520704 | tf_op jit(solution)/shard_map/dot_general | solution.py:100
  253.6 3.5 %broadcast_select_fusion.1 = (bf16[256,256]{1,0:T(8,128)(2,1)S(1)}, bf16[256,256]{1,0:T(8,128)(2,1)S(1)}) fusion(bf16[256,256]{1,0:T(8,128)(2,1)S(1)} %fusion.46, pred[]{:T(512)S(6)} %eq.58, f32[256]{0:T(256)S(1)} %bitcast.136, bf16[256,8192]{1,0:T(8,128)(2,1)} %collective-permute-done, bf16[1,8192,256]{1,2,0:T(8,128)(2,1)S(1)} %copy-done.5), kind=kOutput, calls=%fused_computation.50 | convolution fusion | flops 1074003968 | bytes 8782849 | tf_op jit(solution)/shard_map/dot_general | solution.py:101
  257.1 0.1 stack.18
  257.2 2.8 pad_maximum_fusion
  260.0 0.0 all-to-all-done
  260.0 4.0 %all-to-all-start.1 = ((bf16[1,512,4,2,128]{4,3,1,0,2:T(2,128)(2,1)}), bf16[1,512,4,2,128]{4,3,1,0,2:T(2,128)(2,1)S(1)}, u32[]{:S(2)}, u32[]{:S(2)}) async-start(bf16[1,512,4,2,128]{4,3,1,0,2:T(2,128)(2,1)} %pad_maximum_fusion), calls=%async_computation.1 | async-start | bytes 2097152 | tf_op jit(solution)/shard_map/all_to_all | solution.py:108
  264.0 0.1 select_reduce_fusion.4
  264.1 13.5 %gather_fusion.1 = bf16[256,8192]{1,0:T(8,128)(2,1)} fusion(bf16[512,8192]{1,0:T(8,128)(2,1)} %bitcast.14, s32[1024]{0:T(1024)S(1)} %pad_clamp_fusion), kind=kCustom, calls=%fused_computation.1 | custom fusion | bytes 8389632 | tf_op jit(solution)/shard_map/jit(_take)/gather | solution.py:52
  277.6 0.0 all-to-all-done.1
  277.6 13.9 %gather_fusion.5 = bf16[2048,2,128]{2,1,0:T(2,128)(2,1)} fusion(bf16[2048,2,128]{2,1,0:T(2,128)(2,1)S(1)} %bitcast.119, s32[2048]{0:T(1024)S(1)} %broadcast_clamp_fusion), kind=kCustom, calls=%fused_computation.5 | custom fusion | bytes 2105344 | tf_op jit(solution)/shard_map/jit(_take)/gather | solution.py:120
  (27 shorter events, 0.2 us)
Async XLA Ops:
  7.2 3.1 %copy-start = (f32[2048]{0:T(1024)S(1)}, f32[2048]{0:T(1024)}, u32[]{:S(2)}) copy-start(f32[2048]{0:T(1024)} %param.11) | copy-start | bytes 24580
  7.2 64.4 %all-gather.9.cloned.1.call-start = ((), (), s32[]{:S(2)}) async-start(), calls=%async_computation.2 | async-start | bytes 4456448 | tf_op jit(solution)/shard_map/all_gather | solution.py:99
  10.3 6.4 %copy-start.3 = (f32[8192]{0:T(1024)S(1)}, f32[8192]{0:T(1024)}, u32[]{:S(2)}) copy-start(f32[8192]{0:T(1024)} %param.9) | copy-start | bytes 98308
  11.3 119.3 %all-gather.11.cloned.1.call-start = ((), (), s32[]{:S(2)}) async-start(), calls=%async_computation.3 | async-start | bytes 4456448 | tf_op jit(solution)/shard_map/all_gather | solution.py:99
  12.1 177.7 %all-gather.13.cloned.1.call-start = ((), (), s32[]{:S(2)}) async-start(), calls=%async_computation.4 | async-start | bytes 4456448 | tf_op jit(solution)/shard_map/all_gather | solution.py:99
  12.8 235.9 %all-gather.15.cloned.1.call-start = ((), (), s32[]{:S(2)}) async-start(), calls=%async_computation.5 | async-start | bytes 4456448 | tf_op jit(solution)/shard_map/all_gather | solution.py:99
  13.4 3.5 %copy-start.1 = (bf16[1,256,8192]{2,1,0:T(8,128)(2,1)S(1)}, bf16[1,256,8192]{2,1,0:T(8,128)(2,1)}, u32[]{:S(2)}) copy-start(bf16[1,256,8192]{2,1,0:T(8,128)(2,1)} %param.6) | copy-start | bytes 12582916
  16.8 4.6 %copy-start.2 = (s32[1,8,8]{2,1,0:T(8,128)S(1)}, s32[1,8,8]{2,1,0:T(8,128)}, u32[]{:S(2)}) copy-start(s32[1,8,8]{2,1,0:T(8,128)} %param.7) | copy-start | bytes 772
  16.8 4.8 %copy-start.4 = (s32[1,8,8]{2,1,0:T(8,128)S(1)}, s32[1,8,8]{2,1,0:T(8,128)}, u32[]{:S(2)}) copy-start(s32[1,8,8]{2,1,0:T(8,128)} %param.8) | copy-start | bytes 772
  20.0 56.4 %collective-permute-start = (bf16[256,8192]{1,0:T(8,128)(2,1)}, bf16[256,8192]{1,0:T(8,128)(2,1)}, u32[]{:S(2)}, u32[]{:S(2)}) collective-permute-start(bf16[256,8192]{1,0:T(8,128)(2,1)} %fusion.2), channel_id=1, source_target_pairs={{0,1},{1,0},{2,3},{3,2},{4,5},{5,4},{6,7},{7,6},{8,9},{9,8},{10,11... | collective-permute-start | bytes 12582920 | tf_op jit(solution)/shard_map/ppermute | solution.py:96
  40.1 219.9 %all-to-all-start = ((bf16[8,64,8192]{2,1,0:T(8,128)(2,1)}), bf16[8,64,8192]{2,1,0:T(8,128)(2,1)}, u32[]{:S(2)}, u32[]{:S(2)}) async-start(bf16[8,64,8192]{2,1,0:T(8,128)(2,1)} %bitcast.117), calls=%async_computation | async-start | bytes 16777216 | tf_op jit(solution)/shard_map/all_to_all | solution.py:115
  71.5 4.9 %copy-start.8 = (bf16[1,8192,256]{1,2,0:T(8,128)(2,1)S(1)}, bf16[1,8192,256]{1,2,0:T(8,128)(2,1)}, u32[]{:S(2)}) copy-start(bf16[1,8192,256]{1,2,0:T(8,128)(2,1)} %all-gather.9.cloned.1.call-done) | copy-start | bytes 12582916
  130.6 4.9 %copy-start.7 = (bf16[1,8192,256]{1,2,0:T(8,128)(2,1)S(1)}, bf16[1,8192,256]{1,2,0:T(8,128)(2,1)}, u32[]{:S(2)}) copy-start(bf16[1,8192,256]{1,2,0:T(8,128)(2,1)} %all-gather.11.cloned.1.call-done) | copy-start | bytes 12582916
  189.8 4.9 %copy-start.6 = (bf16[1,8192,256]{1,2,0:T(8,128)(2,1)S(1)}, bf16[1,8192,256]{1,2,0:T(8,128)(2,1)}, u32[]{:S(2)}) copy-start(bf16[1,8192,256]{1,2,0:T(8,128)(2,1)} %all-gather.13.cloned.1.call-done) | copy-start | bytes 12582916
  248.7 4.9 %copy-start.5 = (bf16[1,8192,256]{1,2,0:T(8,128)(2,1)S(1)}, bf16[1,8192,256]{1,2,0:T(8,128)(2,1)}, u32[]{:S(2)}) copy-start(bf16[1,8192,256]{1,2,0:T(8,128)(2,1)} %all-gather.15.cloned.1.call-done) | copy-start | bytes 12582916
  260.0 17.6 %all-to-all-start.1 = ((bf16[1,512,4,2,128]{4,3,1,0,2:T(2,128)(2,1)}), bf16[1,512,4,2,128]{4,3,1,0,2:T(2,128)(2,1)S(1)}, u32[]{:S(2)}, u32[]{:S(2)}) async-start(bf16[1,512,4,2,128]{4,3,1,0,2:T(2,128)(2,1)} %pad_maximum_fusion), calls=%async_computation.1 | async-start | bytes 2097152 | tf_op jit(solution)/shard_map/all_to_all | solution.py:108
Sparse Core Ops, SparseCore 0:
  11.4 60.0 all-gather.8
  73.7 56.9 all-gather.10
  132.8 56.9 all-gather.12
  191.7 56.9 all-gather.14

commit v4 on v2

--- a/solution.py
+++ b/solution.py
@@ -2,6 +2,8 @@
 import jax.numpy as jnp
 import numpy as np
 from jax import lax
+from jax.experimental import pallas as pl
+from jax.experimental.pallas import tpu as pltpu
 from jax.sharding import Mesh, PartitionSpec as P
 
 KVH = 8
@@ -34,25 +36,63 @@
     return (as_float * inverse_rms * norm_gain[None, :]).astype(jnp.bfloat16)
 
 
-def pack_document_runs(rows, counts, anchors, myself, peer_count):
-    row_count = rows.shape[0]
-    capacity = 2 * row_count // peer_count
-    slot_index = jnp.arange(capacity, dtype=jnp.int32)
-    my_counts = counts[myself]
-    my_anchors = anchors[myself]
-    wanted = jnp.minimum(my_anchors[:, None] + slot_index[None, :], row_count - 1)
-    is_live = slot_index[None, :] < my_counts[:, None]
-    picked = jnp.take(rows, wanted.reshape(-1), axis=0).reshape(peer_count, capacity, -1)
-    return jnp.where(is_live[:, :, None], picked, jnp.zeros_like(picked))
+def window_starts(anchors, row_count, capacity):
+    return jnp.minimum(anchors, row_count - capacity)
 
 
-def unpack_runs(arriving_rows, positions, run_ends, offsets, anchors, myself, peer_count):
-    capacity = arriving_rows.shape[1]
-    source, within, anchor = source_of(
-        positions, run_ends[:, myself], offsets[:, myself], anchors[:, myself], peer_count
-    )
-    flat_rows = arriving_rows.reshape(peer_count * capacity, -1)
-    return jnp.take(flat_rows, source * capacity + within, axis=0)
+def _pack_kernel(starts_ref, rows_hbm, out_hbm, sems):
+    peer_count, capacity = out_hbm.shape[0], out_hbm.shape[1]
+    copies = [
+        pltpu.make_async_copy(
+            rows_hbm.at[pl.ds(starts_ref[k], capacity)], out_hbm.at[k], sems.at[k]
+        )
+        for k in range(peer_count)
+    ]
+    for copy in copies:
+        copy.start()
+    for copy in copies:
+        copy.wait()
+
+
+def pack_document_runs(rows, starts, peer_count, capacity):
+    return pl.pallas_call(
+        _pack_kernel,
+        out_shape=jax.ShapeDtypeStruct((peer_count, capacity) + rows.shape[1:], rows.dtype),
+        grid_spec=pltpu.PrefetchScalarGridSpec(
+            num_scalar_prefetch=1,
+            grid=(1,),
+            in_specs=[pl.BlockSpec(memory_space=pl.ANY)],
+            out_specs=pl.BlockSpec(memory_space=pl.ANY),
+            scratch_shapes=[pltpu.SemaphoreType.DMA((peer_count,))],
+        ),
+    )(starts, rows)
+
+
+def _unpack_kernel(index_ref, flat_hbm, out_hbm, sem):
+    row_count = out_hbm.shape[0]
+
+    def start_row(p, carry):
+        pltpu.make_async_copy(
+            flat_hbm.at[pl.ds(index_ref[p], 1)], out_hbm.at[pl.ds(p, 1)], sem.at[0]
+        ).start()
+        return carry
+
+    lax.fori_loop(0, row_count, start_row, 0)
+    pltpu.make_async_copy(flat_hbm.at[pl.ds(0, row_count)], out_hbm, sem.at[0]).wait()
+
+
+def unpack_runs(flat_rows, index, row_count):
+    return pl.pallas_call(
+        _unpack_kernel,
+        out_shape=jax.ShapeDtypeStruct((row_count,) + flat_rows.shape[1:], flat_rows.dtype),
+        grid_spec=pltpu.PrefetchScalarGridSpec(
+            num_scalar_prefetch=1,
+            grid=(1,),
+            in_specs=[pl.BlockSpec(memory_space=pl.ANY)],
+            out_specs=pl.BlockSpec(memory_space=pl.ANY),
+            scratch_shapes=[pltpu.SemaphoreType.DMA((1,))],
+        ),
+    )(index, flat_rows)
 
 
 CTX = ("cx", "cc")
@@ -84,11 +124,21 @@
         segment_entry_counts[0], segment_destination_part[0], peer_count
     )
     positions = jnp.arange(row_count, dtype=jnp.int32)
-    outgoing = pack_document_runs(input_entries[0], counts, anchors, myself, peer_count)
+    capacity = 2 * row_count // peer_count
+    starts = window_starts(anchors, row_count, capacity)
+    lanes = 128
+    width = input_entries.shape[2]
+    row_blocks = input_entries[0].reshape(row_count, width // lanes, lanes)
+    outgoing = pack_document_runs(row_blocks, starts[myself], peer_count, capacity)
     arriving_rows = lax.all_to_all(outgoing, CTX, split_axis=0, concat_axis=0, tiled=True)
+    source, within, anchor = source_of(
+        positions, run_ends[:, myself], offsets[:, myself], anchors[:, myself], peer_count
+    )
+    shift = anchor - jnp.take(starts[:, myself], source, mode="clip")
+    index = source * capacity + shift + within
     moved_rows = unpack_runs(
-        arriving_rows, positions, run_ends, offsets, anchors, myself, peer_count
-    )
+        arriving_rows.reshape((peer_count * capacity,) + row_blocks.shape[1:]), index, row_count
+    ).reshape(row_count, width)
     normed = rms_normed(moved_rows, norm_gain)
     sibling_rows = lax.ppermute(normed, "cc", perm=[(0, 1), (1, 0)])
 

time: 213 us -> 569 us (2.67)
  Pallas kernels: 0 us -> 385 us
  local copies, waits for them, and re-layouts: 39.5 us -> 21.8 us
  waiting for transfers between devices: 104 us -> 95.1 us
    pallas_call x0 -> x2, Pallas kernels: none -> 385 us  [the longest x1 256 us: pack_document_runs(): pl.pallas_call(_pack_kernel, out_shape=jax.ShapeDtypeStruct((peer_count,...]
    gather x2 -> x1, local copies, waits for them, and re-layouts: 31.7 us -> 0.62 us  [on_device(): shift = anchor - jnp.take(starts[:, myself], source, mode='clip')]
    select_n x4 -> x0, other arithmetic: 12.3 us -> none  [the longest x1 7.62 us: pack_document_runs(): return jnp.where(is_live[:, :, None], picked, jnp.zeros_like(picked))]
    another operation x0 -> x1, local copies, waits for them, and re-layouts: none -> 7.28 us  [on_device(): return (moved_rows[None], by_heads)]
    all_to_all x1, waiting for transfers between devices: 93.4 us -> 87.1 us  [on_device(): lax.all_to_all(outgoing, CTX, split_axis=0, concat_axis=0, tiled=True)]
  transfers between devices with their start and end apart: 4 -> 4, of which waited for: 2 -> 2; matrix products, arithmetic and copies ran while one was open for 30% -> 8% of each run, Pallas kernels for 0% -> 68%
where the time goes in v4:
time: 569 us
  Pallas kernels  385 us (68%)
  waiting for transfers between devices  95.1 us (17%)
  matrix products  23.1 us (4%)
  local copies, waits for them, and re-layouts  21.8 us (4%)
  other arithmetic  18.9 us (3%)
  between operations  14.2 us (2%)
  starting transfers between devices  10.7 us (2%)
    pallas_call x1, Pallas kernels, pack_document_runs(): pl.pallas_call(_pack_kernel, out_shape=jax.ShapeDtypeStruct((peer_count,...  256 us
    pallas_call x1, Pallas kernels, unpack_runs(): pl.pallas_call(_unpack_kernel, out_shape=jax.ShapeDtypeStruct((row_count,...  129 us
    all_to_all x1, waiting for transfers between devices, on_device(): lax.all_to_all(outgoing, CTX, split_axis=0, concat_axis=0, tiled=True)  87.1 us
    dot_general x2, matrix products, project(): jnp.dot(rows, gathered_weight, preferred_element_type=jnp.float32)  23.1 us
  transfers between devices with their start and end apart: 4, of which 2 were waited for; matrix products, arithmetic and copies ran while one was open for 8% of the time, Pallas kernels for 68%

profile of v4, /device:TPU:1, one launch (start us, length us, event | category | flops | bytes accessed | tf_op | source)
XLA Modules:
  0.0 568.6 jit_solution(10890521928566784480)
XLA Ops:
  7.2 0.0 copy-start
  7.2 0.0 copy-start.3
  7.2 0.0 all-gather.2.cloned.1.call-start
  7.2 2.9 copy.18
  10.1 1.1 constant_dynamic-slice_fusion
  11.2 0.0 copy-done
  11.2 0.0 all-gather.2.cloned.1.call-update
  11.2 0.0 copy-done.3
  11.3 0.2 reduce_window_sum.23
  11.4 0.0 copy-start.5
  11.4 5.4 copy.21
  16.8 0.0 copy-done.5
  16.8 0.1 select_reduce_fusion
  17.0 0.5 fusion.6.starts_ref
  17.5 255.9 %shard_map.77 = bf16[8,64,64,128]{3,2,1,0:T(8,128)(2,1)} custom-call(s32[8]{0:T(128)} %fusion.6.starts_ref, bf16[256,64,128]{2,1,0:T(8,128)(2,1)} %bitcast.42), custom_call_target="tpu_custom_call" | custom-call | tf_op jit(solution)/shard_map/pallas_call | solution.py:58
  273.4 6.3 %all-to-all-start = ((bf16[8,64,64,128]{3,2,1,0:T(8,128)(2,1)}), bf16[8,64,64,128]{3,2,1,0:T(8,128)(2,1)}, u32[]{:S(2)}, u32[]{:S(2)}) async-start(bf16[8,64,64,128]{3,2,1,0:T(8,128)(2,1)} %shard_map.77), calls=%async_computation | async-start | bytes 16777216 | tf_op jit(solution)/shard_map/all_to_all | solution.py:133
  279.7 0.2 dynamic-slice_reduce_fusion.1
  280.0 0.2 dynamic-slice_reduce_fusion
  280.1 0.6 fusion.7
  280.8 0.1 convert_reduce_fusion
  280.8 0.1 select_reduce_fusion.3
  280.9 5.5 subtract_add_fusion.index_ref
  286.4 87.1 %all-to-all-done = bf16[8,64,64,128]{3,2,1,0:T(8,128)(2,1)} async-done(((bf16[8,64,64,128]{3,2,1,0:T(8,128)(2,1)}), bf16[8,64,64,128]{3,2,1,0:T(8,128)(2,1)}, u32[]{:S(2)}, u32[]{:S(2)}) %all-to-all-start) | async-done | bytes 8388640 | tf_op jit(solution)/shard_map/all_to_all | solution.py:133
  373.6 128.9 %shard_map.78 = bf16[256,64,128]{2,1,0:T(8,128)(2,1)} custom-call(s32[256]{0:T(256)} %subtract_add_fusion.index_ref, bf16[512,64,128]{2,1,0:T(8,128)(2,1)} %bitcast.15.flat_hbm), custom_call_target="tpu_custom_call" | custom-call | tf_op jit(solution)/shard_map/pallas_call | solution.py:85
  502.4 0.0 copy-start.2
  502.5 3.4 convert.1
  505.9 0.0 copy-done.2
  505.9 0.0 copy-start.4
  505.9 1.5 multiply_reduce_fusion
  507.4 0.0 copy-done.4
  507.4 7.9 %fusion.1 = bf16[256,8192]{1,0:T(8,128)(2,1)} fusion(f32[32,8,64,128]{3,2,1,0:T(8,128)S(1)} %convert.1, f32[8192]{0:T(1024)S(1)} %copy-done.4, f32[256]{0:T(256)S(1)} %add_rsqrt_fusion), kind=kLoop, calls=%fused_computation.2 | loop fusion | flops 6291456 | bytes 12616704 | tf_op jit(solution)/shard_map/convert_element_type | solution.py:36
  515.3 0.9 collective-permute-start
  516.2 0.0 all-gather.2.cloned.1.call-done
  516.2 11.6 %fusion.2 = bf16[256,1024]{1,0:T(8,128)(2,1)S(1)} fusion(bf16[256,8192]{1,0:T(8,128)(2,1)} %fusion.1, bf16[8192,1024]{0,1:T(8,128)(2,1)} %all-gather.2.cloned.1.call-done, f32[1024]{0:T(1024)S(1)} %bitcast.50), kind=kOutput, calls=%fused_computation.6 | convolution fusion | flops 4295491584 | bytes 21499904 | tf_op jit(solution)/shard_map/dot_general | solution.py:146
  527.8 0.0 collective-permute-done
  527.8 11.6 %broadcast_select_fusion.1 = (bf16[256,1024]{1,0:T(8,128)(2,1)S(1)}, bf16[256,1024]{1,0:T(8,128)(2,1)S(1)}) fusion(bf16[256,1024]{1,0:T(8,128)(2,1)S(1)} %fusion.2, pred[]{:T(512)S(6)} %eq.39, f32[1024]{0:T(1024)S(1)} %bitcast.51, bf16[256,8192]{1,0:T(8,128)(2,1)} %collective-permute-done, bf16[8192,1024]{0,1:T(8,128)(2,1)} %all-gather.2.cloned.1.call-done), kind=kOutput, calls=%fused_computation.10 | convolution fusion | flops 4296015872 | bytes 22548480 | tf_op jit(solution)/shard_map/dot_general | solution.py:146
  539.4 0.1 pad_maximum_fusion
  539.5 0.8 reshape.60
  540.2 1.8 copy.19
  542.0 3.5 all-to-all-start.1
  545.5 0.0 copy-start.1
  545.5 7.3 %broadcast_in_dim_reshape.3 = bf16[1,256,8192]{2,1,0:T(8,128)(2,1)} reshape(bf16[256,64,128]{2,1,0:T(8,128)(2,1)} %shard_map.78) | data formatting | bytes 8388608 | tf_op jit(solution)/shard_map/broadcast_in_dim;reshape | solution.py:156
  552.8 7.9 %all-to-all-done.1 = bf16[1,512,2,4,128]{4,2,1,0,3:T(2,128)(2,1)S(1)} async-done(((bf16[1,512,2,4,128]{4,2,1,0,3:T(2,128)(2,1)}), bf16[1,512,2,4,128]{4,2,1,0,3:T(2,128)(2,1)S(1)}, u32[]{:S(2)}, u32[]{:S(2)}) %all-to-all-start.1) | async-done | bytes 1048608 | tf_op jit(solution)/shard_map/all_to_all | solution.py:155
  560.8 1.0 copy.25
  561.7 0.0 copy-done.1
  (6 shorter events, 0.1 us)
Async XLA Ops:
  7.2 4.0 copy-start
  7.2 4.1 copy-start.3
  7.2 509.0 %all-gather.2.cloned.1.call-start = ((), (), s32[]{:S(2)}) async-start(), calls=%async_computation.2 | async-start | bytes 17825792 | tf_op jit(solution)/shard_map/all_gather | solution.py:121
  11.4 5.4 copy-start.5
  273.4 100.1 %all-to-all-start = ((bf16[8,64,64,128]{3,2,1,0:T(8,128)(2,1)}), bf16[8,64,64,128]{3,2,1,0:T(8,128)(2,1)}, u32[]{:S(2)}, u32[]{:S(2)}) async-start(bf16[8,64,64,128]{3,2,1,0:T(8,128)(2,1)} %shard_map.77), calls=%async_computation | async-start | bytes 16777216 | tf_op jit(solution)/shard_map/all_to_all | solution.py:133
  502.4 3.5 copy-start.2
  505.9 1.5 copy-start.4
  515.3 12.4 %collective-permute-start = (bf16[256,8192]{1,0:T(8,128)(2,1)}, bf16[256,8192]{1,0:T(8,128)(2,1)}, u32[]{:S(2)}, u32[]{:S(2)}) collective-permute-start(bf16[256,8192]{1,0:T(8,128)(2,1)} %fusion.1), channel_id=1, source_target_pairs={{0,1},{1,0},{2,3},{3,2},{4,5},{5,4},{6,7},{7,6},{8,9},{9,8},{10,11... | collective-permute-start | bytes 12582920 | tf_op jit(solution)/shard_map/ppermute | solution.py:143
  542.0 18.7 %all-to-all-start.1 = ((bf16[1,512,2,4,128]{4,2,1,0,3:T(2,128)(2,1)}), bf16[1,512,2,4,128]{4,2,1,0,3:T(2,128)(2,1)S(1)}, u32[]{:S(2)}, u32[]{:S(2)}) async-start(bf16[1,512,2,4,128]{4,2,1,0,3:T(2,128)(2,1)} %copy.19), calls=%async_computation.1 | async-start | bytes 2097152 | tf_op jit(solution)/shard_map/all_to_all | solution.py:155
  545.5 16.2 %copy-start.1 = (f32[2048]{0:T(1024)S(1)}, f32[2048]{0:T(1024)}, u32[]{:S(2)}) copy-start(f32[2048]{0:T(1024)} %param.11) | copy-start | bytes 24580
Sparse Core Ops, SparseCore 0:
  11.4 123.5 all-gather.1

commit v5 on v4

--- a/solution.py
+++ b/solution.py
@@ -40,57 +40,48 @@
     return jnp.minimum(anchors, row_count - capacity)
 
 
-def _pack_kernel(starts_ref, rows_hbm, out_hbm, sems):
-    peer_count, capacity = out_hbm.shape[0], out_hbm.shape[1]
-    copies = [
-        pltpu.make_async_copy(
-            rows_hbm.at[pl.ds(starts_ref[k], capacity)], out_hbm.at[k], sems.at[k]
-        )
-        for k in range(peer_count)
-    ]
-    for copy in copies:
-        copy.start()
-    for copy in copies:
-        copy.wait()
+def _pack_kernel(starts_ref, rows_ref, out_ref):
+    peer_count, capacity = out_ref.shape[0], out_ref.shape[1]
+    for k in range(peer_count):
+        out_ref[k] = rows_ref[pl.ds(starts_ref[k], capacity)]
+
+
+def _whole(shape):
+    return pl.BlockSpec(shape, lambda i, *_: (0,) * len(shape))
 
 
 def pack_document_runs(rows, starts, peer_count, capacity):
+    out_shape = (peer_count, capacity) + rows.shape[1:]
     return pl.pallas_call(
         _pack_kernel,
-        out_shape=jax.ShapeDtypeStruct((peer_count, capacity) + rows.shape[1:], rows.dtype),
+        out_shape=jax.ShapeDtypeStruct(out_shape, rows.dtype),
         grid_spec=pltpu.PrefetchScalarGridSpec(
             num_scalar_prefetch=1,
             grid=(1,),
-            in_specs=[pl.BlockSpec(memory_space=pl.ANY)],
-            out_specs=pl.BlockSpec(memory_space=pl.ANY),
-            scratch_shapes=[pltpu.SemaphoreType.DMA((peer_count,))],
+            in_specs=[_whole(rows.shape)],
+            out_specs=_whole(out_shape),
         ),
     )(starts, rows)
 
 
-def _unpack_kernel(index_ref, flat_hbm, out_hbm, sem):
-    row_count = out_hbm.shape[0]
-
-    def start_row(p, carry):
-        pltpu.make_async_copy(
-            flat_hbm.at[pl.ds(index_ref[p], 1)], out_hbm.at[pl.ds(p, 1)], sem.at[0]
-        ).start()
+def _unpack_kernel(index_ref, flat_ref, out_ref):
+    def move_row(p, carry):
+        out_ref[p] = flat_ref[index_ref[p]]
         return carry
 
-    lax.fori_loop(0, row_count, start_row, 0)
-    pltpu.make_async_copy(flat_hbm.at[pl.ds(0, row_count)], out_hbm, sem.at[0]).wait()
+    lax.fori_loop(0, out_ref.shape[0], move_row, 0, unroll=8)
 
 
 def unpack_runs(flat_rows, index, row_count):
+    out_shape = (row_count,) + flat_rows.shape[1:]
     return pl.pallas_call(
         _unpack_kernel,
-        out_shape=jax.ShapeDtypeStruct((row_count,) + flat_rows.shape[1:], flat_rows.dtype),
+        out_shape=jax.ShapeDtypeStruct(out_shape, flat_rows.dtype),
         grid_spec=pltpu.PrefetchScalarGridSpec(
             num_scalar_prefetch=1,
             grid=(1,),
-            in_specs=[pl.BlockSpec(memory_space=pl.ANY)],
-            out_specs=pl.BlockSpec(memory_space=pl.ANY),
-            scratch_shapes=[pltpu.SemaphoreType.DMA((1,))],
+            in_specs=[_whole(flat_rows.shape)],
+            out_specs=_whole(out_shape),
         ),
     )(index, flat_rows)
 

time: 569 us -> 198 us (0.35)
  Pallas kernels: 385 us -> 13.1 us
    pallas_call x2, Pallas kernels: 385 us -> 13.1 us  [the longest x1 6.59 us: pack_document_runs(): pl.pallas_call(_pack_kernel, out_shape=jax.ShapeDtypeStruct(out_shape, ro...]
  transfers between devices with their start and end apart: 4 -> 4, of which waited for: 2 -> 2; matrix products, arithmetic and copies ran while one was open for 8% -> 23% of each run, Pallas kernels for 68% -> 7%
where the time goes in v5:
time: 198 us; the launch traced here: 197 us
  waiting for transfers between devices  95.1 us (48%)
  matrix products  23.1 us (12%)
  local copies, waits for them, and re-layouts  21.8 us (11%)
  other arithmetic  18.9 us (10%)
  between operations  14.2 us (7%)
  Pallas kernels  13.1 us (7%)
  starting transfers between devices  10.9 us (6%)
    all_to_all x1, waiting for transfers between devices, on_device(): lax.all_to_all(outgoing, CTX, split_axis=0, concat_axis=0, tiled=True)  87.1 us
    dot_general x2, matrix products, project(): jnp.dot(rows, gathered_weight, preferred_element_type=jnp.float32)  23.1 us
    unnamed x15, local copies, waits for them, and re-layouts  9.33 us
    all_to_all x1, waiting for transfers between devices, on_device(): lax.all_to_all(mapped, 'cx', split_axis=3, concat_axis=1, tiled=True)  7.95 us
    convert_element_type x1, other arithmetic, rms_normed(): return (as_float * inverse_rms * norm_gain[None, :]).astype(jnp.bfloat16)  7.91 us
    another operation x1, local copies, waits for them, and re-layouts, on_device(): return (moved_rows[None], by_heads)  7.28 us
    pallas_call x1, Pallas kernels, pack_document_runs(): pl.pallas_call(_pack_kernel, out_shape=jax.ShapeDtypeStruct(out_shape, ro...  6.59 us
    all_to_all x1, starting transfers between devices, on_device(): lax.all_to_all(outgoing, CTX, split_axis=0, concat_axis=0, tiled=True)  6.52 us
  transfers between devices with their start and end apart: 4, of which 2 were waited for; matrix products, arithmetic and copies ran while one was open for 23% of the time, Pallas kernels for 7%

profile of v5, /device:TPU:1, one launch (start us, length us, event | category | flops | bytes accessed | tf_op | source)
XLA Modules:
  0.0 197.1 jit_solution(8651520007055104580)
XLA Ops:
  7.2 0.0 copy-start
  7.2 0.0 copy-start.3
  7.2 0.0 all-gather.2.cloned.1.call-start
  7.2 2.9 %copy.18 = bf16[512,2048]{0,1:T(8,128)(2,1)S(1)} copy(bf16[512,2048]{1,0:T(8,128)(2,1)} %param.10) | data formatting | bytes 4194304 | tf_op args[4]
  10.1 1.1 constant_dynamic-slice_fusion
  11.2 0.0 copy-done
  11.2 0.0 all-gather.2.cloned.1.call-update
  11.2 0.0 copy-done.3
  11.3 0.2 reduce_window_sum.23
  11.4 0.0 copy-start.5
  11.4 5.4 %copy.21 = bf16[32,8,64,128]{3,2,1,0:T(8,128)(2,1)} copy(bf16[32,8,64,128]{3,1,2,0:T(8,128)(2,1)} %bitcast.45) | data formatting | bytes 8388608
  16.8 0.0 copy-done.5
  16.8 0.1 select_reduce_fusion
  17.0 0.5 fusion.6.starts_ref
  17.5 6.6 %shard_map.77 = bf16[8,64,64,128]{3,2,1,0:T(8,128)(2,1)} custom-call(s32[8]{0:T(128)} %fusion.6.starts_ref, bf16[256,64,128]{2,1,0:T(8,128)(2,1)} %bitcast.42), custom_call_target="tpu_custom_call" | custom-call | tf_op jit(solution)/shard_map/pallas_call | solution.py:55
  24.1 6.5 %all-to-all-start = ((bf16[8,64,64,128]{3,2,1,0:T(8,128)(2,1)}), bf16[8,64,64,128]{3,2,1,0:T(8,128)(2,1)}, u32[]{:S(2)}, u32[]{:S(2)}) async-start(bf16[8,64,64,128]{3,2,1,0:T(8,128)(2,1)} %shard_map.77), calls=%async_computation | async-start | bytes 16777216 | tf_op jit(solution)/shard_map/all_to_all | solution.py:124
  30.6 0.2 dynamic-slice_reduce_fusion.1
  30.8 0.2 dynamic-slice_reduce_fusion
  31.0 0.6 fusion.7
  31.6 0.1 convert_reduce_fusion
  31.7 0.1 select_reduce_fusion.3
  31.8 5.5 %subtract_add_fusion.index_ref = s32[256]{0:T(256)} fusion(s32[256]{0:T(256)S(1)} %get-tuple-element.17, s32[256]{0:T(256)S(1)} %get-tuple-element.16, s32[256]{0:T(256)S(1)} %convert_reduce_fusion, s32[]{:T(128)} %bitcast.2, s32[]{:T(128)} %bitcast.3, s32[]{:T(128)} %bitcast.4, s32[]{:T(128)} %bitcast.5, s32[]{:T(128)} %bitcast.6, s32[]{:T(128)} %bitcast.7, ...), kind=kLoop, calls=%fused_computation.37 | loop fusion | flops 4864 | bytes 4128 | tf_op jit(solution)/shard_map/add | solution.py:129
  37.3 87.1 %all-to-all-done = bf16[8,64,64,128]{3,2,1,0:T(8,128)(2,1)} async-done(((bf16[8,64,64,128]{3,2,1,0:T(8,128)(2,1)}), bf16[8,64,64,128]{3,2,1,0:T(8,128)(2,1)}, u32[]{:S(2)}, u32[]{:S(2)}) %all-to-all-start) | async-done | bytes 8388640 | tf_op jit(solution)/shard_map/all_to_all | solution.py:124
  124.5 6.5 %shard_map.78 = bf16[256,64,128]{2,1,0:T(8,128)(2,1)} custom-call(s32[256]{0:T(256)} %subtract_add_fusion.index_ref, bf16[512,64,128]{2,1,0:T(8,128)(2,1)} %bitcast.15.flat_ref), custom_call_target="tpu_custom_call" | custom-call | tf_op jit(solution)/shard_map/pallas_call | solution.py:77
  130.9 0.0 copy-start.2
  130.9 3.4 %convert.1 = f32[32,8,64,128]{3,2,1,0:T(8,128)S(1)} convert(bf16[32,8,64,128]{3,2,1,0:T(8,128)(2,1)} %bitcast.41) | non-fusion elementwise | flops 2097152 | bytes 12582912
  134.3 0.0 copy-done.2
  134.4 0.0 copy-start.4
  134.4 1.5 multiply_reduce_fusion
  135.9 0.0 copy-done.4
  135.9 7.9 %fusion.1 = bf16[256,8192]{1,0:T(8,128)(2,1)} fusion(f32[32,8,64,128]{3,2,1,0:T(8,128)S(1)} %convert.1, f32[8192]{0:T(1024)S(1)} %copy-done.4, f32[256]{0:T(256)S(1)} %add_rsqrt_fusion), kind=kLoop, calls=%fused_computation.2 | loop fusion | flops 6291456 | bytes 12616704 | tf_op jit(solution)/shard_map/convert_element_type | solution.py:36
  143.8 0.9 collective-permute-start
  144.7 0.0 all-gather.2.cloned.1.call-done
  144.7 11.6 %fusion.2 = bf16[256,1024]{1,0:T(8,128)(2,1)S(1)} fusion(bf16[256,8192]{1,0:T(8,128)(2,1)} %fusion.1, bf16[8192,1024]{0,1:T(8,128)(2,1)} %all-gather.2.cloned.1.call-done, f32[1024]{0:T(1024)S(1)} %bitcast.50), kind=kOutput, calls=%fused_computation.6 | convolution fusion | flops 4295491584 | bytes 21499904 | tf_op jit(solution)/shard_map/dot_general | solution.py:137
  156.3 0.0 collective-permute-done
  156.3 11.6 %broadcast_select_fusion.1 = (bf16[256,1024]{1,0:T(8,128)(2,1)S(1)}, bf16[256,1024]{1,0:T(8,128)(2,1)S(1)}) fusion(bf16[256,1024]{1,0:T(8,128)(2,1)S(1)} %fusion.2, pred[]{:T(512)S(6)} %eq.39, f32[1024]{0:T(1024)S(1)} %bitcast.51, bf16[256,8192]{1,0:T(8,128)(2,1)} %collective-permute-done, bf16[8192,1024]{0,1:T(8,128)(2,1)} %all-gather.2.cloned.1.call-done), kind=kOutput, calls=%fused_computation.10 | convolution fusion | flops 4296015872 | bytes 22548480 | tf_op jit(solution)/shard_map/dot_general | solution.py:137
  167.9 0.1 pad_maximum_fusion
  168.0 0.8 reshape.60
  168.7 1.8 copy.19
  170.5 3.5 %all-to-all-start.1 = ((bf16[1,512,2,4,128]{4,2,1,0,3:T(2,128)(2,1)}), bf16[1,512,2,4,128]{4,2,1,0,3:T(2,128)(2,1)S(1)}, u32[]{:S(2)}, u32[]{:S(2)}) async-start(bf16[1,512,2,4,128]{4,2,1,0,3:T(2,128)(2,1)} %copy.19), calls=%async_computation.1 | async-start | bytes 2097152 | tf_op jit(solution)/shard_map/all_to_all | solution.py:146
  174.0 0.0 copy-start.1
  174.0 7.3 %broadcast_in_dim_reshape.3 = bf16[1,256,8192]{2,1,0:T(8,128)(2,1)} reshape(bf16[256,64,128]{2,1,0:T(8,128)(2,1)} %shard_map.78) | data formatting | bytes 8388608 | tf_op jit(solution)/shard_map/broadcast_in_dim;reshape | solution.py:147
  181.3 8.0 %all-to-all-done.1 = bf16[1,512,2,4,128]{4,2,1,0,3:T(2,128)(2,1)S(1)} async-done(((bf16[1,512,2,4,128]{4,2,1,0,3:T(2,128)(2,1)}), bf16[1,512,2,4,128]{4,2,1,0,3:T(2,128)(2,1)S(1)}, u32[]{:S(2)}, u32[]{:S(2)}) %all-to-all-start.1) | async-done | bytes 1048608 | tf_op jit(solution)/shard_map/all_to_all | solution.py:146
  189.3 1.0 copy.25
  190.2 0.0 copy-done.1
  (6 shorter events, 0.1 us)
Async XLA Ops:
  7.2 4.0 %copy-start = (f32[2048]{0:T(1024)S(1)}, f32[2048]{0:T(1024)}, u32[]{:S(2)}) copy-start(f32[2048]{0:T(1024)} %param.11) | copy-start | bytes 24580
  7.2 4.1 %copy-start.3 = (s32[1,8,8]{2,1,0:T(8,128)S(1)}, s32[1,8,8]{2,1,0:T(8,128)}, u32[]{:S(2)}) copy-start(s32[1,8,8]{2,1,0:T(8,128)} %param.7) | copy-start | bytes 772
  7.2 137.5 %all-gather.2.cloned.1.call-start = ((), (), s32[]{:S(2)}) async-start(), calls=%async_computation.2 | async-start | bytes 17825792 | tf_op jit(solution)/shard_map/all_gather | solution.py:112
  11.4 5.4 %copy-start.5 = (s32[1,8,8]{2,1,0:T(8,128)S(1)}, s32[1,8,8]{2,1,0:T(8,128)}, u32[]{:S(2)}) copy-start(s32[1,8,8]{2,1,0:T(8,128)} %param.8) | copy-start | bytes 772
  24.1 100.4 %all-to-all-start = ((bf16[8,64,64,128]{3,2,1,0:T(8,128)(2,1)}), bf16[8,64,64,128]{3,2,1,0:T(8,128)(2,1)}, u32[]{:S(2)}, u32[]{:S(2)}) async-start(bf16[8,64,64,128]{3,2,1,0:T(8,128)(2,1)} %shard_map.77), calls=%async_computation | async-start | bytes 16777216 | tf_op jit(solution)/shard_map/all_to_all | solution.py:124
  130.9 3.4 %copy-start.2 = (bf16[256,64,128]{2,1,0:T(8,128)(2,1)S(1)}, bf16[256,64,128]{2,1,0:T(8,128)(2,1)}, u32[]{:S(2)}) copy-start(bf16[256,64,128]{2,1,0:T(8,128)(2,1)} %shard_map.78) | copy-start | bytes 12582916
  134.4 1.5 copy-start.4
  143.8 12.4 %collective-permute-start = (bf16[256,8192]{1,0:T(8,128)(2,1)}, bf16[256,8192]{1,0:T(8,128)(2,1)}, u32[]{:S(2)}, u32[]{:S(2)}) collective-permute-start(bf16[256,8192]{1,0:T(8,128)(2,1)} %fusion.1), channel_id=1, source_target_pairs={{0,1},{1,0},{2,3},{3,2},{4,5},{5,4},{6,7},{7,6},{8,9},{9,8},{10,11... | collective-permute-start | bytes 12582920 | tf_op jit(solution)/shard_map/ppermute | solution.py:134
  170.5 18.8 %all-to-all-start.1 = ((bf16[1,512,2,4,128]{4,2,1,0,3:T(2,128)(2,1)}), bf16[1,512,2,4,128]{4,2,1,0,3:T(2,128)(2,1)S(1)}, u32[]{:S(2)}, u32[]{:S(2)}) async-start(bf16[1,512,2,4,128]{4,2,1,0,3:T(2,128)(2,1)} %copy.19), calls=%async_computation.1 | async-start | bytes 2097152 | tf_op jit(solution)/shard_map/all_to_all | solution.py:146
  174.0 16.2 %copy-start.1 = (f32[2048]{0:T(1024)S(1)}, f32[2048]{0:T(1024)}, u32[]{:S(2)}) copy-start(f32[2048]{0:T(1024)} %param.11) | copy-start | bytes 24580
Sparse Core Ops, SparseCore 0:
  11.4 123.5 all-gather.1

commit v6 on v5

--- a/solution.py
+++ b/solution.py
@@ -102,10 +102,11 @@
     heads_per_core = KVH // cores
     local_weight = kv_weight.reshape(width, 2, heads_per_core, cores, HD)
     local_weight = lax.dynamic_index_in_dim(local_weight, core, axis=3, keepdims=False)
-    local_weight = local_weight.reshape(width, 2 * heads_per_core * HD)
+    local_weight = jnp.swapaxes(local_weight, 1, 2).reshape(width, heads_per_core * 2 * HD)
     local_bias = lax.dynamic_index_in_dim(
         kv_bias.reshape(2, heads_per_core, cores, HD), core, axis=2, keepdims=False
-    ).reshape(-1)
+    )
+    local_bias = jnp.swapaxes(local_bias, 0, 1).reshape(-1)
     local_weight, local_bias, input_entries = lax.optimization_barrier(
         (local_weight, local_bias, input_entries)
     )
@@ -135,15 +136,16 @@
 
     def project(rows):
         products = jnp.dot(rows, gathered_weight, preferred_element_type=jnp.float32)
-        return (products + local_bias[None, :]).astype(jnp.bfloat16)
+        products = (products + local_bias[None, :]).astype(jnp.bfloat16)
+        return jnp.swapaxes(products.reshape(row_count, heads_per_core, 2 * HD), 0, 1)
 
     own = project(normed)
     other = project(sibling_rows)
     first = jnp.where(core == 0, own, other)
     second = jnp.where(core == 0, other, own)
-    mapped = jnp.concatenate([first, second], axis=0)
-    mapped = mapped.reshape(1, cores * row_count, 2, heads_per_core, HD)
-    by_heads = lax.all_to_all(mapped, "cx", split_axis=3, concat_axis=1, tiled=True)
+    mapped = jnp.concatenate([first, second], axis=1)
+    by_heads = lax.all_to_all(mapped, "cx", split_axis=0, concat_axis=0, tiled=True)
+    by_heads = by_heads.reshape(1, chips * cores * row_count, 2, 1, HD)
     return (moved_rows[None], by_heads)
 
 

time: 198 us -> 196 us (0.990)
  local copies, waits for them, and re-layouts: 21.8 us -> 19.5 us
    unnamed x15 -> x14, local copies, waits for them, and re-layouts: 9.33 us -> 8.36 us
where the time goes in v6:
time: 196 us
  waiting for transfers between devices  95.1 us (49%)
  matrix products  23.1 us (12%)
  other arithmetic  19.9 us (10%)
  local copies, waits for them, and re-layouts  19.5 us (10%)
  between operations  14.2 us (7%)
  Pallas kernels  13.1 us (7%)
  starting transfers between devices  10.9 us (6%)
    all_to_all x1, waiting for transfers between devices, on_device(): lax.all_to_all(outgoing, CTX, split_axis=0, concat_axis=0, tiled=True)  87.1 us
    dot_general x2, matrix products, project(): jnp.dot(rows, gathered_weight, preferred_element_type=jnp.float32)  23.1 us
    unnamed x14, local copies, waits for them, and re-layouts  8.36 us
    all_to_all x1, waiting for transfers between devices, on_device(): lax.all_to_all(mapped, 'cx', split_axis=0, concat_axis=0, tiled=True)  7.93 us
    convert_element_type x1, other arithmetic, rms_normed(): return (as_float * inverse_rms * norm_gain[None, :]).astype(jnp.bfloat16)  7.91 us
    another operation x1, local copies, waits for them, and re-layouts, on_device(): return (moved_rows[None], by_heads)  7.28 us
    pallas_call x1, Pallas kernels, pack_document_runs(): pl.pallas_call(_pack_kernel, out_shape=jax.ShapeDtypeStruct(out_shape, ro...  6.59 us
    all_to_all x1, starting transfers between devices, on_device(): lax.all_to_all(outgoing, CTX, split_axis=0, concat_axis=0, tiled=True)  6.52 us
  transfers between devices with their start and end apart: 4, of which 2 were waited for; matrix products, arithmetic and copies ran while one was open for 23% of the time, Pallas kernels for 7%

profile of v6, /device:TPU:1, one launch (start us, length us, event | category | flops | bytes accessed | tf_op | source)
XLA Modules:
  0.0 195.8 jit_solution(13898283051639081330)
XLA Ops:
  7.2 0.0 copy-start
  7.2 0.0 all-gather.2.cloned.1.call-start
  7.2 0.0 copy-start.3
  7.2 2.9 %copy.34 = bf16[512,2048]{0,1:T(8,128)(2,1)S(1)} copy(bf16[512,2048]{1,0:T(8,128)(2,1)} %param.10) | data formatting | bytes 4194304 | tf_op args[4]
  10.1 0.1 dynamic-slice_bitcast_fusion
  10.2 1.1 copy.36
  11.3 0.0 copy-done
  11.3 0.0 all-gather.2.cloned.1.call-update
  11.3 0.0 copy-done.3
  11.3 0.2 reduce_window_sum.23
  11.5 0.0 copy-start.5
  11.5 5.4 %copy.44 = bf16[32,8,64,128]{3,2,1,0:T(8,128)(2,1)} copy(bf16[32,8,64,128]{3,1,2,0:T(8,128)(2,1)} %bitcast.59) | data formatting | bytes 8388608
  16.9 0.0 copy-done.5
  16.9 0.1 select_reduce_fusion
  17.1 0.5 fusion.6.starts_ref
  17.6 6.6 %shard_map.77 = bf16[8,64,64,128]{3,2,1,0:T(8,128)(2,1)} custom-call(s32[8]{0:T(128)} %fusion.6.starts_ref, bf16[256,64,128]{2,1,0:T(8,128)(2,1)} %bitcast.57), custom_call_target="tpu_custom_call" | custom-call | tf_op jit(solution)/shard_map/pallas_call | solution.py:55
  24.2 6.5 %all-to-all-start = ((bf16[8,64,64,128]{3,2,1,0:T(8,128)(2,1)}), bf16[8,64,64,128]{3,2,1,0:T(8,128)(2,1)}, u32[]{:S(2)}, u32[]{:S(2)}) async-start(bf16[8,64,64,128]{3,2,1,0:T(8,128)(2,1)} %shard_map.77), calls=%async_computation | async-start | bytes 16777216 | tf_op jit(solution)/shard_map/all_to_all | solution.py:125
  30.7 0.2 dynamic-slice_reduce_fusion.1
  30.9 0.2 dynamic-slice_reduce_fusion
  31.1 0.6 fusion.7
  31.7 0.1 convert_reduce_fusion
  31.8 0.1 select_reduce_fusion.3
  31.9 5.5 %subtract_add_fusion.index_ref = s32[256]{0:T(256)} fusion(s32[256]{0:T(256)S(1)} %get-tuple-element.17, s32[256]{0:T(256)S(1)} %get-tuple-element.16, s32[256]{0:T(256)S(1)} %convert_reduce_fusion, s32[]{:T(128)} %bitcast.2, s32[]{:T(128)} %bitcast.3, s32[]{:T(128)} %bitcast.4, s32[]{:T(128)} %bitcast.5, s32[]{:T(128)} %bitcast.6, s32[]{:T(128)} %bitcast.7, ...), kind=kLoop, calls=%fused_computation.39 | loop fusion | flops 4864 | bytes 4128 | tf_op jit(solution)/shard_map/add | solution.py:130
  37.4 87.1 %all-to-all-done = bf16[8,64,64,128]{3,2,1,0:T(8,128)(2,1)} async-done(((bf16[8,64,64,128]{3,2,1,0:T(8,128)(2,1)}), bf16[8,64,64,128]{3,2,1,0:T(8,128)(2,1)}, u32[]{:S(2)}, u32[]{:S(2)}) %all-to-all-start) | async-done | bytes 8388640 | tf_op jit(solution)/shard_map/all_to_all | solution.py:125
  124.6 6.5 %shard_map.78 = bf16[256,64,128]{2,1,0:T(8,128)(2,1)} custom-call(s32[256]{0:T(256)} %subtract_add_fusion.index_ref, bf16[512,64,128]{2,1,0:T(8,128)(2,1)} %bitcast.20.flat_ref), custom_call_target="tpu_custom_call" | custom-call | tf_op jit(solution)/shard_map/pallas_call | solution.py:77
  131.0 0.0 copy-start.2
  131.0 3.4 %convert.1 = f32[32,8,64,128]{3,2,1,0:T(8,128)S(1)} convert(bf16[32,8,64,128]{3,2,1,0:T(8,128)(2,1)} %bitcast.56) | non-fusion elementwise | flops 2097152 | bytes 12582912
  134.4 0.0 copy-done.2
  134.5 0.0 copy-start.4
  134.5 1.5 multiply_reduce_fusion
  136.0 0.0 copy-done.4
  136.0 7.9 %fusion.1 = bf16[256,8192]{1,0:T(8,128)(2,1)} fusion(f32[32,8,64,128]{3,2,1,0:T(8,128)S(1)} %convert.1, f32[8192]{0:T(1024)S(1)} %copy-done.4, f32[256]{0:T(256)S(1)} %add_rsqrt_fusion), kind=kLoop, calls=%fused_computation.2 | loop fusion | flops 6291456 | bytes 12616704 | tf_op jit(solution)/shard_map/convert_element_type | solution.py:36
  143.9 0.9 collective-permute-start
  144.8 0.0 all-gather.2.cloned.1.call-done
  144.8 11.6 %fusion.2 = bf16[256,1024]{1,0:T(8,128)(2,1)S(1)} fusion(bf16[256,8192]{1,0:T(8,128)(2,1)} %fusion.1, bf16[8192,1024]{0,1:T(8,128)(2,1)} %all-gather.2.cloned.1.call-done, f32[1024]{0:T(1024)S(1)} %bitcast.70), kind=kOutput, calls=%fused_computation.6 | convolution fusion | flops 4295491584 | bytes 21499904 | tf_op jit(solution)/shard_map/dot_general | solution.py:138
  156.4 0.0 collective-permute-done
  156.4 11.6 %broadcast_select_fusion.1 = (bf16[256,1024]{1,0:T(8,128)(2,1)S(1)}, bf16[256,1024]{1,0:T(8,128)(2,1)S(1)}) fusion(bf16[256,1024]{1,0:T(8,128)(2,1)S(1)} %fusion.2, pred[]{:T(512)S(6)} %eq.39, f32[1024]{0:T(1024)S(1)} %bitcast.71, bf16[256,8192]{1,0:T(8,128)(2,1)} %collective-permute-done, bf16[8192,1024]{0,1:T(8,128)(2,1)} %all-gather.2.cloned.1.call-done), kind=kOutput, calls=%fused_computation.13 | convolution fusion | flops 4296015872 | bytes 22548480 | tf_op jit(solution)/shard_map/dot_general | solution.py:138
  168.1 1.0 pad_maximum_fusion
  169.1 3.5 %all-to-all-start.1 = ((bf16[4,512,256]{2,1,0:T(8,128)(2,1)}), bf16[4,512,256]{2,1,0:T(8,128)(2,1)S(1)}, u32[]{:S(2)}, u32[]{:S(2)}) async-start(bf16[4,512,256]{2,1,0:T(8,128)(2,1)} %pad_maximum_fusion), calls=%async_computation.1 | async-start | bytes 2097152 | tf_op jit(solution)/shard_map/all_to_all | solution.py:147
  172.6 0.0 copy-start.1
  172.6 7.3 %broadcast_in_dim_reshape.3 = bf16[1,256,8192]{2,1,0:T(8,128)(2,1)} reshape(bf16[256,64,128]{2,1,0:T(8,128)(2,1)} %shard_map.78) | data formatting | bytes 8388608 | tf_op jit(solution)/shard_map/broadcast_in_dim;reshape | solution.py:149
  179.9 7.9 %all-to-all-done.1 = bf16[4,512,256]{2,1,0:T(8,128)(2,1)S(1)} async-done(((bf16[4,512,256]{2,1,0:T(8,128)(2,1)}), bf16[4,512,256]{2,1,0:T(8,128)(2,1)S(1)}, u32[]{:S(2)}, u32[]{:S(2)}) %all-to-all-start.1) | async-done | bytes 1048608 | tf_op jit(solution)/shard_map/all_to_all | solution.py:147
  187.8 1.1 reshape.64
  188.9 0.0 copy-done.1
  (9 shorter events, 0.1 us)
Async XLA Ops:
  7.2 4.1 %copy-start = (f32[2048]{0:T(1024)S(1)}, f32[2048]{0:T(1024)}, u32[]{:S(2)}) copy-start(f32[2048]{0:T(1024)} %param.11) | copy-start | bytes 24580
  7.2 137.6 %all-gather.2.cloned.1.call-start = ((), (), s32[]{:S(2)}) async-start(), calls=%async_computation.2 | async-start | bytes 17825792 | tf_op jit(solution)/shard_map/all_gather | solution.py:113
  7.2 4.1 %copy-start.3 = (s32[1,8,8]{2,1,0:T(8,128)S(1)}, s32[1,8,8]{2,1,0:T(8,128)}, u32[]{:S(2)}) copy-start(s32[1,8,8]{2,1,0:T(8,128)} %param.7) | copy-start | bytes 772
  11.5 5.4 %copy-start.5 = (s32[1,8,8]{2,1,0:T(8,128)S(1)}, s32[1,8,8]{2,1,0:T(8,128)}, u32[]{:S(2)}) copy-start(s32[1,8,8]{2,1,0:T(8,128)} %param.8) | copy-start | bytes 772
  24.2 100.4 %all-to-all-start = ((bf16[8,64,64,128]{3,2,1,0:T(8,128)(2,1)}), bf16[8,64,64,128]{3,2,1,0:T(8,128)(2,1)}, u32[]{:S(2)}, u32[]{:S(2)}) async-start(bf16[8,64,64,128]{3,2,1,0:T(8,128)(2,1)} %shard_map.77), calls=%async_computation | async-start | bytes 16777216 | tf_op jit(solution)/shard_map/all_to_all | solution.py:125
  131.0 3.4 %copy-start.2 = (bf16[256,64,128]{2,1,0:T(8,128)(2,1)S(1)}, bf16[256,64,128]{2,1,0:T(8,128)(2,1)}, u32[]{:S(2)}) copy-start(bf16[256,64,128]{2,1,0:T(8,128)(2,1)} %shard_map.78) | copy-start | bytes 12582916
  134.5 1.5 copy-start.4
  143.9 12.4 %collective-permute-start = (bf16[256,8192]{1,0:T(8,128)(2,1)}, bf16[256,8192]{1,0:T(8,128)(2,1)}, u32[]{:S(2)}, u32[]{:S(2)}) collective-permute-start(bf16[256,8192]{1,0:T(8,128)(2,1)} %fusion.1), channel_id=1, source_target_pairs={{0,1},{1,0},{2,3},{3,2},{4,5},{5,4},{6,7},{7,6},{8,9},{9,8},{10,11... | collective-permute-start | bytes 12582920 | tf_op jit(solution)/shard_map/ppermute | solution.py:135
  169.1 18.7 %all-to-all-start.1 = ((bf16[4,512,256]{2,1,0:T(8,128)(2,1)}), bf16[4,512,256]{2,1,0:T(8,128)(2,1)S(1)}, u32[]{:S(2)}, u32[]{:S(2)}) async-start(bf16[4,512,256]{2,1,0:T(8,128)(2,1)} %pad_maximum_fusion), calls=%async_computation.1 | async-start | bytes 2097152 | tf_op jit(solution)/shard_map/all_to_all | solution.py:147
  172.6 16.3 %copy-start.1 = (f32[2048]{0:T(1024)S(1)}, f32[2048]{0:T(1024)}, u32[]{:S(2)}) copy-start(f32[2048]{0:T(1024)} %param.11) | copy-start | bytes 24580
Sparse Core Ops, SparseCore 0:
  11.5 123.5 all-gather.1

commit v7 on v6

--- a/solution.py
+++ b/solution.py
@@ -86,6 +86,13 @@
     )(index, flat_rows)
 
 
+def select_rows(rows, index):
+    picks = (index[:, None] == jnp.arange(rows.shape[0], dtype=index.dtype)[None, :])
+    return jnp.dot(
+        picks.astype(rows.dtype), rows, preferred_element_type=jnp.float32
+    ).astype(rows.dtype)
+
+
 CTX = ("cx", "cc")
 
 
@@ -118,19 +125,17 @@
     positions = jnp.arange(row_count, dtype=jnp.int32)
     capacity = 2 * row_count // peer_count
     starts = window_starts(anchors, row_count, capacity)
-    lanes = 128
-    width = input_entries.shape[2]
-    row_blocks = input_entries[0].reshape(row_count, width // lanes, lanes)
-    outgoing = pack_document_runs(row_blocks, starts[myself], peer_count, capacity)
-    arriving_rows = lax.all_to_all(outgoing, CTX, split_axis=0, concat_axis=0, tiled=True)
+    rows = input_entries[0]
+    outgoing = select_rows(rows, (starts[myself][:, None] + jnp.arange(capacity)).reshape(-1))
+    arriving_rows = lax.all_to_all(
+        outgoing.reshape(peer_count, capacity, -1), CTX, split_axis=0, concat_axis=0, tiled=True
+    )
     source, within, anchor = source_of(
         positions, run_ends[:, myself], offsets[:, myself], anchors[:, myself], peer_count
     )
     shift = anchor - jnp.take(starts[:, myself], source, mode="clip")
     index = source * capacity + shift + within
-    moved_rows = unpack_runs(
-        arriving_rows.reshape((peer_count * capacity,) + row_blocks.shape[1:]), index, row_count
-    ).reshape(row_count, width)
+    moved_rows = select_rows(arriving_rows.reshape(peer_count * capacity, -1), index)
     normed = rms_normed(moved_rows, norm_gain)
     sibling_rows = lax.ppermute(normed, "cc", perm=[(0, 1), (1, 0)])
 

time: 196 us -> 185 us (0.944)
  blocking collectives: 0 us -> 17.1 us
  matrix products: 23.1 us -> 37.1 us
  Pallas kernels: 13.1 us -> 0 us
  local copies, waits for them, and re-layouts: 19.5 us -> 8.32 us
  other arithmetic: 19.9 us -> 8.75 us
  waiting for transfers between devices: 95.1 us -> 90.8 us
  starting transfers between devices: 10.9 us -> 7.18 us
    all_to_all x0 -> x1, blocking collectives: none -> 17.1 us  [on_device(): lax.all_to_all(mapped, 'cx', split_axis=0, concat_axis=0, tiled=True)]
    dot_general x0 -> x2, matrix products: none -> 13.9 us  [select_rows(): jnp.dot(picks.astype(rows.dtype), rows, preferred_element_type=jnp.float32)]
    pallas_call x2 -> x0, Pallas kernels: 13.1 us -> none  [the longest x1 6.59 us: pack_document_runs(): pl.pallas_call(_pack_kernel, out_shape=jax.ShapeDtypeStruct(out_shape, ro...]
    all_to_all x2 -> x1, waiting for transfers between devices: 95.1 us -> 87.7 us  [on_device(): lax.all_to_all(outgoing.reshape(peer_count, capacity, -1), CTX, split_axi...]
    another operation x1 -> x0, local copies, waits for them, and re-layouts: 7.28 us -> none  [on_device(): return (moved_rows[None], by_heads)]
    convert_element_type x1, other arithmetic: 7.91 us -> 3.16 us  [rms_normed(): return (as_float * inverse_rms * norm_gain[None, :]).astype(jnp.bfloat16)]
    all_to_all x2 -> x1, starting transfers between devices: 10 us -> 6.26 us  [on_device(): lax.all_to_all(outgoing.reshape(peer_count, capacity, -1), CTX, split_axi...]
    unnamed x14 -> x11, local copies, waits for them, and re-layouts: 8.36 us -> 4.89 us
  transfers between devices with their start and end apart: 4 -> 3, of which waited for: 2 -> 2; matrix products, arithmetic and copies ran while one was open for 23% -> 19% of each run, Pallas kernels for 7% -> 0%
where the time goes in v7:
time: 185 us; the launch traced here: 183 us
  waiting for transfers between devices  90.8 us (49%)
  matrix products  37.1 us (20%)
  blocking collectives  17.1 us (9%)
  between operations  14.2 us (8%)
  other arithmetic  8.75 us (5%)
  local copies, waits for them, and re-layouts  8.32 us (4%)
  starting transfers between devices  7.18 us (4%)
    all_to_all x1, waiting for transfers between devices, on_device(): lax.all_to_all(outgoing.reshape(peer_count, capacity, -1), CTX, split_axi...  87.7 us
    dot_general x2, matrix products, project(): jnp.dot(rows, gathered_weight, preferred_element_type=jnp.float32)  23.1 us
    all_to_all x1, blocking collectives, on_device(): lax.all_to_all(mapped, 'cx', split_axis=0, concat_axis=0, tiled=True)  17.1 us
    dot_general x2, matrix products, select_rows(): jnp.dot(picks.astype(rows.dtype), rows, preferred_element_type=jnp.float32)  13.9 us
    all_to_all x1, starting transfers between devices, on_device(): lax.all_to_all(outgoing.reshape(peer_count, capacity, -1), CTX, split_axi...  6.26 us
    add x1, other arithmetic, on_device(): index = source * capacity + shift + within  4.97 us
    unnamed x11, local copies, waits for them, and re-layouts  4.89 us
  transfers between devices with their start and end apart: 3, of which 2 were waited for; matrix products, arithmetic and copies ran while one was open for 19% of the time, Pallas kernels for 0%

profile of v7, /device:TPU:1, one launch (start us, length us, event | category | flops | bytes accessed | tf_op | source)
XLA Modules:
  0.0 183.4 jit_solution(10368564953617263755)
XLA Ops:
  7.2 0.0 copy-start
  7.2 0.0 copy-start.2
  7.2 0.0 copy-start.4
  7.2 0.0 all-gather.2.cloned.1.call-start
  7.2 2.9 %copy.34 = bf16[512,2048]{0,1:T(8,128)(2,1)S(1)} copy(bf16[512,2048]{1,0:T(8,128)(2,1)} %param.10) | data formatting | bytes 4194304 | tf_op args[4]
  10.1 0.1 dynamic-slice_bitcast_fusion
  10.2 1.1 copy.36
  11.3 0.0 copy-done
  11.3 0.0 all-gather.2.cloned.1.call-update
  11.3 0.0 copy-done.2
  11.4 0.2 reduce_window_sum.23
  11.5 0.0 copy-done.4
  11.5 0.1 select_reduce_fusion.1
  11.7 0.1 iota_add_fusion
  11.7 0.1 add.85
  11.8 7.8 %convolution_convert_fusion = bf16[512,8192]{1,0:T(8,128)(2,1)} fusion(bf16[1,256,8192]{2,1,0:T(8,128)(2,1)} %param.6, s32[512]{0:T(512)S(1)} %add.85), kind=kOutput, calls=%fused_computation | convolution fusion | flops 2151809024 | bytes 12584960 | tf_op jit(solution)/shard_map/dot_general | solution.py:91
  19.6 6.3 %all-to-all-start = ((bf16[8,64,8192]{2,1,0:T(8,128)(2,1)}), bf16[8,64,8192]{2,1,0:T(8,128)(2,1)}, u32[]{:S(2)}, u32[]{:S(2)}) async-start(bf16[8,64,8192]{2,1,0:T(8,128)(2,1)} %bitcast.51), calls=%async_computation | async-start | bytes 16777216 | tf_op jit(solution)/shard_map/all_to_all | solution.py:130
  25.9 0.2 dynamic-slice_reduce_fusion
  26.1 0.2 dynamic-slice_reduce_fusion.2
  26.3 0.6 fusion.11
  26.9 0.1 convert_reduce_fusion
  27.0 0.1 select_reduce_fusion.3
  27.1 5.0 %subtract_add_fusion = s32[256]{0:T(256)S(1)} fusion(s32[256]{0:T(256)S(1)} %get-tuple-element.17, s32[256]{0:T(256)S(1)} %get-tuple-element.16, s32[256]{0:T(256)S(1)} %convert_reduce_fusion, s32[]{:T(128)} %bitcast.2, s32[]{:T(128)} %bitcast.3, s32[]{:T(128)} %bitcast.4, s32[]{:T(128)} %bitcast.5, s32[]{:T(128)} %bitcast.6, s32[]{:T(128)} %bitcast.7, ...), kind=kLoop, calls=%fused_computation.48 | loop fusion | flops 4864 | bytes 4128 | tf_op jit(solution)/shard_map/add | solution.py:137
  32.0 87.7 %all-to-all-done = bf16[8,64,8192]{2,1,0:T(8,128)(2,1)} async-done(((bf16[8,64,8192]{2,1,0:T(8,128)(2,1)}), bf16[8,64,8192]{2,1,0:T(8,128)(2,1)}, u32[]{:S(2)}, u32[]{:S(2)}) %all-to-all-start) | async-done | bytes 8388640 | tf_op jit(solution)/shard_map/all_to_all | solution.py:130
  119.7 0.0 copy-start.3
  119.7 6.1 %fusion = (f32[256]{0:T(256)S(1)}, bf16[256,8192]{1,0:T(8,128)(2,1)S(1)}) fusion(bf16[512,8192]{1,0:T(8,128)(2,1)} %bitcast.22, s32[256]{0:T(256)S(1)} %subtract_add_fusion), kind=kOutput, calls=%fused_computation.4 | convolution fusion | flops 2156003072 | bytes 12584960 | tf_op jit(solution)/shard_map/dot_general | solution.py:91
  125.9 0.0 copy-start.1
  125.9 2.0 %copy-done.1 = bf16[256,8192]{1,0:T(8,128)(2,1)} copy-done((bf16[256,8192]{1,0:T(8,128)(2,1)}, bf16[256,8192]{1,0:T(8,128)(2,1)S(1)}, u32[]{:S(2)}) %copy-start.1) | copy-done | bytes 4194328
  127.9 0.0 copy-done.3
  127.9 3.2 %fusion.2 = bf16[256,8192]{1,0:T(8,128)(2,1)} fusion(bf16[256,8192]{1,0:T(8,128)(2,1)S(1)} %get-tuple-element.29, f32[8192]{0:T(1024)S(1)} %copy-done.3, f32[256]{0:T(256)S(1)} %add_rsqrt_fusion), kind=kLoop, calls=%fused_computation.6 | loop fusion | flops 8388608 | bytes 8422400 | tf_op jit(solution)/shard_map/convert_element_type | solution.py:36
  131.0 0.9 collective-permute-start
  131.9 3.1 %all-gather.2.cloned.1.call-done = bf16[8192,1024]{0,1:T(8,128)(2,1)} async-done(((bf16[512,1024]{0,1:T(8,128)(2,1)}), bf16[8192,1024]{0,1:T(8,128)(2,1)}) %all-gather.2.cloned.1.call-update) | async-done | bytes 16777232 | tf_op jit(solution)/shard_map/all_gather | solution.py:120
  135.0 11.6 %fusion.4 = bf16[256,1024]{1,0:T(8,128)(2,1)S(1)} fusion(bf16[256,8192]{1,0:T(8,128)(2,1)} %fusion.2, bf16[8192,1024]{0,1:T(8,128)(2,1)} %all-gather.2.cloned.1.call-done, f32[1024]{0:T(1024)S(1)} %bitcast.64), kind=kOutput, calls=%fused_computation.10 | convolution fusion | flops 4295491584 | bytes 21499904 | tf_op jit(solution)/shard_map/dot_general | solution.py:143
  146.6 0.0 collective-permute-done
  146.6 11.6 %broadcast_select_fusion.1 = (bf16[256,1024]{1,0:T(8,128)(2,1)S(1)}, bf16[256,1024]{1,0:T(8,128)(2,1)S(1)}) fusion(bf16[256,1024]{1,0:T(8,128)(2,1)S(1)} %fusion.4, pred[]{:T(512)S(6)} %eq.71, f32[1024]{0:T(1024)S(1)} %bitcast.65, bf16[256,8192]{1,0:T(8,128)(2,1)} %collective-permute-done, bf16[8192,1024]{0,1:T(8,128)(2,1)} %all-gather.2.cloned.1.call-done), kind=kOutput, calls=%fused_computation.19 | convolution fusion | flops 4296015872 | bytes 22548480 | tf_op jit(solution)/shard_map/dot_general | solution.py:143
  158.3 0.1 pad_maximum_fusion
  158.4 17.1 %all_to_all.10 = bf16[4,512,256]{2,1,0:T(8,128)(2,1)S(1)} all-to-all(bf16[4,512,256]{2,1,0:T(8,128)(2,1)S(1)} %pad_maximum_fusion), channel_id=1, replica_groups=mesh['dp'=16,'cx'=4,'cc'=2] {'cx'}, dimensions={0} | all-to-all | bytes 2097152 | tf_op jit(solution)/shard_map/all_to_all | solution.py:152
  175.4 1.1 reshape.96
  (10 shorter events, 0.1 us)
Async XLA Ops:
  7.2 4.1 %copy-start = (f32[2048]{0:T(1024)S(1)}, f32[2048]{0:T(1024)}, u32[]{:S(2)}) copy-start(f32[2048]{0:T(1024)} %param.11) | copy-start | bytes 24580
  7.2 4.2 %copy-start.2 = (s32[1,8,8]{2,1,0:T(8,128)S(1)}, s32[1,8,8]{2,1,0:T(8,128)}, u32[]{:S(2)}) copy-start(s32[1,8,8]{2,1,0:T(8,128)} %param.7) | copy-start | bytes 772
  7.2 4.3 %copy-start.4 = (s32[1,8,8]{2,1,0:T(8,128)S(1)}, s32[1,8,8]{2,1,0:T(8,128)}, u32[]{:S(2)}) copy-start(s32[1,8,8]{2,1,0:T(8,128)} %param.8) | copy-start | bytes 772
  7.2 127.8 %all-gather.2.cloned.1.call-start = ((), (), s32[]{:S(2)}) async-start(), calls=%async_computation.2 | async-start | bytes 17825792 | tf_op jit(solution)/shard_map/all_gather | solution.py:120
  19.6 100.1 %all-to-all-start = ((bf16[8,64,8192]{2,1,0:T(8,128)(2,1)}), bf16[8,64,8192]{2,1,0:T(8,128)(2,1)}, u32[]{:S(2)}, u32[]{:S(2)}) async-start(bf16[8,64,8192]{2,1,0:T(8,128)(2,1)} %bitcast.51), calls=%async_computation | async-start | bytes 16777216 | tf_op jit(solution)/shard_map/all_to_all | solution.py:130
  119.7 8.2 %copy-start.3 = (f32[8192]{0:T(1024)S(1)}, f32[8192]{0:T(1024)}, u32[]{:S(2)}) copy-start(f32[8192]{0:T(1024)} %param.9) | copy-start | bytes 98308
  125.9 2.0 %copy-start.1 = (bf16[256,8192]{1,0:T(8,128)(2,1)}, bf16[256,8192]{1,0:T(8,128)(2,1)S(1)}, u32[]{:S(2)}) copy-start(bf16[256,8192]{1,0:T(8,128)(2,1)S(1)} %get-tuple-element.29) | copy-start | bytes 12582916
  131.0 15.6 %collective-permute-start = (bf16[256,8192]{1,0:T(8,128)(2,1)}, bf16[256,8192]{1,0:T(8,128)(2,1)}, u32[]{:S(2)}, u32[]{:S(2)}) collective-permute-start(bf16[256,8192]{1,0:T(8,128)(2,1)} %fusion.2), channel_id=1, source_target_pairs={{0,1},{1,0},{2,3},{3,2},{4,5},{5,4},{6,7},{7,6},{8,9},{9,8},{10,11... | collective-permute-start | bytes 12582920 | tf_op jit(solution)/shard_map/ppermute | solution.py:140
Sparse Core Ops, SparseCore 0:
  11.5 123.5 all-gather.1

commit v8 on v7

--- a/solution.py
+++ b/solution.py
@@ -144,12 +144,27 @@
         products = (products + local_bias[None, :]).astype(jnp.bfloat16)
         return jnp.swapaxes(products.reshape(row_count, heads_per_core, 2 * HD), 0, 1)
 
-    own = project(normed)
-    other = project(sibling_rows)
+    def exchange(blocks):
+        here = lax.axis_index("cx")
+        gathered = jnp.zeros_like(blocks)
+        gathered = lax.dynamic_update_index_in_dim(
+            gathered, lax.dynamic_index_in_dim(blocks, here, 0), here, 0
+        )
+        for step in range(1, chips):
+            outgoing_block = lax.dynamic_index_in_dim(blocks, (here + step) % chips, 0)
+            arrived = lax.ppermute(
+                outgoing_block, "cx", perm=[(i, (i + step) % chips) for i in range(chips)]
+            )
+            gathered = lax.dynamic_update_index_in_dim(
+                gathered, arrived, (here + chips - step) % chips, 0
+            )
+        return gathered
+
+    own = exchange(project(normed))
+    other = exchange(project(sibling_rows))
     first = jnp.where(core == 0, own, other)
     second = jnp.where(core == 0, other, own)
-    mapped = jnp.concatenate([first, second], axis=1)
-    by_heads = lax.all_to_all(mapped, "cx", split_axis=0, concat_axis=0, tiled=True)
+    by_heads = jnp.concatenate([first, second], axis=1)
     by_heads = by_heads.reshape(1, chips * cores * row_count, 2, 1, HD)
     return (moved_rows[None], by_heads)
 

time: 185 us -> 187 us (1.011)
  blocking collectives: 17.1 us -> 0 us
  starting transfers between devices: 7.18 us -> 15 us
  waiting for transfers between devices: 90.8 us -> 98.5 us
  local copies, waits for them, and re-layouts: 8.32 us -> 11.5 us
    all_to_all x1 -> x0, blocking collectives: 17.1 us -> none  [on_device(): lax.all_to_all(mapped, 'cx', split_axis=0, concat_axis=0, tiled=True)]
    ppermute x0 -> x6, starting transfers between devices: none -> 7.77 us  [exchange(): lax.ppermute(outgoing_block, 'cx', perm=[(i, (i + step) % chips) for i in...]
    ppermute x1, waiting for transfers between devices: 0.01 us -> 7.13 us  [on_device(): sibling_rows = lax.ppermute(normed, 'cc', perm=[(0, 1), (1, 0)])]
    ppermute x0 -> x6, waiting for transfers between devices: none -> 3.66 us  [exchange(): lax.ppermute(outgoing_block, 'cx', perm=[(i, (i + step) % chips) for i in...]
    all_gather x1, waiting for transfers between devices: 3.13 us -> 0.01 us  [on_device(): gathered_weight = lax.all_gather(local_weight, 'dp', axis=0, tiled=True)]
    another operation x0 -> x4, local copies, waits for them, and re-layouts: none -> 2.25 us
    unnamed x11 -> x17, local copies, waits for them, and re-layouts: 4.89 us -> 5 us
  transfers between devices with their start and end apart: 3 -> 9, of which waited for: 2 -> 5; matrix products, arithmetic and copies ran while one was open for 19% -> 20% of each run, Pallas kernels for 0% -> 0%
where the time goes in v8:
time: 187 us; the launch traced here: 185 us
  waiting for transfers between devices  98.5 us (53%)
  matrix products  37 us (20%)
  starting transfers between devices  15 us (8%)
  between operations  14.3 us (8%)
  local copies, waits for them, and re-layouts  11.5 us (6%)
  other arithmetic  8.76 us (5%)
    all_to_all x1, waiting for transfers between devices, on_device(): lax.all_to_all(outgoing.reshape(peer_count, capacity, -1), CTX, split_axi...  87.7 us
    dot_general x2, matrix products, project(): jnp.dot(rows, gathered_weight, preferred_element_type=jnp.float32)  23.1 us
    dot_general x2, matrix products, select_rows(): jnp.dot(picks.astype(rows.dtype), rows, preferred_element_type=jnp.float32)  13.9 us
    ppermute x6, starting transfers between devices, exchange(): lax.ppermute(outgoing_block, 'cx', perm=[(i, (i + step) % chips) for i in...  7.77 us
    ppermute x1, waiting for transfers between devices, on_device(): sibling_rows = lax.ppermute(normed, 'cc', perm=[(0, 1), (1, 0)])  7.13 us
    all_to_all x1, starting transfers between devices, on_device(): lax.all_to_all(outgoing.reshape(peer_count, capacity, -1), CTX, split_axi...  6.27 us
    unnamed x17, local copies, waits for them, and re-layouts  5 us
    add x1, other arithmetic, on_device(): index = source * capacity + shift + within  4.97 us
  transfers between devices with their start and end apart: 9, of which 5 were waited for; matrix products, arithmetic and copies ran while one was open for 20% of the time, Pallas kernels for 0%

profile of v8, /device:TPU:1, one launch (start us, length us, event | category | flops | bytes accessed | tf_op | source)
XLA Modules:
  0.0 185.1 jit_solution(13288338241801035515)
XLA Ops:
  7.2 0.0 copy-start
  7.2 0.0 copy-start.2
  7.2 0.0 copy-start.4
  7.2 0.0 all-gather.2.cloned.1.call-start
  7.3 2.9 %copy.52 = bf16[512,2048]{0,1:T(8,128)(2,1)S(1)} copy(bf16[512,2048]{1,0:T(8,128)(2,1)} %param.10) | data formatting | bytes 4194304 | tf_op args[4]
  10.1 0.1 dynamic-slice_bitcast_fusion
  10.2 1.1 copy.54
  11.3 0.0 copy-done
  11.4 0.0 all-gather.2.cloned.1.call-update
  11.4 0.0 copy-done.2
  11.4 0.2 reduce_window_sum.23
  11.6 0.0 copy-done.4
  11.6 0.1 select_reduce_fusion.1
  11.7 0.1 iota_add_fusion
  11.8 0.1 add.155
  11.9 7.8 %convolution_convert_fusion = bf16[512,8192]{1,0:T(8,128)(2,1)} fusion(bf16[1,256,8192]{2,1,0:T(8,128)(2,1)} %param.6, s32[512]{0:T(512)S(1)} %add.155), kind=kOutput, calls=%fused_computation | convolution fusion | flops 2151809024 | bytes 12584960 | tf_op jit(solution)/shard_map/dot_general | solution.py:91
  19.6 6.3 %all-to-all-start = ((bf16[8,64,8192]{2,1,0:T(8,128)(2,1)}), bf16[8,64,8192]{2,1,0:T(8,128)(2,1)}, u32[]{:S(2)}, u32[]{:S(2)}) async-start(bf16[8,64,8192]{2,1,0:T(8,128)(2,1)} %bitcast.62), calls=%async_computation | async-start | bytes 16777216 | tf_op jit(solution)/shard_map/all_to_all | solution.py:130
  25.9 0.2 fusion.10
  26.1 0.2 constant_dynamic-slice_fusion.11
  26.3 0.6 fusion.16
  26.9 0.1 convert_reduce_fusion
  27.0 0.1 select_reduce_fusion.3
  27.1 5.0 %subtract_add_fusion = s32[256]{0:T(256)S(1)} fusion(s32[256]{0:T(256)S(1)} %get-tuple-element.11, s32[256]{0:T(256)S(1)} %get-tuple-element.10, s32[256]{0:T(256)S(1)} %convert_reduce_fusion, s32[]{:T(128)} %bitcast.2, s32[]{:T(128)} %bitcast.3, s32[]{:T(128)} %bitcast.4, s32[]{:T(128)} %bitcast.5, s32[]{:T(128)} %bitcast.6, s32[]{:T(128)} %bitcast.7, ...), kind=kLoop, calls=%fused_computation.73 | loop fusion | flops 4864 | bytes 4128 | tf_op jit(solution)/shard_map/add | solution.py:137
  32.1 87.7 %all-to-all-done = bf16[8,64,8192]{2,1,0:T(8,128)(2,1)} async-done(((bf16[8,64,8192]{2,1,0:T(8,128)(2,1)}), bf16[8,64,8192]{2,1,0:T(8,128)(2,1)}, u32[]{:S(2)}, u32[]{:S(2)}) %all-to-all-start) | async-done | bytes 8388640 | tf_op jit(solution)/shard_map/all_to_all | solution.py:130
  119.8 0.0 copy-start.3
  119.8 6.1 %fusion = (f32[256]{0:T(256)S(1)}, bf16[256,8192]{1,0:T(8,128)(2,1)S(1)}) fusion(bf16[512,8192]{1,0:T(8,128)(2,1)} %bitcast.22, s32[256]{0:T(256)S(1)} %subtract_add_fusion), kind=kOutput, calls=%fused_computation.4 | convolution fusion | flops 2156003072 | bytes 12584960 | tf_op jit(solution)/shard_map/dot_general | solution.py:91
  125.9 0.0 copy-start.1
  125.9 2.0 %copy-done.1 = bf16[256,8192]{1,0:T(8,128)(2,1)} copy-done((bf16[256,8192]{1,0:T(8,128)(2,1)}, bf16[256,8192]{1,0:T(8,128)(2,1)S(1)}, u32[]{:S(2)}) %copy-start.1) | copy-done | bytes 4194328
  127.9 0.0 copy-done.3
  127.9 3.1 %fusion.2 = bf16[256,8192]{1,0:T(8,128)(2,1)} fusion(bf16[256,8192]{1,0:T(8,128)(2,1)S(1)} %get-tuple-element.31, f32[8192]{0:T(1024)S(1)} %copy-done.3, f32[256]{0:T(256)S(1)} %add_rsqrt_fusion), kind=kLoop, calls=%fused_computation.6 | loop fusion | flops 8388608 | bytes 8422400 | tf_op jit(solution)/shard_map/convert_element_type | solution.py:36
  131.0 0.9 collective-permute-start.3
  131.9 7.1 %collective-permute-done.3 = bf16[256,8192]{1,0:T(8,128)(2,1)} collective-permute-done((bf16[256,8192]{1,0:T(8,128)(2,1)}, bf16[256,8192]{1,0:T(8,128)(2,1)}, u32[]{:S(2)}, u32[]{:S(2)}) %collective-permute-start.3) | collective-permute-done | bytes 4194336 | tf_op jit(solution)/shard_map/ppermute | solution.py:140
  139.0 0.0 all-gather.2.cloned.1.call-done
  139.0 11.6 %fusion.5 = bf16[256,1024]{1,0:T(8,128)(2,1)S(1)} fusion(bf16[256,8192]{1,0:T(8,128)(2,1)} %collective-permute-done.3, bf16[8192,1024]{0,1:T(8,128)(2,1)} %all-gather.2.cloned.1.call-done, f32[1024]{0:T(1024)S(1)} %bitcast.76), kind=kOutput, calls=%fused_computation.11 | convolution fusion | flops 4295491584 | bytes 21499904 | tf_op jit(solution)/shard_map/dot_general | solution.py:143
  150.6 0.4 reshape.105
  151.0 1.1 constant_dynamic-slice_fusion
  152.1 0.4 collective-permute-start.4
  152.6 1.9 %collective-permute-start.5 = (bf16[1,256,256]{2,1,0:T(8,128)(2,1)S(1)}, bf16[1,256,256]{2,1,0:T(8,128)(2,1)S(1)}, u32[]{:S(2)}, u32[]{:S(2)}) collective-permute-start(bf16[1,256,256]{2,1,0:T(8,128)(2,1)S(1)} %bitcast.67), channel_id=1, source_target_pairs={{0,4},{2,6},{4,0},{6,2},{1,5},{3,7},{5,1},{7,3},{8,12},{10,14},{12... | collective-permute-start | bytes 393224 | tf_op jit(solution)/shard_map/ppermute | solution.py:155
  154.5 0.9 collective-permute-start.6
  155.4 11.6 %fusion.4 = bf16[256,1024]{1,0:T(8,128)(2,1)S(1)} fusion(bf16[256,8192]{1,0:T(8,128)(2,1)} %fusion.2, bf16[8192,1024]{0,1:T(8,128)(2,1)} %all-gather.2.cloned.1.call-done, f32[1024]{0:T(1024)S(1)} %bitcast.77), kind=kOutput, calls=%fused_computation.10 | convolution fusion | flops 4295491584 | bytes 21499904 | tf_op jit(solution)/shard_map/dot_general | solution.py:143
  166.9 0.4 reshape.104
  167.3 1.1 constant_dynamic-slice_fusion.4
  168.4 0.9 collective-permute-start
  169.4 1.5 collective-permute-start.1
  171.1 0.0 collective-permute-done.4
  171.1 2.1 %collective-permute-start.2 = (bf16[1,256,256]{2,1,0:T(8,128)(2,1)S(1)}, bf16[1,256,256]{2,1,0:T(8,128)(2,1)S(1)}, u32[]{:S(2)}, u32[]{:S(2)}) collective-permute-start(bf16[1,256,256]{2,1,0:T(8,128)(2,1)S(1)} %bitcast.71), channel_id=1, source_target_pairs={{0,6},{2,0},{4,2},{6,4},{1,7},{3,1},{5,3},{7,5},{8,14},{10,8},{12,... | collective-permute-start | bytes 393224 | tf_op jit(solution)/shard_map/ppermute | solution.py:155
  173.2 0.0 collective-permute-done.5
  173.2 0.0 collective-permute-done.6
  173.3 0.7 collective-permute-done
  174.0 2.4 %collective-permute-done.1 = bf16[1,256,256]{2,1,0:T(8,128)(2,1)S(1)} collective-permute-done((bf16[1,256,256]{2,1,0:T(8,128)(2,1)S(1)}, bf16[1,256,256]{2,1,0:T(8,128)(2,1)S(1)}, u32[]{:S(2)}, u32[]{:S(2)}) %collective-permute-start.1) | collective-permute-done | bytes 131104 | tf_op jit(solution)/shard_map/ppermute | solution.py:155
  176.5 0.5 collective-permute-done.2
  177.0 0.1 broadcast_select_fusion.1
  177.1 0.1 pad_maximum_fusion
  177.1 1.1 reshape.106
  (24 shorter events, 0.4 us)
Async XLA Ops:
  7.2 4.2 %copy-start = (f32[2048]{0:T(1024)S(1)}, f32[2048]{0:T(1024)}, u32[]{:S(2)}) copy-start(f32[2048]{0:T(1024)} %param.11) | copy-start | bytes 24580
  7.2 4.2 %copy-start.2 = (s32[1,8,8]{2,1,0:T(8,128)S(1)}, s32[1,8,8]{2,1,0:T(8,128)}, u32[]{:S(2)}) copy-start(s32[1,8,8]{2,1,0:T(8,128)} %param.7) | copy-start | bytes 772
  7.2 4.4 %copy-start.4 = (s32[1,8,8]{2,1,0:T(8,128)S(1)}, s32[1,8,8]{2,1,0:T(8,128)}, u32[]{:S(2)}) copy-start(s32[1,8,8]{2,1,0:T(8,128)} %param.8) | copy-start | bytes 772
  7.2 131.8 %all-gather.2.cloned.1.call-start = ((), (), s32[]{:S(2)}) async-start(), calls=%async_computation.1 | async-start | bytes 17825792 | tf_op jit(solution)/shard_map/all_gather | solution.py:120
  19.6 100.1 %all-to-all-start = ((bf16[8,64,8192]{2,1,0:T(8,128)(2,1)}), bf16[8,64,8192]{2,1,0:T(8,128)(2,1)}, u32[]{:S(2)}, u32[]{:S(2)}) async-start(bf16[8,64,8192]{2,1,0:T(8,128)(2,1)} %bitcast.62), calls=%async_computation | async-start | bytes 16777216 | tf_op jit(solution)/shard_map/all_to_all | solution.py:130
  119.8 8.1 %copy-start.3 = (f32[8192]{0:T(1024)S(1)}, f32[8192]{0:T(1024)}, u32[]{:S(2)}) copy-start(f32[8192]{0:T(1024)} %param.9) | copy-start | bytes 98308
  125.9 2.0 %copy-start.1 = (bf16[256,8192]{1,0:T(8,128)(2,1)}, bf16[256,8192]{1,0:T(8,128)(2,1)S(1)}, u32[]{:S(2)}) copy-start(bf16[256,8192]{1,0:T(8,128)(2,1)S(1)} %get-tuple-element.31) | copy-start | bytes 12582916
  131.0 8.0 %collective-permute-start.3 = (bf16[256,8192]{1,0:T(8,128)(2,1)}, bf16[256,8192]{1,0:T(8,128)(2,1)}, u32[]{:S(2)}, u32[]{:S(2)}) collective-permute-start(bf16[256,8192]{1,0:T(8,128)(2,1)} %fusion.2), channel_id=1, source_target_pairs={{0,1},{1,0},{2,3},{3,2},{4,5},{5,4},{6,7},{7,6},{8,9},{9,8},{10,11... | collective-permute-start | bytes 12582920 | tf_op jit(solution)/shard_map/ppermute | solution.py:140
  152.1 19.0 %collective-permute-start.4 = (bf16[1,256,256]{2,1,0:T(8,128)(2,1)S(1)}, bf16[1,256,256]{2,1,0:T(8,128)(2,1)S(1)}, u32[]{:S(2)}, u32[]{:S(2)}) collective-permute-start(bf16[1,256,256]{2,1,0:T(8,128)(2,1)S(1)} %bitcast.68), channel_id=1, source_target_pairs={{0,2},{2,4},{4,6},{6,0},{1,3},{3,5},{5,7},{7,1},{8,10},{10,12},{12... | collective-permute-start | bytes 393224 | tf_op jit(solution)/shard_map/ppermute | solution.py:155
  152.6 20.7 %collective-permute-start.5 = (bf16[1,256,256]{2,1,0:T(8,128)(2,1)S(1)}, bf16[1,256,256]{2,1,0:T(8,128)(2,1)S(1)}, u32[]{:S(2)}, u32[]{:S(2)}) collective-permute-start(bf16[1,256,256]{2,1,0:T(8,128)(2,1)S(1)} %bitcast.67), channel_id=1, source_target_pairs={{0,4},{2,6},{4,0},{6,2},{1,5},{3,7},{5,1},{7,3},{8,12},{10,14},{12... | collective-permute-start | bytes 393224 | tf_op jit(solution)/shard_map/ppermute | solution.py:155
  154.5 18.8 %collective-permute-start.6 = (bf16[1,256,256]{2,1,0:T(8,128)(2,1)S(1)}, bf16[1,256,256]{2,1,0:T(8,128)(2,1)S(1)}, u32[]{:S(2)}, u32[]{:S(2)}) collective-permute-start(bf16[1,256,256]{2,1,0:T(8,128)(2,1)S(1)} %bitcast.66), channel_id=1, source_target_pairs={{0,6},{2,0},{4,2},{6,4},{1,7},{3,1},{5,3},{7,5},{8,14},{10,8},{12,... | collective-permute-start | bytes 393224 | tf_op jit(solution)/shard_map/ppermute | solution.py:155
  168.4 5.6 %collective-permute-start = (bf16[1,256,256]{2,1,0:T(8,128)(2,1)S(1)}, bf16[1,256,256]{2,1,0:T(8,128)(2,1)S(1)}, u32[]{:S(2)}, u32[]{:S(2)}) collective-permute-start(bf16[1,256,256]{2,1,0:T(8,128)(2,1)S(1)} %bitcast.70), channel_id=1, source_target_pairs={{0,2},{2,4},{4,6},{6,0},{1,3},{3,5},{5,7},{7,1},{8,10},{10,12},{12... | collective-permute-start | bytes 393224 | tf_op jit(solution)/shard_map/ppermute | solution.py:155
  169.4 7.1 %collective-permute-start.1 = (bf16[1,256,256]{2,1,0:T(8,128)(2,1)S(1)}, bf16[1,256,256]{2,1,0:T(8,128)(2,1)S(1)}, u32[]{:S(2)}, u32[]{:S(2)}) collective-permute-start(bf16[1,256,256]{2,1,0:T(8,128)(2,1)S(1)} %bitcast.69), channel_id=1, source_target_pairs={{0,4},{2,6},{4,0},{6,2},{1,5},{3,7},{5,1},{7,3},{8,12},{10,14},{12... | collective-permute-start | bytes 393224 | tf_op jit(solution)/shard_map/ppermute | solution.py:155
  171.1 5.9 %collective-permute-start.2 = (bf16[1,256,256]{2,1,0:T(8,128)(2,1)S(1)}, bf16[1,256,256]{2,1,0:T(8,128)(2,1)S(1)}, u32[]{:S(2)}, u32[]{:S(2)}) collective-permute-start(bf16[1,256,256]{2,1,0:T(8,128)(2,1)S(1)} %bitcast.71), channel_id=1, source_target_pairs={{0,6},{2,0},{4,2},{6,4},{1,7},{3,1},{5,3},{7,5},{8,14},{10,8},{12,... | collective-permute-start | bytes 393224 | tf_op jit(solution)/shard_map/ppermute | solution.py:155
Sparse Core Ops, SparseCore 0:
  11.5 123.5 all-gather.1

commit v9 on v7

--- a/solution.py
+++ b/solution.py
@@ -107,13 +107,15 @@
     row_count = input_entries.shape[1]
     width = kv_weight.shape[0]
     heads_per_core = KVH // cores
+    here = lax.axis_index("cx")
     local_weight = kv_weight.reshape(width, 2, heads_per_core, cores, HD)
     local_weight = lax.dynamic_index_in_dim(local_weight, core, axis=3, keepdims=False)
-    local_weight = jnp.swapaxes(local_weight, 1, 2).reshape(width, heads_per_core * 2 * HD)
+    local_weight = jnp.roll(jnp.swapaxes(local_weight, 1, 2), -here, axis=1)
+    local_weight = local_weight.reshape(width, heads_per_core * 2 * HD)
     local_bias = lax.dynamic_index_in_dim(
         kv_bias.reshape(2, heads_per_core, cores, HD), core, axis=2, keepdims=False
     )
-    local_bias = jnp.swapaxes(local_bias, 0, 1).reshape(-1)
+    local_bias = jnp.roll(jnp.swapaxes(local_bias, 0, 1), -here, axis=0).reshape(-1)
     local_weight, local_bias, input_entries = lax.optimization_barrier(
         (local_weight, local_bias, input_entries)
     )
@@ -149,7 +151,15 @@
     first = jnp.where(core == 0, own, other)
     second = jnp.where(core == 0, other, own)
     mapped = jnp.concatenate([first, second], axis=1)
-    by_heads = lax.all_to_all(mapped, "cx", split_axis=0, concat_axis=0, tiled=True)
+    by_heads = jnp.zeros_like(mapped)
+    by_heads = lax.dynamic_update_index_in_dim(by_heads, mapped[0], here, 0)
+    for step in range(1, chips):
+        arrived = lax.ppermute(
+            mapped[step], "cx", perm=[(i, (i + step) % chips) for i in range(chips)]
+        )
+        by_heads = lax.dynamic_update_index_in_dim(
+            by_heads, arrived, (here + chips - step) % chips, 0
+        )
     by_heads = by_heads.reshape(1, chips * cores * row_count, 2, 1, HD)
     return (moved_rows[None], by_heads)
 

time: 185 us -> 183 us (0.989)
  blocking collectives: 17.1 us -> 0 us
  waiting for transfers between devices: 90.8 us -> 100 us
  starting transfers between devices: 7.18 us -> 12 us
    all_to_all x1 -> x0, blocking collectives: 17.1 us -> none  [on_device(): lax.all_to_all(mapped, 'cx', split_axis=0, concat_axis=0, tiled=True)]
    ppermute x0 -> x3, waiting for transfers between devices: none -> 9.27 us  [on_device(): lax.ppermute(mapped[step], 'cx', perm=[(i, (i + step) % chips) for i in r...]
    ppermute x0 -> x3, starting transfers between devices: none -> 4.84 us  [on_device(): lax.ppermute(mapped[step], 'cx', perm=[(i, (i + step) % chips) for i in r...]
    dynamic_slice x0 -> x4, local copies, waits for them, and re-layouts: none -> 2.05 us  [the longest x1 1.31 us: on_device(): local_weight = jnp.roll(jnp.swapaxes(local_weight, 1, 2), -here, axis=1)]
  transfers between devices with their start and end apart: 3 -> 6, of which waited for: 2 -> 5; matrix products, arithmetic and copies ran while one was open for 19% -> 19% of each run, Pallas kernels for 0% -> 0%
where the time goes in v9:
time: 183 us; the launch traced here: 182 us
  waiting for transfers between devices  100 us (55%)
  matrix products  37.1 us (20%)
  between operations  14.3 us (8%)
  starting transfers between devices  12 us (7%)
  local copies, waits for them, and re-layouts  9.36 us (5%)
  other arithmetic  9.16 us (5%)
    all_to_all x1, waiting for transfers between devices, on_device(): lax.all_to_all(outgoing.reshape(peer_count, capacity, -1), CTX, split_axi...  87.7 us
    dot_general x2, matrix products, project(): jnp.dot(rows, gathered_weight, preferred_element_type=jnp.float32)  23.1 us
    dot_general x2, matrix products, select_rows(): jnp.dot(picks.astype(rows.dtype), rows, preferred_element_type=jnp.float32)  13.9 us
    ppermute x3, waiting for transfers between devices, on_device(): lax.ppermute(mapped[step], 'cx', perm=[(i, (i + step) % chips) for i in r...  9.27 us
    all_to_all x1, starting transfers between devices, on_device(): lax.all_to_all(outgoing.reshape(peer_count, capacity, -1), CTX, split_axi...  6.26 us
    add x1, other arithmetic, on_device(): index = source * capacity + shift + within  4.97 us
    unnamed x11, local copies, waits for them, and re-layouts  4.89 us
    ppermute x3, starting transfers between devices, on_device(): lax.ppermute(mapped[step], 'cx', perm=[(i, (i + step) % chips) for i in r...  4.84 us
  transfers between devices with their start and end apart: 6, of which 5 were waited for; matrix products, arithmetic and copies ran while one was open for 19% of the time, Pallas kernels for 0%

profile of v9, /device:TPU:1, one launch (start us, length us, event | category | flops | bytes accessed | tf_op | source)
XLA Modules:
  0.0 182.0 jit_solution(17027521904950441647)
XLA Ops:
  7.2 0.0 copy-start
  7.2 0.0 copy-start.2
  7.2 0.0 copy-start.4
  7.2 0.0 all-gather.2.cloned.1.call-start
  7.3 2.9 %copy.29 = bf16[512,2048]{0,1:T(8,128)(2,1)S(1)} copy(bf16[512,2048]{1,0:T(8,128)(2,1)} %param.10) | data formatting | bytes 4194304 | tf_op args[4]
  10.1 0.1 constant_dynamic-slice_fusion.1
  10.2 0.7 copy.30
  10.9 0.4 fusion.6
  11.3 1.3 copy.31
  12.6 0.0 copy-done
  12.7 0.0 all-gather.2.cloned.1.call-update
  12.7 0.0 copy-done.2
  12.7 0.2 reduce_window_sum.23
  12.9 0.0 copy-done.4
  12.9 0.1 select_reduce_fusion.1
  13.0 0.1 iota_add_fusion
  13.1 0.1 add.134
  13.2 7.8 %convolution_convert_fusion = bf16[512,8192]{1,0:T(8,128)(2,1)} fusion(bf16[1,256,8192]{2,1,0:T(8,128)(2,1)} %param.6, s32[512]{0:T(512)S(1)} %add.134), kind=kOutput, calls=%fused_computation | convolution fusion | flops 2151809024 | bytes 12584960 | tf_op jit(solution)/shard_map/dot_general | solution.py:91
  20.9 6.3 %all-to-all-start = ((bf16[8,64,8192]{2,1,0:T(8,128)(2,1)}), bf16[8,64,8192]{2,1,0:T(8,128)(2,1)}, u32[]{:S(2)}, u32[]{:S(2)}) async-start(bf16[8,64,8192]{2,1,0:T(8,128)(2,1)} %bitcast.61), calls=%async_computation | async-start | bytes 16777216 | tf_op jit(solution)/shard_map/all_to_all | solution.py:132
  27.2 0.2 dynamic-slice_reduce_fusion
  27.4 0.2 dynamic-slice_reduce_fusion.2
  27.6 0.6 fusion.20
  28.2 0.1 convert_reduce_fusion
  28.3 0.1 select_reduce_fusion.3
  28.4 5.0 %subtract_add_fusion = s32[256]{0:T(256)S(1)} fusion(s32[256]{0:T(256)S(1)} %get-tuple-element.11, s32[256]{0:T(256)S(1)} %get-tuple-element.10, s32[256]{0:T(256)S(1)} %convert_reduce_fusion, s32[]{:T(128)} %bitcast.2, s32[]{:T(128)} %bitcast.3, s32[]{:T(128)} %bitcast.4, s32[]{:T(128)} %bitcast.5, s32[]{:T(128)} %bitcast.6, s32[]{:T(128)} %bitcast.7, ...), kind=kLoop, calls=%fused_computation.70 | loop fusion | flops 4864 | bytes 4128 | tf_op jit(solution)/shard_map/add | solution.py:139
  33.4 87.7 %all-to-all-done = bf16[8,64,8192]{2,1,0:T(8,128)(2,1)} async-done(((bf16[8,64,8192]{2,1,0:T(8,128)(2,1)}), bf16[8,64,8192]{2,1,0:T(8,128)(2,1)}, u32[]{:S(2)}, u32[]{:S(2)}) %all-to-all-start) | async-done | bytes 8388640 | tf_op jit(solution)/shard_map/all_to_all | solution.py:132
  121.1 0.0 copy-start.3
  121.1 6.1 %fusion = (f32[256]{0:T(256)S(1)}, bf16[256,8192]{1,0:T(8,128)(2,1)S(1)}) fusion(bf16[512,8192]{1,0:T(8,128)(2,1)} %bitcast.21, s32[256]{0:T(256)S(1)} %subtract_add_fusion), kind=kOutput, calls=%fused_computation.4 | convolution fusion | flops 2156003072 | bytes 12584960 | tf_op jit(solution)/shard_map/dot_general | solution.py:91
  127.2 0.0 copy-start.1
  127.2 2.0 %copy-done.1 = bf16[256,8192]{1,0:T(8,128)(2,1)} copy-done((bf16[256,8192]{1,0:T(8,128)(2,1)}, bf16[256,8192]{1,0:T(8,128)(2,1)S(1)}, u32[]{:S(2)}) %copy-start.1) | copy-done | bytes 4194328
  129.2 0.0 copy-done.3
  129.2 3.2 %fusion.2 = bf16[256,8192]{1,0:T(8,128)(2,1)} fusion(bf16[256,8192]{1,0:T(8,128)(2,1)S(1)} %get-tuple-element.27, f32[8192]{0:T(1024)S(1)} %copy-done.3, f32[256]{0:T(256)S(1)} %add_rsqrt_fusion), kind=kLoop, calls=%fused_computation.6 | loop fusion | flops 8388608 | bytes 8422400 | tf_op jit(solution)/shard_map/convert_element_type | solution.py:36
  132.4 0.9 collective-permute-start
  133.3 3.1 %all-gather.2.cloned.1.call-done = bf16[8192,1024]{0,1:T(8,128)(2,1)} async-done(((bf16[512,1024]{0,1:T(8,128)(2,1)}), bf16[8192,1024]{0,1:T(8,128)(2,1)}) %all-gather.2.cloned.1.call-update) | async-done | bytes 16777232 | tf_op jit(solution)/shard_map/all_gather | solution.py:122
  136.4 11.6 %fusion.4 = bf16[256,1024]{1,0:T(8,128)(2,1)S(1)} fusion(bf16[256,8192]{1,0:T(8,128)(2,1)} %fusion.2, bf16[8192,1024]{0,1:T(8,128)(2,1)} %all-gather.2.cloned.1.call-done, f32[1024]{0:T(1024)S(1)} %bitcast.74), kind=kOutput, calls=%fused_computation.18 | convolution fusion | flops 4295491584 | bytes 21499904 | tf_op jit(solution)/shard_map/dot_general | solution.py:145
  148.0 0.0 collective-permute-done
  148.0 11.6 %broadcast_select_fusion = (bf16[256,1024]{1,0:T(8,128)(2,1)S(1)}, bf16[256,1024]{1,0:T(8,128)(2,1)S(1)}) fusion(bf16[256,1024]{1,0:T(8,128)(2,1)S(1)} %fusion.4, pred[]{:T(512)S(6)} %eq.80, f32[1024]{0:T(1024)S(1)} %bitcast.75, bf16[256,8192]{1,0:T(8,128)(2,1)} %collective-permute-done, bf16[8192,1024]{0,1:T(8,128)(2,1)} %all-gather.2.cloned.1.call-done), kind=kOutput, calls=%fused_computation.25 | convolution fusion | flops 4296015872 | bytes 22548480 | tf_op jit(solution)/shard_map/dot_general | solution.py:145
  159.7 0.1 broadcast_in_dim.18
  159.7 0.1 fusion.13
  159.8 1.3 collective-permute-start.1
  161.1 2.4 %collective-permute-start.2 = (bf16[512,256]{1,0:T(8,128)(2,1)S(1)}, bf16[512,256]{1,0:T(8,128)(2,1)S(1)}, u32[]{:S(2)}, u32[]{:S(2)}) collective-permute-start(bf16[512,256]{1,0:T(8,128)(2,1)S(1)} %get-tuple-element.15), channel_id=1, source_target_pairs={{0,4},{2,6},{4,0},{6,2},{1,5},{3,7},{5,1},{7,3},{8,12},{10,14},{12... | collective-permute-start | bytes 786440 | tf_op jit(solution)/shard_map/ppermute | solution.py:157
  163.5 1.2 collective-permute-start.3
  164.7 2.7 %collective-permute-done.1 = bf16[512,256]{1,0:T(8,128)(2,1)S(1)} collective-permute-done((bf16[512,256]{1,0:T(8,128)(2,1)S(1)}, bf16[512,256]{1,0:T(8,128)(2,1)S(1)}, u32[]{:S(2)}, u32[]{:S(2)}) %collective-permute-start.1) | collective-permute-done | bytes 262176 | tf_op jit(solution)/shard_map/ppermute | solution.py:157
  167.4 6.5 %collective-permute-done.2 = bf16[512,256]{1,0:T(8,128)(2,1)S(1)} collective-permute-done((bf16[512,256]{1,0:T(8,128)(2,1)S(1)}, bf16[512,256]{1,0:T(8,128)(2,1)S(1)}, u32[]{:S(2)}, u32[]{:S(2)}) %collective-permute-start.2) | collective-permute-done | bytes 262176 | tf_op jit(solution)/shard_map/ppermute | solution.py:157
  173.9 0.1 collective-permute-done.3
  174.0 1.1 reshape.96
  (14 shorter events, 0.2 us)
Async XLA Ops:
  7.2 5.5 %copy-start = (f32[2048]{0:T(1024)S(1)}, f32[2048]{0:T(1024)}, u32[]{:S(2)}) copy-start(f32[2048]{0:T(1024)} %param.11) | copy-start | bytes 24580
  7.2 5.5 %copy-start.2 = (s32[1,8,8]{2,1,0:T(8,128)S(1)}, s32[1,8,8]{2,1,0:T(8,128)}, u32[]{:S(2)}) copy-start(s32[1,8,8]{2,1,0:T(8,128)} %param.7) | copy-start | bytes 772
  7.2 5.7 %copy-start.4 = (s32[1,8,8]{2,1,0:T(8,128)S(1)}, s32[1,8,8]{2,1,0:T(8,128)}, u32[]{:S(2)}) copy-start(s32[1,8,8]{2,1,0:T(8,128)} %param.8) | copy-start | bytes 772
  7.2 129.2 %all-gather.2.cloned.1.call-start = ((), (), s32[]{:S(2)}) async-start(), calls=%async_computation.1 | async-start | bytes 17825792 | tf_op jit(solution)/shard_map/all_gather | solution.py:122
  20.9 100.1 %all-to-all-start = ((bf16[8,64,8192]{2,1,0:T(8,128)(2,1)}), bf16[8,64,8192]{2,1,0:T(8,128)(2,1)}, u32[]{:S(2)}, u32[]{:S(2)}) async-start(bf16[8,64,8192]{2,1,0:T(8,128)(2,1)} %bitcast.61), calls=%async_computation | async-start | bytes 16777216 | tf_op jit(solution)/shard_map/all_to_all | solution.py:132
  121.1 8.2 %copy-start.3 = (f32[8192]{0:T(1024)S(1)}, f32[8192]{0:T(1024)}, u32[]{:S(2)}) copy-start(f32[8192]{0:T(1024)} %param.9) | copy-start | bytes 98308
  127.2 2.0 %copy-start.1 = (bf16[256,8192]{1,0:T(8,128)(2,1)}, bf16[256,8192]{1,0:T(8,128)(2,1)S(1)}, u32[]{:S(2)}) copy-start(bf16[256,8192]{1,0:T(8,128)(2,1)S(1)} %get-tuple-element.27) | copy-start | bytes 12582916
  132.4 15.6 %collective-permute-start = (bf16[256,8192]{1,0:T(8,128)(2,1)}, bf16[256,8192]{1,0:T(8,128)(2,1)}, u32[]{:S(2)}, u32[]{:S(2)}) collective-permute-start(bf16[256,8192]{1,0:T(8,128)(2,1)} %fusion.2), channel_id=1, source_target_pairs={{0,1},{1,0},{2,3},{3,2},{4,5},{5,4},{6,7},{7,6},{8,9},{9,8},{10,11... | collective-permute-start | bytes 12582920 | tf_op jit(solution)/shard_map/ppermute | solution.py:142
  159.8 7.5 %collective-permute-start.1 = (bf16[512,256]{1,0:T(8,128)(2,1)S(1)}, bf16[512,256]{1,0:T(8,128)(2,1)S(1)}, u32[]{:S(2)}, u32[]{:S(2)}) collective-permute-start(bf16[512,256]{1,0:T(8,128)(2,1)S(1)} %get-tuple-element.14), channel_id=1, source_target_pairs={{0,2},{2,4},{4,6},{6,0},{1,3},{3,5},{5,7},{7,1},{8,10},{10,12},{12... | collective-permute-start | bytes 786440 | tf_op jit(solution)/shard_map/ppermute | solution.py:157
  161.1 12.8 %collective-permute-start.2 = (bf16[512,256]{1,0:T(8,128)(2,1)S(1)}, bf16[512,256]{1,0:T(8,128)(2,1)S(1)}, u32[]{:S(2)}, u32[]{:S(2)}) collective-permute-start(bf16[512,256]{1,0:T(8,128)(2,1)S(1)} %get-tuple-element.15), channel_id=1, source_target_pairs={{0,4},{2,6},{4,0},{6,2},{1,5},{3,7},{5,1},{7,3},{8,12},{10,14},{12... | collective-permute-start | bytes 786440 | tf_op jit(solution)/shard_map/ppermute | solution.py:157
  163.5 10.5 %collective-permute-start.3 = (bf16[512,256]{1,0:T(8,128)(2,1)S(1)}, bf16[512,256]{1,0:T(8,128)(2,1)S(1)}, u32[]{:S(2)}, u32[]{:S(2)}) collective-permute-start(bf16[512,256]{1,0:T(8,128)(2,1)S(1)} %get-tuple-element.12), channel_id=1, source_target_pairs={{0,6},{2,0},{4,2},{6,4},{1,7},{3,1},{5,3},{7,5},{8,14},{10,8},{12,... | collective-permute-start | bytes 786440 | tf_op jit(solution)/shard_map/ppermute | solution.py:157
Sparse Core Ops, SparseCore 0:
  12.8 123.5 all-gather.1

commit v10 on v9

--- a/solution.py
+++ b/solution.py
@@ -108,14 +108,17 @@
     width = kv_weight.shape[0]
     heads_per_core = KVH // cores
     here = lax.axis_index("cx")
-    local_weight = kv_weight.reshape(width, 2, heads_per_core, cores, HD)
-    local_weight = lax.dynamic_index_in_dim(local_weight, core, axis=3, keepdims=False)
-    local_weight = jnp.roll(jnp.swapaxes(local_weight, 1, 2), -here, axis=1)
-    local_weight = local_weight.reshape(width, heads_per_core * 2 * HD)
-    local_bias = lax.dynamic_index_in_dim(
-        kv_bias.reshape(2, heads_per_core, cores, HD), core, axis=2, keepdims=False
+    columns = []
+    for step in range(heads_per_core):
+        head = ((here + step) % heads_per_core) * cores + core
+        for kind in range(2):
+            columns.append(kind * KVH * HD + head * HD)
+    local_weight = jnp.concatenate(
+        [lax.dynamic_slice_in_dim(kv_weight, c, HD, axis=1) for c in columns], axis=1
     )
-    local_bias = jnp.roll(jnp.swapaxes(local_bias, 0, 1), -here, axis=0).reshape(-1)
+    local_bias = jnp.concatenate(
+        [lax.dynamic_slice_in_dim(kv_bias, c, HD, axis=0) for c in columns], axis=0
+    )
     local_weight, local_bias, input_entries = lax.optimization_barrier(
         (local_weight, local_bias, input_entries)
     )

time: 183 us -> 185 us (1.011)
  local copies, waits for them, and re-layouts: 9.36 us -> 16.4 us
  matrix products: 37.1 us -> 32 us
    unnamed x11 -> x22, local copies, waits for them, and re-layouts: 4.89 us -> 12.3 us
    dot_general x2, matrix products: 23.1 us -> 18.3 us  [project(): jnp.dot(rows, gathered_weight, preferred_element_type=jnp.float32)]
    all_gather x1, waiting for transfers between devices: 3.13 us -> 0.01 us  [on_device(): gathered_weight = lax.all_gather(local_weight, 'dp', axis=0, tiled=True)]
    ppermute x3, waiting for transfers between devices: 9.27 us -> 12.2 us  [on_device(): lax.ppermute(mapped[step], 'cx', perm=[(i, (i + step) % chips) for i in r...]
    dynamic_slice x6 -> x1, local copies, waits for them, and re-layouts: 2.28 us -> 0.19 us  [on_device(): shift = anchor - jnp.take(starts[:, myself], source, mode='clip')]
    ppermute x3, starting transfers between devices: 4.84 us -> 2.85 us  [on_device(): lax.ppermute(mapped[step], 'cx', perm=[(i, (i + step) % chips) for i in r...]
  transfers between devices with their start and end apart: 6 -> 6, of which waited for: 5 -> 3; matrix products, arithmetic and copies ran while one was open for 19% -> 20% of each run, Pallas kernels for 0% -> 0%
where the time goes in v10:
time: 185 us; the launch traced here: 184 us
  waiting for transfers between devices  99.9 us (54%)
  matrix products  32 us (17%)
  local copies, waits for them, and re-layouts  16.4 us (9%)
  between operations  14.4 us (8%)
  other arithmetic  11 us (6%)
  starting transfers between devices  10.2 us (6%)
    all_to_all x1, waiting for transfers between devices, on_device(): lax.all_to_all(outgoing.reshape(peer_count, capacity, -1), CTX, split_axi...  87.7 us
    dot_general x2, matrix products, project(): jnp.dot(rows, gathered_weight, preferred_element_type=jnp.float32)  18.3 us
    dot_general x2, matrix products, select_rows(): jnp.dot(picks.astype(rows.dtype), rows, preferred_element_type=jnp.float32)  13.7 us
    unnamed x22, local copies, waits for them, and re-layouts  12.3 us
    ppermute x3, waiting for transfers between devices, on_device(): lax.ppermute(mapped[step], 'cx', perm=[(i, (i + step) % chips) for i in r...  12.2 us
    all_to_all x1, starting transfers between devices, on_device(): lax.all_to_all(outgoing.reshape(peer_count, capacity, -1), CTX, split_axi...  6.42 us
    add x1, other arithmetic, on_device(): index = source * capacity + shift + within  4.97 us
  transfers between devices with their start and end apart: 6, of which 3 were waited for; matrix products, arithmetic and copies ran while one was open for 20% of the time, Pallas kernels for 0%

profile of v10, /device:TPU:1, one launch (start us, length us, event | category | flops | bytes accessed | tf_op | source)
XLA Modules:
  0.0 183.9 jit_solution(4183626416342207435)
XLA Ops:
  7.2 0.0 all-gather.2.cloned.1.call-start
  7.3 0.9 dynamic-slice_dynamic-update-slice_fusion.7
  8.3 0.9 dynamic-slice_dynamic-update-slice_fusion.6
  9.2 0.8 constant_dynamic-update-slice_fusion
  10.0 0.8 constant_dynamic-update-slice_fusion.7
  10.8 0.9 dynamic-slice_dynamic-update-slice_fusion.5
  11.7 0.8 constant_dynamic-update-slice_fusion.6
  12.5 0.9 dynamic-slice_dynamic-update-slice_fusion.4
  13.4 0.8 constant_dynamic-update-slice_fusion.5
  14.2 0.9 dynamic-slice_dynamic-update-slice_fusion.3
  15.1 0.8 constant_dynamic-update-slice_fusion.4
  15.9 0.9 dynamic-slice_dynamic-update-slice_fusion.2
  16.8 0.8 constant_dynamic-update-slice_fusion.3
  17.6 0.9 dynamic-slice_dynamic-update-slice_fusion.1
  18.6 0.8 constant_dynamic-update-slice_fusion.2
  19.3 0.9 dynamic-slice_dynamic-update-slice_fusion
  20.3 0.0 copy-start.1
  20.3 0.8 constant_dynamic-update-slice_fusion.1
  21.1 0.2 copy-done.1
  21.3 0.0 all-gather.2.cloned.1.call-update
  21.3 0.8 reduce_window_sum.23
  22.1 0.7 bitcast_subtract_fusion
  22.8 0.8 select_reduce_fusion.1
  23.7 0.1 iota_add_fusion
  23.7 0.1 add.193
  23.8 7.8 %convolution_convert_fusion = bf16[512,8192]{1,0:T(8,128)(2,1)} fusion(bf16[1,256,8192]{2,1,0:T(8,128)(2,1)} %param.6, s32[512]{0:T(512)S(1)} %add.193), kind=kOutput, calls=%fused_computation | convolution fusion | flops 2151809024 | bytes 12584960 | tf_op jit(solution)/shard_map/dot_general | solution.py:91
  31.6 6.4 %all-to-all-start = ((bf16[8,64,8192]{2,1,0:T(8,128)(2,1)}), bf16[8,64,8192]{2,1,0:T(8,128)(2,1)}, u32[]{:S(2)}, u32[]{:S(2)}) async-start(bf16[8,64,8192]{2,1,0:T(8,128)(2,1)} %bitcast.50), calls=%async_computation | async-start | bytes 16777216 | tf_op jit(solution)/shard_map/all_to_all | solution.py:135
  38.0 0.2 fusion.15
  38.2 0.2 constant_dynamic-slice_fusion.2
  38.4 0.6 fusion.21
  39.0 0.1 convert_reduce_fusion
  39.1 0.1 select_reduce_fusion.3
  39.2 5.0 %subtract_add_fusion = s32[256]{0:T(256)S(1)} fusion(s32[256]{0:T(256)S(1)} %get-tuple-element.11, s32[256]{0:T(256)S(1)} %get-tuple-element.10, s32[256]{0:T(256)S(1)} %convert_reduce_fusion, s32[]{:T(128)} %bitcast.2, s32[]{:T(128)} %bitcast.3, s32[]{:T(128)} %bitcast.4, s32[]{:T(128)} %bitcast.5, s32[]{:T(128)} %bitcast.6, s32[]{:T(128)} %bitcast.7, ...), kind=kLoop, calls=%fused_computation.81 | loop fusion | flops 4864 | bytes 4128 | tf_op jit(solution)/shard_map/add | solution.py:142
  44.2 87.7 %all-to-all-done = bf16[8,64,8192]{2,1,0:T(8,128)(2,1)} async-done(((bf16[8,64,8192]{2,1,0:T(8,128)(2,1)}), bf16[8,64,8192]{2,1,0:T(8,128)(2,1)}, u32[]{:S(2)}, u32[]{:S(2)}) %all-to-all-start) | async-done | bytes 8388640 | tf_op jit(solution)/shard_map/all_to_all | solution.py:135
  131.9 0.0 copy-start.2
  131.9 5.9 %fusion = (f32[256]{0:T(256)S(1)}, bf16[256,8192]{1,0:T(8,128)(2,1)S(1)}) fusion(bf16[512,8192]{1,0:T(8,128)(2,1)} %bitcast.13, s32[256]{0:T(256)S(1)} %subtract_add_fusion), kind=kOutput, calls=%fused_computation.4 | convolution fusion | flops 2156003072 | bytes 12584960 | tf_op jit(solution)/shard_map/dot_general | solution.py:91
  137.8 0.0 copy-start
  137.8 0.0 copy-done.2
  137.8 3.3 %fusion.2 = bf16[256,8192]{1,0:T(8,128)(2,1)} fusion(bf16[256,8192]{1,0:T(8,128)(2,1)S(1)} %get-tuple-element.27, f32[8192]{0:T(1024)S(1)} %copy-done.2, f32[256]{0:T(256)S(1)} %add_rsqrt_fusion), kind=kLoop, calls=%fused_computation.6 | loop fusion | flops 8388608 | bytes 8422400 | tf_op jit(solution)/shard_map/convert_element_type | solution.py:36
  141.1 0.0 copy-done
  141.1 0.9 collective-permute-start
  142.0 0.0 all-gather.2.cloned.1.call-done
  142.0 0.0 copy-start.3
  142.0 11.7 %fusion.4 = bf16[256,1024]{1,0:T(8,128)(2,1)S(1)} fusion(bf16[256,8192]{1,0:T(8,128)(2,1)} %fusion.2, bf16[8192,1024]{1,0:T(8,128)(2,1)} %all-gather.2.cloned.1.call-done, f32[1024]{0:T(1024)S(1)} %constant_dynamic-update-slice_fusion.1), kind=kOutput, calls=%fused_computation.16 | convolution fusion | flops 4295491584 | bytes 21499904 | tf_op jit(solution)/shard_map/dot_general | solution.py:148
  153.7 0.0 collective-permute-done
  153.7 0.1 copy-done.3
  153.8 6.7 %broadcast_select_fusion = (bf16[256,1024]{1,0:T(8,128)(2,1)S(1)}, bf16[256,1024]{1,0:T(8,128)(2,1)S(1)}) fusion(bf16[256,1024]{1,0:T(8,128)(2,1)S(1)} %fusion.4, pred[]{:T(512)S(6)} %eq.79, f32[1024]{0:T(1024)S(1)} %constant_dynamic-update-slice_fusion.1, bf16[256,8192]{1,0:T(8,128)(2,1)} %collective-permute-done, bf16[8192,1024]{1,0:T(8,128)(2,1)S(1)} %copy-done.3), kind=kOutput, calls=%fused_computation.22 | convolution fusion | flops 4296015872 | bytes 22548480 | tf_op jit(solution)/shard_map/dot_general | solution.py:148
  160.6 0.1 broadcast_in_dim.18
  160.6 0.1 fusion.12
  160.7 0.4 collective-permute-start.1
  161.1 1.8 collective-permute-start.2
  162.9 0.7 collective-permute-start.3
  163.6 12.0 %collective-permute-done.1 = bf16[512,256]{1,0:T(8,128)(2,1)S(1)} collective-permute-done((bf16[512,256]{1,0:T(8,128)(2,1)S(1)}, bf16[512,256]{1,0:T(8,128)(2,1)S(1)}, u32[]{:S(2)}, u32[]{:S(2)}) %collective-permute-start.1) | collective-permute-done | bytes 262176 | tf_op jit(solution)/shard_map/ppermute | solution.py:160
  175.6 0.0 collective-permute-done.2
  175.6 0.2 collective-permute-done.3
  175.9 1.1 reshape.80
  (11 shorter events, 0.2 us)
Async XLA Ops:
  7.2 134.8 %all-gather.2.cloned.1.call-start = ((), (), s32[]{:S(2)}) async-start(), calls=%async_computation.1 | async-start | bytes 17825792 | tf_op jit(solution)/shard_map/all_gather | solution.py:125
  20.3 1.0 copy-start.1
  31.6 100.3 %all-to-all-start = ((bf16[8,64,8192]{2,1,0:T(8,128)(2,1)}), bf16[8,64,8192]{2,1,0:T(8,128)(2,1)}, u32[]{:S(2)}, u32[]{:S(2)}) async-start(bf16[8,64,8192]{2,1,0:T(8,128)(2,1)} %bitcast.50), calls=%async_computation | async-start | bytes 16777216 | tf_op jit(solution)/shard_map/all_to_all | solution.py:135
  131.9 5.9 %copy-start.2 = (f32[8192]{0:T(1024)S(1)}, f32[8192]{0:T(1024)}, u32[]{:S(2)}) copy-start(f32[8192]{0:T(1024)} %param.9) | copy-start | bytes 98308
  137.8 3.4 %copy-start = (bf16[256,8192]{1,0:T(8,128)(2,1)}, bf16[256,8192]{1,0:T(8,128)(2,1)S(1)}, u32[]{:S(2)}) copy-start(bf16[256,8192]{1,0:T(8,128)(2,1)S(1)} %get-tuple-element.27) | copy-start | bytes 12582916
  141.1 12.5 %collective-permute-start = (bf16[256,8192]{1,0:T(8,128)(2,1)}, bf16[256,8192]{1,0:T(8,128)(2,1)}, u32[]{:S(2)}, u32[]{:S(2)}) collective-permute-start(bf16[256,8192]{1,0:T(8,128)(2,1)} %fusion.2), channel_id=1, source_target_pairs={{0,1},{1,0},{2,3},{3,2},{4,5},{5,4},{6,7},{7,6},{8,9},{9,8},{10,11... | collective-permute-start | bytes 12582920 | tf_op jit(solution)/shard_map/ppermute | solution.py:145
  142.0 11.8 %copy-start.3 = (bf16[8192,1024]{1,0:T(8,128)(2,1)S(1)}, bf16[8192,1024]{1,0:T(8,128)(2,1)}, u32[]{:S(2)}) copy-start(bf16[8192,1024]{1,0:T(8,128)(2,1)} %all-gather.2.cloned.1.call-done) | copy-start | bytes 50331652
  160.7 14.8 %collective-permute-start.1 = (bf16[512,256]{1,0:T(8,128)(2,1)S(1)}, bf16[512,256]{1,0:T(8,128)(2,1)S(1)}, u32[]{:S(2)}, u32[]{:S(2)}) collective-permute-start(bf16[512,256]{1,0:T(8,128)(2,1)S(1)} %get-tuple-element.14), channel_id=1, source_target_pairs={{0,2},{2,4},{4,6},{6,0},{1,3},{3,5},{5,7},{7,1},{8,10},{10,12},{12... | collective-permute-start | bytes 786440 | tf_op jit(solution)/shard_map/ppermute | solution.py:160
  161.1 14.5 %collective-permute-start.2 = (bf16[512,256]{1,0:T(8,128)(2,1)S(1)}, bf16[512,256]{1,0:T(8,128)(2,1)S(1)}, u32[]{:S(2)}, u32[]{:S(2)}) collective-permute-start(bf16[512,256]{1,0:T(8,128)(2,1)S(1)} %get-tuple-element.15), channel_id=1, source_target_pairs={{0,4},{2,6},{4,0},{6,2},{1,5},{3,7},{5,1},{7,3},{8,12},{10,14},{12... | collective-permute-start | bytes 786440 | tf_op jit(solution)/shard_map/ppermute | solution.py:160
  162.9 13.0 %collective-permute-start.3 = (bf16[512,256]{1,0:T(8,128)(2,1)S(1)}, bf16[512,256]{1,0:T(8,128)(2,1)S(1)}, u32[]{:S(2)}, u32[]{:S(2)}) collective-permute-start(bf16[512,256]{1,0:T(8,128)(2,1)S(1)} %get-tuple-element.12), channel_id=1, source_target_pairs={{0,6},{2,0},{4,2},{6,4},{1,7},{3,1},{5,3},{7,5},{8,14},{10,8},{12,... | collective-permute-start | bytes 786440 | tf_op jit(solution)/shard_map/ppermute | solution.py:160
Sparse Core Ops, SparseCore 0:
  21.4 114.6 all-gather.1

commit v11 on v9

--- a/solution.py
+++ b/solution.py
@@ -108,14 +108,17 @@
     width = kv_weight.shape[0]
     heads_per_core = KVH // cores
     here = lax.axis_index("cx")
-    local_weight = kv_weight.reshape(width, 2, heads_per_core, cores, HD)
-    local_weight = lax.dynamic_index_in_dim(local_weight, core, axis=3, keepdims=False)
-    local_weight = jnp.roll(jnp.swapaxes(local_weight, 1, 2), -here, axis=1)
-    local_weight = local_weight.reshape(width, heads_per_core * 2 * HD)
-    local_bias = lax.dynamic_index_in_dim(
-        kv_bias.reshape(2, heads_per_core, cores, HD), core, axis=2, keepdims=False
-    )
-    local_bias = jnp.roll(jnp.swapaxes(local_bias, 0, 1), -here, axis=0).reshape(-1)
+
+    def pick_columns(table, parity):
+        starts = [
+            kind * KVH * HD + (block * cores + parity) * HD
+            for block in range(heads_per_core)
+            for kind in range(2)
+        ]
+        return jnp.concatenate([table[..., c:c + HD] for c in starts], axis=-1)
+
+    local_weight = jnp.where(core == 0, pick_columns(kv_weight, 0), pick_columns(kv_weight, 1))
+    local_bias = jnp.where(core == 0, pick_columns(kv_bias, 0), pick_columns(kv_bias, 1))
     local_weight, local_bias, input_entries = lax.optimization_barrier(
         (local_weight, local_bias, input_entries)
     )
@@ -150,7 +153,7 @@
     other = project(sibling_rows)
     first = jnp.where(core == 0, own, other)
     second = jnp.where(core == 0, other, own)
-    mapped = jnp.concatenate([first, second], axis=1)
+    mapped = jnp.roll(jnp.concatenate([first, second], axis=1), -here, axis=0)
     by_heads = jnp.zeros_like(mapped)
     by_heads = lax.dynamic_update_index_in_dim(by_heads, mapped[0], here, 0)
     for step in range(1, chips):

time: 183 us -> 181 us (0.989)
  matrix products: 37.1 us -> 32 us
  other arithmetic: 9.16 us -> 12.5 us
  starting transfers between devices: 12 us -> 10 us
    dot_general x2, matrix products: 23.1 us -> 18.3 us  [project(): jnp.dot(rows, gathered_weight, preferred_element_type=jnp.float32)]
    all_gather x1, waiting for transfers between devices: 3.13 us -> 0.01 us  [on_device(): gathered_weight = lax.all_gather(local_weight, 'dp', axis=0, tiled=True)]
    ppermute x3, waiting for transfers between devices: 9.27 us -> 12.2 us  [on_device(): lax.ppermute(mapped[step], 'cx', perm=[(i, (i + step) % chips) for i in r...]
    unnamed x11 -> x26, local copies, waits for them, and re-layouts: 4.89 us -> 7.6 us
    concatenate x2 -> x1, other arithmetic: 0.41 us -> 2.69 us  [on_device(): mapped = jnp.roll(jnp.concatenate([first, second], axis=1), -here, axis=0)]
    dynamic_slice x5 -> x0, local copies, waits for them, and re-layouts: 2.06 us -> none  [the longest x1 1.31 us: on_device(): local_weight = jnp.roll(jnp.swapaxes(local_weight, 1, 2), -here, axis=1)]
    ppermute x3, starting transfers between devices: 4.84 us -> 2.86 us  [on_device(): lax.ppermute(mapped[step], 'cx', perm=[(i, (i + step) % chips) for i in r...]
  transfers between devices with their start and end apart: 6 -> 6, of which waited for: 5 -> 3; matrix products, arithmetic and copies ran while one was open for 19% -> 20% of each run, Pallas kernels for 0% -> 0%
where the time goes in v11:
time: 181 us; the launch traced here: 180 us
  waiting for transfers between devices  100 us (55%)
  matrix products  32 us (18%)
  between operations  14.4 us (8%)
  other arithmetic  12.5 us (7%)
  local copies, waits for them, and re-layouts  11.1 us (6%)
  starting transfers between devices  10 us (6%)
    all_to_all x1, waiting for transfers between devices, on_device(): lax.all_to_all(outgoing.reshape(peer_count, capacity, -1), CTX, split_axi...  87.9 us
    dot_general x2, matrix products, project(): jnp.dot(rows, gathered_weight, preferred_element_type=jnp.float32)  18.3 us
    dot_general x2, matrix products, select_rows(): jnp.dot(picks.astype(rows.dtype), rows, preferred_element_type=jnp.float32)  13.7 us
    ppermute x3, waiting for transfers between devices, on_device(): lax.ppermute(mapped[step], 'cx', perm=[(i, (i + step) % chips) for i in r...  12.2 us
    unnamed x26, local copies, waits for them, and re-layouts  7.6 us
    all_to_all x1, starting transfers between devices, on_device(): lax.all_to_all(outgoing.reshape(peer_count, capacity, -1), CTX, split_axi...  6.25 us
    add x1, other arithmetic, on_device(): index = source * capacity + shift + within  4.82 us
  transfers between devices with their start and end apart: 6, of which 3 were waited for; matrix products, arithmetic and copies ran while one was open for 20% of the time, Pallas kernels for 0%

profile of v11, /device:TPU:1, one launch (start us, length us, event | category | flops | bytes accessed | tf_op | source)
XLA Modules:
  0.0 180.1 jit_solution(15427288924709997923)
XLA Ops:
  7.2 0.0 copy-start.3
  7.2 0.0 all-gather.2.cloned.1.call-start
  7.2 0.0 copy-start.1
  7.3 0.0 copy-start.4
  7.3 1.0 slice_dynamic-update-slice_fusion.8
  8.3 1.1 slice_dynamic-update-slice_fusion.7
  9.4 1.1 slice_dynamic-update-slice_fusion.6
  10.5 1.1 slice_dynamic-update-slice_fusion.5
  11.5 1.1 slice_dynamic-update-slice_fusion.4
  12.6 1.1 slice_dynamic-update-slice_fusion.3
  13.7 1.1 slice_dynamic-update-slice_fusion.2
  14.7 1.1 slice_dynamic-update-slice_fusion.1
  15.8 0.0 copy-done.3
  15.9 1.1 broadcast_select_fusion
  17.0 0.0 all-gather.2.cloned.1.call-update
  17.0 0.0 copy-done.1
  17.0 0.2 reduce_window_sum.23
  17.2 0.0 copy-done.4
  17.2 0.1 select_reduce_fusion.1
  17.3 0.1 iota_add_fusion
  17.4 0.1 add.124
  17.5 7.8 %convolution_convert_fusion = bf16[512,8192]{1,0:T(8,128)(2,1)} fusion(bf16[1,256,8192]{2,1,0:T(8,128)(2,1)} %param.6, s32[512]{0:T(512)S(1)} %add.124), kind=kOutput, calls=%fused_computation | convolution fusion | flops 2151809024 | bytes 12584960 | tf_op jit(solution)/shard_map/dot_general | solution.py:91
  25.3 6.2 %all-to-all-start = ((bf16[8,64,8192]{2,1,0:T(8,128)(2,1)}), bf16[8,64,8192]{2,1,0:T(8,128)(2,1)}, u32[]{:S(2)}, u32[]{:S(2)}) async-start(bf16[8,64,8192]{2,1,0:T(8,128)(2,1)} %bitcast.50), calls=%async_computation | async-start | bytes 16777216 | tf_op jit(solution)/shard_map/all_to_all | solution.py:135
  31.6 0.2 dynamic-slice_reduce_fusion
  31.8 0.2 dynamic-slice_reduce_fusion.2
  32.0 0.6 fusion.14
  32.6 0.1 convert_reduce_fusion
  32.6 0.1 select_reduce_fusion.3
  32.7 4.8 %subtract_add_fusion = s32[256]{0:T(256)S(1)} fusion(s32[256]{0:T(256)S(1)} %get-tuple-element.11, s32[256]{0:T(256)S(1)} %get-tuple-element.10, s32[256]{0:T(256)S(1)} %convert_reduce_fusion, s32[]{:T(128)} %bitcast.2, s32[]{:T(128)} %bitcast.3, s32[]{:T(128)} %bitcast.4, s32[]{:T(128)} %bitcast.5, s32[]{:T(128)} %bitcast.6, s32[]{:T(128)} %bitcast.7, ...), kind=kLoop, calls=%fused_computation.93 | loop fusion | flops 4864 | bytes 4128 | tf_op jit(solution)/shard_map/add | solution.py:142
  37.6 87.9 %all-to-all-done = bf16[8,64,8192]{2,1,0:T(8,128)(2,1)} async-done(((bf16[8,64,8192]{2,1,0:T(8,128)(2,1)}), bf16[8,64,8192]{2,1,0:T(8,128)(2,1)}, u32[]{:S(2)}, u32[]{:S(2)}) %all-to-all-start) | async-done | bytes 8388640 | tf_op jit(solution)/shard_map/all_to_all | solution.py:135
  125.4 0.0 copy-start.2
  125.4 5.9 %fusion = (f32[256]{0:T(256)S(1)}, bf16[256,8192]{1,0:T(8,128)(2,1)S(1)}) fusion(bf16[512,8192]{1,0:T(8,128)(2,1)} %bitcast.13, s32[256]{0:T(256)S(1)} %subtract_add_fusion), kind=kOutput, calls=%fused_computation.4 | convolution fusion | flops 2156003072 | bytes 12584960 | tf_op jit(solution)/shard_map/dot_general | solution.py:91
  131.3 0.0 copy-start
  131.3 0.0 copy-done.2
  131.3 3.3 %fusion.2 = bf16[256,8192]{1,0:T(8,128)(2,1)} fusion(bf16[256,8192]{1,0:T(8,128)(2,1)S(1)} %get-tuple-element.59, f32[8192]{0:T(1024)S(1)} %copy-done.2, f32[256]{0:T(256)S(1)} %add_rsqrt_fusion), kind=kLoop, calls=%fused_computation.6 | loop fusion | flops 8388608 | bytes 8422400 | tf_op jit(solution)/shard_map/convert_element_type | solution.py:36
  134.7 0.0 copy-done
  134.7 0.9 collective-permute-start
  135.5 0.0 all-gather.2.cloned.1.call-done
  135.5 0.0 copy-start.5
  135.5 11.7 %fusion.4 = bf16[256,1024]{1,0:T(8,128)(2,1)S(1)} fusion(bf16[256,8192]{1,0:T(8,128)(2,1)} %fusion.2, bf16[8192,1024]{1,0:T(8,128)(2,1)} %all-gather.2.cloned.1.call-done, f32[1024]{0:T(1024)S(1)} %broadcast_select_fusion.3), kind=kOutput, calls=%fused_computation.14 | convolution fusion | flops 4295491584 | bytes 21499904 | tf_op jit(solution)/shard_map/dot_general | solution.py:148
  147.2 0.0 collective-permute-done
  147.2 0.1 copy-done.5
  147.3 6.7 %broadcast_select_fusion.1 = (bf16[256,1024]{1,0:T(8,128)(2,1)S(1)}, bf16[256,1024]{1,0:T(8,128)(2,1)S(1)}) fusion(bf16[256,1024]{1,0:T(8,128)(2,1)S(1)} %fusion.4, pred[]{:T(512)S(6)} %eq.80, f32[1024]{0:T(1024)S(1)} %broadcast_select_fusion.3, bf16[256,8192]{1,0:T(8,128)(2,1)} %collective-permute-done, bf16[8192,1024]{1,0:T(8,128)(2,1)S(1)} %copy-done.5), kind=kOutput, calls=%fused_computation.24 | convolution fusion | flops 4296015872 | bytes 22548480 | tf_op jit(solution)/shard_map/dot_general | solution.py:148
  154.1 2.7 %fusion.7 = bf16[4,512,256]{2,1,0:T(8,128)(2,1)S(1)} fusion(s32[]{:T(128)S(6)} %select_n.100, bf16[4,256,256]{2,1,0:T(8,128)(2,1)S(1)} %bitcast.52, bf16[4,256,256]{2,1,0:T(8,128)(2,1)S(1)} %bitcast.53), kind=kLoop, calls=%fused_computation.17 | loop fusion | flops 4194304 | bytes 2097156 | tf_op jit(solution)/shard_map/jit(_roll_dynamic)/concatenate | solution.py:156
  156.8 0.1 broadcast_in_dim.18
  156.9 0.1 slice_bitcast_fusion
  157.0 0.4 collective-permute-start.1
  157.3 1.8 collective-permute-start.2
  159.1 0.7 collective-permute-start.3
  159.8 12.0 %collective-permute-done.1 = bf16[512,256]{1,0:T(8,128)(2,1)S(1)} collective-permute-done((bf16[512,256]{1,0:T(8,128)(2,1)S(1)}, bf16[512,256]{1,0:T(8,128)(2,1)S(1)}, u32[]{:S(2)}, u32[]{:S(2)}) %collective-permute-start.1) | collective-permute-done | bytes 262176 | tf_op jit(solution)/shard_map/ppermute | solution.py:160
  171.8 0.0 collective-permute-done.2
  171.9 0.2 collective-permute-done.3
  172.1 1.1 reshape.80
  (22 shorter events, 0.3 us)
Async XLA Ops:
  7.2 8.6 %copy-start.3 = (f32[2048]{0:T(1024)S(1)}, f32[2048]{0:T(1024)}, u32[]{:S(2)}) copy-start(f32[2048]{0:T(1024)} %param.11) | copy-start | bytes 24580
  7.2 128.4 %all-gather.2.cloned.1.call-start = ((), (), s32[]{:S(2)}) async-start(), calls=%async_computation.1 | async-start | bytes 17825792 | tf_op jit(solution)/shard_map/all_gather | solution.py:125
  7.2 9.8 %copy-start.1 = (s32[1,8,8]{2,1,0:T(8,128)S(1)}, s32[1,8,8]{2,1,0:T(8,128)}, u32[]{:S(2)}) copy-start(s32[1,8,8]{2,1,0:T(8,128)} %param.7) | copy-start | bytes 772
  7.3 10.0 %copy-start.4 = (s32[1,8,8]{2,1,0:T(8,128)S(1)}, s32[1,8,8]{2,1,0:T(8,128)}, u32[]{:S(2)}) copy-start(s32[1,8,8]{2,1,0:T(8,128)} %param.8) | copy-start | bytes 772
  25.3 100.1 %all-to-all-start = ((bf16[8,64,8192]{2,1,0:T(8,128)(2,1)}), bf16[8,64,8192]{2,1,0:T(8,128)(2,1)}, u32[]{:S(2)}, u32[]{:S(2)}) async-start(bf16[8,64,8192]{2,1,0:T(8,128)(2,1)} %bitcast.50), calls=%async_computation | async-start | bytes 16777216 | tf_op jit(solution)/shard_map/all_to_all | solution.py:135
  125.4 5.9 %copy-start.2 = (f32[8192]{0:T(1024)S(1)}, f32[8192]{0:T(1024)}, u32[]{:S(2)}) copy-start(f32[8192]{0:T(1024)} %param.9) | copy-start | bytes 98308
  131.3 3.4 %copy-start = (bf16[256,8192]{1,0:T(8,128)(2,1)}, bf16[256,8192]{1,0:T(8,128)(2,1)S(1)}, u32[]{:S(2)}) copy-start(bf16[256,8192]{1,0:T(8,128)(2,1)S(1)} %get-tuple-element.59) | copy-start | bytes 12582916
  134.7 12.5 %collective-permute-start = (bf16[256,8192]{1,0:T(8,128)(2,1)}, bf16[256,8192]{1,0:T(8,128)(2,1)}, u32[]{:S(2)}, u32[]{:S(2)}) collective-permute-start(bf16[256,8192]{1,0:T(8,128)(2,1)} %fusion.2), channel_id=1, source_target_pairs={{0,1},{1,0},{2,3},{3,2},{4,5},{5,4},{6,7},{7,6},{8,9},{9,8},{10,11... | collective-permute-start | bytes 12582920 | tf_op jit(solution)/shard_map/ppermute | solution.py:145
  135.5 11.8 %copy-start.5 = (bf16[8192,1024]{1,0:T(8,128)(2,1)S(1)}, bf16[8192,1024]{1,0:T(8,128)(2,1)}, u32[]{:S(2)}) copy-start(bf16[8192,1024]{1,0:T(8,128)(2,1)} %all-gather.2.cloned.1.call-done) | copy-start | bytes 50331652
  157.0 14.8 %collective-permute-start.1 = (bf16[512,256]{1,0:T(8,128)(2,1)S(1)}, bf16[512,256]{1,0:T(8,128)(2,1)S(1)}, u32[]{:S(2)}, u32[]{:S(2)}) collective-permute-start(bf16[512,256]{1,0:T(8,128)(2,1)S(1)} %get-tuple-element.30), channel_id=1, source_target_pairs={{0,2},{2,4},{4,6},{6,0},{1,3},{3,5},{5,7},{7,1},{8,10},{10,12},{12... | collective-permute-start | bytes 786440 | tf_op jit(solution)/shard_map/ppermute | solution.py:160
  157.3 14.5 %collective-permute-start.2 = (bf16[512,256]{1,0:T(8,128)(2,1)S(1)}, bf16[512,256]{1,0:T(8,128)(2,1)S(1)}, u32[]{:S(2)}, u32[]{:S(2)}) collective-permute-start(bf16[512,256]{1,0:T(8,128)(2,1)S(1)} %get-tuple-element.29), channel_id=1, source_target_pairs={{0,4},{2,6},{4,0},{6,2},{1,5},{3,7},{5,1},{7,3},{8,12},{10,14},{12... | collective-permute-start | bytes 786440 | tf_op jit(solution)/shard_map/ppermute | solution.py:160
  159.1 13.0 %collective-permute-start.3 = (bf16[512,256]{1,0:T(8,128)(2,1)S(1)}, bf16[512,256]{1,0:T(8,128)(2,1)S(1)}, u32[]{:S(2)}, u32[]{:S(2)}) collective-permute-start(bf16[512,256]{1,0:T(8,128)(2,1)S(1)} %get-tuple-element.28), channel_id=1, source_target_pairs={{0,6},{2,0},{4,2},{6,4},{1,7},{3,1},{5,3},{7,5},{8,14},{10,8},{12,... | collective-permute-start | bytes 786440 | tf_op jit(solution)/shard_map/ppermute | solution.py:160
Sparse Core Ops, SparseCore 0:
  17.2 114.6 all-gather.1

commit v12 on v9

--- a/solution.py
+++ b/solution.py
@@ -4,6 +4,7 @@
 from jax import lax
 from jax.experimental import pallas as pl
 from jax.experimental.pallas import tpu as pltpu
+from jax.experimental.layout import Layout, with_layout_constraint
 from jax.sharding import Mesh, PartitionSpec as P
 
 KVH = 8
@@ -108,18 +109,23 @@
     width = kv_weight.shape[0]
     heads_per_core = KVH // cores
     here = lax.axis_index("cx")
-    local_weight = kv_weight.reshape(width, 2, heads_per_core, cores, HD)
-    local_weight = lax.dynamic_index_in_dim(local_weight, core, axis=3, keepdims=False)
-    local_weight = jnp.roll(jnp.swapaxes(local_weight, 1, 2), -here, axis=1)
-    local_weight = local_weight.reshape(width, heads_per_core * 2 * HD)
-    local_bias = lax.dynamic_index_in_dim(
-        kv_bias.reshape(2, heads_per_core, cores, HD), core, axis=2, keepdims=False
+
+    block, kind, lane = jnp.unravel_index(
+        jnp.arange(heads_per_core * 2 * HD, dtype=jnp.int32), (heads_per_core, 2, HD)
     )
-    local_bias = jnp.roll(jnp.swapaxes(local_bias, 0, 1), -here, axis=0).reshape(-1)
+    head = ((here + block) % heads_per_core) * cores + core
+    columns = kind * KVH * HD + head * HD + lane
+    picks = jnp.arange(kv_weight.shape[1], dtype=jnp.int32)[:, None] == columns[None, :]
+    local_weight = jnp.dot(
+        kv_weight, picks.astype(kv_weight.dtype), preferred_element_type=jnp.float32
+    ).astype(kv_weight.dtype)
+    local_bias = jnp.take(kv_bias, columns, mode="clip")
     local_weight, local_bias, input_entries = lax.optimization_barrier(
         (local_weight, local_bias, input_entries)
     )
+    local_weight = with_layout_constraint(local_weight, Layout(major_to_minor=(0, 1)))
     gathered_weight = lax.all_gather(local_weight, "dp", axis=0, tiled=True)
+    gathered_weight = with_layout_constraint(gathered_weight, Layout(major_to_minor=(0, 1)))
 
     counts, anchors, offsets, run_ends = plan_tables(
         segment_entry_counts[0], segment_destination_part[0], peer_count

time: 183 us -> 184 us (level)
  local copies, waits for them, and re-layouts: 9.36 us -> 14.1 us
  starting transfers between devices: 12 us -> 9.87 us
    gather x0 -> x1, local copies, waits for them, and re-layouts: none -> 6.15 us  [on_device(): local_bias = jnp.take(kv_bias, columns, mode='clip')]
    dot_general x2, matrix products: 23.1 us -> 18.3 us  [project(): jnp.dot(rows, gathered_weight, preferred_element_type=jnp.float32)]
    dot_general x0 -> x1, matrix products: none -> 3.42 us  [on_device(): jnp.dot(kv_weight, picks.astype(kv_weight.dtype), preferred_element_type=...]
    all_gather x1, waiting for transfers between devices: 3.13 us -> 0.01 us  [on_device(): gathered_weight = lax.all_gather(local_weight, 'dp', axis=0, tiled=True)]
    ppermute x3, waiting for transfers between devices: 9.27 us -> 12.4 us  [on_device(): lax.ppermute(mapped[step], 'cx', perm=[(i, (i + step) % chips) for i in r...]
    ppermute x3, starting transfers between devices: 4.84 us -> 2.69 us  [on_device(): lax.ppermute(mapped[step], 'cx', perm=[(i, (i + step) % chips) for i in r...]
    dynamic_slice x5 -> x0, local copies, waits for them, and re-layouts: 2.06 us -> none  [the longest x1 1.31 us: on_device(): local_weight = jnp.roll(jnp.swapaxes(local_weight, 1, 2), -here, axis=1)]
    dynamic_update_slice x3, local copies, waits for them, and re-layouts: 0.06 us -> 1.97 us  [on_device(): lax.dynamic_update_index_in_dim(by_heads, arrived, (here + chips - step)...]
  transfers between devices with their start and end apart: 6 -> 6, of which waited for: 5 -> 2; matrix products, arithmetic and copies ran while one was open for 19% -> 20% of each run, Pallas kernels for 0% -> 0%
where the time goes in v12:
time: 184 us; the launch traced here: 183 us
  waiting for transfers between devices  100 us (54%)
  matrix products  35.4 us (19%)
  between operations  14.2 us (8%)
  local copies, waits for them, and re-layouts  14.1 us (8%)
  starting transfers between devices  9.87 us (5%)
  other arithmetic  9.56 us (5%)
    all_to_all x1, waiting for transfers between devices, on_device(): lax.all_to_all(outgoing.reshape(peer_count, capacity, -1), CTX, split_axi...  87.7 us
    dot_general x2, matrix products, project(): jnp.dot(rows, gathered_weight, preferred_element_type=jnp.float32)  18.3 us
    dot_general x2, matrix products, select_rows(): jnp.dot(picks.astype(rows.dtype), rows, preferred_element_type=jnp.float32)  13.7 us
    ppermute x3, waiting for transfers between devices, on_device(): lax.ppermute(mapped[step], 'cx', perm=[(i, (i + step) % chips) for i in r...  12.4 us
    all_to_all x1, starting transfers between devices, on_device(): lax.all_to_all(outgoing.reshape(peer_count, capacity, -1), CTX, split_axi...  6.27 us
    gather x1, local copies, waits for them, and re-layouts, on_device(): local_bias = jnp.take(kv_bias, columns, mode='clip')  6.15 us
    add x1, other arithmetic, on_device(): index = source * capacity + shift + within  4.97 us
  transfers between devices with their start and end apart: 6, of which 2 were waited for; matrix products, arithmetic and copies ran while one was open for 20% of the time, Pallas kernels for 0%

profile of v12, /device:TPU:1, one launch (start us, length us, event | category | flops | bytes accessed | tf_op | source)
XLA Modules:
  0.0 183.2 jit_solution(14490350275579545552)
XLA Ops:
  7.2 0.0 copy-start
  7.2 0.0 copy-start.1
  7.2 0.0 all-gather.2.cloned.1.call-start
  7.3 1.5 copy-done
  8.8 0.0 copy-start.3
  8.8 0.0 copy-start.5
  8.8 3.4 %fusion.7 = bf16[512,1024]{1,0:T(8,128)(2,1)} fusion(bf16[512,2048]{1,0:T(8,128)(2,1)S(1)} %copy-done, s32[1024]{0:T(1024)S(1)} %get-tuple-element.46), kind=kOutput, calls=%fused_computation.15 | convolution fusion | flops 2150105088 | bytes 3149824 | tf_op jit(solution)/shard_map/dot_general | solution.py:119
  12.2 0.0 copy-done.1
  12.2 6.1 %gather_fusion = f32[1024]{0:T(1024)S(1)} fusion(f32[2048]{0:T(1024)S(1)} %copy-done.1, s32[1024]{0:T(1024)S(1)} %get-tuple-element.47), kind=kCustom, calls=%fused_computation | custom fusion | bytes 12288 | tf_op jit(solution)/shard_map/jit(_take)/gather | solution.py:122
  18.3 0.0 all-gather.2.cloned.1.call-update
  18.4 0.0 copy-done.3
  18.4 0.2 reduce_window_sum.23
  18.5 0.0 copy-done.5
  18.6 0.1 select_reduce_fusion.1
  18.7 0.1 iota_add_fusion
  18.8 0.1 add.153
  18.8 7.8 %convolution_convert_fusion = bf16[512,8192]{1,0:T(8,128)(2,1)} fusion(bf16[1,256,8192]{2,1,0:T(8,128)(2,1)} %param.12, s32[512]{0:T(512)S(1)} %add.153), kind=kOutput, calls=%fused_computation.1 | convolution fusion | flops 2151809024 | bytes 12584960 | tf_op jit(solution)/shard_map/dot_general | solution.py:92
  26.6 6.3 %all-to-all-start = ((bf16[8,64,8192]{2,1,0:T(8,128)(2,1)}), bf16[8,64,8192]{2,1,0:T(8,128)(2,1)}, u32[]{:S(2)}, u32[]{:S(2)}) async-start(bf16[8,64,8192]{2,1,0:T(8,128)(2,1)} %bitcast.53), calls=%async_computation | async-start | bytes 16777216 | tf_op jit(solution)/shard_map/all_to_all | solution.py:138
  32.9 0.2 dynamic-slice_reduce_fusion
  33.1 0.2 dynamic-slice_reduce_fusion.2
  33.3 0.6 fusion.48
  33.9 0.1 convert_reduce_fusion
  34.0 0.1 select_reduce_fusion.3
  34.1 5.0 %subtract_add_fusion = s32[256]{0:T(256)S(1)} fusion(s32[256]{0:T(256)S(1)} %get-tuple-element.29, s32[256]{0:T(256)S(1)} %get-tuple-element.28, s32[256]{0:T(256)S(1)} %convert_reduce_fusion, s32[]{:T(128)} %bitcast.2, s32[]{:T(128)} %bitcast.3, s32[]{:T(128)} %bitcast.4, s32[]{:T(128)} %bitcast.5, s32[]{:T(128)} %bitcast.6, s32[]{:T(128)} %bitcast.7, ...), kind=kLoop, calls=%fused_computation.113 | loop fusion | flops 4864 | bytes 4128 | tf_op jit(solution)/shard_map/add | solution.py:145
  39.1 87.7 %all-to-all-done = bf16[8,64,8192]{2,1,0:T(8,128)(2,1)} async-done(((bf16[8,64,8192]{2,1,0:T(8,128)(2,1)}), bf16[8,64,8192]{2,1,0:T(8,128)(2,1)}, u32[]{:S(2)}, u32[]{:S(2)}) %all-to-all-start) | async-done | bytes 8388640 | tf_op jit(solution)/shard_map/all_to_all | solution.py:138
  126.8 0.0 copy-start.4
  126.8 5.9 %fusion = (f32[256]{0:T(256)S(1)}, bf16[256,8192]{1,0:T(8,128)(2,1)S(1)}) fusion(bf16[512,8192]{1,0:T(8,128)(2,1)} %bitcast.14, s32[256]{0:T(256)S(1)} %subtract_add_fusion), kind=kOutput, calls=%fused_computation.5 | convolution fusion | flops 2156003072 | bytes 12584960 | tf_op jit(solution)/shard_map/dot_general | solution.py:92
  132.7 0.0 copy-start.2
  132.7 2.0 %copy-done.2 = bf16[256,8192]{1,0:T(8,128)(2,1)} copy-done((bf16[256,8192]{1,0:T(8,128)(2,1)}, bf16[256,8192]{1,0:T(8,128)(2,1)S(1)}, u32[]{:S(2)}) %copy-start.2) | copy-done | bytes 4194328
  134.7 0.0 copy-done.4
  134.7 3.1 %fusion.2 = bf16[256,8192]{1,0:T(8,128)(2,1)} fusion(bf16[256,8192]{1,0:T(8,128)(2,1)S(1)} %get-tuple-element.45, f32[8192]{0:T(1024)S(1)} %copy-done.4, f32[256]{0:T(256)S(1)} %add_rsqrt_fusion), kind=kLoop, calls=%fused_computation.7 | loop fusion | flops 8388608 | bytes 8422400 | tf_op jit(solution)/shard_map/convert_element_type | solution.py:37
  137.8 0.9 collective-permute-start
  138.7 0.0 all-gather.2.cloned.1.call-done
  138.7 0.0 copy-start.6
  138.7 11.7 %fusion.8 = bf16[256,1024]{1,0:T(8,128)(2,1)S(1)} fusion(bf16[256,8192]{1,0:T(8,128)(2,1)} %fusion.2, bf16[8192,1024]{1,0:T(8,128)(2,1)} %all-gather.2.cloned.1.call-done, f32[1024]{0:T(1024)S(1)} %gather_fusion), kind=kOutput, calls=%fused_computation.22 | convolution fusion | flops 4295491584 | bytes 21499904 | tf_op jit(solution)/shard_map/dot_general | solution.py:151
  150.4 0.0 collective-permute-done
  150.4 0.1 copy-done.6
  150.5 6.7 %broadcast_select_fusion = (bf16[256,1024]{1,0:T(8,128)(2,1)S(1)}, bf16[256,1024]{1,0:T(8,128)(2,1)S(1)}) fusion(bf16[256,1024]{1,0:T(8,128)(2,1)S(1)} %fusion.8, pred[]{:T(512)S(6)} %eq.97, f32[1024]{0:T(1024)S(1)} %gather_fusion, bf16[256,8192]{1,0:T(8,128)(2,1)} %collective-permute-done, bf16[8192,1024]{1,0:T(8,128)(2,1)S(1)} %copy-done.6), kind=kOutput, calls=%fused_computation.28 | convolution fusion | flops 4296015872 | bytes 22548480 | tf_op jit(solution)/shard_map/dot_general | solution.py:151
  157.3 0.1 broadcast_in_dim.56
  157.3 0.9 fusion.16
  158.2 0.3 collective-permute-start.1
  158.5 1.8 collective-permute-start.2
  160.3 0.6 collective-permute-start.3
  160.9 12.4 %collective-permute-done.1 = bf16[512,256]{1,0:T(8,128)(2,1)} collective-permute-done((bf16[512,256]{1,0:T(8,128)(2,1)}, bf16[512,256]{1,0:T(8,128)(2,1)}, u32[]{:S(2)}, u32[]{:S(2)}) %collective-permute-start.1) | collective-permute-done | bytes 262176 | tf_op jit(solution)/shard_map/ppermute | solution.py:163
  173.3 1.0 bitcast_dynamic-update-slice_fusion.2
  174.3 0.0 collective-permute-done.2
  174.3 1.0 bitcast_dynamic-update-slice_fusion.1
  175.2 0.0 collective-permute-done.3
  175.3 1.1 reshape.81
  (10 shorter events, 0.2 us)
Async XLA Ops:
  7.2 1.6 copy-start
  7.2 5.0 %copy-start.1 = (f32[2048]{0:T(1024)S(1)}, f32[2048]{0:T(1024)}, u32[]{:S(2)}) copy-start(f32[2048]{0:T(1024)} %param.17) | copy-start | bytes 24580
  7.2 131.5 %all-gather.2.cloned.1.call-start = ((), (), s32[]{:S(2)}) async-start(), calls=%async_computation.1 | async-start | bytes 17825792 | tf_op jit(solution)/shard_map/all_gather | solution.py:127
  8.8 9.6 %copy-start.3 = (s32[1,8,8]{2,1,0:T(8,128)S(1)}, s32[1,8,8]{2,1,0:T(8,128)}, u32[]{:S(2)}) copy-start(s32[1,8,8]{2,1,0:T(8,128)} %param.13) | copy-start | bytes 772
  8.8 9.8 %copy-start.5 = (s32[1,8,8]{2,1,0:T(8,128)S(1)}, s32[1,8,8]{2,1,0:T(8,128)}, u32[]{:S(2)}) copy-start(s32[1,8,8]{2,1,0:T(8,128)} %param.14) | copy-start | bytes 772
  26.6 100.1 %all-to-all-start = ((bf16[8,64,8192]{2,1,0:T(8,128)(2,1)}), bf16[8,64,8192]{2,1,0:T(8,128)(2,1)}, u32[]{:S(2)}, u32[]{:S(2)}) async-start(bf16[8,64,8192]{2,1,0:T(8,128)(2,1)} %bitcast.53), calls=%async_computation | async-start | bytes 16777216 | tf_op jit(solution)/shard_map/all_to_all | solution.py:138
  126.8 7.9 %copy-start.4 = (f32[8192]{0:T(1024)S(1)}, f32[8192]{0:T(1024)}, u32[]{:S(2)}) copy-start(f32[8192]{0:T(1024)} %param.15) | copy-start | bytes 98308
  132.7 2.0 %copy-start.2 = (bf16[256,8192]{1,0:T(8,128)(2,1)}, bf16[256,8192]{1,0:T(8,128)(2,1)S(1)}, u32[]{:S(2)}) copy-start(bf16[256,8192]{1,0:T(8,128)(2,1)S(1)} %get-tuple-element.45) | copy-start | bytes 12582916
  137.8 12.5 %collective-permute-start = (bf16[256,8192]{1,0:T(8,128)(2,1)}, bf16[256,8192]{1,0:T(8,128)(2,1)}, u32[]{:S(2)}, u32[]{:S(2)}) collective-permute-start(bf16[256,8192]{1,0:T(8,128)(2,1)} %fusion.2), channel_id=1, source_target_pairs={{0,1},{1,0},{2,3},{3,2},{4,5},{5,4},{6,7},{7,6},{8,9},{9,8},{10,11... | collective-permute-start | bytes 12582920 | tf_op jit(solution)/shard_map/ppermute | solution.py:148
  138.7 11.8 %copy-start.6 = (bf16[8192,1024]{1,0:T(8,128)(2,1)S(1)}, bf16[8192,1024]{1,0:T(8,128)(2,1)}, u32[]{:S(2)}) copy-start(bf16[8192,1024]{1,0:T(8,128)(2,1)} %all-gather.2.cloned.1.call-done) | copy-start | bytes 50331652
  158.2 15.1 %collective-permute-start.1 = (bf16[512,256]{1,0:T(8,128)(2,1)}, bf16[512,256]{1,0:T(8,128)(2,1)}, u32[]{:S(2)}, u32[]{:S(2)}) collective-permute-start(bf16[512,256]{1,0:T(8,128)(2,1)} %get-tuple-element.32), channel_id=1, source_target_pairs={{0,2},{2,4},{4,6},{6,0},{1,3},{3,5},{5,7},{7,1},{8,10},{10,12},{12... | collective-permute-start | bytes 786440 | tf_op jit(solution)/shard_map/ppermute | solution.py:163
  158.5 15.8 %collective-permute-start.2 = (bf16[512,256]{1,0:T(8,128)(2,1)}, bf16[512,256]{1,0:T(8,128)(2,1)}, u32[]{:S(2)}, u32[]{:S(2)}) collective-permute-start(bf16[512,256]{1,0:T(8,128)(2,1)} %get-tuple-element.33), channel_id=1, source_target_pairs={{0,4},{2,6},{4,0},{6,2},{1,5},{3,7},{5,1},{7,3},{8,12},{10,14},{12... | collective-permute-start | bytes 786440 | tf_op jit(solution)/shard_map/ppermute | solution.py:163
  160.3 15.0 %collective-permute-start.3 = (bf16[512,256]{1,0:T(8,128)(2,1)S(1)}, bf16[512,256]{1,0:T(8,128)(2,1)S(1)}, u32[]{:S(2)}, u32[]{:S(2)}) collective-permute-start(bf16[512,256]{1,0:T(8,128)(2,1)S(1)} %get-tuple-element.30), channel_id=1, source_target_pairs={{0,6},{2,0},{4,2},{6,4},{1,7},{3,1},{5,3},{7,5},{8,14},{10,8},{12,... | collective-permute-start | bytes 786440 | tf_op jit(solution)/shard_map/ppermute | solution.py:163
Sparse Core Ops, SparseCore 0:
  18.5 114.6 all-gather.1

commit v13 on v12

--- a/solution.py
+++ b/solution.py
@@ -120,9 +120,7 @@
         kv_weight, picks.astype(kv_weight.dtype), preferred_element_type=jnp.float32
     ).astype(kv_weight.dtype)
     local_bias = jnp.take(kv_bias, columns, mode="clip")
-    local_weight, local_bias, input_entries = lax.optimization_barrier(
-        (local_weight, local_bias, input_entries)
-    )
+    local_weight, input_entries = lax.optimization_barrier((local_weight, input_entries))
     local_weight = with_layout_constraint(local_weight, Layout(major_to_minor=(0, 1)))
     gathered_weight = lax.all_gather(local_weight, "dp", axis=0, tiled=True)
     gathered_weight = with_layout_constraint(gathered_weight, Layout(major_to_minor=(0, 1)))

time: 184 us -> 184 us (level)
  transfers between devices with their start and end apart: 6 -> 6, of which waited for: 2 -> 2; matrix products, arithmetic and copies ran while one was open for 20% -> 24% of each run, Pallas kernels for 0% -> 0%
where the time goes in v13:
time: 184 us; the launch traced here: 183 us
  waiting for transfers between devices  100 us (54%)
  matrix products  35.4 us (19%)
  between operations  14.2 us (8%)
  local copies, waits for them, and re-layouts  14.1 us (8%)
  starting transfers between devices  9.86 us (5%)
  other arithmetic  9.59 us (5%)
    all_to_all x1, waiting for transfers between devices, on_device(): lax.all_to_all(outgoing.reshape(peer_count, capacity, -1), CTX, split_axi...  87.7 us
    dot_general x2, matrix products, project(): jnp.dot(rows, gathered_weight, preferred_element_type=jnp.float32)  18.3 us
    dot_general x2, matrix products, select_rows(): jnp.dot(picks.astype(rows.dtype), rows, preferred_element_type=jnp.float32)  13.7 us
    ppermute x3, waiting for transfers between devices, on_device(): lax.ppermute(mapped[step], 'cx', perm=[(i, (i + step) % chips) for i in r...  12.4 us
    all_to_all x1, starting transfers between devices, on_device(): lax.all_to_all(outgoing.reshape(peer_count, capacity, -1), CTX, split_axi...  6.26 us
    gather x1, local copies, waits for them, and re-layouts, on_device(): local_bias = jnp.take(kv_bias, columns, mode='clip')  6.15 us
    add x1, other arithmetic, on_device(): index = source * capacity + shift + within  4.97 us
  transfers between devices with their start and end apart: 6, of which 2 were waited for; matrix products, arithmetic and copies ran while one was open for 24% of the time, Pallas kernels for 0%

profile of v13, /device:TPU:1, one launch (start us, length us, event | category | flops | bytes accessed | tf_op | source)
XLA Modules:
  0.0 183.3 jit_solution(4415876500454008330)
XLA Ops:
  7.2 0.0 copy-start
  7.2 0.0 copy-start.3
  7.2 0.0 copy-start.5
  7.2 0.0 all-gather.2.cloned.1.call-start
  7.3 1.5 copy-done
  8.8 3.4 %fusion.7 = bf16[512,1024]{1,0:T(8,128)(2,1)} fusion(bf16[512,2048]{1,0:T(8,128)(2,1)S(1)} %copy-done, s32[1024]{0:T(1024)S(1)} %fusion.30), kind=kOutput, calls=%fused_computation.15 | convolution fusion | flops 2150105088 | bytes 3149824 | tf_op jit(solution)/shard_map/dot_general | solution.py:119
  12.2 0.0 all-gather.2.cloned.1.call-update
  12.2 0.0 copy-done.3
  12.2 0.2 reduce_window_sum.23
  12.4 0.0 copy-done.5
  12.4 0.1 select_reduce_fusion.1
  12.5 0.1 iota_add_fusion
  12.6 0.1 add.153
  12.7 7.8 %convolution_convert_fusion = bf16[512,8192]{1,0:T(8,128)(2,1)} fusion(bf16[1,256,8192]{2,1,0:T(8,128)(2,1)} %param.12, s32[512]{0:T(512)S(1)} %add.153), kind=kOutput, calls=%fused_computation.1 | convolution fusion | flops 2151809024 | bytes 12584960 | tf_op jit(solution)/shard_map/dot_general | solution.py:92
  20.5 6.3 %all-to-all-start = ((bf16[8,64,8192]{2,1,0:T(8,128)(2,1)}), bf16[8,64,8192]{2,1,0:T(8,128)(2,1)}, u32[]{:S(2)}, u32[]{:S(2)}) async-start(bf16[8,64,8192]{2,1,0:T(8,128)(2,1)} %bitcast.53), calls=%async_computation | async-start | bytes 16777216 | tf_op jit(solution)/shard_map/all_to_all | solution.py:136
  26.8 0.2 dynamic-slice_reduce_fusion
  27.0 0.2 dynamic-slice_reduce_fusion.2
  27.2 0.6 fusion.48
  27.8 0.1 convert_reduce_fusion
  27.9 0.1 select_reduce_fusion.3
  27.9 5.0 %subtract_add_fusion = s32[256]{0:T(256)S(1)} fusion(s32[256]{0:T(256)S(1)} %get-tuple-element.27, s32[256]{0:T(256)S(1)} %get-tuple-element.26, s32[256]{0:T(256)S(1)} %convert_reduce_fusion, s32[]{:T(128)} %bitcast.2, s32[]{:T(128)} %bitcast.3, s32[]{:T(128)} %bitcast.4, s32[]{:T(128)} %bitcast.5, s32[]{:T(128)} %bitcast.6, s32[]{:T(128)} %bitcast.7, ...), kind=kLoop, calls=%fused_computation.113 | loop fusion | flops 4864 | bytes 4128 | tf_op jit(solution)/shard_map/add | solution.py:143
  32.9 87.7 %all-to-all-done = bf16[8,64,8192]{2,1,0:T(8,128)(2,1)} async-done(((bf16[8,64,8192]{2,1,0:T(8,128)(2,1)}), bf16[8,64,8192]{2,1,0:T(8,128)(2,1)}, u32[]{:S(2)}, u32[]{:S(2)}) %all-to-all-start) | async-done | bytes 8388640 | tf_op jit(solution)/shard_map/all_to_all | solution.py:136
  120.6 0.0 copy-start.4
  120.6 5.9 %fusion = (f32[256]{0:T(256)S(1)}, bf16[256,8192]{1,0:T(8,128)(2,1)S(1)}) fusion(bf16[512,8192]{1,0:T(8,128)(2,1)} %bitcast.14, s32[256]{0:T(256)S(1)} %subtract_add_fusion), kind=kOutput, calls=%fused_computation.5 | convolution fusion | flops 2156003072 | bytes 12584960 | tf_op jit(solution)/shard_map/dot_general | solution.py:92
  126.5 0.0 copy-start.2
  126.5 0.0 copy-start.1
  126.5 2.0 %copy-done.2 = bf16[256,8192]{1,0:T(8,128)(2,1)} copy-done((bf16[256,8192]{1,0:T(8,128)(2,1)}, bf16[256,8192]{1,0:T(8,128)(2,1)S(1)}, u32[]{:S(2)}) %copy-start.2) | copy-done | bytes 4194328
  128.5 0.0 copy-done.4
  128.5 3.2 %fusion.2 = bf16[256,8192]{1,0:T(8,128)(2,1)} fusion(bf16[256,8192]{1,0:T(8,128)(2,1)S(1)} %get-tuple-element.43, f32[8192]{0:T(1024)S(1)} %copy-done.4, f32[256]{0:T(256)S(1)} %add_rsqrt_fusion), kind=kLoop, calls=%fused_computation.7 | loop fusion | flops 8388608 | bytes 8422400 | tf_op jit(solution)/shard_map/convert_element_type | solution.py:37
  131.7 0.9 collective-permute-start
  132.6 0.0 copy-done.1
  132.6 6.2 %gather_fusion = f32[1024]{0:T(1024)S(1)} fusion(f32[2048]{0:T(1024)S(1)} %copy-done.1, s32[1024]{0:T(1024)S(1)} %broadcast_clamp_fusion), kind=kCustom, calls=%fused_computation | custom fusion | bytes 12288 | tf_op jit(solution)/shard_map/jit(_take)/gather | solution.py:122
  138.7 0.0 all-gather.2.cloned.1.call-done
  138.8 0.0 copy-start.6
  138.8 11.7 %fusion.8 = bf16[256,1024]{1,0:T(8,128)(2,1)S(1)} fusion(bf16[256,8192]{1,0:T(8,128)(2,1)} %fusion.2, bf16[8192,1024]{1,0:T(8,128)(2,1)} %all-gather.2.cloned.1.call-done, f32[1024]{0:T(1024)S(1)} %gather_fusion), kind=kOutput, calls=%fused_computation.22 | convolution fusion | flops 4295491584 | bytes 21499904 | tf_op jit(solution)/shard_map/dot_general | solution.py:149
  150.5 0.0 collective-permute-done
  150.5 0.1 copy-done.6
  150.6 6.7 %broadcast_select_fusion = (bf16[256,1024]{1,0:T(8,128)(2,1)S(1)}, bf16[256,1024]{1,0:T(8,128)(2,1)S(1)}) fusion(bf16[256,1024]{1,0:T(8,128)(2,1)S(1)} %fusion.8, pred[]{:T(512)S(6)} %eq.97, f32[1024]{0:T(1024)S(1)} %gather_fusion, bf16[256,8192]{1,0:T(8,128)(2,1)} %collective-permute-done, bf16[8192,1024]{1,0:T(8,128)(2,1)S(1)} %copy-done.6), kind=kOutput, calls=%fused_computation.28 | convolution fusion | flops 4296015872 | bytes 22548480 | tf_op jit(solution)/shard_map/dot_general | solution.py:149
  157.3 0.1 broadcast_in_dim.55
  157.4 0.9 fusion.16
  158.3 0.3 collective-permute-start.1
  158.6 1.8 collective-permute-start.2
  160.3 0.6 collective-permute-start.3
  161.0 12.4 %collective-permute-done.1 = bf16[512,256]{1,0:T(8,128)(2,1)} collective-permute-done((bf16[512,256]{1,0:T(8,128)(2,1)}, bf16[512,256]{1,0:T(8,128)(2,1)}, u32[]{:S(2)}, u32[]{:S(2)}) %collective-permute-start.1) | collective-permute-done | bytes 262176 | tf_op jit(solution)/shard_map/ppermute | solution.py:161
  173.4 1.0 bitcast_dynamic-update-slice_fusion.2
  174.3 0.0 collective-permute-done.2
  174.3 1.0 bitcast_dynamic-update-slice_fusion.1
  175.3 0.0 collective-permute-done.3
  175.4 1.1 reshape.81
  (11 shorter events, 0.2 us)
Async XLA Ops:
  7.2 1.6 copy-start
  7.2 5.0 %copy-start.3 = (s32[1,8,8]{2,1,0:T(8,128)S(1)}, s32[1,8,8]{2,1,0:T(8,128)}, u32[]{:S(2)}) copy-start(s32[1,8,8]{2,1,0:T(8,128)} %param.13) | copy-start | bytes 772
  7.2 5.2 %copy-start.5 = (s32[1,8,8]{2,1,0:T(8,128)S(1)}, s32[1,8,8]{2,1,0:T(8,128)}, u32[]{:S(2)}) copy-start(s32[1,8,8]{2,1,0:T(8,128)} %param.14) | copy-start | bytes 772
  7.2 131.6 %all-gather.2.cloned.1.call-start = ((), (), s32[]{:S(2)}) async-start(), calls=%async_computation.1 | async-start | bytes 17825792 | tf_op jit(solution)/shard_map/all_gather | solution.py:125
  20.5 100.1 %all-to-all-start = ((bf16[8,64,8192]{2,1,0:T(8,128)(2,1)}), bf16[8,64,8192]{2,1,0:T(8,128)(2,1)}, u32[]{:S(2)}, u32[]{:S(2)}) async-start(bf16[8,64,8192]{2,1,0:T(8,128)(2,1)} %bitcast.53), calls=%async_computation | async-start | bytes 16777216 | tf_op jit(solution)/shard_map/all_to_all | solution.py:136
  120.6 7.9 %copy-start.4 = (f32[8192]{0:T(1024)S(1)}, f32[8192]{0:T(1024)}, u32[]{:S(2)}) copy-start(f32[8192]{0:T(1024)} %param.15) | copy-start | bytes 98308
  126.5 2.0 %copy-start.2 = (bf16[256,8192]{1,0:T(8,128)(2,1)}, bf16[256,8192]{1,0:T(8,128)(2,1)S(1)}, u32[]{:S(2)}) copy-start(bf16[256,8192]{1,0:T(8,128)(2,1)S(1)} %get-tuple-element.43) | copy-start | bytes 12582916
  126.5 6.1 %copy-start.1 = (f32[2048]{0:T(1024)S(1)}, f32[2048]{0:T(1024)}, u32[]{:S(2)}) copy-start(f32[2048]{0:T(1024)} %param.17) | copy-start | bytes 24580
  131.7 18.8 %collective-permute-start = (bf16[256,8192]{1,0:T(8,128)(2,1)}, bf16[256,8192]{1,0:T(8,128)(2,1)}, u32[]{:S(2)}, u32[]{:S(2)}) collective-permute-start(bf16[256,8192]{1,0:T(8,128)(2,1)} %fusion.2), channel_id=1, source_target_pairs={{0,1},{1,0},{2,3},{3,2},{4,5},{5,4},{6,7},{7,6},{8,9},{9,8},{10,11... | collective-permute-start | bytes 12582920 | tf_op jit(solution)/shard_map/ppermute | solution.py:146
  138.8 11.8 %copy-start.6 = (bf16[8192,1024]{1,0:T(8,128)(2,1)S(1)}, bf16[8192,1024]{1,0:T(8,128)(2,1)}, u32[]{:S(2)}) copy-start(bf16[8192,1024]{1,0:T(8,128)(2,1)} %all-gather.2.cloned.1.call-done) | copy-start | bytes 50331652
  158.3 15.1 %collective-permute-start.1 = (bf16[512,256]{1,0:T(8,128)(2,1)}, bf16[512,256]{1,0:T(8,128)(2,1)}, u32[]{:S(2)}, u32[]{:S(2)}) collective-permute-start(bf16[512,256]{1,0:T(8,128)(2,1)} %get-tuple-element.30), channel_id=1, source_target_pairs={{0,2},{2,4},{4,6},{6,0},{1,3},{3,5},{5,7},{7,1},{8,10},{10,12},{12... | collective-permute-start | bytes 786440 | tf_op jit(solution)/shard_map/ppermute | solution.py:161
  158.6 15.8 %collective-permute-start.2 = (bf16[512,256]{1,0:T(8,128)(2,1)}, bf16[512,256]{1,0:T(8,128)(2,1)}, u32[]{:S(2)}, u32[]{:S(2)}) collective-permute-start(bf16[512,256]{1,0:T(8,128)(2,1)} %get-tuple-element.31), channel_id=1, source_target_pairs={{0,4},{2,6},{4,0},{6,2},{1,5},{3,7},{5,1},{7,3},{8,12},{10,14},{12... | collective-permute-start | bytes 786440 | tf_op jit(solution)/shard_map/ppermute | solution.py:161
  160.3 15.0 %collective-permute-start.3 = (bf16[512,256]{1,0:T(8,128)(2,1)S(1)}, bf16[512,256]{1,0:T(8,128)(2,1)S(1)}, u32[]{:S(2)}, u32[]{:S(2)}) collective-permute-start(bf16[512,256]{1,0:T(8,128)(2,1)S(1)} %get-tuple-element.28), channel_id=1, source_target_pairs={{0,6},{2,0},{4,2},{6,4},{1,7},{3,1},{5,3},{7,5},{8,14},{10,8},{12,... | collective-permute-start | bytes 786440 | tf_op jit(solution)/shard_map/ppermute | solution.py:161
Sparse Core Ops, SparseCore 0:
  12.3 114.6 all-gather.1

commit v14 on v13

--- a/solution.py
+++ b/solution.py
@@ -141,6 +141,7 @@
     )
     shift = anchor - jnp.take(starts[:, myself], source, mode="clip")
     index = source * capacity + shift + within
+    local_bias, index = lax.optimization_barrier((local_bias, index))
     moved_rows = select_rows(arriving_rows.reshape(peer_count * capacity, -1), index)
     normed = rms_normed(moved_rows, norm_gain)
     sibling_rows = lax.ppermute(normed, "cc", perm=[(0, 1), (1, 0)])

time: 184 us -> 178 us (0.967)
  waiting for transfers between devices: 100 us -> 93.9 us
    all_to_all x1, waiting for transfers between devices: 87.7 us -> 81.5 us  [on_device(): lax.all_to_all(outgoing.reshape(peer_count, capacity, -1), CTX, split_axi...]
where the time goes in v14:
time: 178 us; the launch traced here: 177 us
  waiting for transfers between devices  93.9 us (53%)
  matrix products  35.4 us (20%)
  between operations  14.2 us (8%)
  local copies, waits for them, and re-layouts  14.1 us (8%)
  starting transfers between devices  9.99 us (6%)
  other arithmetic  9.56 us (5%)
    all_to_all x1, waiting for transfers between devices, on_device(): lax.all_to_all(outgoing.reshape(peer_count, capacity, -1), CTX, split_axi...  81.5 us
    dot_general x2, matrix products, project(): jnp.dot(rows, gathered_weight, preferred_element_type=jnp.float32)  18.3 us
    dot_general x2, matrix products, select_rows(): jnp.dot(picks.astype(rows.dtype), rows, preferred_element_type=jnp.float32)  13.7 us
    ppermute x3, waiting for transfers between devices, on_device(): lax.ppermute(mapped[step], 'cx', perm=[(i, (i + step) % chips) for i in r...  12.4 us
    all_to_all x1, starting transfers between devices, on_device(): lax.all_to_all(outgoing.reshape(peer_count, capacity, -1), CTX, split_axi...  6.39 us
    gather x1, local copies, waits for them, and re-layouts, on_device(): local_bias = jnp.take(kv_bias, columns, mode='clip')  6.15 us
    add x1, other arithmetic, on_device(): index = source * capacity + shift + within  4.97 us
    unnamed x14, local copies, waits for them, and re-layouts  3.62 us
  transfers between devices with their start and end apart: 6, of which 2 were waited for; matrix products, arithmetic and copies ran while one was open for 24% of the time, Pallas kernels for 0%

profile of v14, /device:TPU:1, one launch (start us, length us, event | category | flops | bytes accessed | tf_op | source)
XLA Modules:
  0.0 177.2 jit_solution(11212134876141765595)
XLA Ops:
  7.2 0.0 copy-start
  7.2 0.0 copy-start.3
  7.2 0.0 copy-start.5
  7.2 0.0 all-gather.2.cloned.1.call-start
  7.3 1.5 copy-done
  8.8 3.4 %fusion.7 = bf16[512,1024]{1,0:T(8,128)(2,1)} fusion(bf16[512,2048]{1,0:T(8,128)(2,1)S(1)} %copy-done, s32[1024]{0:T(1024)S(1)} %get-tuple-element.48), kind=kOutput, calls=%fused_computation.15 | convolution fusion | flops 2150105088 | bytes 3149824 | tf_op jit(solution)/shard_map/dot_general | solution.py:119
  12.2 0.0 all-gather.2.cloned.1.call-update
  12.2 0.0 copy-done.3
  12.2 0.2 reduce_window_sum.23
  12.4 0.0 copy-done.5
  12.4 0.1 select_reduce_fusion.1
  12.5 0.1 iota_add_fusion
  12.6 0.1 add.152
  12.7 7.8 %convolution_convert_fusion = bf16[512,8192]{1,0:T(8,128)(2,1)} fusion(bf16[1,256,8192]{2,1,0:T(8,128)(2,1)} %param.12, s32[512]{0:T(512)S(1)} %add.152), kind=kOutput, calls=%fused_computation.1 | convolution fusion | flops 2151809024 | bytes 12584960 | tf_op jit(solution)/shard_map/dot_general | solution.py:92
  20.5 0.0 copy-start.1
  20.5 6.4 %all-to-all-start = ((bf16[8,64,8192]{2,1,0:T(8,128)(2,1)}), bf16[8,64,8192]{2,1,0:T(8,128)(2,1)}, u32[]{:S(2)}, u32[]{:S(2)}) async-start(bf16[8,64,8192]{2,1,0:T(8,128)(2,1)} %bitcast.53), calls=%async_computation | async-start | bytes 16777216 | tf_op jit(solution)/shard_map/all_to_all | solution.py:136
  26.9 0.0 copy-done.1
  26.9 6.2 %gather_fusion = f32[1024]{0:T(1024)S(1)} fusion(f32[2048]{0:T(1024)S(1)} %copy-done.1, s32[1024]{0:T(1024)S(1)} %get-tuple-element.49), kind=kCustom, calls=%fused_computation | custom fusion | bytes 12288 | tf_op jit(solution)/shard_map/jit(_take)/gather | solution.py:122
  33.1 0.2 dynamic-slice_reduce_fusion
  33.3 0.2 dynamic-slice_reduce_fusion.2
  33.5 0.6 fusion.48
  34.1 0.1 convert_reduce_fusion
  34.2 0.1 select_reduce_fusion.3
  34.2 5.0 %subtract_add_fusion = s32[256]{0:T(256)S(1)} fusion(s32[256]{0:T(256)S(1)} %get-tuple-element.31, s32[256]{0:T(256)S(1)} %get-tuple-element.30, s32[256]{0:T(256)S(1)} %convert_reduce_fusion, s32[]{:T(128)} %bitcast.2, s32[]{:T(128)} %bitcast.3, s32[]{:T(128)} %bitcast.4, s32[]{:T(128)} %bitcast.5, s32[]{:T(128)} %bitcast.6, s32[]{:T(128)} %bitcast.7, ...), kind=kLoop, calls=%fused_computation.113 | loop fusion | flops 4864 | bytes 4128 | tf_op jit(solution)/shard_map/add | solution.py:143
  39.2 81.5 %all-to-all-done = bf16[8,64,8192]{2,1,0:T(8,128)(2,1)} async-done(((bf16[8,64,8192]{2,1,0:T(8,128)(2,1)}), bf16[8,64,8192]{2,1,0:T(8,128)(2,1)}, u32[]{:S(2)}, u32[]{:S(2)}) %all-to-all-start) | async-done | bytes 8388640 | tf_op jit(solution)/shard_map/all_to_all | solution.py:136
  120.7 0.0 copy-start.4
  120.7 5.9 %fusion = (f32[256]{0:T(256)S(1)}, bf16[256,8192]{1,0:T(8,128)(2,1)S(1)}) fusion(bf16[512,8192]{1,0:T(8,128)(2,1)} %bitcast.14, s32[256]{0:T(256)S(1)} %subtract_add_fusion), kind=kOutput, calls=%fused_computation.5 | convolution fusion | flops 2156003072 | bytes 12584960 | tf_op jit(solution)/shard_map/dot_general | solution.py:92
  126.6 0.0 copy-start.2
  126.6 2.0 %copy-done.2 = bf16[256,8192]{1,0:T(8,128)(2,1)} copy-done((bf16[256,8192]{1,0:T(8,128)(2,1)}, bf16[256,8192]{1,0:T(8,128)(2,1)S(1)}, u32[]{:S(2)}) %copy-start.2) | copy-done | bytes 4194328
  128.6 0.0 copy-done.4
  128.6 3.1 %fusion.2 = bf16[256,8192]{1,0:T(8,128)(2,1)} fusion(bf16[256,8192]{1,0:T(8,128)(2,1)S(1)} %get-tuple-element.47, f32[8192]{0:T(1024)S(1)} %copy-done.4, f32[256]{0:T(256)S(1)} %add_rsqrt_fusion), kind=kLoop, calls=%fused_computation.7 | loop fusion | flops 8388608 | bytes 8422400 | tf_op jit(solution)/shard_map/convert_element_type | solution.py:37
  131.8 0.9 collective-permute-start
  132.7 0.0 all-gather.2.cloned.1.call-done
  132.7 0.0 copy-start.6
  132.7 11.7 %fusion.8 = bf16[256,1024]{1,0:T(8,128)(2,1)S(1)} fusion(bf16[256,8192]{1,0:T(8,128)(2,1)} %fusion.2, bf16[8192,1024]{1,0:T(8,128)(2,1)} %all-gather.2.cloned.1.call-done, f32[1024]{0:T(1024)S(1)} %gather_fusion), kind=kOutput, calls=%fused_computation.22 | convolution fusion | flops 4295491584 | bytes 21499904 | tf_op jit(solution)/shard_map/dot_general | solution.py:150
  144.3 0.0 collective-permute-done
  144.4 0.1 copy-done.6
  144.5 6.7 %broadcast_select_fusion = (bf16[256,1024]{1,0:T(8,128)(2,1)S(1)}, bf16[256,1024]{1,0:T(8,128)(2,1)S(1)}) fusion(bf16[256,1024]{1,0:T(8,128)(2,1)S(1)} %fusion.8, pred[]{:T(512)S(6)} %eq.97, f32[1024]{0:T(1024)S(1)} %gather_fusion, bf16[256,8192]{1,0:T(8,128)(2,1)} %collective-permute-done, bf16[8192,1024]{1,0:T(8,128)(2,1)S(1)} %copy-done.6), kind=kOutput, calls=%fused_computation.28 | convolution fusion | flops 4296015872 | bytes 22548480 | tf_op jit(solution)/shard_map/dot_general | solution.py:150
  151.2 0.1 broadcast_in_dim.59
  151.3 0.9 fusion.16
  152.2 0.3 collective-permute-start.1
  152.5 1.8 collective-permute-start.2
  154.2 0.6 collective-permute-start.3
  154.9 12.4 %collective-permute-done.1 = bf16[512,256]{1,0:T(8,128)(2,1)} collective-permute-done((bf16[512,256]{1,0:T(8,128)(2,1)}, bf16[512,256]{1,0:T(8,128)(2,1)}, u32[]{:S(2)}, u32[]{:S(2)}) %collective-permute-start.1) | collective-permute-done | bytes 262176 | tf_op jit(solution)/shard_map/ppermute | solution.py:162
  167.3 1.0 bitcast_dynamic-update-slice_fusion.2
  168.2 0.0 collective-permute-done.2
  168.2 1.0 bitcast_dynamic-update-slice_fusion.1
  169.2 0.0 collective-permute-done.3
  169.3 1.1 reshape.66
  (10 shorter events, 0.2 us)
Async XLA Ops:
  7.2 1.6 copy-start
  7.2 5.0 %copy-start.3 = (s32[1,8,8]{2,1,0:T(8,128)S(1)}, s32[1,8,8]{2,1,0:T(8,128)}, u32[]{:S(2)}) copy-start(s32[1,8,8]{2,1,0:T(8,128)} %param.13) | copy-start | bytes 772
  7.2 5.2 %copy-start.5 = (s32[1,8,8]{2,1,0:T(8,128)S(1)}, s32[1,8,8]{2,1,0:T(8,128)}, u32[]{:S(2)}) copy-start(s32[1,8,8]{2,1,0:T(8,128)} %param.14) | copy-start | bytes 772
  7.2 125.5 %all-gather.2.cloned.1.call-start = ((), (), s32[]{:S(2)}) async-start(), calls=%async_computation.1 | async-start | bytes 17825792 | tf_op jit(solution)/shard_map/all_gather | solution.py:125
  20.5 6.4 %copy-start.1 = (f32[2048]{0:T(1024)S(1)}, f32[2048]{0:T(1024)}, u32[]{:S(2)}) copy-start(f32[2048]{0:T(1024)} %param.17) | copy-start | bytes 24580
  20.5 100.3 %all-to-all-start = ((bf16[8,64,8192]{2,1,0:T(8,128)(2,1)}), bf16[8,64,8192]{2,1,0:T(8,128)(2,1)}, u32[]{:S(2)}, u32[]{:S(2)}) async-start(bf16[8,64,8192]{2,1,0:T(8,128)(2,1)} %bitcast.53), calls=%async_computation | async-start | bytes 16777216 | tf_op jit(solution)/shard_map/all_to_all | solution.py:136
  120.7 7.9 %copy-start.4 = (f32[8192]{0:T(1024)S(1)}, f32[8192]{0:T(1024)}, u32[]{:S(2)}) copy-start(f32[8192]{0:T(1024)} %param.15) | copy-start | bytes 98308
  126.6 2.0 %copy-start.2 = (bf16[256,8192]{1,0:T(8,128)(2,1)}, bf16[256,8192]{1,0:T(8,128)(2,1)S(1)}, u32[]{:S(2)}) copy-start(bf16[256,8192]{1,0:T(8,128)(2,1)S(1)} %get-tuple-element.47) | copy-start | bytes 12582916
  131.8 12.5 %collective-permute-start = (bf16[256,8192]{1,0:T(8,128)(2,1)}, bf16[256,8192]{1,0:T(8,128)(2,1)}, u32[]{:S(2)}, u32[]{:S(2)}) collective-permute-start(bf16[256,8192]{1,0:T(8,128)(2,1)} %fusion.2), channel_id=1, source_target_pairs={{0,1},{1,0},{2,3},{3,2},{4,5},{5,4},{6,7},{7,6},{8,9},{9,8},{10,11... | collective-permute-start | bytes 12582920 | tf_op jit(solution)/shard_map/ppermute | solution.py:147
  132.7 11.8 %copy-start.6 = (bf16[8192,1024]{1,0:T(8,128)(2,1)S(1)}, bf16[8192,1024]{1,0:T(8,128)(2,1)}, u32[]{:S(2)}) copy-start(bf16[8192,1024]{1,0:T(8,128)(2,1)} %all-gather.2.cloned.1.call-done) | copy-start | bytes 50331652
  152.2 15.1 %collective-permute-start.1 = (bf16[512,256]{1,0:T(8,128)(2,1)}, bf16[512,256]{1,0:T(8,128)(2,1)}, u32[]{:S(2)}, u32[]{:S(2)}) collective-permute-start(bf16[512,256]{1,0:T(8,128)(2,1)} %get-tuple-element.34), channel_id=1, source_target_pairs={{0,2},{2,4},{4,6},{6,0},{1,3},{3,5},{5,7},{7,1},{8,10},{10,12},{12... | collective-permute-start | bytes 786440 | tf_op jit(solution)/shard_map/ppermute | solution.py:162
  152.5 15.8 %collective-permute-start.2 = (bf16[512,256]{1,0:T(8,128)(2,1)}, bf16[512,256]{1,0:T(8,128)(2,1)}, u32[]{:S(2)}, u32[]{:S(2)}) collective-permute-start(bf16[512,256]{1,0:T(8,128)(2,1)} %get-tuple-element.35), channel_id=1, source_target_pairs={{0,4},{2,6},{4,0},{6,2},{1,5},{3,7},{5,1},{7,3},{8,12},{10,14},{12... | collective-permute-start | bytes 786440 | tf_op jit(solution)/shard_map/ppermute | solution.py:162
  154.2 15.0 %collective-permute-start.3 = (bf16[512,256]{1,0:T(8,128)(2,1)S(1)}, bf16[512,256]{1,0:T(8,128)(2,1)S(1)}, u32[]{:S(2)}, u32[]{:S(2)}) collective-permute-start(bf16[512,256]{1,0:T(8,128)(2,1)S(1)} %get-tuple-element.32), channel_id=1, source_target_pairs={{0,6},{2,0},{4,2},{6,4},{1,7},{3,1},{5,3},{7,5},{8,14},{10,8},{12,... | collective-permute-start | bytes 786440 | tf_op jit(solution)/shard_map/ppermute | solution.py:162
Sparse Core Ops, SparseCore 0:
  12.3 114.6 all-gather.1

commit v15 on v14

--- a/solution.py
+++ b/solution.py
@@ -143,6 +143,7 @@
     index = source * capacity + shift + within
     local_bias, index = lax.optimization_barrier((local_bias, index))
     moved_rows = select_rows(arriving_rows.reshape(peer_count * capacity, -1), index)
+    gathered_weight, moved_rows = lax.optimization_barrier((gathered_weight, moved_rows))
     normed = rms_normed(moved_rows, norm_gain)
     sibling_rows = lax.ppermute(normed, "cc", perm=[(0, 1), (1, 0)])
 

time: 178 us -> 187 us (1.051)
  matrix products: 35.4 us -> 42 us
  other arithmetic: 9.56 us -> 14.8 us
  local copies, waits for them, and re-layouts: 14.1 us -> 12 us
    dot_general x2, matrix products: 18.3 us -> 23.1 us  [project(): jnp.dot(rows, gathered_weight, preferred_element_type=jnp.float32)]
    reduce_sum x0 -> x1, other arithmetic: none -> 3.1 us  [rms_normed(): jnp.mean(as_float * as_float, axis=-1, keepdims=True) + 1e-06]
    convert_element_type x1, other arithmetic: 3.15 us -> 5.33 us  [rms_normed(): return (as_float * inverse_rms * norm_gain[None, :]).astype(jnp.bfloat16)]
    unnamed x14 -> x10, local copies, waits for them, and re-layouts: 3.62 us -> 1.5 us
    dot_general x2, matrix products: 13.7 us -> 15.6 us  [select_rows(): jnp.dot(picks.astype(rows.dtype), rows, preferred_element_type=jnp.float32)]
  transfers between devices with their start and end apart: 6 -> 6, of which waited for: 2 -> 2; matrix products, arithmetic and copies ran while one was open for 24% -> 22% of each run, Pallas kernels for 0% -> 0%
where the time goes in v15:
time: 187 us
  waiting for transfers between devices  93.5 us (50%)
  matrix products  42 us (22%)
  other arithmetic  14.8 us (8%)
  between operations  14.2 us (8%)
  local copies, waits for them, and re-layouts  12 us (6%)
  starting transfers between devices  10.4 us (6%)
    all_to_all x1, waiting for transfers between devices, on_device(): lax.all_to_all(outgoing.reshape(peer_count, capacity, -1), CTX, split_axi...  81.5 us
    dot_general x2, matrix products, project(): jnp.dot(rows, gathered_weight, preferred_element_type=jnp.float32)  23.1 us
    dot_general x2, matrix products, select_rows(): jnp.dot(picks.astype(rows.dtype), rows, preferred_element_type=jnp.float32)  15.6 us
    ppermute x3, waiting for transfers between devices, on_device(): lax.ppermute(mapped[step], 'cx', perm=[(i, (i + step) % chips) for i in r...  12 us
    all_to_all x1, starting transfers between devices, on_device(): lax.all_to_all(outgoing.reshape(peer_count, capacity, -1), CTX, split_axi...  6.39 us
    gather x1, local copies, waits for them, and re-layouts, on_device(): local_bias = jnp.take(kv_bias, columns, mode='clip')  6.15 us
    convert_element_type x1, other arithmetic, rms_normed(): return (as_float * inverse_rms * norm_gain[None, :]).astype(jnp.bfloat16)  5.33 us
    add x1, other arithmetic, on_device(): index = source * capacity + shift + within  4.97 us
  transfers between devices with their start and end apart: 6, of which 2 were waited for; matrix products, arithmetic and copies ran while one was open for 22% of the time, Pallas kernels for 0%

profile of v15, /device:TPU:1, one launch (start us, length us, event | category | flops | bytes accessed | tf_op | source)
XLA Modules:
  0.0 187.0 jit_solution(897358734603954979)
XLA Ops:
  7.2 0.0 copy-start
  7.2 0.0 copy-start.2
  7.2 0.0 copy-start.4
  7.2 0.0 all-gather.2.cloned.1.call-start
  7.3 1.5 copy-done
  8.8 3.4 %fusion.7 = bf16[512,1024]{1,0:T(8,128)(2,1)} fusion(bf16[512,2048]{1,0:T(8,128)(2,1)S(1)} %copy-done, s32[1024]{0:T(1024)S(1)} %get-tuple-element.50), kind=kOutput, calls=%fused_computation.15 | convolution fusion | flops 2150105088 | bytes 3149824 | tf_op jit(solution)/shard_map/dot_general | solution.py:119
  12.2 0.0 all-gather.2.cloned.1.call-update
  12.2 0.0 copy-done.2
  12.2 0.2 reduce_window_sum.23
  12.4 0.0 copy-done.4
  12.4 0.1 select_reduce_fusion.1
  12.5 0.1 iota_add_fusion
  12.6 0.1 add.152
  12.7 7.8 %convolution_convert_fusion = bf16[512,8192]{1,0:T(8,128)(2,1)} fusion(bf16[1,256,8192]{2,1,0:T(8,128)(2,1)} %param.12, s32[512]{0:T(512)S(1)} %add.152), kind=kOutput, calls=%fused_computation.1 | convolution fusion | flops 2151809024 | bytes 12584960 | tf_op jit(solution)/shard_map/dot_general | solution.py:92
  20.5 0.0 copy-start.1
  20.5 6.4 %all-to-all-start = ((bf16[8,64,8192]{2,1,0:T(8,128)(2,1)}), bf16[8,64,8192]{2,1,0:T(8,128)(2,1)}, u32[]{:S(2)}, u32[]{:S(2)}) async-start(bf16[8,64,8192]{2,1,0:T(8,128)(2,1)} %bitcast.53), calls=%async_computation | async-start | bytes 16777216 | tf_op jit(solution)/shard_map/all_to_all | solution.py:136
  26.9 0.0 copy-done.1
  26.9 6.2 %gather_fusion = f32[1024]{0:T(1024)S(1)} fusion(f32[2048]{0:T(1024)S(1)} %copy-done.1, s32[1024]{0:T(1024)S(1)} %get-tuple-element.51), kind=kCustom, calls=%fused_computation | custom fusion | bytes 12288 | tf_op jit(solution)/shard_map/jit(_take)/gather | solution.py:122
  33.0 0.2 dynamic-slice_reduce_fusion
  33.3 0.2 dynamic-slice_reduce_fusion.2
  33.5 0.6 fusion.48
  34.1 0.1 convert_reduce_fusion
  34.1 0.1 select_reduce_fusion.3
  34.2 5.0 %subtract_add_fusion = s32[256]{0:T(256)S(1)} fusion(s32[256]{0:T(256)S(1)} %get-tuple-element.35, s32[256]{0:T(256)S(1)} %get-tuple-element.34, s32[256]{0:T(256)S(1)} %convert_reduce_fusion, s32[]{:T(128)} %bitcast.3, s32[]{:T(128)} %bitcast.4, s32[]{:T(128)} %bitcast.5, s32[]{:T(128)} %bitcast.6, s32[]{:T(128)} %bitcast.7, s32[]{:T(128)} %bitcast.8, ...), kind=kLoop, calls=%fused_computation.113 | loop fusion | flops 4864 | bytes 4128 | tf_op jit(solution)/shard_map/add | solution.py:143
  39.2 81.5 %all-to-all-done = bf16[8,64,8192]{2,1,0:T(8,128)(2,1)} async-done(((bf16[8,64,8192]{2,1,0:T(8,128)(2,1)}), bf16[8,64,8192]{2,1,0:T(8,128)(2,1)}, u32[]{:S(2)}, u32[]{:S(2)}) %all-to-all-start) | async-done | bytes 8388640 | tf_op jit(solution)/shard_map/all_to_all | solution.py:136
  120.7 0.0 copy-start.3
  120.7 7.8 %convolution_convert_fusion.1 = bf16[256,8192]{1,0:T(8,128)(2,1)} fusion(bf16[512,8192]{1,0:T(8,128)(2,1)} %bitcast.14, s32[256]{0:T(256)S(1)} %subtract_add_fusion), kind=kOutput, calls=%fused_computation.4 | convolution fusion | flops 2149711872 | bytes 12583936 | tf_op jit(solution)/shard_map/dot_general | solution.py:92
  128.5 0.0 all-gather.2.cloned.1.call-done
  128.5 3.1 %fusion = f32[256]{0:T(256)S(1)} fusion(bf16[256,8192]{1,0:T(8,128)(2,1)} %convolution_convert_fusion.1), kind=kLoop, calls=%fused_computation.5 | loop fusion | flops 6291200 | bytes 4195328 | tf_op jit(solution)/shard_map/reduce_sum | solution.py:36
  131.6 0.0 copy-done.3
  131.6 5.3 %fusion.2 = bf16[256,8192]{1,0:T(8,128)(2,1)} fusion(bf16[256,8192]{1,0:T(8,128)(2,1)} %convolution_convert_fusion.1, f32[8192]{0:T(1024)S(1)} %copy-done.3, f32[256]{0:T(256)S(1)} %add_rsqrt_fusion), kind=kLoop, calls=%fused_computation.7 | loop fusion | flops 8388608 | bytes 8422400 | tf_op jit(solution)/shard_map/convert_element_type | solution.py:37
  137.0 0.9 collective-permute-start
  137.8 11.5 %fusion.8 = bf16[256,1024]{1,0:T(8,128)(2,1)S(1)} fusion(bf16[256,8192]{1,0:T(8,128)(2,1)} %fusion.2, bf16[8192,1024]{1,0:T(8,128)(2,1)} %all-gather.2.cloned.1.call-done, f32[1024]{0:T(1024)S(1)} %gather_fusion), kind=kOutput, calls=%fused_computation.22 | convolution fusion | flops 4295491584 | bytes 21499904 | tf_op jit(solution)/shard_map/dot_general | solution.py:151
  149.4 0.0 collective-permute-done
  149.4 11.5 %broadcast_select_fusion = (bf16[256,1024]{1,0:T(8,128)(2,1)S(1)}, bf16[256,1024]{1,0:T(8,128)(2,1)S(1)}) fusion(bf16[256,1024]{1,0:T(8,128)(2,1)S(1)} %fusion.8, pred[]{:T(512)S(6)} %eq.97, f32[1024]{0:T(1024)S(1)} %gather_fusion, bf16[256,8192]{1,0:T(8,128)(2,1)} %collective-permute-done, bf16[8192,1024]{1,0:T(8,128)(2,1)} %all-gather.2.cloned.1.call-done), kind=kOutput, calls=%fused_computation.28 | convolution fusion | flops 4296015872 | bytes 22548480 | tf_op jit(solution)/shard_map/dot_general | solution.py:151
  161.0 0.1 broadcast_in_dim.59
  161.1 0.9 fusion.16
  162.0 0.3 collective-permute-start.1
  162.2 1.8 collective-permute-start.2
  164.0 1.0 collective-permute-start.3
  165.1 12.0 %collective-permute-done.1 = bf16[512,256]{1,0:T(8,128)(2,1)} collective-permute-done((bf16[512,256]{1,0:T(8,128)(2,1)}, bf16[512,256]{1,0:T(8,128)(2,1)}, u32[]{:S(2)}, u32[]{:S(2)}) %collective-permute-start.1) | collective-permute-done | bytes 262176 | tf_op jit(solution)/shard_map/ppermute | solution.py:163
  177.0 1.0 bitcast_dynamic-update-slice_fusion.2
  178.0 0.0 collective-permute-done.2
  178.0 1.0 bitcast_dynamic-update-slice_fusion.1
  179.0 0.0 collective-permute-done.3
  179.0 1.1 reshape.66
  (10 shorter events, 0.2 us)
Async XLA Ops:
  7.2 1.6 copy-start
  7.2 5.0 %copy-start.2 = (s32[1,8,8]{2,1,0:T(8,128)S(1)}, s32[1,8,8]{2,1,0:T(8,128)}, u32[]{:S(2)}) copy-start(s32[1,8,8]{2,1,0:T(8,128)} %param.13) | copy-start | bytes 772
  7.2 5.2 %copy-start.4 = (s32[1,8,8]{2,1,0:T(8,128)S(1)}, s32[1,8,8]{2,1,0:T(8,128)}, u32[]{:S(2)}) copy-start(s32[1,8,8]{2,1,0:T(8,128)} %param.14) | copy-start | bytes 772
  7.2 121.3 %all-gather.2.cloned.1.call-start = ((), (), s32[]{:S(2)}) async-start(), calls=%async_computation.1 | async-start | bytes 17825792 | tf_op jit(solution)/shard_map/all_gather | solution.py:125
  20.5 6.4 %copy-start.1 = (f32[2048]{0:T(1024)S(1)}, f32[2048]{0:T(1024)}, u32[]{:S(2)}) copy-start(f32[2048]{0:T(1024)} %param.17) | copy-start | bytes 24580
  20.5 100.3 %all-to-all-start = ((bf16[8,64,8192]{2,1,0:T(8,128)(2,1)}), bf16[8,64,8192]{2,1,0:T(8,128)(2,1)}, u32[]{:S(2)}, u32[]{:S(2)}) async-start(bf16[8,64,8192]{2,1,0:T(8,128)(2,1)} %bitcast.53), calls=%async_computation | async-start | bytes 16777216 | tf_op jit(solution)/shard_map/all_to_all | solution.py:136
  120.7 10.9 %copy-start.3 = (f32[8192]{0:T(1024)S(1)}, f32[8192]{0:T(1024)}, u32[]{:S(2)}) copy-start(f32[8192]{0:T(1024)} %param.15) | copy-start | bytes 98308
  137.0 12.4 %collective-permute-start = (bf16[256,8192]{1,0:T(8,128)(2,1)}, bf16[256,8192]{1,0:T(8,128)(2,1)}, u32[]{:S(2)}, u32[]{:S(2)}) collective-permute-start(bf16[256,8192]{1,0:T(8,128)(2,1)} %fusion.2), channel_id=1, source_target_pairs={{0,1},{1,0},{2,3},{3,2},{4,5},{5,4},{6,7},{7,6},{8,9},{9,8},{10,11... | collective-permute-start | bytes 12582920 | tf_op jit(solution)/shard_map/ppermute | solution.py:148
  162.0 15.1 %collective-permute-start.1 = (bf16[512,256]{1,0:T(8,128)(2,1)}, bf16[512,256]{1,0:T(8,128)(2,1)}, u32[]{:S(2)}, u32[]{:S(2)}) collective-permute-start(bf16[512,256]{1,0:T(8,128)(2,1)} %get-tuple-element.38), channel_id=1, source_target_pairs={{0,2},{2,4},{4,6},{6,0},{1,3},{3,5},{5,7},{7,1},{8,10},{10,12},{12... | collective-permute-start | bytes 786440 | tf_op jit(solution)/shard_map/ppermute | solution.py:163
  162.2 15.8 %collective-permute-start.2 = (bf16[512,256]{1,0:T(8,128)(2,1)}, bf16[512,256]{1,0:T(8,128)(2,1)}, u32[]{:S(2)}, u32[]{:S(2)}) collective-permute-start(bf16[512,256]{1,0:T(8,128)(2,1)} %get-tuple-element.39), channel_id=1, source_target_pairs={{0,4},{2,6},{4,0},{6,2},{1,5},{3,7},{5,1},{7,3},{8,12},{10,14},{12... | collective-permute-start | bytes 786440 | tf_op jit(solution)/shard_map/ppermute | solution.py:163
  164.0 15.0 %collective-permute-start.3 = (bf16[512,256]{1,0:T(8,128)(2,1)S(1)}, bf16[512,256]{1,0:T(8,128)(2,1)S(1)}, u32[]{:S(2)}, u32[]{:S(2)}) collective-permute-start(bf16[512,256]{1,0:T(8,128)(2,1)S(1)} %get-tuple-element.36), channel_id=1, source_target_pairs={{0,6},{2,0},{4,2},{6,4},{1,7},{3,1},{5,3},{7,5},{8,14},{10,8},{12,... | collective-permute-start | bytes 786440 | tf_op jit(solution)/shard_map/ppermute | solution.py:163
Sparse Core Ops, SparseCore 0:
  12.3 114.6 all-gather.1

commit v16 on v14

--- a/solution.py
+++ b/solution.py
@@ -156,16 +156,20 @@
     first = jnp.where(core == 0, own, other)
     second = jnp.where(core == 0, other, own)
     mapped = jnp.concatenate([first, second], axis=1)
-    by_heads = jnp.zeros_like(mapped)
-    by_heads = lax.dynamic_update_index_in_dim(by_heads, mapped[0], here, 0)
+    chip_rows = cores * row_count
+
+    def as_rows(block):
+        return block.reshape(1, chip_rows, 2, 1, HD)
+
+    by_heads = jnp.zeros((1, chips * chip_rows, 2, 1, HD), mapped.dtype)
+    by_heads = lax.dynamic_update_slice_in_dim(by_heads, as_rows(mapped[0]), here * chip_rows, 1)
     for step in range(1, chips):
         arrived = lax.ppermute(
             mapped[step], "cx", perm=[(i, (i + step) % chips) for i in range(chips)]
         )
-        by_heads = lax.dynamic_update_index_in_dim(
-            by_heads, arrived, (here + chips - step) % chips, 0
+        by_heads = lax.dynamic_update_slice_in_dim(
+            by_heads, as_rows(arrived), ((here + chips - step) % chips) * chip_rows, 1
         )
-    by_heads = by_heads.reshape(1, chips * cores * row_count, 2, 1, HD)
     return (moved_rows[None], by_heads)
 
 

time: 178 us -> 184 us (1.034)
  local copies, waits for them, and re-layouts: 14.1 us -> 23.3 us
  waiting for transfers between devices: 93.9 us -> 90.1 us
    slice x0 -> x3, local copies, waits for them, and re-layouts: none -> 4.42 us  [on_device(): mapped[step]]
    ppermute x3, waiting for transfers between devices: 12.4 us -> 8.56 us  [on_device(): lax.ppermute(mapped[step], 'cx', perm=[(i, (i + step) % chips) for i in r...]
    reshape x1 -> x3, local copies, waits for them, and re-layouts: 1.11 us -> 3.05 us  [as_rows(): return block.reshape(1, chip_rows, 2, 1, HD)]
    unnamed x14 -> x16, local copies, waits for them, and re-layouts: 3.62 us -> 4.59 us
  transfers between devices with their start and end apart: 6 -> 6, of which waited for: 2 -> 3; matrix products, arithmetic and copies ran while one was open for 24% -> 26% of each run, Pallas kernels for 0% -> 0%
where the time goes in v16:
time: 184 us; the launch traced here: 183 us
  waiting for transfers between devices  90.1 us (49%)
  matrix products  36.2 us (20%)
  local copies, waits for them, and re-layouts  23.3 us (13%)
  between operations  14.2 us (8%)
  starting transfers between devices  9.99 us (5%)
  other arithmetic  9.6 us (5%)
    all_to_all x1, waiting for transfers between devices, on_device(): lax.all_to_all(outgoing.reshape(peer_count, capacity, -1), CTX, split_axi...  81.5 us
    dot_general x2, matrix products, project(): jnp.dot(rows, gathered_weight, preferred_element_type=jnp.float32)  19.1 us
    dot_general x2, matrix products, select_rows(): jnp.dot(picks.astype(rows.dtype), rows, preferred_element_type=jnp.float32)  13.7 us
    ppermute x3, waiting for transfers between devices, on_device(): lax.ppermute(mapped[step], 'cx', perm=[(i, (i + step) % chips) for i in r...  8.56 us
    all_to_all x1, starting transfers between devices, on_device(): lax.all_to_all(outgoing.reshape(peer_count, capacity, -1), CTX, split_axi...  6.39 us
    gather x1, local copies, waits for them, and re-layouts, on_device(): local_bias = jnp.take(kv_bias, columns, mode='clip')  6.15 us
    add x1, other arithmetic, on_device(): index = source * capacity + shift + within  4.97 us
    unnamed x16, local copies, waits for them, and re-layouts  4.59 us
  transfers between devices with their start and end apart: 6, of which 3 were waited for; matrix products, arithmetic and copies ran while one was open for 26% of the time, Pallas kernels for 0%

profile of v16, /device:TPU:1, one launch (start us, length us, event | category | flops | bytes accessed | tf_op | source)
XLA Modules:
  0.0 183.4 jit_solution(398228761268675639)
XLA Ops:
  7.2 0.0 copy-start
  7.2 0.0 copy-start.4
  7.2 0.0 copy-start.6
  7.2 0.0 all-gather.2.cloned.1.call-start
  7.3 1.5 copy-done
  8.8 3.4 %fusion.7 = bf16[512,1024]{1,0:T(8,128)(2,1)} fusion(bf16[512,2048]{1,0:T(8,128)(2,1)S(1)} %copy-done, s32[1024]{0:T(1024)S(1)} %get-tuple-element.48), kind=kOutput, calls=%fused_computation.15 | convolution fusion | flops 2150105088 | bytes 3149824 | tf_op jit(solution)/shard_map/dot_general | solution.py:119
  12.2 0.0 all-gather.2.cloned.1.call-update
  12.2 0.0 copy-done.4
  12.2 0.2 reduce_window_sum.23
  12.4 0.0 copy-done.6
  12.4 0.1 select_reduce_fusion.1
  12.5 0.1 iota_add_fusion
  12.6 0.1 add.151
  12.7 7.8 %convolution_convert_fusion = bf16[512,8192]{1,0:T(8,128)(2,1)} fusion(bf16[1,256,8192]{2,1,0:T(8,128)(2,1)} %param.12, s32[512]{0:T(512)S(1)} %add.151), kind=kOutput, calls=%fused_computation.1 | convolution fusion | flops 2151809024 | bytes 12584960 | tf_op jit(solution)/shard_map/dot_general | solution.py:92
  20.5 0.0 copy-start.1
  20.5 6.4 %all-to-all-start = ((bf16[8,64,8192]{2,1,0:T(8,128)(2,1)}), bf16[8,64,8192]{2,1,0:T(8,128)(2,1)}, u32[]{:S(2)}, u32[]{:S(2)}) async-start(bf16[8,64,8192]{2,1,0:T(8,128)(2,1)} %bitcast.43), calls=%async_computation | async-start | bytes 16777216 | tf_op jit(solution)/shard_map/all_to_all | solution.py:136
  26.9 0.0 copy-done.1
  26.9 6.2 %gather_fusion = f32[1024]{0:T(1024)S(1)} fusion(f32[2048]{0:T(1024)S(1)} %copy-done.1, s32[1024]{0:T(1024)S(1)} %get-tuple-element.49), kind=kCustom, calls=%fused_computation | custom fusion | bytes 12288 | tf_op jit(solution)/shard_map/jit(_take)/gather | solution.py:122
  33.1 0.2 dynamic-slice_reduce_fusion
  33.3 0.2 dynamic-slice_reduce_fusion.2
  33.5 0.6 fusion.44
  34.1 0.1 convert_reduce_fusion
  34.2 0.1 select_reduce_fusion.3
  34.2 5.0 %subtract_add_fusion = s32[256]{0:T(256)S(1)} fusion(s32[256]{0:T(256)S(1)} %get-tuple-element.31, s32[256]{0:T(256)S(1)} %get-tuple-element.30, s32[256]{0:T(256)S(1)} %convert_reduce_fusion, s32[]{:T(128)} %bitcast.2, s32[]{:T(128)} %bitcast.3, s32[]{:T(128)} %bitcast.4, s32[]{:T(128)} %bitcast.5, s32[]{:T(128)} %bitcast.6, s32[]{:T(128)} %bitcast.7, ...), kind=kLoop, calls=%fused_computation.108 | loop fusion | flops 4864 | bytes 4128 | tf_op jit(solution)/shard_map/add | solution.py:143
  39.2 81.5 %all-to-all-done = bf16[8,64,8192]{2,1,0:T(8,128)(2,1)} async-done(((bf16[8,64,8192]{2,1,0:T(8,128)(2,1)}), bf16[8,64,8192]{2,1,0:T(8,128)(2,1)}, u32[]{:S(2)}, u32[]{:S(2)}) %all-to-all-start) | async-done | bytes 8388640 | tf_op jit(solution)/shard_map/all_to_all | solution.py:136
  120.7 0.0 copy-start.5
  120.7 5.9 %fusion = (f32[256]{0:T(256)S(1)}, bf16[256,8192]{1,0:T(8,128)(2,1)S(1)}) fusion(bf16[512,8192]{1,0:T(8,128)(2,1)} %bitcast.14, s32[256]{0:T(256)S(1)} %subtract_add_fusion), kind=kOutput, calls=%fused_computation.5 | convolution fusion | flops 2156003072 | bytes 12584960 | tf_op jit(solution)/shard_map/dot_general | solution.py:92
  126.6 0.0 copy-start.2
  126.6 2.0 %copy-done.2 = bf16[256,8192]{1,0:T(8,128)(2,1)} copy-done((bf16[256,8192]{1,0:T(8,128)(2,1)}, bf16[256,8192]{1,0:T(8,128)(2,1)S(1)}, u32[]{:S(2)}) %copy-start.2) | copy-done | bytes 4194328
  128.6 0.0 copy-done.5
  128.6 3.1 %fusion.2 = bf16[256,8192]{1,0:T(8,128)(2,1)} fusion(bf16[256,8192]{1,0:T(8,128)(2,1)S(1)} %get-tuple-element.47, f32[8192]{0:T(1024)S(1)} %copy-done.5, f32[256]{0:T(256)S(1)} %add_rsqrt_fusion), kind=kLoop, calls=%fused_computation.7 | loop fusion | flops 8388608 | bytes 8422400 | tf_op jit(solution)/shard_map/convert_element_type | solution.py:37
  131.8 0.9 collective-permute-start
  132.7 0.0 all-gather.2.cloned.1.call-done
  132.7 0.0 copy-start.7
  132.7 11.7 %fusion.8 = bf16[256,1024]{1,0:T(8,128)(2,1)S(1)} fusion(bf16[256,8192]{1,0:T(8,128)(2,1)} %fusion.2, bf16[8192,1024]{1,0:T(8,128)(2,1)} %all-gather.2.cloned.1.call-done, f32[1024]{0:T(1024)S(1)} %gather_fusion), kind=kOutput, calls=%fused_computation.22 | convolution fusion | flops 4295491584 | bytes 21499904 | tf_op jit(solution)/shard_map/dot_general | solution.py:150
  144.3 0.0 collective-permute-done
  144.4 0.1 copy-done.7
  144.5 7.5 %broadcast_select_fusion = (bf16[256,1024]{1,0:T(8,128)(2,1)}, bf16[256,1024]{1,0:T(8,128)(2,1)S(1)}) fusion(bf16[256,1024]{1,0:T(8,128)(2,1)S(1)} %fusion.8, pred[]{:T(512)S(6)} %eq.97, f32[1024]{0:T(1024)S(1)} %gather_fusion, bf16[256,8192]{1,0:T(8,128)(2,1)} %collective-permute-done, bf16[8192,1024]{1,0:T(8,128)(2,1)S(1)} %copy-done.7), kind=kOutput, calls=%fused_computation.26 | convolution fusion | flops 4296015872 | bytes 22548480 | tf_op jit(solution)/shard_map/dot_general | solution.py:150
  152.0 0.2 copy.40
  152.2 1.2 copy.41
  153.4 0.9 pad_maximum_fusion
  154.3 1.8 copy.33
  156.1 0.3 collective-permute-start.1
  156.4 1.1 copy.32
  157.5 1.8 copy.35
  159.3 1.8 collective-permute-start.2
  161.1 0.8 copy.37
  161.9 0.6 collective-permute-start.3
  162.5 0.6 broadcast_in_dim.48
  163.1 0.2 constant_dynamic-update-slice_fusion
  163.3 7.8 %collective-permute-done.1 = bf16[512,256]{1,0:T(8,128)(2,1)} collective-permute-done((bf16[512,256]{1,0:T(8,128)(2,1)}, bf16[512,256]{1,0:T(8,128)(2,1)}, u32[]{:S(2)}, u32[]{:S(2)}) %collective-permute-start.1) | collective-permute-done | bytes 262176 | tf_op jit(solution)/shard_map/ppermute | solution.py:167
  171.2 1.0 reshape.72
  172.2 0.2 bitcast_dynamic-update-slice_fusion.2
  172.4 0.0 collective-permute-done.2
  172.4 1.0 reshape.73
  173.4 0.2 bitcast_dynamic-update-slice_fusion.1
  173.6 0.7 collective-permute-done.3
  174.4 1.0 reshape.74
  175.4 0.2 bitcast_dynamic-update-slice_fusion
  175.6 0.0 copy-start.3
  175.6 1.0 copy-done.3
  (7 shorter events, 0.1 us)
Async XLA Ops:
  7.2 1.6 copy-start
  7.2 5.0 %copy-start.4 = (s32[1,8,8]{2,1,0:T(8,128)S(1)}, s32[1,8,8]{2,1,0:T(8,128)}, u32[]{:S(2)}) copy-start(s32[1,8,8]{2,1,0:T(8,128)} %param.13) | copy-start | bytes 772
  7.2 5.2 %copy-start.6 = (s32[1,8,8]{2,1,0:T(8,128)S(1)}, s32[1,8,8]{2,1,0:T(8,128)}, u32[]{:S(2)}) copy-start(s32[1,8,8]{2,1,0:T(8,128)} %param.14) | copy-start | bytes 772
  7.2 125.5 %all-gather.2.cloned.1.call-start = ((), (), s32[]{:S(2)}) async-start(), calls=%async_computation.1 | async-start | bytes 17825792 | tf_op jit(solution)/shard_map/all_gather | solution.py:125
  20.5 6.4 %copy-start.1 = (f32[2048]{0:T(1024)S(1)}, f32[2048]{0:T(1024)}, u32[]{:S(2)}) copy-start(f32[2048]{0:T(1024)} %param.17) | copy-start | bytes 24580
  20.5 100.3 %all-to-all-start = ((bf16[8,64,8192]{2,1,0:T(8,128)(2,1)}), bf16[8,64,8192]{2,1,0:T(8,128)(2,1)}, u32[]{:S(2)}, u32[]{:S(2)}) async-start(bf16[8,64,8192]{2,1,0:T(8,128)(2,1)} %bitcast.43), calls=%async_computation | async-start | bytes 16777216 | tf_op jit(solution)/shard_map/all_to_all | solution.py:136
  120.7 7.9 %copy-start.5 = (f32[8192]{0:T(1024)S(1)}, f32[8192]{0:T(1024)}, u32[]{:S(2)}) copy-start(f32[8192]{0:T(1024)} %param.15) | copy-start | bytes 98308
  126.6 2.0 %copy-start.2 = (bf16[256,8192]{1,0:T(8,128)(2,1)}, bf16[256,8192]{1,0:T(8,128)(2,1)S(1)}, u32[]{:S(2)}) copy-start(bf16[256,8192]{1,0:T(8,128)(2,1)S(1)} %get-tuple-element.47) | copy-start | bytes 12582916
  131.8 12.5 %collective-permute-start = (bf16[256,8192]{1,0:T(8,128)(2,1)}, bf16[256,8192]{1,0:T(8,128)(2,1)}, u32[]{:S(2)}, u32[]{:S(2)}) collective-permute-start(bf16[256,8192]{1,0:T(8,128)(2,1)} %fusion.2), channel_id=1, source_target_pairs={{0,1},{1,0},{2,3},{3,2},{4,5},{5,4},{6,7},{7,6},{8,9},{9,8},{10,11... | collective-permute-start | bytes 12582920 | tf_op jit(solution)/shard_map/ppermute | solution.py:147
  132.7 11.8 %copy-start.7 = (bf16[8192,1024]{1,0:T(8,128)(2,1)S(1)}, bf16[8192,1024]{1,0:T(8,128)(2,1)}, u32[]{:S(2)}) copy-start(bf16[8192,1024]{1,0:T(8,128)(2,1)} %all-gather.2.cloned.1.call-done) | copy-start | bytes 50331652
  156.1 15.1 %collective-permute-start.1 = (bf16[512,256]{1,0:T(8,128)(2,1)}, bf16[512,256]{1,0:T(8,128)(2,1)}, u32[]{:S(2)}, u32[]{:S(2)}) collective-permute-start(bf16[512,256]{1,0:T(8,128)(2,1)} %bitcast.21), channel_id=1, source_target_pairs={{0,2},{2,4},{4,6},{6,0},{1,3},{3,5},{5,7},{7,1},{8,10},{10,12},{12... | collective-permute-start | bytes 786440 | tf_op jit(solution)/shard_map/ppermute | solution.py:167
  159.3 13.1 %collective-permute-start.2 = (bf16[512,256]{1,0:T(8,128)(2,1)}, bf16[512,256]{1,0:T(8,128)(2,1)}, u32[]{:S(2)}, u32[]{:S(2)}) collective-permute-start(bf16[512,256]{1,0:T(8,128)(2,1)} %bitcast.23), channel_id=1, source_target_pairs={{0,4},{2,6},{4,0},{6,2},{1,5},{3,7},{5,1},{7,3},{8,12},{10,14},{12... | collective-permute-start | bytes 786440 | tf_op jit(solution)/shard_map/ppermute | solution.py:167
  161.9 12.5 %collective-permute-start.3 = (bf16[512,256]{1,0:T(8,128)(2,1)}, bf16[512,256]{1,0:T(8,128)(2,1)}, u32[]{:S(2)}, u32[]{:S(2)}) collective-permute-start(bf16[512,256]{1,0:T(8,128)(2,1)} %bitcast.25), channel_id=1, source_target_pairs={{0,6},{2,0},{4,2},{6,4},{1,7},{3,1},{5,3},{7,5},{8,14},{10,8},{12,... | collective-permute-start | bytes 786440 | tf_op jit(solution)/shard_map/ppermute | solution.py:167
  175.6 1.0 copy-start.3
Sparse Core Ops, SparseCore 0:
  12.3 114.6 all-gather.1

commit v17 on v14

--- a/solution.py
+++ b/solution.py
@@ -45,6 +45,52 @@
     peer_count, capacity = out_ref.shape[0], out_ref.shape[1]
     for k in range(peer_count):
         out_ref[k] = rows_ref[pl.ds(starts_ref[k], capacity)]
+
+
+def _exchange_kernel(blocks_ref, out_ref, landed, send_sems, recv_sems):
+    chips = blocks_ref.shape[0]
+    here = lax.axis_index("cx")
+    barrier = pltpu.get_barrier_semaphore()
+    for step in range(1, chips):
+        pl.semaphore_signal(
+            barrier, inc=1, device_id={"cx": (here + step) % chips},
+            device_id_type=pl.DeviceIdType.MESH,
+        )
+    pl.semaphore_wait(barrier, chips - 1)
+    copies = []
+    for step in range(1, chips):
+        copy = pltpu.make_async_remote_copy(
+            src_ref=blocks_ref.at[step],
+            dst_ref=landed.at[step - 1],
+            send_sem=send_sems.at[step - 1],
+            recv_sem=recv_sems.at[step - 1],
+            device_id={"cx": (here + step) % chips},
+            device_id_type=pl.DeviceIdType.MESH,
+        )
+        copy.start()
+        copies.append(copy)
+    out_ref[here] = blocks_ref[0]
+    for step in range(1, chips):
+        copies[step - 1].wait_send()
+        copies[step - 1].wait_recv()
+        out_ref[(here + chips - step) % chips] = landed[step - 1]
+
+
+def exchange_blocks(blocks):
+    chips = blocks.shape[0]
+    whole = pl.BlockSpec(memory_space=pltpu.VMEM)
+    return pl.pallas_call(
+        _exchange_kernel,
+        out_shape=jax.ShapeDtypeStruct(blocks.shape, blocks.dtype),
+        in_specs=[whole],
+        out_specs=whole,
+        scratch_shapes=[
+            pltpu.VMEM((chips - 1,) + blocks.shape[1:], blocks.dtype),
+            pltpu.SemaphoreType.DMA((chips - 1,)),
+            pltpu.SemaphoreType.DMA((chips - 1,)),
+        ],
+        compiler_params=pltpu.CompilerParams(collective_id=0, has_side_effects=True),
+    )(blocks)
 
 
 def _whole(shape):
@@ -156,16 +202,7 @@
     first = jnp.where(core == 0, own, other)
     second = jnp.where(core == 0, other, own)
     mapped = jnp.concatenate([first, second], axis=1)
-    by_heads = jnp.zeros_like(mapped)
-    by_heads = lax.dynamic_update_index_in_dim(by_heads, mapped[0], here, 0)
-    for step in range(1, chips):
-        arrived = lax.ppermute(
-            mapped[step], "cx", perm=[(i, (i + step) % chips) for i in range(chips)]
-        )
-        by_heads = lax.dynamic_update_index_in_dim(
-            by_heads, arrived, (here + chips - step) % chips, 0
-        )
-    by_heads = by_heads.reshape(1, chips * cores * row_count, 2, 1, HD)
+    by_heads = exchange_blocks(mapped).reshape(1, chips * cores * row_count, 2, 1, HD)
     return (moved_rows[None], by_heads)
 
 

time: 178 us -> 182 us (1.022)
  Pallas kernels: 0 us -> 17.4 us
  waiting for transfers between devices: 93.9 us -> 81.5 us
  starting transfers between devices: 9.99 us -> 7.3 us
    pallas_call x0 -> x1, Pallas kernels: none -> 17.4 us  [exchange_blocks(): pl.pallas_call(_exchange_kernel, out_shape=jax.ShapeDtypeStruct(blocks.sh...]
    ppermute x3 -> x0, waiting for transfers between devices: 12.4 us -> none  [on_device(): lax.ppermute(mapped[step], 'cx', perm=[(i, (i + step) % chips) for i in r...]
    ppermute x3 -> x0, starting transfers between devices: 2.69 us -> none  [on_device(): lax.ppermute(mapped[step], 'cx', perm=[(i, (i + step) % chips) for i in r...]
    select_n x1 -> x2, local copies, waits for them, and re-layouts: 0.04 us -> 2.24 us  [on_device(): first = jnp.where(core == 0, own, other)]
    concatenate x0 -> x1, other arithmetic: none -> 2.08 us  [on_device(): mapped = jnp.concatenate([first, second], axis=1)]
    unnamed x14, local copies, waits for them, and re-layouts: 3.62 us -> 1.65 us
    dynamic_update_slice x3 -> x0, local copies, waits for them, and re-layouts: 1.97 us -> none  [on_device(): lax.dynamic_update_index_in_dim(by_heads, arrived, (here + chips - step)...]
  transfers between devices with their start and end apart: 6 -> 3, of which waited for: 2 -> 1; matrix products, arithmetic and copies ran while one was open for 24% -> 23% of each run, Pallas kernels for 0% -> 0%
where the time goes in v17:
time: 182 us; the launch traced here: 181 us
  waiting for transfers between devices  81.5 us (45%)
  matrix products  36.2 us (20%)
  Pallas kernels  17.4 us (10%)
  between operations  14.2 us (8%)
  local copies, waits for them, and re-layouts  13.7 us (8%)
  other arithmetic  11 us (6%)
  starting transfers between devices  7.3 us (4%)
    all_to_all x1, waiting for transfers between devices, on_device(): lax.all_to_all(outgoing.reshape(peer_count, capacity, -1), CTX, split_axi...  81.5 us
    dot_general x2, matrix products, project(): jnp.dot(rows, gathered_weight, preferred_element_type=jnp.float32)  19.1 us
    pallas_call x1, Pallas kernels, exchange_blocks(): pl.pallas_call(_exchange_kernel, out_shape=jax.ShapeDtypeStruct(blocks.sh...  17.4 us
    dot_general x2, matrix products, select_rows(): jnp.dot(picks.astype(rows.dtype), rows, preferred_element_type=jnp.float32)  13.7 us
    all_to_all x1, starting transfers between devices, on_device(): lax.all_to_all(outgoing.reshape(peer_count, capacity, -1), CTX, split_axi...  6.39 us
    gather x1, local copies, waits for them, and re-layouts, on_device(): local_bias = jnp.take(kv_bias, columns, mode='clip')  6.15 us
    add x1, other arithmetic, on_device(): index = source * capacity + shift + within  4.97 us
  transfers between devices with their start and end apart: 3, of which 1 were waited for; matrix products, arithmetic and copies ran while one was open for 23% of the time, Pallas kernels for 0%

profile of v17, /device:TPU:1, one launch (start us, length us, event | category | flops | bytes accessed | tf_op | source)
XLA Modules:
  0.0 181.2 jit_solution(14813954003607247817)
XLA Ops:
  7.2 0.0 copy-start
  7.2 0.0 all-gather.2.cloned.1.call-start
  7.3 1.5 copy-done
  8.8 0.0 copy-start.3
  8.8 0.0 copy-start.5
  8.8 3.4 %fusion.7 = bf16[512,1024]{1,0:T(8,128)(2,1)} fusion(bf16[512,2048]{1,0:T(8,128)(2,1)S(1)} %copy-done, s32[1024]{0:T(1024)S(1)} %get-tuple-element.52), kind=kOutput, calls=%fused_computation.15 | convolution fusion | flops 2150105088 | bytes 3149824 | tf_op jit(solution)/shard_map/dot_general | solution.py:165
  12.2 0.0 all-gather.2.cloned.1.call-update
  12.2 0.0 copy-done.3
  12.2 0.2 reduce_window_sum.23
  12.4 0.0 copy-done.5
  12.4 0.1 select_reduce_fusion.1
  12.5 0.1 iota_add_fusion
  12.6 0.1 add.117
  12.7 7.8 %convolution_convert_fusion = bf16[512,8192]{1,0:T(8,128)(2,1)} fusion(bf16[1,256,8192]{2,1,0:T(8,128)(2,1)} %param.12, s32[512]{0:T(512)S(1)} %add.117), kind=kOutput, calls=%fused_computation.1 | convolution fusion | flops 2151809024 | bytes 12584960 | tf_op jit(solution)/shard_map/dot_general | solution.py:138
  20.5 0.0 copy-start.1
  20.5 6.4 %all-to-all-start = ((bf16[8,64,8192]{2,1,0:T(8,128)(2,1)}), bf16[8,64,8192]{2,1,0:T(8,128)(2,1)}, u32[]{:S(2)}, u32[]{:S(2)}) async-start(bf16[8,64,8192]{2,1,0:T(8,128)(2,1)} %bitcast.32), calls=%async_computation | async-start | bytes 16777216 | tf_op jit(solution)/shard_map/all_to_all | solution.py:182
  26.9 0.0 copy-done.1
  26.9 6.2 %gather_fusion = f32[1024]{0:T(1024)S(1)} fusion(f32[2048]{0:T(1024)S(1)} %copy-done.1, s32[1024]{0:T(1024)S(1)} %get-tuple-element.53), kind=kCustom, calls=%fused_computation | custom fusion | bytes 12288 | tf_op jit(solution)/shard_map/jit(_take)/gather | solution.py:168
  33.1 0.2 dynamic-slice_reduce_fusion
  33.3 0.2 dynamic-slice_reduce_fusion.2
  33.5 0.6 fusion.41
  34.1 0.1 convert_reduce_fusion
  34.2 0.1 select_reduce_fusion.3
  34.2 5.0 %subtract_add_fusion = s32[256]{0:T(256)S(1)} fusion(s32[256]{0:T(256)S(1)} %get-tuple-element.39, s32[256]{0:T(256)S(1)} %get-tuple-element.38, s32[256]{0:T(256)S(1)} %convert_reduce_fusion, s32[]{:T(128)} %bitcast.2, s32[]{:T(128)} %bitcast.3, s32[]{:T(128)} %bitcast.4, s32[]{:T(128)} %bitcast.5, s32[]{:T(128)} %bitcast.6, s32[]{:T(128)} %bitcast.7, ...), kind=kLoop, calls=%fused_computation.95 | loop fusion | flops 4864 | bytes 4128 | tf_op jit(solution)/shard_map/add | solution.py:189
  39.2 81.5 %all-to-all-done = bf16[8,64,8192]{2,1,0:T(8,128)(2,1)} async-done(((bf16[8,64,8192]{2,1,0:T(8,128)(2,1)}), bf16[8,64,8192]{2,1,0:T(8,128)(2,1)}, u32[]{:S(2)}, u32[]{:S(2)}) %all-to-all-start) | async-done | bytes 8388640 | tf_op jit(solution)/shard_map/all_to_all | solution.py:182
  120.7 0.0 copy-start.4
  120.7 5.9 %fusion = (f32[256]{0:T(256)S(1)}, bf16[256,8192]{1,0:T(8,128)(2,1)S(1)}) fusion(bf16[512,8192]{1,0:T(8,128)(2,1)} %bitcast.14, s32[256]{0:T(256)S(1)} %subtract_add_fusion), kind=kOutput, calls=%fused_computation.5 | convolution fusion | flops 2156003072 | bytes 12584960 | tf_op jit(solution)/shard_map/dot_general | solution.py:138
  126.6 0.0 copy-start.2
  126.7 0.0 copy-done.4
  126.7 3.3 %fusion.2 = bf16[256,8192]{1,0:T(8,128)(2,1)} fusion(bf16[256,8192]{1,0:T(8,128)(2,1)S(1)} %get-tuple-element.51, f32[8192]{0:T(1024)S(1)} %copy-done.4, f32[256]{0:T(256)S(1)} %add_rsqrt_fusion), kind=kLoop, calls=%fused_computation.7 | loop fusion | flops 8388608 | bytes 8422400 | tf_op jit(solution)/shard_map/convert_element_type | solution.py:37
  130.0 0.0 copy-done.2
  130.0 0.9 collective-permute-start
  130.9 0.0 all-gather.2.cloned.1.call-done
  130.9 0.0 copy-start.6
  130.9 11.7 %fusion.8 = bf16[256,1024]{1,0:T(8,128)(2,1)S(1)} fusion(bf16[256,8192]{1,0:T(8,128)(2,1)} %fusion.2, bf16[8192,1024]{1,0:T(8,128)(2,1)} %all-gather.2.cloned.1.call-done, f32[1024]{0:T(1024)S(1)} %gather_fusion), kind=kOutput, calls=%fused_computation.16 | convolution fusion | flops 4295491584 | bytes 21499904 | tf_op jit(solution)/shard_map/dot_general | solution.py:196
  142.5 0.0 collective-permute-done
  142.5 0.1 copy-done.6
  142.7 7.5 %broadcast_select_fusion.1 = (bf16[256,1024]{1,0:T(8,128)(2,1)}, bf16[256,1024]{1,0:T(8,128)(2,1)S(1)}) fusion(bf16[256,1024]{1,0:T(8,128)(2,1)S(1)} %fusion.8, pred[]{:T(512)S(6)} %eq.93, f32[1024]{0:T(1024)S(1)} %gather_fusion, bf16[256,8192]{1,0:T(8,128)(2,1)} %collective-permute-done, bf16[8192,1024]{1,0:T(8,128)(2,1)S(1)} %copy-done.6), kind=kOutput, calls=%fused_computation.22 | convolution fusion | flops 4296015872 | bytes 22548480 | tf_op jit(solution)/shard_map/dot_general | solution.py:196
  150.1 0.2 copy.25
  150.3 0.2 copy.26
  150.6 1.2 copy.23
  151.8 1.0 copy.24
  152.8 2.1 %pad_maximum_fusion.blocks_ref = bf16[4,512,256]{2,1,0:T(8,128)(2,1)} fusion(bf16[4,256,256]{2,1,0:T(8,128)(2,1)S(1)} %bitcast.36, bf16[4,256,256]{2,1,0:T(8,128)(2,1)} %bitcast.37), kind=kLoop, calls=%fused_computation.18 | loop fusion | flops 2097152 | bytes 2097152 | tf_op jit(solution)/shard_map/concatenate | solution.py:204
  154.9 17.4 %shard_map.77 = bf16[4,512,256]{2,1,0:T(8,128)(2,1)} custom-call(bf16[4,512,256]{2,1,0:T(8,128)(2,1)} %pad_maximum_fusion.blocks_ref), custom_call_target="tpu_custom_call" | custom-call | tf_op jit(solution)/shard_map/pallas_call | solution.py:82
  172.2 2.1 %reshape.66 = bf16[1,2048,2,1,128]{4,2,1,3,0:T(2,128)(2,1)} reshape(bf16[4,512,256]{2,1,0:T(8,128)(2,1)} %shard_map.77) | data formatting | bytes 2097152 | tf_op jit(solution)/shard_map/reshape | solution.py:205
  (7 shorter events, 0.1 us)
Async XLA Ops:
  7.2 1.6 copy-start
  7.2 123.7 %all-gather.2.cloned.1.call-start = ((), (), s32[]{:S(2)}) async-start(), calls=%async_computation.1 | async-start | bytes 17825792 | tf_op jit(solution)/shard_map/all_gather | solution.py:171
  8.8 3.5 %copy-start.3 = (s32[1,8,8]{2,1,0:T(8,128)S(1)}, s32[1,8,8]{2,1,0:T(8,128)}, u32[]{:S(2)}) copy-start(s32[1,8,8]{2,1,0:T(8,128)} %param.13) | copy-start | bytes 772
  8.8 3.6 %copy-start.5 = (s32[1,8,8]{2,1,0:T(8,128)S(1)}, s32[1,8,8]{2,1,0:T(8,128)}, u32[]{:S(2)}) copy-start(s32[1,8,8]{2,1,0:T(8,128)} %param.14) | copy-start | bytes 772
  20.5 6.4 %copy-start.1 = (f32[2048]{0:T(1024)S(1)}, f32[2048]{0:T(1024)}, u32[]{:S(2)}) copy-start(f32[2048]{0:T(1024)} %param.17) | copy-start | bytes 24580
  20.5 100.3 %all-to-all-start = ((bf16[8,64,8192]{2,1,0:T(8,128)(2,1)}), bf16[8,64,8192]{2,1,0:T(8,128)(2,1)}, u32[]{:S(2)}, u32[]{:S(2)}) async-start(bf16[8,64,8192]{2,1,0:T(8,128)(2,1)} %bitcast.32), calls=%async_computation | async-start | bytes 16777216 | tf_op jit(solution)/shard_map/all_to_all | solution.py:182
  120.7 5.9 %copy-start.4 = (f32[8192]{0:T(1024)S(1)}, f32[8192]{0:T(1024)}, u32[]{:S(2)}) copy-start(f32[8192]{0:T(1024)} %param.15) | copy-start | bytes 98308
  126.6 3.4 %copy-start.2 = (bf16[256,8192]{1,0:T(8,128)(2,1)}, bf16[256,8192]{1,0:T(8,128)(2,1)S(1)}, u32[]{:S(2)}) copy-start(bf16[256,8192]{1,0:T(8,128)(2,1)S(1)} %get-tuple-element.51) | copy-start | bytes 12582916
  130.0 12.6 %collective-permute-start = (bf16[256,8192]{1,0:T(8,128)(2,1)}, bf16[256,8192]{1,0:T(8,128)(2,1)}, u32[]{:S(2)}, u32[]{:S(2)}) collective-permute-start(bf16[256,8192]{1,0:T(8,128)(2,1)} %fusion.2), channel_id=1, source_target_pairs={{0,1},{1,0},{2,3},{3,2},{4,5},{5,4},{6,7},{7,6},{8,9},{9,8},{10,11... | collective-permute-start | bytes 12582920 | tf_op jit(solution)/shard_map/ppermute | solution.py:193
  130.9 11.8 %copy-start.6 = (bf16[8192,1024]{1,0:T(8,128)(2,1)S(1)}, bf16[8192,1024]{1,0:T(8,128)(2,1)}, u32[]{:S(2)}) copy-start(bf16[8192,1024]{1,0:T(8,128)(2,1)} %all-gather.2.cloned.1.call-done) | copy-start | bytes 50331652
Sparse Core Ops, SparseCore 0:
  12.3 114.6 all-gather.1

commit v18 on v14

--- a/solution.py
+++ b/solution.py
@@ -151,20 +151,22 @@
         products = (products + local_bias[None, :]).astype(jnp.bfloat16)
         return jnp.swapaxes(products.reshape(row_count, heads_per_core, 2 * HD), 0, 1)
 
-    own = project(normed)
-    other = project(sibling_rows)
-    first = jnp.where(core == 0, own, other)
-    second = jnp.where(core == 0, other, own)
-    mapped = jnp.concatenate([first, second], axis=1)
-    by_heads = jnp.zeros_like(mapped)
-    by_heads = lax.dynamic_update_index_in_dim(by_heads, mapped[0], here, 0)
-    for step in range(1, chips):
-        arrived = lax.ppermute(
-            mapped[step], "cx", perm=[(i, (i + step) % chips) for i in range(chips)]
-        )
-        by_heads = lax.dynamic_update_index_in_dim(
-            by_heads, arrived, (here + chips - step) % chips, 0
-        )
+    by_heads = jnp.zeros((chips, cores, row_count, 2 * HD), kv_weight.dtype)
+
+    def send_half(blocks, half, by_heads):
+        by_heads = lax.dynamic_update_slice(by_heads, blocks[0][None, None], (here, half, 0, 0))
+        for step in range(1, chips):
+            arrived = lax.ppermute(
+                blocks[step], "cx", perm=[(i, (i + step) % chips) for i in range(chips)]
+            )
+            source = (here + chips - step) % chips
+            by_heads = lax.dynamic_update_slice(by_heads, arrived[None, None], (source, half, 0, 0))
+        return by_heads
+
+    own_blocks = project(normed)
+    own_blocks, sibling_rows = lax.optimization_barrier((own_blocks, sibling_rows))
+    by_heads = send_half(own_blocks, core, by_heads)
+    by_heads = send_half(project(sibling_rows), 1 - core, by_heads)
     by_heads = by_heads.reshape(1, chips * cores * row_count, 2, 1, HD)
     return (moved_rows[None], by_heads)
 

time: 178 us -> 172 us (0.966)
  waiting for transfers between devices: 93.9 us -> 85.7 us
  starting transfers between devices: 9.99 us -> 14.6 us
  local copies, waits for them, and re-layouts: 14.1 us -> 12.2 us
    ppermute x3 -> x6, waiting for transfers between devices: 12.4 us -> 4.13 us  [send_half(): lax.ppermute(blocks[step], 'cx', perm=[(i, (i + step) % chips) for i in r...]
    ppermute x3 -> x6, starting transfers between devices: 2.69 us -> 7.32 us  [send_half(): lax.ppermute(blocks[step], 'cx', perm=[(i, (i + step) % chips) for i in r...]
    dynamic_update_slice x3 -> x8, local copies, waits for them, and re-layouts: 1.97 us -> 0.12 us  [the longest x6 0.09 us: send_half(): lax.dynamic_update_slice(by_heads, arrived[None, None], (source, half, 0,...]
  transfers between devices with their start and end apart: 6 -> 9, of which waited for: 2 -> 4; matrix products, arithmetic and copies ran while one was open for 24% -> 28% of each run, Pallas kernels for 0% -> 0%
where the time goes in v18:
time: 172 us; the launch traced here: 171 us
  waiting for transfers between devices  85.7 us (50%)
  matrix products  35.6 us (21%)
  starting transfers between devices  14.6 us (8%)
  between operations  14.3 us (8%)
  local copies, waits for them, and re-layouts  12.2 us (7%)
  other arithmetic  8.71 us (5%)
    all_to_all x1, waiting for transfers between devices, on_device(): lax.all_to_all(outgoing.reshape(peer_count, capacity, -1), CTX, split_axi...  81.5 us
    dot_general x2, matrix products, project(): jnp.dot(rows, gathered_weight, preferred_element_type=jnp.float32)  18.5 us
    dot_general x2, matrix products, select_rows(): jnp.dot(picks.astype(rows.dtype), rows, preferred_element_type=jnp.float32)  13.7 us
    ppermute x6, starting transfers between devices, send_half(): lax.ppermute(blocks[step], 'cx', perm=[(i, (i + step) % chips) for i in r...  7.32 us
    all_to_all x1, starting transfers between devices, on_device(): lax.all_to_all(outgoing.reshape(peer_count, capacity, -1), CTX, split_axi...  6.39 us
    gather x1, local copies, waits for them, and re-layouts, on_device(): local_bias = jnp.take(kv_bias, columns, mode='clip')  6.15 us
    add x1, other arithmetic, on_device(): index = source * capacity + shift + within  4.97 us
    ppermute x6, waiting for transfers between devices, send_half(): lax.ppermute(blocks[step], 'cx', perm=[(i, (i + step) % chips) for i in r...  4.13 us
  transfers between devices with their start and end apart: 9, of which 4 were waited for; matrix products, arithmetic and copies ran while one was open for 28% of the time, Pallas kernels for 0%

profile of v18, /device:TPU:1, one launch (start us, length us, event | category | flops | bytes accessed | tf_op | source)
XLA Modules:
  0.0 171.0 jit_solution(9517534934169882467)
XLA Ops:
  7.2 0.0 copy-start
  7.2 0.0 copy-start.3
  7.2 0.0 copy-start.5
  7.2 0.0 all-gather.2.cloned.1.call-start
  7.3 1.5 copy-done
  8.8 3.4 %fusion.7 = bf16[512,1024]{1,0:T(8,128)(2,1)} fusion(bf16[512,2048]{1,0:T(8,128)(2,1)S(1)} %copy-done, s32[1024]{0:T(1024)S(1)} %get-tuple-element.52), kind=kOutput, calls=%fused_computation.15 | convolution fusion | flops 2150105088 | bytes 3149824 | tf_op jit(solution)/shard_map/dot_general | solution.py:119
  12.2 0.0 all-gather.2.cloned.1.call-update
  12.2 0.0 copy-done.3
  12.2 0.2 reduce_window_sum.23
  12.4 0.0 copy-done.5
  12.4 0.1 select_reduce_fusion.1
  12.5 0.1 iota_add_fusion
  12.6 0.1 add.174
  12.7 7.8 %convolution_convert_fusion = bf16[512,8192]{1,0:T(8,128)(2,1)} fusion(bf16[1,256,8192]{2,1,0:T(8,128)(2,1)} %param.12, s32[512]{0:T(512)S(1)} %add.174), kind=kOutput, calls=%fused_computation.1 | convolution fusion | flops 2151809024 | bytes 12584960 | tf_op jit(solution)/shard_map/dot_general | solution.py:92
  20.5 0.0 copy-start.1
  20.5 6.4 %all-to-all-start = ((bf16[8,64,8192]{2,1,0:T(8,128)(2,1)}), bf16[8,64,8192]{2,1,0:T(8,128)(2,1)}, u32[]{:S(2)}, u32[]{:S(2)}) async-start(bf16[8,64,8192]{2,1,0:T(8,128)(2,1)} %bitcast.73), calls=%async_computation | async-start | bytes 16777216 | tf_op jit(solution)/shard_map/all_to_all | solution.py:136
  26.9 0.0 copy-done.1
  26.9 6.2 %gather_fusion = f32[1024]{0:T(1024)S(1)} fusion(f32[2048]{0:T(1024)S(1)} %copy-done.1, s32[1024]{0:T(1024)S(1)} %get-tuple-element.53), kind=kCustom, calls=%fused_computation | custom fusion | bytes 12288 | tf_op jit(solution)/shard_map/jit(_take)/gather | solution.py:122
  33.1 0.2 dynamic-slice_reduce_fusion
  33.3 0.2 dynamic-slice_reduce_fusion.2
  33.5 0.6 fusion.42
  34.1 0.1 convert_reduce_fusion
  34.2 0.1 select_reduce_fusion.3
  34.2 5.0 %subtract_add_fusion = s32[256]{0:T(256)S(1)} fusion(s32[256]{0:T(256)S(1)} %get-tuple-element.35, s32[256]{0:T(256)S(1)} %get-tuple-element.34, s32[256]{0:T(256)S(1)} %convert_reduce_fusion, s32[]{:T(128)} %bitcast.2, s32[]{:T(128)} %bitcast.3, s32[]{:T(128)} %bitcast.4, s32[]{:T(128)} %bitcast.5, s32[]{:T(128)} %bitcast.6, s32[]{:T(128)} %bitcast.7, ...), kind=kLoop, calls=%fused_computation.109 | loop fusion | flops 4864 | bytes 4128 | tf_op jit(solution)/shard_map/add | solution.py:143
  39.2 81.5 %all-to-all-done = bf16[8,64,8192]{2,1,0:T(8,128)(2,1)} async-done(((bf16[8,64,8192]{2,1,0:T(8,128)(2,1)}), bf16[8,64,8192]{2,1,0:T(8,128)(2,1)}, u32[]{:S(2)}, u32[]{:S(2)}) %all-to-all-start) | async-done | bytes 8388640 | tf_op jit(solution)/shard_map/all_to_all | solution.py:136
  120.7 0.0 copy-start.4
  120.7 5.9 %fusion = (f32[256]{0:T(256)S(1)}, bf16[256,8192]{1,0:T(8,128)(2,1)S(1)}) fusion(bf16[512,8192]{1,0:T(8,128)(2,1)} %bitcast.14, s32[256]{0:T(256)S(1)} %subtract_add_fusion), kind=kOutput, calls=%fused_computation.5 | convolution fusion | flops 2156003072 | bytes 12584960 | tf_op jit(solution)/shard_map/dot_general | solution.py:92
  126.6 0.0 copy-start.2
  126.6 2.0 %copy-done.2 = bf16[256,8192]{1,0:T(8,128)(2,1)} copy-done((bf16[256,8192]{1,0:T(8,128)(2,1)}, bf16[256,8192]{1,0:T(8,128)(2,1)S(1)}, u32[]{:S(2)}) %copy-start.2) | copy-done | bytes 4194328
  128.6 0.0 copy-done.4
  128.6 3.2 %fusion.2 = bf16[256,8192]{1,0:T(8,128)(2,1)} fusion(bf16[256,8192]{1,0:T(8,128)(2,1)S(1)} %get-tuple-element.51, f32[8192]{0:T(1024)S(1)} %copy-done.4, f32[256]{0:T(256)S(1)} %add_rsqrt_fusion), kind=kLoop, calls=%fused_computation.7 | loop fusion | flops 8388608 | bytes 8422400 | tf_op jit(solution)/shard_map/convert_element_type | solution.py:37
  131.8 0.9 collective-permute-start
  132.7 0.0 all-gather.2.cloned.1.call-done
  132.7 0.0 copy-start.6
  132.7 11.7 %fusion.8 = bf16[256,1024]{1,0:T(8,128)(2,1)S(1)} fusion(bf16[256,8192]{1,0:T(8,128)(2,1)} %fusion.2, bf16[8192,1024]{1,0:T(8,128)(2,1)} %all-gather.2.cloned.1.call-done, f32[1024]{0:T(1024)S(1)} %gather_fusion), kind=kOutput, calls=%fused_computation.16 | convolution fusion | flops 4295491584 | bytes 21499904 | tf_op jit(solution)/shard_map/dot_general | solution.py:150
  144.4 0.0 collective-permute-done
  144.4 0.4 collective-permute-start.1
  144.8 1.8 %collective-permute-start.2 = (bf16[256,256]{1,0:T(8,128)(2,1)S(1)}, bf16[256,256]{1,0:T(8,128)(2,1)S(1)}, u32[]{:S(2)}, u32[]{:S(2)}) collective-permute-start(bf16[256,256]{1,0:T(8,128)(2,1)S(1)} %get-tuple-element.40), channel_id=1, source_target_pairs={{0,4},{2,6},{4,0},{6,2},{1,5},{3,7},{5,1},{7,3},{8,12},{10,14},{12... | collective-permute-start | bytes 393224 | tf_op jit(solution)/shard_map/ppermute | solution.py:159
  146.6 0.7 collective-permute-start.3
  147.3 0.0 copy-done.6
  147.3 6.8 %fusion.9 = bf16[256,1024]{1,0:T(8,128)(2,1)S(1)} fusion(bf16[256,8192]{1,0:T(8,128)(2,1)} %collective-permute-done, bf16[8192,1024]{1,0:T(8,128)(2,1)S(1)} %copy-done.6, f32[1024]{0:T(1024)S(1)} %gather_fusion), kind=kOutput, calls=%fused_computation.17 | convolution fusion | flops 4295491584 | bytes 21499904 | tf_op jit(solution)/shard_map/dot_general | solution.py:150
  154.2 0.8 collective-permute-start.4
  155.0 1.6 collective-permute-start.5
  156.6 0.1 broadcast_in_dim.66
  156.7 0.0 collective-permute-done.1
  156.7 2.0 %collective-permute-start.6 = (bf16[256,256]{1,0:T(8,128)(2,1)S(1)}, bf16[256,256]{1,0:T(8,128)(2,1)S(1)}, u32[]{:S(2)}, u32[]{:S(2)}) collective-permute-start(bf16[256,256]{1,0:T(8,128)(2,1)S(1)} %get-tuple-element.36), channel_id=1, source_target_pairs={{0,6},{2,0},{4,2},{6,4},{1,7},{3,1},{5,3},{7,5},{8,14},{10,8},{12,... | collective-permute-start | bytes 393224 | tf_op jit(solution)/shard_map/ppermute | solution.py:159
  158.8 0.0 collective-permute-done.2
  158.8 0.0 collective-permute-done.3
  158.9 1.5 collective-permute-done.4
  160.4 1.9 %collective-permute-done.5 = bf16[256,256]{1,0:T(8,128)(2,1)S(1)} collective-permute-done((bf16[256,256]{1,0:T(8,128)(2,1)S(1)}, bf16[256,256]{1,0:T(8,128)(2,1)S(1)}, u32[]{:S(2)}, u32[]{:S(2)}) %collective-permute-start.5) | collective-permute-done | bytes 131104 | tf_op jit(solution)/shard_map/ppermute | solution.py:159
  162.4 0.7 collective-permute-done.6
  163.1 1.1 reshape.68
  (19 shorter events, 0.3 us)
Async XLA Ops:
  7.2 1.6 copy-start
  7.2 5.0 %copy-start.3 = (s32[1,8,8]{2,1,0:T(8,128)S(1)}, s32[1,8,8]{2,1,0:T(8,128)}, u32[]{:S(2)}) copy-start(s32[1,8,8]{2,1,0:T(8,128)} %param.13) | copy-start | bytes 772
  7.2 5.2 %copy-start.5 = (s32[1,8,8]{2,1,0:T(8,128)S(1)}, s32[1,8,8]{2,1,0:T(8,128)}, u32[]{:S(2)}) copy-start(s32[1,8,8]{2,1,0:T(8,128)} %param.14) | copy-start | bytes 772
  7.2 125.5 %all-gather.2.cloned.1.call-start = ((), (), s32[]{:S(2)}) async-start(), calls=%async_computation.1 | async-start | bytes 17825792 | tf_op jit(solution)/shard_map/all_gather | solution.py:125
  20.5 6.4 %copy-start.1 = (f32[2048]{0:T(1024)S(1)}, f32[2048]{0:T(1024)}, u32[]{:S(2)}) copy-start(f32[2048]{0:T(1024)} %param.17) | copy-start | bytes 24580
  20.5 100.3 %all-to-all-start = ((bf16[8,64,8192]{2,1,0:T(8,128)(2,1)}), bf16[8,64,8192]{2,1,0:T(8,128)(2,1)}, u32[]{:S(2)}, u32[]{:S(2)}) async-start(bf16[8,64,8192]{2,1,0:T(8,128)(2,1)} %bitcast.73), calls=%async_computation | async-start | bytes 16777216 | tf_op jit(solution)/shard_map/all_to_all | solution.py:136
  120.7 7.9 %copy-start.4 = (f32[8192]{0:T(1024)S(1)}, f32[8192]{0:T(1024)}, u32[]{:S(2)}) copy-start(f32[8192]{0:T(1024)} %param.15) | copy-start | bytes 98308
  126.6 2.0 %copy-start.2 = (bf16[256,8192]{1,0:T(8,128)(2,1)}, bf16[256,8192]{1,0:T(8,128)(2,1)S(1)}, u32[]{:S(2)}) copy-start(bf16[256,8192]{1,0:T(8,128)(2,1)S(1)} %get-tuple-element.51) | copy-start | bytes 12582916
  131.8 12.6 %collective-permute-start = (bf16[256,8192]{1,0:T(8,128)(2,1)}, bf16[256,8192]{1,0:T(8,128)(2,1)}, u32[]{:S(2)}, u32[]{:S(2)}) collective-permute-start(bf16[256,8192]{1,0:T(8,128)(2,1)} %fusion.2), channel_id=1, source_target_pairs={{0,1},{1,0},{2,3},{3,2},{4,5},{5,4},{6,7},{7,6},{8,9},{9,8},{10,11... | collective-permute-start | bytes 12582920 | tf_op jit(solution)/shard_map/ppermute | solution.py:147
  132.7 14.6 %copy-start.6 = (bf16[8192,1024]{1,0:T(8,128)(2,1)S(1)}, bf16[8192,1024]{1,0:T(8,128)(2,1)}, u32[]{:S(2)}) copy-start(bf16[8192,1024]{1,0:T(8,128)(2,1)} %all-gather.2.cloned.1.call-done) | copy-start | bytes 50331652
  144.4 12.3 %collective-permute-start.1 = (bf16[256,256]{1,0:T(8,128)(2,1)S(1)}, bf16[256,256]{1,0:T(8,128)(2,1)S(1)}, u32[]{:S(2)}, u32[]{:S(2)}) collective-permute-start(bf16[256,256]{1,0:T(8,128)(2,1)S(1)} %get-tuple-element.41), channel_id=1, source_target_pairs={{0,2},{2,4},{4,6},{6,0},{1,3},{3,5},{5,7},{7,1},{8,10},{10,12},{12... | collective-permute-start | bytes 393224 | tf_op jit(solution)/shard_map/ppermute | solution.py:159
  144.8 14.0 %collective-permute-start.2 = (bf16[256,256]{1,0:T(8,128)(2,1)S(1)}, bf16[256,256]{1,0:T(8,128)(2,1)S(1)}, u32[]{:S(2)}, u32[]{:S(2)}) collective-permute-start(bf16[256,256]{1,0:T(8,128)(2,1)S(1)} %get-tuple-element.40), channel_id=1, source_target_pairs={{0,4},{2,6},{4,0},{6,2},{1,5},{3,7},{5,1},{7,3},{8,12},{10,14},{12... | collective-permute-start | bytes 393224 | tf_op jit(solution)/shard_map/ppermute | solution.py:159
  146.6 12.3 %collective-permute-start.3 = (bf16[256,256]{1,0:T(8,128)(2,1)S(1)}, bf16[256,256]{1,0:T(8,128)(2,1)S(1)}, u32[]{:S(2)}, u32[]{:S(2)}) collective-permute-start(bf16[256,256]{1,0:T(8,128)(2,1)S(1)} %get-tuple-element.39), channel_id=1, source_target_pairs={{0,6},{2,0},{4,2},{6,4},{1,7},{3,1},{5,3},{7,5},{8,14},{10,8},{12,... | collective-permute-start | bytes 393224 | tf_op jit(solution)/shard_map/ppermute | solution.py:159
  154.2 6.2 %collective-permute-start.4 = (bf16[256,256]{1,0:T(8,128)(2,1)S(1)}, bf16[256,256]{1,0:T(8,128)(2,1)S(1)}, u32[]{:S(2)}, u32[]{:S(2)}) collective-permute-start(bf16[256,256]{1,0:T(8,128)(2,1)S(1)} %get-tuple-element.38), channel_id=1, source_target_pairs={{0,2},{2,4},{4,6},{6,0},{1,3},{3,5},{5,7},{7,1},{8,10},{10,12},{12... | collective-permute-start | bytes 393224 | tf_op jit(solution)/shard_map/ppermute | solution.py:159
  155.0 7.4 %collective-permute-start.5 = (bf16[256,256]{1,0:T(8,128)(2,1)S(1)}, bf16[256,256]{1,0:T(8,128)(2,1)S(1)}, u32[]{:S(2)}, u32[]{:S(2)}) collective-permute-start(bf16[256,256]{1,0:T(8,128)(2,1)S(1)} %get-tuple-element.37), channel_id=1, source_target_pairs={{0,4},{2,6},{4,0},{6,2},{1,5},{3,7},{5,1},{7,3},{8,12},{10,14},{12... | collective-permute-start | bytes 393224 | tf_op jit(solution)/shard_map/ppermute | solution.py:159
  156.7 6.3 %collective-permute-start.6 = (bf16[256,256]{1,0:T(8,128)(2,1)S(1)}, bf16[256,256]{1,0:T(8,128)(2,1)S(1)}, u32[]{:S(2)}, u32[]{:S(2)}) collective-permute-start(bf16[256,256]{1,0:T(8,128)(2,1)S(1)} %get-tuple-element.36), channel_id=1, source_target_pairs={{0,6},{2,0},{4,2},{6,4},{1,7},{3,1},{5,3},{7,5},{8,14},{10,8},{12,... | collective-permute-start | bytes 393224 | tf_op jit(solution)/shard_map/ppermute | solution.py:159
Sparse Core Ops, SparseCore 0:
  12.3 114.6 all-gather.1

commit v19 on v18

--- a/solution.py
+++ b/solution.py
@@ -143,7 +143,10 @@
     index = source * capacity + shift + within
     local_bias, index = lax.optimization_barrier((local_bias, index))
     moved_rows = select_rows(arriving_rows.reshape(peer_count * capacity, -1), index)
-    normed = rms_normed(moved_rows, norm_gain)
+    as_float = moved_rows.astype(jnp.float32)
+    inverse_rms = lax.rsqrt(jnp.mean(as_float * as_float, axis=-1, keepdims=True) + 1e-06)
+    gathered_weight, inverse_rms = lax.optimization_barrier((gathered_weight, inverse_rms))
+    normed = (as_float * inverse_rms * norm_gain[None, :]).astype(jnp.bfloat16)
     sibling_rows = lax.ppermute(normed, "cc", perm=[(0, 1), (1, 0)])
 
     def project(rows):

time: 172 us -> 177 us (1.029)
  waiting for transfers between devices: 85.7 us -> 91.2 us
  other arithmetic: 8.71 us -> 10.9 us
  starting transfers between devices: 14.6 us -> 12.6 us
  matrix products: 35.6 us -> 37.5 us
  local copies, waits for them, and re-layouts: 12.2 us -> 10.3 us
    ppermute x6, waiting for transfers between devices: 4.13 us -> 9.62 us  [send_half(): lax.ppermute(blocks[step], 'cx', perm=[(i, (i + step) % chips) for i in r...]
    convert_element_type x1, other arithmetic: 3.15 us -> 5.33 us  [on_device(): normed = (as_float * inverse_rms * norm_gain[None, :]).astype(jnp.bfloat16)]
    ppermute x6, starting transfers between devices: 7.32 us -> 5.27 us  [send_half(): lax.ppermute(blocks[step], 'cx', perm=[(i, (i + step) % chips) for i in r...]
    dot_general x2, matrix products: 13.7 us -> 15.6 us  [select_rows(): jnp.dot(picks.astype(rows.dtype), rows, preferred_element_type=jnp.float32)]
    unnamed x14 -> x12, local copies, waits for them, and re-layouts: 3.5 us -> 1.58 us
  transfers between devices with their start and end apart: 9 -> 9, of which waited for: 4 -> 5; matrix products, arithmetic and copies ran while one was open for 28% -> 23% of each run, Pallas kernels for 0% -> 0%
where the time goes in v19:
time: 177 us
  waiting for transfers between devices  91.2 us (52%)
  matrix products  37.5 us (21%)
  between operations  14.2 us (8%)
  starting transfers between devices  12.6 us (7%)
  other arithmetic  10.9 us (6%)
  local copies, waits for them, and re-layouts  10.3 us (6%)
    all_to_all x1, waiting for transfers between devices, on_device(): lax.all_to_all(outgoing.reshape(peer_count, capacity, -1), CTX, split_axi...  81.5 us
    dot_general x2, matrix products, project(): jnp.dot(rows, gathered_weight, preferred_element_type=jnp.float32)  18.5 us
    dot_general x2, matrix products, select_rows(): jnp.dot(picks.astype(rows.dtype), rows, preferred_element_type=jnp.float32)  15.6 us
    ppermute x6, waiting for transfers between devices, send_half(): lax.ppermute(blocks[step], 'cx', perm=[(i, (i + step) % chips) for i in r...  9.62 us
    all_to_all x1, starting transfers between devices, on_device(): lax.all_to_all(outgoing.reshape(peer_count, capacity, -1), CTX, split_axi...  6.39 us
    gather x1, local copies, waits for them, and re-layouts, on_device(): local_bias = jnp.take(kv_bias, columns, mode='clip')  6.15 us
    convert_element_type x1, other arithmetic, on_device(): normed = (as_float * inverse_rms * norm_gain[None, :]).astype(jnp.bfloat16)  5.33 us
    ppermute x6, starting transfers between devices, send_half(): lax.ppermute(blocks[step], 'cx', perm=[(i, (i + step) % chips) for i in r...  5.27 us
  transfers between devices with their start and end apart: 9, of which 5 were waited for; matrix products, arithmetic and copies ran while one was open for 23% of the time, Pallas kernels for 0%

profile of v19, /device:TPU:1, one launch (start us, length us, event | category | flops | bytes accessed | tf_op | source)
XLA Modules:
  0.0 176.6 jit_solution(9306381972004150878)
XLA Ops:
  7.2 0.0 copy-start
  7.2 0.0 copy-start.2
  7.2 0.0 copy-start.4
  7.2 0.0 all-gather.2.cloned.1.call-start
  7.3 1.5 copy-done
  8.8 3.4 %fusion.7 = bf16[512,1024]{1,0:T(8,128)(2,1)} fusion(bf16[512,2048]{1,0:T(8,128)(2,1)S(1)} %copy-done, s32[1024]{0:T(1024)S(1)} %get-tuple-element.56), kind=kOutput, calls=%fused_computation.15 | convolution fusion | flops 2150105088 | bytes 3149824 | tf_op jit(solution)/shard_map/dot_general | solution.py:119
  12.2 0.0 all-gather.2.cloned.1.call-update
  12.2 0.0 copy-done.2
  12.2 0.2 reduce_window_sum.23
  12.4 0.0 copy-done.4
  12.4 0.1 select_reduce_fusion.1
  12.5 0.1 iota_add_fusion
  12.6 0.1 add.178
  12.7 7.8 %convolution_convert_fusion = bf16[512,8192]{1,0:T(8,128)(2,1)} fusion(bf16[1,256,8192]{2,1,0:T(8,128)(2,1)} %param.12, s32[512]{0:T(512)S(1)} %add.178), kind=kOutput, calls=%fused_computation.1 | convolution fusion | flops 2151809024 | bytes 12584960 | tf_op jit(solution)/shard_map/dot_general | solution.py:92
  20.5 0.0 copy-start.1
  20.5 6.4 %all-to-all-start = ((bf16[8,64,8192]{2,1,0:T(8,128)(2,1)}), bf16[8,64,8192]{2,1,0:T(8,128)(2,1)}, u32[]{:S(2)}, u32[]{:S(2)}) async-start(bf16[8,64,8192]{2,1,0:T(8,128)(2,1)} %bitcast.75), calls=%async_computation | async-start | bytes 16777216 | tf_op jit(solution)/shard_map/all_to_all | solution.py:136
  26.9 0.0 copy-done.1
  26.9 6.2 %gather_fusion = f32[1024]{0:T(1024)S(1)} fusion(f32[2048]{0:T(1024)S(1)} %copy-done.1, s32[1024]{0:T(1024)S(1)} %get-tuple-element.57), kind=kCustom, calls=%fused_computation | custom fusion | bytes 12288 | tf_op jit(solution)/shard_map/jit(_take)/gather | solution.py:122
  33.1 0.2 dynamic-slice_reduce_fusion
  33.3 0.2 dynamic-slice_reduce_fusion.2
  33.5 0.6 fusion.42
  34.1 0.1 convert_reduce_fusion
  34.2 0.1 select_reduce_fusion.3
  34.2 5.0 %subtract_add_fusion = s32[256]{0:T(256)S(1)} fusion(s32[256]{0:T(256)S(1)} %get-tuple-element.39, s32[256]{0:T(256)S(1)} %get-tuple-element.38, s32[256]{0:T(256)S(1)} %convert_reduce_fusion, s32[]{:T(128)} %bitcast.2, s32[]{:T(128)} %bitcast.3, s32[]{:T(128)} %bitcast.4, s32[]{:T(128)} %bitcast.5, s32[]{:T(128)} %bitcast.6, s32[]{:T(128)} %bitcast.7, ...), kind=kLoop, calls=%fused_computation.109 | loop fusion | flops 4864 | bytes 4128 | tf_op jit(solution)/shard_map/add | solution.py:143
  39.2 81.5 %all-to-all-done = bf16[8,64,8192]{2,1,0:T(8,128)(2,1)} async-done(((bf16[8,64,8192]{2,1,0:T(8,128)(2,1)}), bf16[8,64,8192]{2,1,0:T(8,128)(2,1)}, u32[]{:S(2)}, u32[]{:S(2)}) %all-to-all-start) | async-done | bytes 8388640 | tf_op jit(solution)/shard_map/all_to_all | solution.py:136
  120.7 0.0 copy-start.3
  120.7 7.8 %fusion = (f32[256]{0:T(256)S(1)}, bf16[256,8192]{1,0:T(8,128)(2,1)}) fusion(bf16[512,8192]{1,0:T(8,128)(2,1)} %bitcast.14, s32[256]{0:T(256)S(1)} %subtract_add_fusion), kind=kOutput, calls=%fused_computation.5 | convolution fusion | flops 2156003072 | bytes 12584960 | tf_op jit(solution)/shard_map/dot_general | solution.py:92
  128.6 0.0 all-gather.2.cloned.1.call-done
  128.6 0.0 copy-done.3
  128.6 5.3 %fusion.2 = bf16[256,8192]{1,0:T(8,128)(2,1)} fusion(bf16[256,8192]{1,0:T(8,128)(2,1)} %get-tuple-element.55, f32[8192]{0:T(1024)S(1)} %copy-done.3, f32[256]{0:T(256)S(1)} %add_rsqrt_fusion), kind=kLoop, calls=%fused_computation.7 | loop fusion | flops 8388608 | bytes 8422400 | tf_op jit(solution)/shard_map/convert_element_type | solution.py:149
  133.9 0.9 collective-permute-start
  134.8 0.0 copy-start.5
  134.8 11.7 %fusion.8 = bf16[256,1024]{1,0:T(8,128)(2,1)S(1)} fusion(bf16[256,8192]{1,0:T(8,128)(2,1)} %fusion.2, bf16[8192,1024]{1,0:T(8,128)(2,1)} %all-gather.2.cloned.1.call-done, f32[1024]{0:T(1024)S(1)} %gather_fusion), kind=kOutput, calls=%fused_computation.16 | convolution fusion | flops 4295491584 | bytes 21499904 | tf_op jit(solution)/shard_map/dot_general | solution.py:153
  146.5 0.0 collective-permute-done
  146.5 0.1 copy-done.5
  146.6 6.8 %fusion.9 = bf16[256,1024]{1,0:T(8,128)(2,1)S(1)} fusion(bf16[256,8192]{1,0:T(8,128)(2,1)} %collective-permute-done, bf16[8192,1024]{1,0:T(8,128)(2,1)S(1)} %copy-done.5, f32[1024]{0:T(1024)S(1)} %gather_fusion), kind=kOutput, calls=%fused_computation.17 | convolution fusion | flops 4295491584 | bytes 21499904 | tf_op jit(solution)/shard_map/dot_general | solution.py:153
  153.5 0.4 collective-permute-start.1
  153.8 1.8 collective-permute-start.2
  155.6 1.0 collective-permute-start.3
  156.6 0.6 collective-permute-start.4
  157.2 1.6 collective-permute-start.5
  158.8 0.1 broadcast_in_dim.66
  158.9 3.6 %collective-permute-done.1 = bf16[256,256]{1,0:T(8,128)(2,1)S(1)} collective-permute-done((bf16[256,256]{1,0:T(8,128)(2,1)S(1)}, bf16[256,256]{1,0:T(8,128)(2,1)S(1)}, u32[]{:S(2)}, u32[]{:S(2)}) %collective-permute-start.1) | collective-permute-done | bytes 131104 | tf_op jit(solution)/shard_map/ppermute | solution.py:162
  162.5 0.0 collective-permute-start.6
  162.5 0.0 collective-permute-done.2
  162.5 0.5 collective-permute-done.3
  163.0 5.3 %collective-permute-done.4 = bf16[256,256]{1,0:T(8,128)(2,1)S(1)} collective-permute-done((bf16[256,256]{1,0:T(8,128)(2,1)S(1)}, bf16[256,256]{1,0:T(8,128)(2,1)S(1)}, u32[]{:S(2)}, u32[]{:S(2)}) %collective-permute-start.4) | collective-permute-done | bytes 131104 | tf_op jit(solution)/shard_map/ppermute | solution.py:162
  168.3 0.0 collective-permute-done.5
  168.4 0.3 collective-permute-done.6
  168.7 1.1 reshape.81
  (19 shorter events, 0.3 us)
Async XLA Ops:
  7.2 1.6 copy-start
  7.2 5.0 %copy-start.2 = (s32[1,8,8]{2,1,0:T(8,128)S(1)}, s32[1,8,8]{2,1,0:T(8,128)}, u32[]{:S(2)}) copy-start(s32[1,8,8]{2,1,0:T(8,128)} %param.13) | copy-start | bytes 772
  7.2 5.2 %copy-start.4 = (s32[1,8,8]{2,1,0:T(8,128)S(1)}, s32[1,8,8]{2,1,0:T(8,128)}, u32[]{:S(2)}) copy-start(s32[1,8,8]{2,1,0:T(8,128)} %param.14) | copy-start | bytes 772
  7.2 121.4 %all-gather.2.cloned.1.call-start = ((), (), s32[]{:S(2)}) async-start(), calls=%async_computation.1 | async-start | bytes 17825792 | tf_op jit(solution)/shard_map/all_gather | solution.py:125
  20.5 6.4 %copy-start.1 = (f32[2048]{0:T(1024)S(1)}, f32[2048]{0:T(1024)}, u32[]{:S(2)}) copy-start(f32[2048]{0:T(1024)} %param.17) | copy-start | bytes 24580
  20.5 100.3 %all-to-all-start = ((bf16[8,64,8192]{2,1,0:T(8,128)(2,1)}), bf16[8,64,8192]{2,1,0:T(8,128)(2,1)}, u32[]{:S(2)}, u32[]{:S(2)}) async-start(bf16[8,64,8192]{2,1,0:T(8,128)(2,1)} %bitcast.75), calls=%async_computation | async-start | bytes 16777216 | tf_op jit(solution)/shard_map/all_to_all | solution.py:136
  120.7 7.8 %copy-start.3 = (f32[8192]{0:T(1024)S(1)}, f32[8192]{0:T(1024)}, u32[]{:S(2)}) copy-start(f32[8192]{0:T(1024)} %param.15) | copy-start | bytes 98308
  133.9 12.6 %collective-permute-start = (bf16[256,8192]{1,0:T(8,128)(2,1)}, bf16[256,8192]{1,0:T(8,128)(2,1)}, u32[]{:S(2)}, u32[]{:S(2)}) collective-permute-start(bf16[256,8192]{1,0:T(8,128)(2,1)} %fusion.2), channel_id=1, source_target_pairs={{0,1},{1,0},{2,3},{3,2},{4,5},{5,4},{6,7},{7,6},{8,9},{9,8},{10,11... | collective-permute-start | bytes 12582920 | tf_op jit(solution)/shard_map/ppermute | solution.py:150
  134.8 11.8 %copy-start.5 = (bf16[8192,1024]{1,0:T(8,128)(2,1)S(1)}, bf16[8192,1024]{1,0:T(8,128)(2,1)}, u32[]{:S(2)}) copy-start(bf16[8192,1024]{1,0:T(8,128)(2,1)} %all-gather.2.cloned.1.call-done) | copy-start | bytes 50331652
  153.5 9.0 %collective-permute-start.1 = (bf16[256,256]{1,0:T(8,128)(2,1)S(1)}, bf16[256,256]{1,0:T(8,128)(2,1)S(1)}, u32[]{:S(2)}, u32[]{:S(2)}) collective-permute-start(bf16[256,256]{1,0:T(8,128)(2,1)S(1)} %get-tuple-element.45), channel_id=1, source_target_pairs={{0,2},{2,4},{4,6},{6,0},{1,3},{3,5},{5,7},{7,1},{8,10},{10,12},{12... | collective-permute-start | bytes 393224 | tf_op jit(solution)/shard_map/ppermute | solution.py:162
  153.8 8.7 %collective-permute-start.2 = (bf16[256,256]{1,0:T(8,128)(2,1)S(1)}, bf16[256,256]{1,0:T(8,128)(2,1)S(1)}, u32[]{:S(2)}, u32[]{:S(2)}) collective-permute-start(bf16[256,256]{1,0:T(8,128)(2,1)S(1)} %get-tuple-element.44), channel_id=1, source_target_pairs={{0,4},{2,6},{4,0},{6,2},{1,5},{3,7},{5,1},{7,3},{8,12},{10,14},{12... | collective-permute-start | bytes 393224 | tf_op jit(solution)/shard_map/ppermute | solution.py:162
  155.6 7.4 %collective-permute-start.3 = (bf16[256,256]{1,0:T(8,128)(2,1)S(1)}, bf16[256,256]{1,0:T(8,128)(2,1)S(1)}, u32[]{:S(2)}, u32[]{:S(2)}) collective-permute-start(bf16[256,256]{1,0:T(8,128)(2,1)S(1)} %get-tuple-element.43), channel_id=1, source_target_pairs={{0,6},{2,0},{4,2},{6,4},{1,7},{3,1},{5,3},{7,5},{8,14},{10,8},{12,... | collective-permute-start | bytes 393224 | tf_op jit(solution)/shard_map/ppermute | solution.py:162
  156.6 11.7 %collective-permute-start.4 = (bf16[256,256]{1,0:T(8,128)(2,1)S(1)}, bf16[256,256]{1,0:T(8,128)(2,1)S(1)}, u32[]{:S(2)}, u32[]{:S(2)}) collective-permute-start(bf16[256,256]{1,0:T(8,128)(2,1)S(1)} %get-tuple-element.42), channel_id=1, source_target_pairs={{0,2},{2,4},{4,6},{6,0},{1,3},{3,5},{5,7},{7,1},{8,10},{10,12},{12... | collective-permute-start | bytes 393224 | tf_op jit(solution)/shard_map/ppermute | solution.py:162
  157.2 11.2 %collective-permute-start.5 = (bf16[256,256]{1,0:T(8,128)(2,1)S(1)}, bf16[256,256]{1,0:T(8,128)(2,1)S(1)}, u32[]{:S(2)}, u32[]{:S(2)}) collective-permute-start(bf16[256,256]{1,0:T(8,128)(2,1)S(1)} %get-tuple-element.41), channel_id=1, source_target_pairs={{0,4},{2,6},{4,0},{6,2},{1,5},{3,7},{5,1},{7,3},{8,12},{10,14},{12... | collective-permute-start | bytes 393224 | tf_op jit(solution)/shard_map/ppermute | solution.py:162
  162.5 6.2 %collective-permute-start.6 = (bf16[256,256]{1,0:T(8,128)(2,1)S(1)}, bf16[256,256]{1,0:T(8,128)(2,1)S(1)}, u32[]{:S(2)}, u32[]{:S(2)}) collective-permute-start(bf16[256,256]{1,0:T(8,128)(2,1)S(1)} %get-tuple-element.40), channel_id=1, source_target_pairs={{0,6},{2,0},{4,2},{6,4},{1,7},{3,1},{5,3},{7,5},{8,14},{10,8},{12,... | collective-permute-start | bytes 393224 | tf_op jit(solution)/shard_map/ppermute | solution.py:162
Sparse Core Ops, SparseCore 0:
  12.3 114.6 all-gather.1

commit v20 on v18

--- a/solution.py
+++ b/solution.py
@@ -132,7 +132,11 @@
     capacity = 2 * row_count // peer_count
     starts = window_starts(anchors, row_count, capacity)
     rows = input_entries[0]
-    outgoing = select_rows(rows, (starts[myself][:, None] + jnp.arange(capacity)).reshape(-1))
+    my_starts = starts[myself]
+    outgoing = jnp.concatenate(
+        [lax.dynamic_slice_in_dim(rows, my_starts[k], capacity, axis=0) for k in range(peer_count)],
+        axis=0,
+    )
     arriving_rows = lax.all_to_all(
         outgoing.reshape(peer_count, capacity, -1), CTX, split_axis=0, concat_axis=0, tiled=True
     )

time: 172 us -> 191 us (1.11)
  between operations: 14.3 us -> 29.5 us
  local copies, waits for them, and re-layouts: 12.2 us -> 23.3 us
  matrix products: 35.6 us -> 27.9 us
    unnamed x14 -> x25, local copies, waits for them, and re-layouts: 3.5 us -> 13.7 us
    dot_general x2 -> x1, matrix products: 13.7 us -> 5.89 us  [select_rows(): jnp.dot(picks.astype(rows.dtype), rows, preferred_element_type=jnp.float32)]
  transfers between devices with their start and end apart: 9 -> 9, of which waited for: 4 -> 4; matrix products, arithmetic and copies ran while one was open for 28% -> 26% of each run, Pallas kernels for 0% -> 0%
where the time goes in v20:
time: 191 us; the launch traced here: 190 us
  waiting for transfers between devices  85.6 us (45%)
  between operations  29.5 us (15%)
  matrix products  27.9 us (15%)
  local copies, waits for them, and re-layouts  23.3 us (12%)
  starting transfers between devices  14.7 us (8%)
  other arithmetic  8.64 us (5%)
    all_to_all x1, waiting for transfers between devices, on_device(): lax.all_to_all(outgoing.reshape(peer_count, capacity, -1), CTX, split_axi...  81.5 us
    dot_general x2, matrix products, project(): jnp.dot(rows, gathered_weight, preferred_element_type=jnp.float32)  18.5 us
    unnamed x25, local copies, waits for them, and re-layouts  13.7 us
    ppermute x6, starting transfers between devices, send_half(): lax.ppermute(blocks[step], 'cx', perm=[(i, (i + step) % chips) for i in r...  7.32 us
    all_to_all x1, starting transfers between devices, on_device(): lax.all_to_all(outgoing.reshape(peer_count, capacity, -1), CTX, split_axi...  6.46 us
    gather x1, local copies, waits for them, and re-layouts, on_device(): local_bias = jnp.take(kv_bias, columns, mode='clip')  6.15 us
    dot_general x1, matrix products, select_rows(): jnp.dot(picks.astype(rows.dtype), rows, preferred_element_type=jnp.float32)  5.89 us
    add x1, other arithmetic, on_device(): index = source * capacity + shift + within  4.98 us
  transfers between devices with their start and end apart: 9, of which 4 were waited for; matrix products, arithmetic and copies ran while one was open for 26% of the time, Pallas kernels for 0%

profile of v20, /device:TPU:1, one launch (start us, length us, event | category | flops | bytes accessed | tf_op | source)
XLA Modules:
  0.0 189.6 jit_solution(5952706682638720975)
XLA Ops:
  7.2 0.0 copy-start
  7.2 0.0 copy-start.5
  7.2 0.0 copy-start.7
  7.2 0.0 all-gather.2.cloned.1.call-start
  7.3 1.5 copy-done
  8.8 3.4 %fusion.6 = bf16[512,1024]{1,0:T(8,128)(2,1)} fusion(bf16[512,2048]{1,0:T(8,128)(2,1)S(1)} %copy-done, s32[1024]{0:T(1024)S(1)} %get-tuple-element.62), kind=kOutput, calls=%fused_computation.13 | convolution fusion | flops 2150105088 | bytes 3149824 | tf_op jit(solution)/shard_map/dot_general | solution.py:119
  12.2 0.0 all-gather.2.cloned.1.call-update
  12.2 0.0 copy-done.5
  12.2 0.2 reduce_window_sum.23
  12.4 0.0 copy-done.7
  12.4 0.1 select_reduce_fusion.1
  12.5 0.7 fusion.43
  28.4 0.0 copy-start.2
  28.4 1.7 bitcast_dynamic-update-slice_fusion.7
  30.1 1.5 bitcast_dynamic-update-slice_fusion.6
  31.6 1.6 bitcast_dynamic-update-slice_fusion.5
  33.1 1.6 bitcast_dynamic-update-slice_fusion.4
  34.7 0.0 copy-done.2
  34.7 0.3 bitcast_dynamic-update-slice_fusion.3
  35.0 0.3 bitcast_dynamic-update-slice_fusion.2
  35.2 0.3 bitcast_dynamic-update-slice_fusion.1
  35.5 0.3 bitcast_dynamic-update-slice_fusion
  35.8 0.0 copy-start.3
  35.8 3.2 %copy-done.3 = bf16[512,8192]{1,0:T(8,128)(2,1)} copy-done((bf16[512,8192]{1,0:T(8,128)(2,1)}, bf16[512,8192]{1,0:T(8,128)(2,1)S(1)}, u32[]{:S(2)}) %copy-start.3) | copy-done | bytes 8388632
  39.0 0.0 copy-start.1
  39.0 6.5 %all-to-all-start = ((bf16[8,64,8192]{2,1,0:T(8,128)(2,1)}), bf16[8,64,8192]{2,1,0:T(8,128)(2,1)}, u32[]{:S(2)}, u32[]{:S(2)}) async-start(bf16[8,64,8192]{2,1,0:T(8,128)(2,1)} %bitcast.92), calls=%async_computation | async-start | bytes 16777216 | tf_op jit(solution)/shard_map/all_to_all | solution.py:140
  45.5 0.0 copy-done.1
  45.5 6.2 %gather_fusion = f32[1024]{0:T(1024)S(1)} fusion(f32[2048]{0:T(1024)S(1)} %copy-done.1, s32[1024]{0:T(1024)S(1)} %get-tuple-element.63), kind=kCustom, calls=%fused_computation | custom fusion | bytes 12288 | tf_op jit(solution)/shard_map/jit(_take)/gather | solution.py:122
  51.6 0.2 fusion.17
  51.8 0.2 constant_dynamic-slice_fusion.2
  52.0 0.6 fusion.42
  52.6 0.1 convert_reduce_fusion
  52.7 0.1 select_reduce_fusion.3
  52.8 5.0 %subtract_add_fusion = s32[256]{0:T(256)S(1)} fusion(s32[256]{0:T(256)S(1)} %get-tuple-element.35, s32[256]{0:T(256)S(1)} %get-tuple-element.34, s32[256]{0:T(256)S(1)} %convert_reduce_fusion, s32[]{:T(128)} %bitcast.2, s32[]{:T(128)} %bitcast.3, s32[]{:T(128)} %bitcast.4, s32[]{:T(128)} %bitcast.5, s32[]{:T(128)} %bitcast.6, s32[]{:T(128)} %bitcast.7, ...), kind=kLoop, calls=%fused_computation.115 | loop fusion | flops 4864 | bytes 4128 | tf_op jit(solution)/shard_map/add | solution.py:147
  57.8 81.5 %all-to-all-done = bf16[8,64,8192]{2,1,0:T(8,128)(2,1)} async-done(((bf16[8,64,8192]{2,1,0:T(8,128)(2,1)}), bf16[8,64,8192]{2,1,0:T(8,128)(2,1)}, u32[]{:S(2)}, u32[]{:S(2)}) %all-to-all-start) | async-done | bytes 8388640 | tf_op jit(solution)/shard_map/all_to_all | solution.py:140
  139.3 0.0 copy-start.6
  139.3 5.9 %fusion = (f32[256]{0:T(256)S(1)}, bf16[256,8192]{1,0:T(8,128)(2,1)S(1)}) fusion(bf16[512,8192]{1,0:T(8,128)(2,1)} %bitcast.28, s32[256]{0:T(256)S(1)} %subtract_add_fusion), kind=kOutput, calls=%fused_computation.4 | convolution fusion | flops 2156003072 | bytes 12584960 | tf_op jit(solution)/shard_map/dot_general | solution.py:92
  145.2 0.0 copy-start.4
  145.2 2.0 %copy-done.4 = bf16[256,8192]{1,0:T(8,128)(2,1)} copy-done((bf16[256,8192]{1,0:T(8,128)(2,1)}, bf16[256,8192]{1,0:T(8,128)(2,1)S(1)}, u32[]{:S(2)}) %copy-start.4) | copy-done | bytes 4194328
  147.2 0.0 copy-done.6
  147.2 3.1 %fusion.2 = bf16[256,8192]{1,0:T(8,128)(2,1)} fusion(bf16[256,8192]{1,0:T(8,128)(2,1)S(1)} %get-tuple-element.59, f32[8192]{0:T(1024)S(1)} %copy-done.6, f32[256]{0:T(256)S(1)} %add_rsqrt_fusion), kind=kLoop, calls=%fused_computation.6 | loop fusion | flops 8388608 | bytes 8422400 | tf_op jit(solution)/shard_map/convert_element_type | solution.py:37
  150.4 0.9 collective-permute-start
  151.2 0.0 all-gather.2.cloned.1.call-done
  151.2 0.0 copy-start.8
  151.2 11.7 %fusion.7 = bf16[256,1024]{1,0:T(8,128)(2,1)S(1)} fusion(bf16[256,8192]{1,0:T(8,128)(2,1)} %fusion.2, bf16[8192,1024]{1,0:T(8,128)(2,1)} %all-gather.2.cloned.1.call-done, f32[1024]{0:T(1024)S(1)} %gather_fusion), kind=kOutput, calls=%fused_computation.14 | convolution fusion | flops 4295491584 | bytes 21499904 | tf_op jit(solution)/shard_map/dot_general | solution.py:154
  163.0 0.0 collective-permute-done
  163.0 0.4 collective-permute-start.1
  163.4 1.8 collective-permute-start.2
  165.1 0.7 collective-permute-start.3
  165.9 0.0 copy-done.8
  165.9 6.9 %fusion.8 = bf16[256,1024]{1,0:T(8,128)(2,1)S(1)} fusion(bf16[256,8192]{1,0:T(8,128)(2,1)} %collective-permute-done, bf16[8192,1024]{1,0:T(8,128)(2,1)S(1)} %copy-done.8, f32[1024]{0:T(1024)S(1)} %gather_fusion), kind=kOutput, calls=%fused_computation.15 | convolution fusion | flops 4295491584 | bytes 21499904 | tf_op jit(solution)/shard_map/dot_general | solution.py:154
  172.8 0.8 collective-permute-start.4
  173.6 1.6 collective-permute-start.5
  175.3 0.1 broadcast_in_dim.64
  175.3 0.0 collective-permute-done.1
  175.4 2.0 %collective-permute-start.6 = (bf16[256,256]{1,0:T(8,128)(2,1)S(1)}, bf16[256,256]{1,0:T(8,128)(2,1)S(1)}, u32[]{:S(2)}, u32[]{:S(2)}) collective-permute-start(bf16[256,256]{1,0:T(8,128)(2,1)S(1)} %get-tuple-element.36), channel_id=1, source_target_pairs={{0,6},{2,0},{4,2},{6,4},{1,7},{3,1},{5,3},{7,5},{8,14},{10,8},{12,... | collective-permute-start | bytes 393224 | tf_op jit(solution)/shard_map/ppermute | solution.py:163
  177.4 0.0 collective-permute-done.2
  177.5 0.0 collective-permute-done.3
  177.5 1.5 collective-permute-done.4
  179.0 2.0 %collective-permute-done.5 = bf16[256,256]{1,0:T(8,128)(2,1)S(1)} collective-permute-done((bf16[256,256]{1,0:T(8,128)(2,1)S(1)}, bf16[256,256]{1,0:T(8,128)(2,1)S(1)}, u32[]{:S(2)}, u32[]{:S(2)}) %collective-permute-start.5) | collective-permute-done | bytes 131104 | tf_op jit(solution)/shard_map/ppermute | solution.py:163
  181.0 0.7 collective-permute-done.6
  181.7 1.1 reshape.77
  (19 shorter events, 0.3 us)
Async XLA Ops:
  7.2 1.6 copy-start
  7.2 5.0 %copy-start.5 = (s32[1,8,8]{2,1,0:T(8,128)S(1)}, s32[1,8,8]{2,1,0:T(8,128)}, u32[]{:S(2)}) copy-start(s32[1,8,8]{2,1,0:T(8,128)} %param.13) | copy-start | bytes 772
  7.2 5.2 %copy-start.7 = (s32[1,8,8]{2,1,0:T(8,128)S(1)}, s32[1,8,8]{2,1,0:T(8,128)}, u32[]{:S(2)}) copy-start(s32[1,8,8]{2,1,0:T(8,128)} %param.14) | copy-start | bytes 772
  7.2 144.0 %all-gather.2.cloned.1.call-start = ((), (), s32[]{:S(2)}) async-start(), calls=%async_computation.1 | async-start | bytes 17825792 | tf_op jit(solution)/shard_map/all_gather | solution.py:125
  28.4 6.3 %copy-start.2 = (bf16[1,256,8192]{2,1,0:T(8,128)(2,1)S(1)}, bf16[1,256,8192]{2,1,0:T(8,128)(2,1)}, u32[]{:S(2)}) copy-start(bf16[1,256,8192]{2,1,0:T(8,128)(2,1)} %param.12) | copy-start | bytes 12582916
  35.8 3.2 %copy-start.3 = (bf16[512,8192]{1,0:T(8,128)(2,1)}, bf16[512,8192]{1,0:T(8,128)(2,1)S(1)}, u32[]{:S(2)}) copy-start(bf16[512,8192]{1,0:T(8,128)(2,1)S(1)} %bitcast_dynamic-update-slice_fusion) | copy-start | bytes 25165828
  39.0 6.5 %copy-start.1 = (f32[2048]{0:T(1024)S(1)}, f32[2048]{0:T(1024)}, u32[]{:S(2)}) copy-start(f32[2048]{0:T(1024)} %param.17) | copy-start | bytes 24580
  39.0 100.3 %all-to-all-start = ((bf16[8,64,8192]{2,1,0:T(8,128)(2,1)}), bf16[8,64,8192]{2,1,0:T(8,128)(2,1)}, u32[]{:S(2)}, u32[]{:S(2)}) async-start(bf16[8,64,8192]{2,1,0:T(8,128)(2,1)} %bitcast.92), calls=%async_computation | async-start | bytes 16777216 | tf_op jit(solution)/shard_map/all_to_all | solution.py:140
  139.3 7.9 %copy-start.6 = (f32[8192]{0:T(1024)S(1)}, f32[8192]{0:T(1024)}, u32[]{:S(2)}) copy-start(f32[8192]{0:T(1024)} %param.15) | copy-start | bytes 98308
  145.2 2.0 %copy-start.4 = (bf16[256,8192]{1,0:T(8,128)(2,1)}, bf16[256,8192]{1,0:T(8,128)(2,1)S(1)}, u32[]{:S(2)}) copy-start(bf16[256,8192]{1,0:T(8,128)(2,1)S(1)} %get-tuple-element.59) | copy-start | bytes 12582916
  150.4 12.6 %collective-permute-start = (bf16[256,8192]{1,0:T(8,128)(2,1)}, bf16[256,8192]{1,0:T(8,128)(2,1)}, u32[]{:S(2)}, u32[]{:S(2)}) collective-permute-start(bf16[256,8192]{1,0:T(8,128)(2,1)} %fusion.2), channel_id=1, source_target_pairs={{0,1},{1,0},{2,3},{3,2},{4,5},{5,4},{6,7},{7,6},{8,9},{9,8},{10,11... | collective-permute-start | bytes 12582920 | tf_op jit(solution)/shard_map/ppermute | solution.py:151
  151.2 14.6 %copy-start.8 = (bf16[8192,1024]{1,0:T(8,128)(2,1)S(1)}, bf16[8192,1024]{1,0:T(8,128)(2,1)}, u32[]{:S(2)}) copy-start(bf16[8192,1024]{1,0:T(8,128)(2,1)} %all-gather.2.cloned.1.call-done) | copy-start | bytes 50331652
  163.0 12.4 %collective-permute-start.1 = (bf16[256,256]{1,0:T(8,128)(2,1)S(1)}, bf16[256,256]{1,0:T(8,128)(2,1)S(1)}, u32[]{:S(2)}, u32[]{:S(2)}) collective-permute-start(bf16[256,256]{1,0:T(8,128)(2,1)S(1)} %get-tuple-element.41), channel_id=1, source_target_pairs={{0,2},{2,4},{4,6},{6,0},{1,3},{3,5},{5,7},{7,1},{8,10},{10,12},{12... | collective-permute-start | bytes 393224 | tf_op jit(solution)/shard_map/ppermute | solution.py:163
  163.4 14.1 %collective-permute-start.2 = (bf16[256,256]{1,0:T(8,128)(2,1)S(1)}, bf16[256,256]{1,0:T(8,128)(2,1)S(1)}, u32[]{:S(2)}, u32[]{:S(2)}) collective-permute-start(bf16[256,256]{1,0:T(8,128)(2,1)S(1)} %get-tuple-element.40), channel_id=1, source_target_pairs={{0,4},{2,6},{4,0},{6,2},{1,5},{3,7},{5,1},{7,3},{8,12},{10,14},{12... | collective-permute-start | bytes 393224 | tf_op jit(solution)/shard_map/ppermute | solution.py:163
  165.1 12.3 %collective-permute-start.3 = (bf16[256,256]{1,0:T(8,128)(2,1)S(1)}, bf16[256,256]{1,0:T(8,128)(2,1)S(1)}, u32[]{:S(2)}, u32[]{:S(2)}) collective-permute-start(bf16[256,256]{1,0:T(8,128)(2,1)S(1)} %get-tuple-element.39), channel_id=1, source_target_pairs={{0,6},{2,0},{4,2},{6,4},{1,7},{3,1},{5,3},{7,5},{8,14},{10,8},{12,... | collective-permute-start | bytes 393224 | tf_op jit(solution)/shard_map/ppermute | solution.py:163
  172.8 6.2 %collective-permute-start.4 = (bf16[256,256]{1,0:T(8,128)(2,1)S(1)}, bf16[256,256]{1,0:T(8,128)(2,1)S(1)}, u32[]{:S(2)}, u32[]{:S(2)}) collective-permute-start(bf16[256,256]{1,0:T(8,128)(2,1)S(1)} %get-tuple-element.38), channel_id=1, source_target_pairs={{0,2},{2,4},{4,6},{6,0},{1,3},{3,5},{5,7},{7,1},{8,10},{10,12},{12... | collective-permute-start | bytes 393224 | tf_op jit(solution)/shard_map/ppermute | solution.py:163
  173.6 7.4 %collective-permute-start.5 = (bf16[256,256]{1,0:T(8,128)(2,1)S(1)}, bf16[256,256]{1,0:T(8,128)(2,1)S(1)}, u32[]{:S(2)}, u32[]{:S(2)}) collective-permute-start(bf16[256,256]{1,0:T(8,128)(2,1)S(1)} %get-tuple-element.37), channel_id=1, source_target_pairs={{0,4},{2,6},{4,0},{6,2},{1,5},{3,7},{5,1},{7,3},{8,12},{10,14},{12... | collective-permute-start | bytes 393224 | tf_op jit(solution)/shard_map/ppermute | solution.py:163
  175.4 6.3 %collective-permute-start.6 = (bf16[256,256]{1,0:T(8,128)(2,1)S(1)}, bf16[256,256]{1,0:T(8,128)(2,1)S(1)}, u32[]{:S(2)}, u32[]{:S(2)}) collective-permute-start(bf16[256,256]{1,0:T(8,128)(2,1)S(1)} %get-tuple-element.36), channel_id=1, source_target_pairs={{0,6},{2,0},{4,2},{6,4},{1,7},{3,1},{5,3},{7,5},{8,14},{10,8},{12,... | collective-permute-start | bytes 393224 | tf_op jit(solution)/shard_map/ppermute | solution.py:163
Sparse Core Ops, SparseCore 0:
  12.3 114.6 all-gather.1

commit v21 on v18

--- a/solution.py
+++ b/solution.py
@@ -155,7 +155,7 @@
 
     def send_half(blocks, half, by_heads):
         by_heads = lax.dynamic_update_slice(by_heads, blocks[0][None, None], (here, half, 0, 0))
-        for step in range(1, chips):
+        for step in sorted(range(1, chips), key=lambda d: -min(d, chips - d)):
             arrived = lax.ppermute(
                 blocks[step], "cx", perm=[(i, (i + step) % chips) for i in range(chips)]
             )

time: 172 us -> 172 us (level)
  transfers between devices with their start and end apart: 9 -> 9, of which waited for: 4 -> 3; matrix products, arithmetic and copies ran while one was open for 28% -> 28% of each run, Pallas kernels for 0% -> 0%
where the time goes in v21:
time: 172 us; the launch traced here: 171 us
  waiting for transfers between devices  85.9 us (50%)
  matrix products  35.6 us (21%)
  starting transfers between devices  14.6 us (8%)
  between operations  14.3 us (8%)
  local copies, waits for them, and re-layouts  12.2 us (7%)
  other arithmetic  8.71 us (5%)
    all_to_all x1, waiting for transfers between devices, on_device(): lax.all_to_all(outgoing.reshape(peer_count, capacity, -1), CTX, split_axi...  81.5 us
    dot_general x2, matrix products, project(): jnp.dot(rows, gathered_weight, preferred_element_type=jnp.float32)  18.5 us
    dot_general x2, matrix products, select_rows(): jnp.dot(picks.astype(rows.dtype), rows, preferred_element_type=jnp.float32)  13.7 us
    ppermute x6, starting transfers between devices, send_half(): lax.ppermute(blocks[step], 'cx', perm=[(i, (i + step) % chips) for i in r...  7.34 us
    all_to_all x1, starting transfers between devices, on_device(): lax.all_to_all(outgoing.reshape(peer_count, capacity, -1), CTX, split_axi...  6.39 us
    gather x1, local copies, waits for them, and re-layouts, on_device(): local_bias = jnp.take(kv_bias, columns, mode='clip')  6.15 us
    add x1, other arithmetic, on_device(): index = source * capacity + shift + within  4.97 us
    ppermute x6, waiting for transfers between devices, send_half(): lax.ppermute(blocks[step], 'cx', perm=[(i, (i + step) % chips) for i in r...  4.36 us
  transfers between devices with their start and end apart: 9, of which 3 were waited for; matrix products, arithmetic and copies ran while one was open for 28% of the time, Pallas kernels for 0%

profile of v21, /device:TPU:1, one launch (start us, length us, event | category | flops | bytes accessed | tf_op | source)
XLA Modules:
  0.0 171.3 jit_solution(16931826679296631398)
XLA Ops:
  7.2 0.0 copy-start
  7.2 0.0 copy-start.3
  7.2 0.0 copy-start.5
  7.2 0.0 all-gather.2.cloned.1.call-start
  7.3 1.5 copy-done
  8.8 3.4 %fusion.7 = bf16[512,1024]{1,0:T(8,128)(2,1)} fusion(bf16[512,2048]{1,0:T(8,128)(2,1)S(1)} %copy-done, s32[1024]{0:T(1024)S(1)} %get-tuple-element.52), kind=kOutput, calls=%fused_computation.15 | convolution fusion | flops 2150105088 | bytes 3149824 | tf_op jit(solution)/shard_map/dot_general | solution.py:119
  12.2 0.0 all-gather.2.cloned.1.call-update
  12.2 0.0 copy-done.3
  12.2 0.2 reduce_window_sum.23
  12.4 0.0 copy-done.5
  12.4 0.1 select_reduce_fusion.1
  12.5 0.1 iota_add_fusion
  12.6 0.1 add.174
  12.7 7.8 %convolution_convert_fusion = bf16[512,8192]{1,0:T(8,128)(2,1)} fusion(bf16[1,256,8192]{2,1,0:T(8,128)(2,1)} %param.12, s32[512]{0:T(512)S(1)} %add.174), kind=kOutput, calls=%fused_computation.1 | convolution fusion | flops 2151809024 | bytes 12584960 | tf_op jit(solution)/shard_map/dot_general | solution.py:92
  20.5 0.0 copy-start.1
  20.5 6.4 %all-to-all-start = ((bf16[8,64,8192]{2,1,0:T(8,128)(2,1)}), bf16[8,64,8192]{2,1,0:T(8,128)(2,1)}, u32[]{:S(2)}, u32[]{:S(2)}) async-start(bf16[8,64,8192]{2,1,0:T(8,128)(2,1)} %bitcast.73), calls=%async_computation | async-start | bytes 16777216 | tf_op jit(solution)/shard_map/all_to_all | solution.py:136
  26.9 0.0 copy-done.1
  26.9 6.2 %gather_fusion = f32[1024]{0:T(1024)S(1)} fusion(f32[2048]{0:T(1024)S(1)} %copy-done.1, s32[1024]{0:T(1024)S(1)} %get-tuple-element.53), kind=kCustom, calls=%fused_computation | custom fusion | bytes 12288 | tf_op jit(solution)/shard_map/jit(_take)/gather | solution.py:122
  33.1 0.2 dynamic-slice_reduce_fusion
  33.3 0.2 dynamic-slice_reduce_fusion.2
  33.5 0.6 fusion.42
  34.1 0.1 convert_reduce_fusion
  34.2 0.1 select_reduce_fusion.3
  34.2 5.0 %subtract_add_fusion = s32[256]{0:T(256)S(1)} fusion(s32[256]{0:T(256)S(1)} %get-tuple-element.35, s32[256]{0:T(256)S(1)} %get-tuple-element.34, s32[256]{0:T(256)S(1)} %convert_reduce_fusion, s32[]{:T(128)} %bitcast.2, s32[]{:T(128)} %bitcast.3, s32[]{:T(128)} %bitcast.4, s32[]{:T(128)} %bitcast.5, s32[]{:T(128)} %bitcast.6, s32[]{:T(128)} %bitcast.7, ...), kind=kLoop, calls=%fused_computation.109 | loop fusion | flops 4864 | bytes 4128 | tf_op jit(solution)/shard_map/add | solution.py:143
  39.2 81.5 %all-to-all-done = bf16[8,64,8192]{2,1,0:T(8,128)(2,1)} async-done(((bf16[8,64,8192]{2,1,0:T(8,128)(2,1)}), bf16[8,64,8192]{2,1,0:T(8,128)(2,1)}, u32[]{:S(2)}, u32[]{:S(2)}) %all-to-all-start) | async-done | bytes 8388640 | tf_op jit(solution)/shard_map/all_to_all | solution.py:136
  120.7 0.0 copy-start.4
  120.7 5.9 %fusion = (f32[256]{0:T(256)S(1)}, bf16[256,8192]{1,0:T(8,128)(2,1)S(1)}) fusion(bf16[512,8192]{1,0:T(8,128)(2,1)} %bitcast.14, s32[256]{0:T(256)S(1)} %subtract_add_fusion), kind=kOutput, calls=%fused_computation.5 | convolution fusion | flops 2156003072 | bytes 12584960 | tf_op jit(solution)/shard_map/dot_general | solution.py:92
  126.6 0.0 copy-start.2
  126.6 2.0 %copy-done.2 = bf16[256,8192]{1,0:T(8,128)(2,1)} copy-done((bf16[256,8192]{1,0:T(8,128)(2,1)}, bf16[256,8192]{1,0:T(8,128)(2,1)S(1)}, u32[]{:S(2)}) %copy-start.2) | copy-done | bytes 4194328
  128.6 0.0 copy-done.4
  128.6 3.2 %fusion.2 = bf16[256,8192]{1,0:T(8,128)(2,1)} fusion(bf16[256,8192]{1,0:T(8,128)(2,1)S(1)} %get-tuple-element.51, f32[8192]{0:T(1024)S(1)} %copy-done.4, f32[256]{0:T(256)S(1)} %add_rsqrt_fusion), kind=kLoop, calls=%fused_computation.7 | loop fusion | flops 8388608 | bytes 8422400 | tf_op jit(solution)/shard_map/convert_element_type | solution.py:37
  131.8 0.9 collective-permute-start
  132.7 0.0 all-gather.2.cloned.1.call-done
  132.7 0.0 copy-start.6
  132.7 11.7 %fusion.8 = bf16[256,1024]{1,0:T(8,128)(2,1)S(1)} fusion(bf16[256,8192]{1,0:T(8,128)(2,1)} %fusion.2, bf16[8192,1024]{1,0:T(8,128)(2,1)} %all-gather.2.cloned.1.call-done, f32[1024]{0:T(1024)S(1)} %gather_fusion), kind=kOutput, calls=%fused_computation.16 | convolution fusion | flops 4295491584 | bytes 21499904 | tf_op jit(solution)/shard_map/dot_general | solution.py:150
  144.4 0.0 collective-permute-done
  144.4 0.1 collective-permute-start.1
  144.6 1.4 collective-permute-start.2
  146.0 1.3 collective-permute-start.3
  147.3 0.0 copy-done.6
  147.3 6.8 %fusion.9 = bf16[256,1024]{1,0:T(8,128)(2,1)S(1)} fusion(bf16[256,8192]{1,0:T(8,128)(2,1)} %collective-permute-done, bf16[8192,1024]{1,0:T(8,128)(2,1)S(1)} %copy-done.6, f32[1024]{0:T(1024)S(1)} %gather_fusion), kind=kOutput, calls=%fused_computation.17 | convolution fusion | flops 4295491584 | bytes 21499904 | tf_op jit(solution)/shard_map/dot_general | solution.py:150
  154.2 1.8 %collective-permute-start.4 = (bf16[256,256]{1,0:T(8,128)(2,1)S(1)}, bf16[256,256]{1,0:T(8,128)(2,1)S(1)}, u32[]{:S(2)}, u32[]{:S(2)}) collective-permute-start(bf16[256,256]{1,0:T(8,128)(2,1)S(1)} %get-tuple-element.38), channel_id=1, source_target_pairs={{0,4},{2,6},{4,0},{6,2},{1,5},{3,7},{5,1},{7,3},{8,12},{10,14},{12... | collective-permute-start | bytes 393224 | tf_op jit(solution)/shard_map/ppermute | solution.py:159
  155.9 0.3 collective-permute-start.5
  156.2 0.1 broadcast_in_dim.66
  156.3 0.0 collective-permute-done.1
  156.3 2.4 %collective-permute-start.6 = (bf16[256,256]{1,0:T(8,128)(2,1)S(1)}, bf16[256,256]{1,0:T(8,128)(2,1)S(1)}, u32[]{:S(2)}, u32[]{:S(2)}) collective-permute-start(bf16[256,256]{1,0:T(8,128)(2,1)S(1)} %get-tuple-element.36), channel_id=1, source_target_pairs={{0,6},{2,0},{4,2},{6,4},{1,7},{3,1},{5,3},{7,5},{8,14},{10,8},{12,... | collective-permute-start | bytes 393224 | tf_op jit(solution)/shard_map/ppermute | solution.py:159
  158.8 0.0 collective-permute-done.2
  158.8 0.0 collective-permute-done.3
  158.9 1.0 collective-permute-done.4
  160.0 3.3 %collective-permute-done.5 = bf16[256,256]{1,0:T(8,128)(2,1)S(1)} collective-permute-done((bf16[256,256]{1,0:T(8,128)(2,1)S(1)}, bf16[256,256]{1,0:T(8,128)(2,1)S(1)}, u32[]{:S(2)}, u32[]{:S(2)}) %collective-permute-start.5) | collective-permute-done | bytes 131104 | tf_op jit(solution)/shard_map/ppermute | solution.py:159
  163.3 0.0 collective-permute-done.6
  163.3 1.1 reshape.68
  (19 shorter events, 0.3 us)
Async XLA Ops:
  7.2 1.6 copy-start
  7.2 5.0 %copy-start.3 = (s32[1,8,8]{2,1,0:T(8,128)S(1)}, s32[1,8,8]{2,1,0:T(8,128)}, u32[]{:S(2)}) copy-start(s32[1,8,8]{2,1,0:T(8,128)} %param.13) | copy-start | bytes 772
  7.2 5.2 %copy-start.5 = (s32[1,8,8]{2,1,0:T(8,128)S(1)}, s32[1,8,8]{2,1,0:T(8,128)}, u32[]{:S(2)}) copy-start(s32[1,8,8]{2,1,0:T(8,128)} %param.14) | copy-start | bytes 772
  7.2 125.5 %all-gather.2.cloned.1.call-start = ((), (), s32[]{:S(2)}) async-start(), calls=%async_computation.1 | async-start | bytes 17825792 | tf_op jit(solution)/shard_map/all_gather | solution.py:125
  20.5 6.4 %copy-start.1 = (f32[2048]{0:T(1024)S(1)}, f32[2048]{0:T(1024)}, u32[]{:S(2)}) copy-start(f32[2048]{0:T(1024)} %param.17) | copy-start | bytes 24580
  20.5 100.3 %all-to-all-start = ((bf16[8,64,8192]{2,1,0:T(8,128)(2,1)}), bf16[8,64,8192]{2,1,0:T(8,128)(2,1)}, u32[]{:S(2)}, u32[]{:S(2)}) async-start(bf16[8,64,8192]{2,1,0:T(8,128)(2,1)} %bitcast.73), calls=%async_computation | async-start | bytes 16777216 | tf_op jit(solution)/shard_map/all_to_all | solution.py:136
  120.7 7.9 %copy-start.4 = (f32[8192]{0:T(1024)S(1)}, f32[8192]{0:T(1024)}, u32[]{:S(2)}) copy-start(f32[8192]{0:T(1024)} %param.15) | copy-start | bytes 98308
  126.6 2.0 %copy-start.2 = (bf16[256,8192]{1,0:T(8,128)(2,1)}, bf16[256,8192]{1,0:T(8,128)(2,1)S(1)}, u32[]{:S(2)}) copy-start(bf16[256,8192]{1,0:T(8,128)(2,1)S(1)} %get-tuple-element.51) | copy-start | bytes 12582916
  131.8 12.6 %collective-permute-start = (bf16[256,8192]{1,0:T(8,128)(2,1)}, bf16[256,8192]{1,0:T(8,128)(2,1)}, u32[]{:S(2)}, u32[]{:S(2)}) collective-permute-start(bf16[256,8192]{1,0:T(8,128)(2,1)} %fusion.2), channel_id=1, source_target_pairs={{0,1},{1,0},{2,3},{3,2},{4,5},{5,4},{6,7},{7,6},{8,9},{9,8},{10,11... | collective-permute-start | bytes 12582920 | tf_op jit(solution)/shard_map/ppermute | solution.py:147
  132.7 14.6 %copy-start.6 = (bf16[8192,1024]{1,0:T(8,128)(2,1)S(1)}, bf16[8192,1024]{1,0:T(8,128)(2,1)}, u32[]{:S(2)}) copy-start(bf16[8192,1024]{1,0:T(8,128)(2,1)} %all-gather.2.cloned.1.call-done) | copy-start | bytes 50331652
  144.4 11.9 %collective-permute-start.1 = (bf16[256,256]{1,0:T(8,128)(2,1)S(1)}, bf16[256,256]{1,0:T(8,128)(2,1)S(1)}, u32[]{:S(2)}, u32[]{:S(2)}) collective-permute-start(bf16[256,256]{1,0:T(8,128)(2,1)S(1)} %get-tuple-element.41), channel_id=1, source_target_pairs={{0,4},{2,6},{4,0},{6,2},{1,5},{3,7},{5,1},{7,3},{8,12},{10,14},{12... | collective-permute-start | bytes 393224 | tf_op jit(solution)/shard_map/ppermute | solution.py:159
  144.6 14.2 %collective-permute-start.2 = (bf16[256,256]{1,0:T(8,128)(2,1)S(1)}, bf16[256,256]{1,0:T(8,128)(2,1)S(1)}, u32[]{:S(2)}, u32[]{:S(2)}) collective-permute-start(bf16[256,256]{1,0:T(8,128)(2,1)S(1)} %get-tuple-element.40), channel_id=1, source_target_pairs={{0,2},{2,4},{4,6},{6,0},{1,3},{3,5},{5,7},{7,1},{8,10},{10,12},{12... | collective-permute-start | bytes 393224 | tf_op jit(solution)/shard_map/ppermute | solution.py:159
  146.0 12.9 %collective-permute-start.3 = (bf16[256,256]{1,0:T(8,128)(2,1)S(1)}, bf16[256,256]{1,0:T(8,128)(2,1)S(1)}, u32[]{:S(2)}, u32[]{:S(2)}) collective-permute-start(bf16[256,256]{1,0:T(8,128)(2,1)S(1)} %get-tuple-element.39), channel_id=1, source_target_pairs={{0,6},{2,0},{4,2},{6,4},{1,7},{3,1},{5,3},{7,5},{8,14},{10,8},{12,... | collective-permute-start | bytes 393224 | tf_op jit(solution)/shard_map/ppermute | solution.py:159
  154.2 5.8 %collective-permute-start.4 = (bf16[256,256]{1,0:T(8,128)(2,1)S(1)}, bf16[256,256]{1,0:T(8,128)(2,1)S(1)}, u32[]{:S(2)}, u32[]{:S(2)}) collective-permute-start(bf16[256,256]{1,0:T(8,128)(2,1)S(1)} %get-tuple-element.38), channel_id=1, source_target_pairs={{0,4},{2,6},{4,0},{6,2},{1,5},{3,7},{5,1},{7,3},{8,12},{10,14},{12... | collective-permute-start | bytes 393224 | tf_op jit(solution)/shard_map/ppermute | solution.py:159
  155.9 7.3 %collective-permute-start.5 = (bf16[256,256]{1,0:T(8,128)(2,1)S(1)}, bf16[256,256]{1,0:T(8,128)(2,1)S(1)}, u32[]{:S(2)}, u32[]{:S(2)}) collective-permute-start(bf16[256,256]{1,0:T(8,128)(2,1)S(1)} %get-tuple-element.37), channel_id=1, source_target_pairs={{0,2},{2,4},{4,6},{6,0},{1,3},{3,5},{5,7},{7,1},{8,10},{10,12},{12... | collective-permute-start | bytes 393224 | tf_op jit(solution)/shard_map/ppermute | solution.py:159
  156.3 7.0 %collective-permute-start.6 = (bf16[256,256]{1,0:T(8,128)(2,1)S(1)}, bf16[256,256]{1,0:T(8,128)(2,1)S(1)}, u32[]{:S(2)}, u32[]{:S(2)}) collective-permute-start(bf16[256,256]{1,0:T(8,128)(2,1)S(1)} %get-tuple-element.36), channel_id=1, source_target_pairs={{0,6},{2,0},{4,2},{6,4},{1,7},{3,1},{5,3},{7,5},{8,14},{10,8},{12,... | collective-permute-start | bytes 393224 | tf_op jit(solution)/shard_map/ppermute | solution.py:159
Sparse Core Ops, SparseCore 0:
  12.3 114.6 all-gather.1

commit v22 on v21

--- a/solution.py
+++ b/solution.py
@@ -144,7 +144,12 @@
     local_bias, index = lax.optimization_barrier((local_bias, index))
     moved_rows = select_rows(arriving_rows.reshape(peer_count * capacity, -1), index)
     normed = rms_normed(moved_rows, norm_gain)
-    sibling_rows = lax.ppermute(normed, "cc", perm=[(0, 1), (1, 0)])
+    split = row_count // 2
+    sibling_rows = jnp.concatenate(
+        [lax.ppermute(normed[:split], "cc", perm=[(0, 1), (1, 0)]),
+         lax.ppermute(normed[split:], "cc", perm=[(0, 1), (1, 0)])],
+        axis=0,
+    )
 
     def project(rows):
         products = jnp.dot(rows, gathered_weight, preferred_element_type=jnp.float32)

time: 172 us -> 181 us (1.052)
  waiting for transfers between devices: 85.9 us -> 92.7 us
  matrix products: 35.6 us -> 33.3 us
  other arithmetic: 8.71 us -> 10.9 us
  local copies, waits for them, and re-layouts: 12.2 us -> 14.2 us
    ppermute x1 -> x2, waiting for transfers between devices: 0.01 us -> 7.12 us  [the longest x1 6.95 us: on_device(): lax.ppermute(normed[:split], 'cc', perm=[(0, 1), (1, 0)])]
    concatenate x0 -> x1, other arithmetic: none -> 4.26 us  [on_device(): jnp.concatenate([lax.ppermute(normed[:split], 'cc', perm=[(0, 1), (1, 0)]...]
    slice x0 -> x1, local copies, waits for them, and re-layouts: none -> 2.66 us  [on_device(): normed[:split]]
    dot_general x2, matrix products: 18.5 us -> 16.2 us  [project(): jnp.dot(rows, gathered_weight, preferred_element_type=jnp.float32)]
    convert_element_type x1, other arithmetic: 3.15 us -> 1.19 us  [rms_normed(): return (as_float * inverse_rms * norm_gain[None, :]).astype(jnp.bfloat16)]
  transfers between devices with their start and end apart: 9 -> 10, of which waited for: 3 -> 5; matrix products, arithmetic and copies ran while one was open for 28% -> 22% of each run, Pallas kernels for 0% -> 0%
where the time goes in v22:
time: 181 us; the launch traced here: 180 us
  waiting for transfers between devices  92.7 us (51%)
  matrix products  33.3 us (18%)
  starting transfers between devices  14.6 us (8%)
  between operations  14.3 us (8%)
  local copies, waits for them, and re-layouts  14.2 us (8%)
  other arithmetic  10.9 us (6%)
    all_to_all x1, waiting for transfers between devices, on_device(): lax.all_to_all(outgoing.reshape(peer_count, capacity, -1), CTX, split_axi...  81.6 us
    dot_general x2, matrix products, project(): jnp.dot(rows, gathered_weight, preferred_element_type=jnp.float32)  16.2 us
    dot_general x2, matrix products, select_rows(): jnp.dot(picks.astype(rows.dtype), rows, preferred_element_type=jnp.float32)  13.7 us
    ppermute x6, starting transfers between devices, send_half(): lax.ppermute(blocks[step], 'cx', perm=[(i, (i + step) % chips) for i in r...  7.34 us
    ppermute x1, waiting for transfers between devices, on_device(): lax.ppermute(normed[:split], 'cc', perm=[(0, 1), (1, 0)])  6.95 us
    all_to_all x1, starting transfers between devices, on_device(): lax.all_to_all(outgoing.reshape(peer_count, capacity, -1), CTX, split_axi...  6.39 us
    gather x1, local copies, waits for them, and re-layouts, on_device(): local_bias = jnp.take(kv_bias, columns, mode='clip')  6.15 us
    add x1, other arithmetic, on_device(): index = source * capacity + shift + within  4.92 us
  transfers between devices with their start and end apart: 10, of which 5 were waited for; matrix products, arithmetic and copies ran while one was open for 22% of the time, Pallas kernels for 0%

profile of v22, /device:TPU:1, one launch (start us, length us, event | category | flops | bytes accessed | tf_op | source)
XLA Modules:
  0.0 180.1 jit_solution(14764138222924667526)
XLA Ops:
  7.2 0.0 copy-start
  7.2 0.0 all-gather.2.cloned.1.call-start
  7.3 1.5 copy-done
  8.8 0.0 copy-start.6
  8.8 0.0 copy-start.8
  8.8 3.4 %fusion.7 = bf16[512,1024]{1,0:T(8,128)(2,1)} fusion(bf16[512,2048]{1,0:T(8,128)(2,1)S(1)} %copy-done, s32[1024]{0:T(1024)S(1)} %get-tuple-element.54), kind=kOutput, calls=%fused_computation.16 | convolution fusion | flops 2150105088 | bytes 3149824 | tf_op jit(solution)/shard_map/dot_general | solution.py:119
  12.2 0.0 all-gather.2.cloned.1.call-update
  12.2 0.0 copy-done.6
  12.2 0.2 reduce_window_sum.23
  12.4 0.0 copy-done.8
  12.4 0.1 select_reduce_fusion.1
  12.5 0.1 iota_add_fusion
  12.6 0.1 add.174
  12.7 7.8 %convolution_convert_fusion = bf16[512,8192]{1,0:T(8,128)(2,1)} fusion(bf16[1,256,8192]{2,1,0:T(8,128)(2,1)} %param.12, s32[512]{0:T(512)S(1)} %add.174), kind=kOutput, calls=%fused_computation.1 | convolution fusion | flops 2151809024 | bytes 12584960 | tf_op jit(solution)/shard_map/dot_general | solution.py:92
  20.5 0.0 copy-start.2
  20.5 6.4 %all-to-all-start = ((bf16[8,64,8192]{2,1,0:T(8,128)(2,1)}), bf16[8,64,8192]{2,1,0:T(8,128)(2,1)}, u32[]{:S(2)}, u32[]{:S(2)}) async-start(bf16[8,64,8192]{2,1,0:T(8,128)(2,1)} %bitcast.73), calls=%async_computation | async-start | bytes 16777216 | tf_op jit(solution)/shard_map/all_to_all | solution.py:136
  26.9 0.0 copy-done.2
  26.9 6.2 %gather_fusion = f32[1024]{0:T(1024)S(1)} fusion(f32[2048]{0:T(1024)S(1)} %copy-done.2, s32[1024]{0:T(1024)S(1)} %get-tuple-element.55), kind=kCustom, calls=%fused_computation | custom fusion | bytes 12288 | tf_op jit(solution)/shard_map/jit(_take)/gather | solution.py:122
  33.1 0.2 dynamic-slice_reduce_fusion
  33.3 0.2 dynamic-slice_reduce_fusion.2
  33.5 0.6 fusion.43
  34.1 0.1 convert_reduce_fusion
  34.2 0.1 select_reduce_fusion.3
  34.2 4.9 %subtract_add_fusion = s32[256]{0:T(256)S(1)} fusion(s32[256]{0:T(256)S(1)} %get-tuple-element.35, s32[256]{0:T(256)S(1)} %get-tuple-element.34, s32[256]{0:T(256)S(1)} %convert_reduce_fusion, s32[]{:T(128)} %bitcast.2, s32[]{:T(128)} %bitcast.3, s32[]{:T(128)} %bitcast.4, s32[]{:T(128)} %bitcast.5, s32[]{:T(128)} %bitcast.6, s32[]{:T(128)} %bitcast.7, ...), kind=kLoop, calls=%fused_computation.110 | loop fusion | flops 4864 | bytes 4128 | tf_op jit(solution)/shard_map/add | solution.py:143
  39.2 81.6 %all-to-all-done = bf16[8,64,8192]{2,1,0:T(8,128)(2,1)} async-done(((bf16[8,64,8192]{2,1,0:T(8,128)(2,1)}), bf16[8,64,8192]{2,1,0:T(8,128)(2,1)}, u32[]{:S(2)}, u32[]{:S(2)}) %all-to-all-start) | async-done | bytes 8388640 | tf_op jit(solution)/shard_map/all_to_all | solution.py:136
  120.7 0.0 copy-start.7
  120.7 5.9 %fusion = (f32[256]{0:T(256)S(1)}, bf16[256,8192]{1,0:T(8,128)(2,1)S(1)}) fusion(bf16[512,8192]{1,0:T(8,128)(2,1)} %bitcast.14, s32[256]{0:T(256)S(1)} %subtract_add_fusion), kind=kOutput, calls=%fused_computation.5 | convolution fusion | flops 2156003072 | bytes 12584960 | tf_op jit(solution)/shard_map/dot_general | solution.py:92
  126.6 0.0 copy-start.4
  126.6 0.0 copy-done.7
  126.7 1.2 fusion.2
  127.9 0.8 copy-done.4
  128.6 0.0 copy-start.3
  128.6 2.7 %fusion.42 = (bf16[128,8192]{1,0:T(8,128)(2,1)}, bf16[128,8192]{1,0:T(8,128)(2,1)}) fusion(bf16[256,8192]{1,0:T(8,128)(2,1)S(1)} %fusion.2), kind=kLoop, calls=%fused_computation.113 | loop fusion | bytes 8388608 | tf_op jit(solution)/shard_map/slice | solution.py:149
  131.3 0.5 copy-done.3
  131.8 0.9 collective-permute-start
  132.7 0.0 collective-permute-start.1
  132.7 7.0 %collective-permute-done = bf16[128,8192]{1,0:T(8,128)(2,1)S(1)} collective-permute-done((bf16[128,8192]{1,0:T(8,128)(2,1)}, bf16[128,8192]{1,0:T(8,128)(2,1)S(1)}, u32[]{:S(2)}, u32[]{:S(2)}) %collective-permute-start) | collective-permute-done | bytes 2097184 | tf_op jit(solution)/shard_map/ppermute | solution.py:149
  139.7 0.2 collective-permute-done.1
  139.8 4.3 %pad_maximum_fusion = bf16[256,8192]{1,0:T(8,128)(2,1)} fusion(bf16[128,8192]{1,0:T(8,128)(2,1)} %collective-permute-done.1, bf16[128,8192]{1,0:T(8,128)(2,1)S(1)} %collective-permute-done), kind=kLoop, calls=%fused_computation.10 | loop fusion | flops 8388608 | bytes 8388608 | tf_op jit(solution)/shard_map/concatenate | solution.py:148
  144.1 0.0 all-gather.2.cloned.1.call-done
  144.1 0.0 copy-start.5
  144.1 0.0 copy-start.9
  144.1 11.7 %fusion.8 = bf16[256,1024]{1,0:T(8,128)(2,1)S(1)} fusion(bf16[256,8192]{1,0:T(8,128)(2,1)} %copy-done.3, bf16[8192,1024]{1,0:T(8,128)(2,1)} %all-gather.2.cloned.1.call-done, f32[1024]{0:T(1024)S(1)} %gather_fusion), kind=kOutput, calls=%fused_computation.17 | convolution fusion | flops 4295491584 | bytes 21499904 | tf_op jit(solution)/shard_map/dot_general | solution.py:155
  155.8 0.1 collective-permute-start.2
  156.0 1.4 collective-permute-start.3
  157.4 1.3 collective-permute-start.4
  158.7 0.0 copy-done.5
  158.7 0.0 copy-done.9
  158.7 0.0 copy-start.1
  158.7 4.5 %fusion.9 = bf16[256,1024]{1,0:T(8,128)(2,1)S(1)} fusion(bf16[256,8192]{1,0:T(8,128)(2,1)S(1)} %copy-done.5, bf16[8192,1024]{1,0:T(8,128)(2,1)S(1)} %copy-done.9, f32[1024]{0:T(1024)S(1)} %gather_fusion), kind=kOutput, calls=%fused_computation.18 | convolution fusion | flops 4295491584 | bytes 21499904 | tf_op jit(solution)/shard_map/dot_general | solution.py:155
  163.3 1.8 collective-permute-start.5
  165.1 0.3 collective-permute-start.6
  165.4 0.1 broadcast_in_dim.66
  165.5 0.0 collective-permute-done.2
  165.5 2.4 %collective-permute-start.7 = (bf16[256,256]{1,0:T(8,128)(2,1)S(1)}, bf16[256,256]{1,0:T(8,128)(2,1)S(1)}, u32[]{:S(2)}, u32[]{:S(2)}) collective-permute-start(bf16[256,256]{1,0:T(8,128)(2,1)S(1)} %get-tuple-element.38), channel_id=1, source_target_pairs={{0,6},{2,0},{4,2},{6,4},{1,7},{3,1},{5,3},{7,5},{8,14},{10,8},{12,... | collective-permute-start | bytes 393224 | tf_op jit(solution)/shard_map/ppermute | solution.py:164
  167.9 0.0 collective-permute-done.3
  168.0 0.0 collective-permute-done.4
  168.0 0.7 collective-permute-done.5
  168.7 3.3 %collective-permute-done.6 = bf16[256,256]{1,0:T(8,128)(2,1)S(1)} collective-permute-done((bf16[256,256]{1,0:T(8,128)(2,1)S(1)}, bf16[256,256]{1,0:T(8,128)(2,1)S(1)}, u32[]{:S(2)}, u32[]{:S(2)}) %collective-permute-start.6) | collective-permute-done | bytes 131104 | tf_op jit(solution)/shard_map/ppermute | solution.py:164
  172.1 0.0 collective-permute-done.7
  172.1 1.1 reshape.68
  173.2 0.0 copy-done.1
  (19 shorter events, 0.3 us)
Async XLA Ops:
  7.2 1.6 copy-start
  7.2 136.9 %all-gather.2.cloned.1.call-start = ((), (), s32[]{:S(2)}) async-start(), calls=%async_computation.1 | async-start | bytes 17825792 | tf_op jit(solution)/shard_map/all_gather | solution.py:125
  8.8 3.5 %copy-start.6 = (s32[1,8,8]{2,1,0:T(8,128)S(1)}, s32[1,8,8]{2,1,0:T(8,128)}, u32[]{:S(2)}) copy-start(s32[1,8,8]{2,1,0:T(8,128)} %param.13) | copy-start | bytes 772
  8.8 3.6 %copy-start.8 = (s32[1,8,8]{2,1,0:T(8,128)S(1)}, s32[1,8,8]{2,1,0:T(8,128)}, u32[]{:S(2)}) copy-start(s32[1,8,8]{2,1,0:T(8,128)} %param.14) | copy-start | bytes 772
  20.5 6.4 %copy-start.2 = (f32[2048]{0:T(1024)S(1)}, f32[2048]{0:T(1024)}, u32[]{:S(2)}) copy-start(f32[2048]{0:T(1024)} %param.17) | copy-start | bytes 24580
  20.5 100.3 %all-to-all-start = ((bf16[8,64,8192]{2,1,0:T(8,128)(2,1)}), bf16[8,64,8192]{2,1,0:T(8,128)(2,1)}, u32[]{:S(2)}, u32[]{:S(2)}) async-start(bf16[8,64,8192]{2,1,0:T(8,128)(2,1)} %bitcast.73), calls=%async_computation | async-start | bytes 16777216 | tf_op jit(solution)/shard_map/all_to_all | solution.py:136
  120.7 5.9 %copy-start.7 = (f32[8192]{0:T(1024)S(1)}, f32[8192]{0:T(1024)}, u32[]{:S(2)}) copy-start(f32[8192]{0:T(1024)} %param.15) | copy-start | bytes 98308
  126.6 2.0 %copy-start.4 = (bf16[256,8192]{1,0:T(8,128)(2,1)}, bf16[256,8192]{1,0:T(8,128)(2,1)S(1)}, u32[]{:S(2)}) copy-start(bf16[256,8192]{1,0:T(8,128)(2,1)S(1)} %get-tuple-element.53) | copy-start | bytes 12582916
  128.6 3.2 %copy-start.3 = (bf16[256,8192]{1,0:T(8,128)(2,1)}, bf16[256,8192]{1,0:T(8,128)(2,1)S(1)}, u32[]{:S(2)}) copy-start(bf16[256,8192]{1,0:T(8,128)(2,1)S(1)} %fusion.2) | copy-start | bytes 12582916
  131.8 7.8 %collective-permute-start = (bf16[128,8192]{1,0:T(8,128)(2,1)}, bf16[128,8192]{1,0:T(8,128)(2,1)S(1)}, u32[]{:S(2)}, u32[]{:S(2)}) collective-permute-start(bf16[128,8192]{1,0:T(8,128)(2,1)} %get-tuple-element.36), channel_id=1, source_target_pairs={{0,1},{1,0},{2,3},{3,2},{4,5},{5,4},{6,7},{7,6},{8,9},{9,8},{10,11... | collective-permute-start | bytes 6291464 | tf_op jit(solution)/shard_map/ppermute | solution.py:149
  132.7 7.1 %collective-permute-start.1 = (bf16[128,8192]{1,0:T(8,128)(2,1)}, bf16[128,8192]{1,0:T(8,128)(2,1)}, u32[]{:S(2)}, u32[]{:S(2)}) collective-permute-start(bf16[128,8192]{1,0:T(8,128)(2,1)} %get-tuple-element.37), channel_id=1, source_target_pairs={{0,1},{1,0},{2,3},{3,2},{4,5},{5,4},{6,7},{7,6},{8,9},{9,8},{10,11... | collective-permute-start | bytes 6291464 | tf_op jit(solution)/shard_map/ppermute | solution.py:150
  144.1 14.6 %copy-start.5 = (bf16[256,8192]{1,0:T(8,128)(2,1)S(1)}, bf16[256,8192]{1,0:T(8,128)(2,1)}, u32[]{:S(2)}) copy-start(bf16[256,8192]{1,0:T(8,128)(2,1)} %pad_maximum_fusion) | copy-start | bytes 12582916
  144.1 14.6 %copy-start.9 = (bf16[8192,1024]{1,0:T(8,128)(2,1)S(1)}, bf16[8192,1024]{1,0:T(8,128)(2,1)}, u32[]{:S(2)}) copy-start(bf16[8192,1024]{1,0:T(8,128)(2,1)} %all-gather.2.cloned.1.call-done) | copy-start | bytes 50331652
  155.8 9.6 %collective-permute-start.2 = (bf16[256,256]{1,0:T(8,128)(2,1)S(1)}, bf16[256,256]{1,0:T(8,128)(2,1)S(1)}, u32[]{:S(2)}, u32[]{:S(2)}) collective-permute-start(bf16[256,256]{1,0:T(8,128)(2,1)S(1)} %get-tuple-element.43), channel_id=1, source_target_pairs={{0,4},{2,6},{4,0},{6,2},{1,5},{3,7},{5,1},{7,3},{8,12},{10,14},{12... | collective-permute-start | bytes 393224 | tf_op jit(solution)/shard_map/ppermute | solution.py:164
  156.0 12.0 %collective-permute-start.3 = (bf16[256,256]{1,0:T(8,128)(2,1)S(1)}, bf16[256,256]{1,0:T(8,128)(2,1)S(1)}, u32[]{:S(2)}, u32[]{:S(2)}) collective-permute-start(bf16[256,256]{1,0:T(8,128)(2,1)S(1)} %get-tuple-element.42), channel_id=1, source_target_pairs={{0,2},{2,4},{4,6},{6,0},{1,3},{3,5},{5,7},{7,1},{8,10},{10,12},{12... | collective-permute-start | bytes 393224 | tf_op jit(solution)/shard_map/ppermute | solution.py:164
  157.4 10.6 %collective-permute-start.4 = (bf16[256,256]{1,0:T(8,128)(2,1)S(1)}, bf16[256,256]{1,0:T(8,128)(2,1)S(1)}, u32[]{:S(2)}, u32[]{:S(2)}) collective-permute-start(bf16[256,256]{1,0:T(8,128)(2,1)S(1)} %get-tuple-element.41), channel_id=1, source_target_pairs={{0,6},{2,0},{4,2},{6,4},{1,7},{3,1},{5,3},{7,5},{8,14},{10,8},{12,... | collective-permute-start | bytes 393224 | tf_op jit(solution)/shard_map/ppermute | solution.py:164
  158.7 14.5 %copy-start.1 = (bf16[512,2048]{1,0:T(8,128)(2,1)S(1)}, bf16[512,2048]{1,0:T(8,128)(2,1)}, u32[]{:S(2)}) copy-start(bf16[512,2048]{1,0:T(8,128)(2,1)} %param.16) | copy-start | bytes 6291460
  163.3 5.4 %collective-permute-start.5 = (bf16[256,256]{1,0:T(8,128)(2,1)S(1)}, bf16[256,256]{1,0:T(8,128)(2,1)S(1)}, u32[]{:S(2)}, u32[]{:S(2)}) collective-permute-start(bf16[256,256]{1,0:T(8,128)(2,1)S(1)} %get-tuple-element.40), channel_id=1, source_target_pairs={{0,4},{2,6},{4,0},{6,2},{1,5},{3,7},{5,1},{7,3},{8,12},{10,14},{12... | collective-permute-start | bytes 393224 | tf_op jit(solution)/shard_map/ppermute | solution.py:164
  165.1 7.0 %collective-permute-start.6 = (bf16[256,256]{1,0:T(8,128)(2,1)S(1)}, bf16[256,256]{1,0:T(8,128)(2,1)S(1)}, u32[]{:S(2)}, u32[]{:S(2)}) collective-permute-start(bf16[256,256]{1,0:T(8,128)(2,1)S(1)} %get-tuple-element.39), channel_id=1, source_target_pairs={{0,2},{2,4},{4,6},{6,0},{1,3},{3,5},{5,7},{7,1},{8,10},{10,12},{12... | collective-permute-start | bytes 393224 | tf_op jit(solution)/shard_map/ppermute | solution.py:164
  165.5 6.6 %collective-permute-start.7 = (bf16[256,256]{1,0:T(8,128)(2,1)S(1)}, bf16[256,256]{1,0:T(8,128)(2,1)S(1)}, u32[]{:S(2)}, u32[]{:S(2)}) collective-permute-start(bf16[256,256]{1,0:T(8,128)(2,1)S(1)} %get-tuple-element.38), channel_id=1, source_target_pairs={{0,6},{2,0},{4,2},{6,4},{1,7},{3,1},{5,3},{7,5},{8,14},{10,8},{12,... | collective-permute-start | bytes 393224 | tf_op jit(solution)/shard_map/ppermute | solution.py:164
Sparse Core Ops, SparseCore 0:
  12.3 114.6 all-gather.1
